TPU v7x, 32 devices: a whole 2x2x4 slice. The times are simulated.
32 devices in a mesh: img: 4 (over z), seq: 4 (over x, core), head: 2 (over y).
Axes of the slice: x: 2, y: 2, z: 4, core: 2. Of those that a mesh axis runs over, the one named last changes fastest.
Arguments:
- self_qkv: bfloat16 [4, 1024, 3072], P('img', ('seq', 'head')), may hold values from -12 to 12
- cross_query: bfloat16 [4, 1024, 1024], P('img', ('seq', 'head')), may hold values from -12 to 12
- thermal_kv: bfloat16 [4, 8, 256, 2048], P('img', ('seq', 'head')), may hold values from -12 to 12
- owners: int32 [4], P('img'), may hold values from 0 to 7
- grad_out: bfloat16 [4, 1024, 1024], P('img', ('seq', 'head')), may hold values from -6 to 6
Outputs:
- combined: bfloat16 [4, 1024, 1024], P('img', ('seq', 'head'))
- grad_qkv: bfloat16 [4, 1024, 3072], P('img', ('seq', 'head'))
- grad_cross_query: bfloat16 [4, 1024, 1024], P('img', ('seq', 'head'))
- grad_thermal: bfloat16 [4, 256, 2048], P('img', ('seq', 'head'))
All inputs are finite; a program needn't handle non-finite values.
Results may differ from a plain program's by a relative error of at most 0.012.
The roundings to bfloat16 on the way count: a program that leaves them out, or rounds other values in their place, can miss the bound.
Values may be sent and summed in bfloat16 or wider, within the bound.
No kernel may reach another device: no remote copies, remote signals or barrier semaphores. Data moves between devices by JAX's collectives and lax.ppermute only.
A program may use at most 128 MiB of HBM per device.

v0:
```python
import math

import jax
import jax.numpy as jnp
from jax import lax
from jax.sharding import PartitionSpec as P

HEADS = 16
HD = 64


def spread(block, axis, owner):
    block = jnp.where(lax.axis_index(axis) == owner, block, jnp.zeros_like(block))
    return lax.psum(block, axis)


def log_total(scores):
    row_max = jnp.max(scores, axis=-1, keepdims=True)
    return row_max + jnp.log(jnp.sum(jnp.exp(scores - row_max), axis=-1, keepdims=True))


def output_delta(upstream, mixed):
    return jnp.sum(upstream.astype(jnp.float32) * mixed, axis=-1).T[:, :, None]


def cross_block(cross_heads, upstream, thermal_keys, thermal_values, score_scale):
    cross_scores = (
        jnp.einsum("qhd,khd->hqk", cross_heads, thermal_keys, preferred_element_type=jnp.float32)
        * score_scale
    )
    cross_lse = log_total(cross_scores)
    cross_probs = jnp.exp(cross_scores - cross_lse).astype(jnp.bfloat16)
    cross_mixed = jnp.einsum(
        "hqk,khd->qhd", cross_probs, thermal_values, preferred_element_type=jnp.float32
    )
    cross_dprobs = jnp.einsum(
        "qhd,khd->hqk", upstream, thermal_values, preferred_element_type=jnp.float32
    )
    cross_delta = output_delta(upstream, cross_mixed)
    cross_dscores = (
        cross_probs.astype(jnp.float32) * (cross_dprobs - cross_delta) * score_scale
    ).astype(jnp.bfloat16)
    cross_dq = jnp.einsum(
        "hqk,khd->qhd", cross_dscores, thermal_keys, preferred_element_type=jnp.float32
    )
    return (cross_mixed, cross_probs, cross_dscores, cross_dq)


def thermal_sums(cross_probs, cross_dscores, cross_heads, upstream, row_span):
    key_grad = jnp.einsum(
        "hqk,qhd->khd", cross_dscores, cross_heads, preferred_element_type=jnp.float32
    )
    value_grad = jnp.einsum(
        "hqk,qhd->khd", cross_probs, upstream, preferred_element_type=jnp.float32
    )
    width = key_grad.shape[1] * key_grad.shape[2]
    return jnp.concatenate(
        [key_grad.reshape(row_span, width), value_grad.reshape(row_span, width)], axis=1
    )


def body(self_qkv, cross_query, thermal_kv, owners, grad_out):
    tokens_here = self_qkv.shape[1]
    model_width = cross_query.shape[2]
    head_devices = lax.axis_size("head")
    heads_local = HEADS // head_devices
    local_width = heads_local * HD
    score_scale = 1.0 / math.sqrt(HD)
    thermal_rows = thermal_kv.shape[2]
    packed = self_qkv[0].reshape(tokens_here, 3, head_devices, local_width)
    by_heads = lax.all_to_all(packed, "head", split_axis=2, concat_axis=0, tiled=True)
    row_count = by_heads.shape[0]
    query_flat = by_heads[:, 0, 0]
    keys_all, values_all = (
        lax.all_gather(by_heads[:, 1, 0], "seq", axis=0, tiled=True),
        lax.all_gather(by_heads[:, 2, 0], "seq", axis=0, tiled=True),
    )
    key_rows = keys_all.shape[0]
    query_here = query_flat.reshape(row_count, heads_local, HD)
    keys_heads = keys_all.reshape(key_rows, heads_local, HD)
    values_heads = values_all.reshape(key_rows, heads_local, HD)
    scores = (
        jnp.einsum("qhd,khd->hqk", query_here, keys_heads, preferred_element_type=jnp.float32)
        * score_scale
    )
    self_lse = log_total(scores)
    self_probs = jnp.exp(scores - self_lse).astype(jnp.bfloat16)
    attended_wide = jnp.einsum(
        "hqk,khd->qhd", self_probs, values_heads, preferred_element_type=jnp.float32
    )
    attended_heads = attended_wide.astype(jnp.bfloat16)
    attended = lax.all_to_all(
        attended_heads.reshape(row_count, 1, local_width),
        "head",
        split_axis=0,
        concat_axis=1,
        tiled=True,
    )
    attended = attended.reshape(tokens_here, model_width)
    thermal = spread(thermal_kv[0, 0], ("seq", "head"), owners[0])
    cross_in = (attended.astype(jnp.float32) + cross_query[0].astype(jnp.float32)).astype(
        jnp.bfloat16
    )
    cross_heads = cross_in.reshape(tokens_here, HEADS, HD)
    upstream = grad_out[0].reshape(tokens_here, HEADS, HD)
    thermal_keys = thermal[:, :model_width].reshape(thermal_rows, HEADS, HD)
    thermal_values = thermal[:, model_width:].reshape(thermal_rows, HEADS, HD)
    cross_mixed, cross_probs, cross_dscores, cross_dq = cross_block(
        cross_heads, upstream, thermal_keys, thermal_values, score_scale
    )
    combined = (
        attended.astype(jnp.float32) + cross_mixed.reshape(tokens_here, model_width)
    ).astype(jnp.bfloat16)
    cross_dq = cross_dq.reshape(tokens_here, model_width)
    group_devices = lax.axis_size("seq") * head_devices
    grad_thermal = lax.psum_scatter(
        thermal_sums(
            cross_probs,
            cross_dscores,
            cross_heads,
            upstream,
            lax.axis_size(("seq", "head")) * (thermal_rows // group_devices),
        ),
        ("seq", "head"),
        scatter_dimension=0,
        tiled=True,
    ).astype(jnp.bfloat16)
    grad_cross = cross_dq.astype(jnp.bfloat16)
    attended_grad = (grad_out[0].astype(jnp.float32) + cross_dq).astype(jnp.bfloat16)
    grad_heads = lax.all_to_all(
        attended_grad.reshape(tokens_here, head_devices, local_width),
        "head",
        split_axis=1,
        concat_axis=0,
        tiled=True,
    )
    grad_flat = grad_heads.reshape(row_count, local_width)
    grad_here = grad_flat.reshape(row_count, heads_local, HD)
    self_dprobs = jnp.einsum(
        "qhd,khd->hqk", grad_here, values_heads, preferred_element_type=jnp.float32
    )
    self_delta = output_delta(grad_here, attended_wide)
    self_dscores = (
        self_probs.astype(jnp.float32) * (self_dprobs - self_delta) * score_scale
    ).astype(jnp.bfloat16)
    query_grad = jnp.einsum(
        "hqk,khd->qhd", self_dscores, keys_heads, preferred_element_type=jnp.float32
    )
    query_grad = query_grad.reshape(row_count, local_width)
    key_grad = jnp.einsum(
        "hqk,qhd->khd", self_dscores, query_here, preferred_element_type=jnp.float32
    )
    value_grad = jnp.einsum(
        "hqk,qhd->khd", self_probs, grad_here, preferred_element_type=jnp.float32
    )
    own_grads = lax.psum_scatter(
        jnp.concatenate(
            [
                key_grad.reshape(lax.axis_size("seq") * row_count, local_width),
                value_grad.reshape(lax.axis_size("seq") * row_count, local_width),
            ],
            axis=1,
        ),
        "seq",
        scatter_dimension=0,
        tiled=True,
    )
    key_own = own_grads[:, :local_width]
    value_own = own_grads[:, local_width:]
    stacked = jnp.stack([query_grad, key_own, value_own], axis=1).astype(jnp.bfloat16)
    stacked = stacked.reshape(row_count, 3, 1, local_width)
    grad_qkv = lax.all_to_all(stacked, "head", split_axis=0, concat_axis=2, tiled=True).reshape(
        tokens_here, 3 * model_width
    )
    return (combined[None], grad_qkv[None], grad_cross[None], grad_thermal[None])


def solution(mesh):
    placed = (
        P("img", ("seq", "head"), None),
        P("img", ("seq", "head"), None),
        P("img", ("seq", "head"), None, None),
        P("img"),
        P("img", ("seq", "head"), None),
    )
    return jax.shard_map(
        body,
        mesh=mesh,
        in_specs=placed,
        out_specs=(
            P("img", ("seq", "head"), None),
            P("img", ("seq", "head"), None),
            P("img", ("seq", "head"), None),
            P("img", ("seq", "head"), None),
        ),
        check_vma=False,
    )
```

profile of v0, /device:TPU:0, one launch (start us, length us, event | category | flops | bytes accessed | tf_op | source)
XLA Modules:
  0.0 235.7 jit_solution(8329508114149124383)
XLA Ops:
  9.9 14.9 %all_to_all.57 = bf16[128,3,2,512]{3,0,1,2:T(8,128)(2,1)S(1)} all-to-all(bf16[128,3,2,512]{3,0,1,2:T(8,128)(2,1)S(1)} %copy.135), channel_id=1, replica_groups=mesh['img'=4,'seq'=4,'head'=2] {'head'}, dimensions={2} | all-to-all | bytes 1572864 | tf_op jit(solution)/shard_map/all_to_all | solution.py:71
  29.9 13.5 %all-gather.5.cloned.1.call-done = bf16[1024,1,1,512]{3,0,1,2:T(8,128)(2,1)} async-done(((bf16[256,1,1,512]{3,0,1,2:T(8,128)(2,1)}), bf16[1024,1,1,512]{3,0,1,2:T(8,128)(2,1)}) %all-gather.5.cloned.1.call-update) | async-done | bytes 1048592 | tf_op jit(solution)/shard_map/all_gather | solution.py:75
  46.3 1.7 exponential_reduce_fusion
  48.0 2.7 %exponential_convert_fusion = bf16[8,256,1024]{2,1,0:T(8,128)(2,1)} fusion(f32[8,256,1024]{2,1,0:T(8,128)S(1)} %get-tuple-element.40, f32[8,256]{1,0:T(8,128)S(1)} %log_add_fusion.1), kind=kLoop, calls=%fused_computation.1 | loop fusion | flops 6291456 | bytes 12591104 | tf_op jit(solution)/shard_map/convert_element_type | solution.py:87
  50.7 11.8 %all-gather.7.cloned.1.call-done = bf16[1024,1,1,512]{3,0,1,2:T(8,128)(2,1)} async-done(((bf16[256,1,1,512]{3,0,1,2:T(8,128)(2,1)}), bf16[1024,1,1,512]{3,0,1,2:T(8,128)(2,1)}) %all-gather.7.cloned.1.call-update) | async-done | bytes 1048592 | tf_op jit(solution)/shard_map/all_gather | solution.py:76
  64.0 4.8 %fusion.10 = (bf16[256,8,64]{0,2,1:T(8,128)(2,1)S(1)}, f32[256,8,64]{0,2,1:T(8,128)}) fusion(bf16[8,256,1024]{2,1,0:T(8,128)(2,1)} %exponential_convert_fusion, bf16[1024,8,64]{0,2,1:T(8,128)(2,1)S(1)} %bitcast.102), kind=kOutput, calls=%fused_computation.33 | convolution fusion | flops 268566528 | bytes 6029312 | tf_op jit(solution)/shard_map/hqk,khd->qhd/dot_general | solution.py:88
  71.1 3.4 %all-to-all-start.1 = ((bf16[2,2,32768]{2,1,0:T(2,128)(2,1)}), bf16[2,2,32768]{2,1,0:T(2,128)(2,1)S(1)}, u32[]{:S(2)}, u32[]{:S(2)}) async-start(bf16[2,2,32768]{2,1,0:T(2,128)(2,1)} %reshape.190), calls=%async_computation.1 | async-start | bytes 524288 | tf_op jit(solution)/shard_map/all_to_all | solution.py:92
  74.6 18.7 %all-reduce.2.cloned.1.call-done = bf16[256,2048]{1,0:T(8,128)(2,1)} async-done(((bf16[256,2048]{1,0:T(8,128)(2,1)}), bf16[256,2048]{1,0:T(8,128)(2,1)}) %all-reduce.2.cloned.1.call-update) | async-done | bytes 1048592 | tf_op jit(solution)/shard_map/psum | solution.py:14
  93.3 2.1 fusion.8
  105.4 7.6 %all_to_all.58 = bf16[128,2,512]{0,2,1:T(8,128)(2,1)S(1)} all-to-all(bf16[128,2,512]{0,2,1:T(8,128)(2,1)S(1)} %add_convert_fusion), channel_id=1, replica_groups=mesh['img'=4,'seq'=4,'head'=2] {'head'}, dimensions={1} | all-to-all | bytes 524288 | tf_op jit(solution)/shard_map/all_to_all | solution.py:130
  115.1 4.5 %fusion.11 = f32[8,64,1024]{2,1,0:T(8,128)} fusion(bf16[256,8,64]{0,2,1:T(8,128)(2,1)S(1)} %reshape_reshape.3, bf16[8,256,1024]{2,1,0:T(8,128)(2,1)} %exponential_convert_fusion), kind=kOutput, calls=%fused_computation.34 | convolution fusion | flops 268435456 | bytes 6553600 | tf_op jit(solution)/shard_map/hqk,qhd->khd/dot_general | solution.py:153
  119.7 1.9 multiply_convert_fusion
  121.7 1.9 copy-done.1
  123.6 2.2 fusion.12
  125.8 3.0 %copy.151 = f32[1024,512]{1,0:T(8,128)} copy(f32[1024,512]{0,1:T(8,128)} %bitcast.105) | data formatting | bytes 4194304 | tf_op jit(solution)/shard_map/reshape | solution.py:159
  128.8 2.9 %copy.152 = f32[1024,512]{1,0:T(8,128)} copy(f32[1024,512]{0,1:T(8,128)} %bitcast.104) | data formatting | bytes 4194304 | tf_op jit(solution)/shard_map/reshape | solution.py:160
  131.7 4.7 %pad_maximum_fusion = f32[1024,1024]{1,0:T(8,128)} fusion(f32[1024,512]{1,0:T(8,128)} %copy.152, f32[1024,512]{1,0:T(8,128)} %copy.151), kind=kLoop, calls=%fused_computation.4 | loop fusion | flops 1048576 | bytes 8388608 | tf_op jit(solution)/shard_map/concatenate | solution.py:157
  136.5 2.5 %fusion.4 = f32[16,64,256]{2,1,0:T(8,128)} fusion(bf16[16,128,256]{2,1,0:T(8,128)(2,1)S(1)} %fusion.1, f32[128,16,64]{0,2,1:T(8,128)} %bitcast.107, bf16[128,16,64]{0,2,1:T(8,128)(2,1)} %bitcast.125), kind=kOutput, calls=%fused_computation.29 | convolution fusion | flops 67502080 | bytes 2883584 | tf_op jit(solution)/shard_map/hqk,qhd->khd/dot_general | solution.py:50
  139.0 2.6 %copy.157 = f32[256,1024]{1,0:T(8,128)} copy(f32[256,1024]{0,1:T(8,128)} %bitcast.117) | data formatting | bytes 2097152 | tf_op jit(solution)/shard_map/reshape | solution.py:58
  143.2 3.8 %pad_maximum_fusion.1 = f32[256,2048]{1,0:T(8,128)} fusion(f32[256,1024]{1,0:T(8,128)} %copy.158, f32[256,1024]{1,0:T(8,128)} %copy.157), kind=kLoop, calls=%fused_computation.5 | loop fusion | flops 524288 | bytes 4194304 | tf_op jit(solution)/shard_map/concatenate | solution.py:57
  149.1 3.6 %convolution_convert_fusion = bf16[8,256,64]{1,2,0:T(8,128)(2,1)S(1)} fusion(bf16[8,256,1024]{2,1,0:T(8,128)(2,1)} %copy-done.1, bf16[1024,8,64]{0,2,1:T(8,128)(2,1)S(1)} %bitcast.101), kind=kOutput, calls=%fused_computation.13 | convolution fusion | flops 268566528 | bytes 5505024 | tf_op jit(solution)/shard_map/hqk,khd->qhd/dot_general | solution.py:146
  152.8 27.6 %reduce-scatter.3.cloned.1.call-done = f32[256,1024]{1,0:T(8,128)} async-done(((f32[1024,1024]{1,0:T(8,128)}), f32[256,1024]{1,0:T(8,128)}) %reduce-scatter.3.cloned.1.call-update) | async-done | bytes 1048592 | tf_op jit(solution)/shard_map/reduce_scatter | solution.py:156
  183.5 3.6 %all-to-all-start.3 = ((bf16[256,3,1,512]{3,1,2,0:T(4,128)(2,1)}), bf16[256,3,1,512]{3,1,2,0:T(4,128)(2,1)S(1)}, u32[]{:S(2)}, u32[]{:S(2)}) async-start(bf16[256,3,1,512]{3,1,2,0:T(4,128)(2,1)} %copy.154), calls=%async_computation.4 | async-start | bytes 2097152 | tf_op jit(solution)/shard_map/all_to_all | solution.py:172
  187.1 38.1 %reduce-scatter.5.cloned.1.call-done = f32[32,2048]{1,0:T(8,128)} async-done(((f32[256,2048]{1,0:T(8,128)}), f32[32,2048]{1,0:T(8,128)}) %reduce-scatter.5.cloned.1.call-update) | async-done | bytes 262160 | tf_op jit(solution)/shard_map/reduce_scatter | solution.py:116
  (100 shorter events, 35.3 us)
Async XLA Ops:
  8.0 19.3 %copy-start.17 = (bf16[1,1,256,2048]{3,2,1,0:T(8,128)(2,1)S(1)}, bf16[1,1,256,2048]{3,2,1,0:T(8,128)(2,1)}, u32[]{:S(2)}) copy-start(bf16[1,1,256,2048]{3,2,1,0:T(8,128)(2,1)} %param.7) | copy-start | bytes 3145732
  8.0 35.4 %all-gather.5.cloned.1.call-start = ((), (), s32[]{:S(2)}) async-start(), calls=%async_computation.9 | async-start | bytes 1310720 | tf_op jit(solution)/shard_map/all_gather | solution.py:75
  9.9 18.5 %copy-start.18 = (bf16[1,128,1024]{2,1,0:T(8,128)(2,1)S(1)}, bf16[1,128,1024]{2,1,0:T(8,128)(2,1)}, u32[]{:S(2)}) copy-start(bf16[1,128,1024]{2,1,0:T(8,128)(2,1)} %param.9) | copy-start | bytes 786436
  24.9 4.7 %copy-start.20 = (bf16[1,128,1024]{2,1,0:T(8,128)(2,1)S(1)}, bf16[1,128,1024]{2,1,0:T(8,128)(2,1)}, u32[]{:S(2)}) copy-start(bf16[1,128,1024]{2,1,0:T(8,128)(2,1)} %param.6) | copy-start | bytes 786436
  25.8 36.6 %all-gather.7.cloned.1.call-start = ((), (), s32[]{:S(2)}) async-start(), calls=%async_computation.10 | async-start | bytes 1310720 | tf_op jit(solution)/shard_map/all_gather | solution.py:76
  26.6 66.7 %all-reduce.2.cloned.1.call-start = ((), (), s32[]{:S(2)}) async-start(), calls=%async_computation.6 | async-start | bytes 2097152 | tf_op jit(solution)/shard_map/psum | solution.py:14
  28.6 73.9 %copy-start.9 = (bf16[1,128,1024]{1,2,0:T(8,128)(2,1)}, bf16[1,128,1024]{1,2,0:T(8,128)(2,1)S(1)}, u32[]{:S(2)}) copy-start(bf16[1,128,1024]{1,2,0:T(8,128)(2,1)S(1)} %copy.148) | copy-start | bytes 786436
  29.7 69.6 %copy-start.13 = (bf16[1,128,1024]{1,2,0:T(8,128)(2,1)}, bf16[1,128,1024]{1,2,0:T(8,128)(2,1)S(1)}, u32[]{:S(2)}) copy-start(bf16[1,128,1024]{1,2,0:T(8,128)(2,1)S(1)} %copy.144) | copy-start | bytes 786436
  29.9 16.4 %copy-start.11 = (bf16[256,1,1,512]{0,3,2,1:T(8,128)(2,1)}, bf16[256,1,1,512]{0,3,2,1:T(8,128)(2,1)S(1)}, u32[]{:S(2)}) copy-start(bf16[256,1,1,512]{0,3,2,1:T(8,128)(2,1)S(1)} %copy.137) | copy-start | bytes 786436
  64.0 31.4 %copy-start.2 = (bf16[1024,1,1,512]{0,3,2,1:T(8,128)(2,1)}, bf16[1024,1,1,512]{0,3,2,1:T(8,128)(2,1)S(1)}, u32[]{:S(2)}) copy-start(bf16[1024,1,1,512]{0,3,2,1:T(8,128)(2,1)S(1)} %copy.139) | copy-start | bytes 3145732
  71.1 25.9 %all-to-all-start.1 = ((bf16[2,2,32768]{2,1,0:T(2,128)(2,1)}), bf16[2,2,32768]{2,1,0:T(2,128)(2,1)S(1)}, u32[]{:S(2)}, u32[]{:S(2)}) async-start(bf16[2,2,32768]{2,1,0:T(2,128)(2,1)} %reshape.190), calls=%async_computation.1 | async-start | bytes 524288 | tf_op jit(solution)/shard_map/all_to_all | solution.py:92
  74.6 105.9 %reduce-scatter.3.cloned.1.call-start = ((), (), s32[]{:S(2)}) async-start(), calls=%async_computation.7 | async-start | bytes 5242880 | tf_op jit(solution)/shard_map/reduce_scatter | solution.py:156
  95.6 5.1 %copy-start.6 = (bf16[256,1024]{0,1:T(8,128)(2,1)}, bf16[256,1024]{0,1:T(8,128)(2,1)S(1)}, u32[]{:S(2)}) copy-start(bf16[256,1024]{0,1:T(8,128)(2,1)S(1)} %copy.145) | copy-start | bytes 1572868
  97.0 4.1 %copy-start.8 = (bf16[256,1024]{0,1:T(8,128)(2,1)}, bf16[256,1024]{0,1:T(8,128)(2,1)S(1)}, u32[]{:S(2)}) copy-start(bf16[256,1024]{0,1:T(8,128)(2,1)S(1)} %copy.143) | copy-start | bytes 1572868
  101.2 4.2 %copy-start.15 = (f32[1,128,1024]{1,2,0:T(8,128)S(1)}, f32[1,128,1024]{1,2,0:T(8,128)}, u32[]{:S(2)}) copy-start(f32[1,128,1024]{1,2,0:T(8,128)} %copy.147) | copy-start | bytes 1572868
  115.0 4.6 %copy-start.14 = (f32[256,8,64]{0,2,1:T(8,128)S(1)}, f32[256,8,64]{0,2,1:T(8,128)}, u32[]{:S(2)}) copy-start(f32[256,8,64]{0,2,1:T(8,128)} %get-tuple-element.42) | copy-start | bytes 1572868
  115.0 4.7 %copy-start = (bf16[8,256,1024]{2,1,0:T(8,128)(2,1)S(1)}, bf16[8,256,1024]{2,1,0:T(8,128)(2,1)}, u32[]{:S(2)}) copy-start(bf16[8,256,1024]{2,1,0:T(8,128)(2,1)} %exponential_convert_fusion) | copy-start | bytes 12582916
  115.1 4.7 %copy-start.3 = (bf16[1024,1,1,512]{0,3,2,1:T(8,128)(2,1)S(1)}, bf16[1024,1,1,512]{0,3,2,1:T(8,128)(2,1)}, u32[]{:S(2)}) copy-start(bf16[1024,1,1,512]{0,3,2,1:T(8,128)(2,1)} %copy-done.2) | copy-start | bytes 3145732
  136.4 5.1 %copy-start.10 = (bf16[1,128,1024]{1,2,0:T(8,128)(2,1)S(1)}, bf16[1,128,1024]{1,2,0:T(8,128)(2,1)}, u32[]{:S(2)}) copy-start(bf16[1,128,1024]{1,2,0:T(8,128)(2,1)} %copy-done.9) | copy-start | bytes 786436
  136.4 88.8 %reduce-scatter.5.cloned.1.call-start = ((), (), s32[]{:S(2)}) async-start(), calls=%async_computation.8 | async-start | bytes 2359296 | tf_op jit(solution)/shard_map/reduce_scatter | solution.py:116
  141.8 5.2 %copy-start.19 = (bf16[128,16,64]{0,2,1:T(8,128)(2,1)S(1)}, bf16[128,16,64]{0,2,1:T(8,128)(2,1)}, u32[]{:S(2)}) copy-start(bf16[128,16,64]{0,2,1:T(8,128)(2,1)} %get-tuple-element.47) | copy-start | bytes 786436
  143.2 4.7 %copy-start.16 = (f32[16,64,128]{2,1,0:T(8,128)S(1)}, f32[16,64,128]{2,1,0:T(8,128)}, u32[]{:S(2)}) copy-start(f32[16,64,128]{2,1,0:T(8,128)} %get-tuple-element.46) | copy-start | bytes 1572868
  143.2 4.9 %copy-start.5 = (f32[2,128,1,512]{1,3,0,2:T(8,128)S(1)}, f32[2,128,1,512]{1,3,0,2:T(8,128)}, u32[]{:S(2)}) copy-start(f32[2,128,1,512]{1,3,0,2:T(8,128)} %copy-done.4) | copy-start | bytes 1572868
  183.5 43.3 %all-to-all-start.3 = ((bf16[256,3,1,512]{3,1,2,0:T(4,128)(2,1)}), bf16[256,3,1,512]{3,1,2,0:T(4,128)(2,1)S(1)}, u32[]{:S(2)}, u32[]{:S(2)}) async-start(bf16[256,3,1,512]{3,1,2,0:T(4,128)(2,1)} %copy.154), calls=%async_computation.4 | async-start | bytes 2097152 | tf_op jit(solution)/shard_map/all_to_all | solution.py:172
  (4 other events, 10.6 us)
Sparse Core Ops, SparseCore 0:
  26.0 17.3 all-gather.4
  45.5 16.9 all-gather.6
  136.6 43.8 reduce-scatter.2
  183.9 41.2 reduce-scatter.4
Sparse Core Ops, SparseCore 1:
  30.2 63.0 all-reduce.1
where the time goes:
time: 237 us; the launch traced here: 236 us
  waiting for transfers between devices  110 us (46%)
  local copies, waits for them, and re-layouts  33.4 us (14%)
  matrix products  25.9 us (11%)
  blocking collectives  22.5 us (9%)
  other arithmetic  20 us (8%)
  between operations  16.3 us (7%)
  starting transfers between devices  7.23 us (3%)
    reduce_scatter x1, waiting for transfers between devices, body(): lax.psum_scatter(thermal_sums(cross_probs, cross_dscores, cross_heads, up...  38.1 us
    reduce_scatter x1, waiting for transfers between devices, body(): lax.psum_scatter(jnp.concatenate([key_grad.reshape(lax.axis_size('seq') *...  27.6 us
    psum x1, waiting for transfers between devices, spread(): return lax.psum(block, axis)  18.7 us
    all_to_all x1, blocking collectives, body(): lax.all_to_all(packed, 'head', split_axis=2, concat_axis=0, tiled=True)  14.9 us
    all_gather x1, waiting for transfers between devices, body(): lax.all_gather(by_heads[:, 1, 0], 'seq', axis=0, tiled=True)  13.5 us
    all_gather x1, waiting for transfers between devices, body(): lax.all_gather(by_heads[:, 2, 0], 'seq', axis=0, tiled=True)  11.8 us
    unnamed x50, local copies, waits for them, and re-layouts  7.98 us
    all_to_all x1, blocking collectives, body(): lax.all_to_all(attended_grad.reshape(tokens_here, head_devices, local_wid...  7.56 us
  transfers between devices with their start and end apart: 7, of which 5 were waited for; matrix products, arithmetic and copies ran while one was open for 18% of the time, Pallas kernels for 0%

commit v1 on v0

v1 whole, which is shorter than its diff:
```python
import functools
import math

import jax
import jax.numpy as jnp
from jax import lax
from jax.experimental import pallas as pl
from jax.experimental.pallas import tpu as pltpu
from jax.sharding import PartitionSpec as P
BF=jnp.bfloat16; F=jnp.float32
HD=64
VM=pl.BlockSpec(memory_space=pltpu.VMEM)
NT=(((1,),(1,)),((),()))
def dot(a,b): return jnp.dot(a,b,preferred_element_type=F)
def dot_nt(a,b): return lax.dot_general(a,b,NT,preferred_element_type=F)
def tr(x): return x.T
def head_only(x,h):
    if x.shape[-1]==HD: return x
    lane=lax.broadcasted_iota(jnp.int32,x.shape,1)
    return jnp.where((lane>=h*HD)&(lane<(h+1)*HD),x,jnp.zeros_like(x))
def softmax_t(sT):
    c=1.0/math.sqrt(HD)
    m=jnp.max(sT,axis=0,keepdims=True)
    e=jnp.exp((sT-m)*c)
    l=jnp.sum(e,axis=0,keepdims=True)
    return (e*(1.0/l)).astype(BF)
def self_fwd_kernel(qkv_ref,pT_ref,oT_ref,vT_ref,*,QB):
    G,R,W3=qkv_ref.shape; W=W3//3; L=G*R; Hl=W//HD
    nb=QB//R
    k=qkv_ref[:,:,W:2*W].reshape(L,W)
    vT_ref[...]=tr(qkv_ref[:,:,2*W:].reshape(L,W))
    for h in range(Hl):
        for b in range(L//QB):
            q=qkv_ref[b*nb:(b+1)*nb,:,:W].reshape(QB,W)
            p=softmax_t(dot_nt(k,head_only(q,h)))
            pT_ref[h,:,b*QB:(b+1)*QB]=p
            oT_ref[h*HD:(h+1)*HD,b*QB:(b+1)*QB]=dot(vT_ref[h*HD:(h+1)*HD,:],p)
def self_fwd(qkv,QB=256):
    G,R,W3=qkv.shape; W=W3//3; L=G*R; Hl=W//HD
    return pl.pallas_call(functools.partial(self_fwd_kernel,QB=QB),
        out_shape=(jax.ShapeDtypeStruct((Hl,L,L),BF),jax.ShapeDtypeStruct((W,L),F)),
        in_specs=[VM],out_specs=(VM,VM),scratch_shapes=[pltpu.VMEM((W,L),BF)],name="self_fwd",
        compiler_params=pltpu.CompilerParams(vmem_limit_bytes=56<<20))(qkv)
def self_bwd_kernel(qkv_ref,pT_ref,oT_ref,ag_ref,out_ref,kT_ref,dk_ref,dv_ref,*,QB):
    G,R,W3=qkv_ref.shape; W=W3//3; L=G*R; Hl=W//HD
    nb=QB//R; c=1.0/math.sqrt(HD)
    v=qkv_ref[:,:,2*W:].reshape(L,W)
    kT_ref[...]=tr(qkv_ref[:,:,W:2*W].reshape(L,W))
    for b in range(L//QB):
        ag=ag_ref[b*nb:(b+1)*nb].reshape(QB,W)
        q=qkv_ref[b*nb:(b+1)*nb,:,:W].reshape(QB,W)
        prod=tr(ag).astype(F)*oT_ref[:,b*QB:(b+1)*QB]
        dqs=[]
        for h in range(Hl):
            delta=jnp.sum(prod[h*HD:(h+1)*HD],axis=0,keepdims=True)
            agh=head_only(ag,h)
            p=pT_ref[h,:,b*QB:(b+1)*QB]
            dv=dot(p,agh)
            dp=dot_nt(v,agh)
            ds=(p.astype(F)*(dp-delta)).astype(BF)
            dk=dot(ds,head_only(q,h))
            dqs.append(dot(kT_ref[h*HD:(h+1)*HD,:],ds))
            if b==0 and h==0:
                dk_ref[...]=dk; dv_ref[...]=dv
            else:
                dk_ref[...]+=dk; dv_ref[...]+=dv
        dqT=jnp.concatenate(dqs,axis=0)*c
        out_ref[b*nb:(b+1)*nb,:,:W]=tr(dqT).astype(BF).reshape(nb,R,W)
    out_ref[:,:,W:2*W]=(dk_ref[...]*c).astype(BF).reshape(G,R,W)
    out_ref[:,:,2*W:]=dv_ref[...].astype(BF).reshape(G,R,W)
def self_bwd(qkv,pT,oT,ag,QB=256):
    G,R,W3=qkv.shape; W=W3//3; L=G*R
    return pl.pallas_call(functools.partial(self_bwd_kernel,QB=QB),
        out_shape=jax.ShapeDtypeStruct(qkv.shape,BF),
        in_specs=[VM]*4,out_specs=VM,scratch_shapes=[pltpu.VMEM((W,L),BF),pltpu.VMEM((L,W),F),pltpu.VMEM((L,W),F)],name="self_bwd",
        compiler_params=pltpu.CompilerParams(vmem_limit_bytes=56<<20))(qkv,pT,oT,ag)
def cross_kernel(idx_ref,oT_ref,cg_ref,out_ref,ag_ref,*,QB):
    G,RM,W2=cg_ref.shape; W=W2//2; L=oT_ref.shape[1]; R=L//G; M2=RM-R; M=2*M2; Hl=W//HD
    nb=QB//R; c=1.0/math.sqrt(HD)
    t0=cg_ref[idx_ref[0],R:,:]; t1=cg_ref[idx_ref[1],R:,:]
    t=jnp.concatenate([t0,t1],axis=0)
    tk=t[:,:W]; tv=t[:,W:]
    tkT=tr(tk); tvT=tr(tv)
    dtk=None; dtv=None
    for b in range(L//QB):
        at=tr(oT_ref[:,b*QB:(b+1)*QB]).astype(BF)
        cq=cg_ref[b*nb:(b+1)*nb,:R,:W].reshape(QB,W)
        go=cg_ref[b*nb:(b+1)*nb,:R,W:].reshape(QB,W)
        goT=tr(go).astype(F)
        x=(at.astype(F)+cq.astype(F)).astype(BF)
        mixs=[];dqs=[]
        for h in range(Hl):
            xh=head_only(x,h); gh=head_only(go,h)
            p=softmax_t(dot_nt(tk,xh))
            mix=dot(tvT[h*HD:(h+1)*HD],p)
            delta=jnp.sum(goT[h*HD:(h+1)*HD]*mix,axis=0,keepdims=True)
            dp=dot_nt(tv,gh)
            ds=(p.astype(F)*(dp-delta)).astype(BF)
            dqs.append(dot(tkT[h*HD:(h+1)*HD],ds))
            mixs.append(mix)
            a=dot(ds,xh); v=dot(p,gh)
            dtk=a if dtk is None else dtk+a
            dtv=v if dtv is None else dtv+v
        mix=tr(jnp.concatenate(mixs,axis=0)); dq=tr(jnp.concatenate(dqs,axis=0))*c
        out_ref[b*nb:(b+1)*nb,:R,:W]=(at.astype(F)+mix).astype(BF).reshape(nb,R,W)
        out_ref[b*nb:(b+1)*nb,:R,W:]=dq.astype(BF).reshape(nb,R,W)
        ag_ref[b*nb:(b+1)*nb]=(go.astype(F)+dq).astype(BF).reshape(nb,R,W)
    MR=M//G
    out_ref[:,R:,:W]=(dtk*c).astype(BF).reshape(G,MR,W)
    out_ref[:,R:,W:]=dtv.astype(BF).reshape(G,MR,W)
def cross(idx,oT,cg,R,QB=256):
    G,RM,W2=cg.shape; W=W2//2; L=oT.shape[1]; M=2*(RM-R)
    return pl.pallas_call(functools.partial(cross_kernel,QB=QB),
        out_shape=(jax.ShapeDtypeStruct((G,R+M//G,2*W),BF),jax.ShapeDtypeStruct((G,R,W),BF)),
        in_specs=[pl.BlockSpec(memory_space=pltpu.SMEM),VM,VM],out_specs=(VM,VM),name="cross",
        compiler_params=pltpu.CompilerParams(vmem_limit_bytes=56<<20))(idx,oT,cg)


HEADS = 16
GROUP = ("seq", "head")


def pack_qkv_kernel(x_ref, out_ref):
    G, R, W3 = out_ref.shape
    W = W3 // 3
    for j in range(G):
        for t in range(3):
            out_ref[j, :, t * W : (t + 1) * W] = x_ref[:, (t * G + j) * W : (t * G + j + 1) * W]


def pack_qkv(x, G):
    R, D3 = x.shape
    return pl.pallas_call(
        pack_qkv_kernel,
        out_shape=jax.ShapeDtypeStruct((G, R, D3 // G), BF),
        in_specs=[VM],
        out_specs=VM,
        name="pack_qkv",
    )(x)


def pack_rest_kernel(pick_ref, cq_ref, go_ref, t_ref, got_ref, out_ref):
    G, RM, W2 = out_ref.shape
    W = W2 // 2
    R = cq_ref.shape[0]
    half = got_ref.shape[0]
    start = pl.multiple_of(pick_ref[0] * half, half)
    own = t_ref[pl.ds(start, half), :]
    kept = jnp.where(pick_ref[1] == 1, own, got_ref[...])
    for j in range(G):
        out_ref[j, :R, :W] = cq_ref[:, j * W : (j + 1) * W]
        out_ref[j, :R, W:] = go_ref[:, j * W : (j + 1) * W]
        out_ref[j, R:, :W] = kept[:, j * W : (j + 1) * W]
        out_ref[j, R:, W:] = kept[:, (G + j) * W : (G + j + 1) * W]


def pack_rest(pick, cq, go, t, got, G):
    R, D = cq.shape
    return pl.pallas_call(
        pack_rest_kernel,
        out_shape=jax.ShapeDtypeStruct((G, R + got.shape[0], 2 * D // G), BF),
        in_specs=[pl.BlockSpec(memory_space=pltpu.SMEM), VM, VM, VM, VM],
        out_specs=VM,
        name="pack_rest",
    )(pick, cq, go, t, got)


def unpack_cross_kernel(x_ref, comb_ref, dcq_ref, dt_ref):
    G, RM, W2 = x_ref.shape
    W = W2 // 2
    R = comb_ref.shape[0]
    for j in range(G):
        comb_ref[:, j * W : (j + 1) * W] = x_ref[j, :R, :W]
        dcq_ref[:, j * W : (j + 1) * W] = x_ref[j, :R, W:]
        dt_ref[:, j * W : (j + 1) * W] = x_ref[j, R:, :W]
        dt_ref[:, (G + j) * W : (G + j + 1) * W] = x_ref[j, R:, W:]


def unpack_cross(x, R):
    G, RM, W2 = x.shape
    D = G * W2 // 2
    return pl.pallas_call(
        unpack_cross_kernel,
        out_shape=(
            jax.ShapeDtypeStruct((R, D), BF),
            jax.ShapeDtypeStruct((R, D), BF),
            jax.ShapeDtypeStruct((RM - R, 2 * D), BF),
        ),
        in_specs=[VM],
        out_specs=(VM, VM, VM),
        name="unpack_cross",
    )(x)


def unpack_qkv_kernel(x_ref, out_ref):
    G, R, W3 = x_ref.shape
    W = W3 // 3
    for j in range(G):
        for t in range(3):
            out_ref[:, (t * G + j) * W : (t * G + j + 1) * W] = x_ref[j, :, t * W : (t + 1) * W]


def unpack_qkv(x):
    G, R, W3 = x.shape
    return pl.pallas_call(
        unpack_qkv_kernel,
        out_shape=jax.ShapeDtypeStruct((R, G * W3), BF),
        in_specs=[VM],
        out_specs=VM,
        name="unpack_qkv",
    )(x)


def exchange(x):
    return lax.all_to_all(x, GROUP, split_axis=0, concat_axis=0, tiled=True)


def body(self_qkv, cross_query, thermal_kv, owners, grad_out):
    seq_size, head_size = lax.axis_size("seq"), lax.axis_size("head")
    G = seq_size * head_size
    R = self_qkv.shape[1]
    half = thermal_kv.shape[2] // 2
    side = lax.axis_index("seq") % 2
    owner = owners[0]
    owner_seq, owner_head = owner // head_size, owner % head_size
    thermal = thermal_kv[0, 0]
    handed = lax.dynamic_slice_in_dim(thermal, (1 - side) * half, half, axis=0)
    got = lax.ppermute(handed, "seq", [(s, s ^ 1) for s in range(seq_size)])
    pick = jnp.stack([side, (owner_seq % 2 == side).astype(jnp.int32)])
    pair = owner_seq - owner_seq % 2
    sources = jnp.stack([pair * head_size + owner_head, (pair + 1) * head_size + owner_head])
    qkv = exchange(pack_qkv(self_qkv[0], G))
    rest = exchange(pack_rest(pick, cross_query[0], grad_out[0], thermal, got, G))
    pT, oT = self_fwd(qkv)
    out, ag = cross(sources, oT, rest, R)
    out_back = exchange(out)
    dqkv_back = exchange(self_bwd(qkv, pT, oT, ag))
    combined, grad_cross, grad_thermal = unpack_cross(out_back, R)
    grad_qkv = unpack_qkv(dqkv_back)
    return (combined[None], grad_qkv[None], grad_cross[None], grad_thermal[None])


def solution(mesh):
    rows = P("img", GROUP, None)
    return jax.shard_map(
        body,
        mesh=mesh,
        in_specs=(rows, rows, P("img", GROUP, None, None), P("img"), rows),
        out_specs=(rows, rows, rows, rows),
        check_vma=False,
    )
```

time: 237 us -> 78.9 us (0.33)
  waiting for transfers between devices: 110 us -> 20.2 us
  Pallas kernels: 0 us -> 35.1 us
  local copies, waits for them, and re-layouts: 33.4 us -> 3.76 us
  matrix products: 25.9 us -> 0 us
  blocking collectives: 22.5 us -> 0 us
  other arithmetic: 20 us -> 1.17 us
  between operations: 16.3 us -> 1.39 us
  starting transfers between devices: 7.23 us -> 16.6 us
    reduce_scatter x2 -> x0, waiting for transfers between devices: 65.7 us -> none  [the longest x1 38.1 us: body(): lax.psum_scatter(thermal_sums(cross_probs, cross_dscores, cross_heads, up...]
    pallas_call x0 -> x7, Pallas kernels: none -> 35.1 us  [the longest x1 10.1 us: self_fwd(): pl.pallas_call(functools.partial(self_fwd_kernel, QB=QB), out_shape=(jax....]
    dot_general x12 -> x0, matrix products: 25.9 us -> none  [the longest x1 4.76 us: body(): jnp.einsum('hqk,khd->qhd', self_probs, values_heads, preferred_element_ty...]
    all_gather x2 -> x0, waiting for transfers between devices: 25.2 us -> none  [the longest x1 13.5 us: body(): lax.all_gather(by_heads[:, 1, 0], 'seq', axis=0, tiled=True)]
    all_to_all x2 -> x0, blocking collectives: 22.5 us -> none  [the longest x1 14.9 us: body(): lax.all_to_all(packed, 'head', split_axis=2, concat_axis=0, tiled=True)]
    all_to_all x2 -> x4, waiting for transfers between devices: 0.01 us -> 20 us  [exchange(): return lax.all_to_all(x, GROUP, split_axis=0, concat_axis=0, tiled=True)]
    psum x1 -> x0, waiting for transfers between devices: 18.7 us -> none  [spread(): return lax.psum(block, axis)]
    reshape x6 -> x0, local copies, waits for them, and re-layouts: 10.5 us -> none  [the longest x1 2.95 us: body(): key_grad.reshape(lax.axis_size('seq') * row_count, local_width)]
  transfers between devices with their start and end apart: 7 -> 5, of which waited for: 5 -> 5; matrix products, arithmetic and copies ran while one was open for 18% -> 3% of each run, Pallas kernels for 0% -> 30%
where the time goes in v1:
time: 78.9 us; the launch traced here: 78.2 us
  Pallas kernels  35.1 us (44%)
  waiting for transfers between devices  20.2 us (26%)
  starting transfers between devices  16.6 us (21%)
  local copies, waits for them, and re-layouts  3.76 us (5%)
  between operations  1.39 us (2%)
  other arithmetic  1.17 us (1%)
    all_to_all x4, waiting for transfers between devices, exchange(): return lax.all_to_all(x, GROUP, split_axis=0, concat_axis=0, tiled=True)  20 us
    all_to_all x4, starting transfers between devices, exchange(): return lax.all_to_all(x, GROUP, split_axis=0, concat_axis=0, tiled=True)  16 us
    pallas_call x1, Pallas kernels, self_fwd(): pl.pallas_call(functools.partial(self_fwd_kernel, QB=QB), out_shape=(jax....  10.1 us
    pallas_call x1, Pallas kernels, self_bwd(): pl.pallas_call(functools.partial(self_bwd_kernel, QB=QB), out_shape=jax.S...  8.42 us
    pallas_call x1, Pallas kernels, cross(): pl.pallas_call(functools.partial(cross_kernel, QB=QB), out_shape=(jax.Sha...  7.34 us
    pallas_call x1, Pallas kernels, pack_rest(): pl.pallas_call(pack_rest_kernel, out_shape=jax.ShapeDtypeStruct((G, R + g...  2.75 us
    unnamed x10, local copies, waits for them, and re-layouts  2.69 us
    pallas_call x1, Pallas kernels, unpack_qkv(): pl.pallas_call(unpack_qkv_kernel, out_shape=jax.ShapeDtypeStruct((R, G *...  2.24 us
  transfers between devices with their start and end apart: 5, of which 5 were waited for; matrix products, arithmetic and copies ran while one was open for 3% of the time, Pallas kernels for 30%

profile of v1, /device:TPU:0, one launch (start us, length us, event | category | flops | bytes accessed | tf_op | source)
XLA Modules:
  0.0 78.2 jit_solution(10133703236094347274)
XLA Ops:
  0.6 2.2 %pack_qkv.1 = bf16[8,128,384]{2,1,0:T(8,128)(2,1)} custom-call(bf16[128,3072]{1,0:T(8,128)(2,1)} %bitcast.20), custom_call_target="tpu_custom_call" | custom-call | tf_op jit(solution)/shard_map/pack_qkv/pallas_call | solution.py:133
  2.8 5.2 %all-to-all-start = ((bf16[8,128,384]{2,1,0:T(8,128)(2,1)}), bf16[8,128,384]{2,1,0:T(8,128)(2,1)S(1)}, u32[]{:S(2)}, u32[]{:S(2)}) async-start(bf16[8,128,384]{2,1,0:T(8,128)(2,1)} %pack_qkv.1), calls=%async_computation | async-start | bytes 1572864 | tf_op jit(solution)/shard_map/all_to_all | solution.py:215
  8.0 1.1 %dynamic-slice_bitcast_fusion = bf16[128,2048]{1,0:T(8,128)(2,1)S(1)} fusion(bf16[1,1,256,2048]{3,2,1,0:T(8,128)(2,1)} %param.7, s32[]{:T(128)S(6)} %select_n.28), kind=kLoop, calls=%fused_computation | loop fusion | bytes 1048580 | tf_op jit(solution)/shard_map/dynamic_slice | solution.py:227
  9.0 0.6 collective-permute-start
  10.3 0.6 pad_add_fusion.1.pick_ref
  10.9 0.3 collective-permute-done.got_ref
  11.1 0.8 %copy-done.4 = bf16[128,2048]{1,0:T(8,128)(2,1)} copy-done((bf16[128,2048]{1,0:T(8,128)(2,1)}, bf16[128,2048]{1,0:T(8,128)(2,1)S(1)}, u32[]{:S(2)}) %copy-start.4) | copy-done | bytes 524312
  11.9 2.8 %pack_rest.1 = bf16[8,256,256]{2,1,0:T(8,128)(2,1)} custom-call(s32[2]{0:T(128)} %pad_add_fusion.1.pick_ref, bf16[128,1024]{1,0:T(8,128)(2,1)} %bitcast.22, bf16[128,1024]{1,0:T(8,128)(2,1)} %bitcast.23, bf16[256,2048]{1,0:T(8,128)(2,1)} %bitcast.19, bf16[128,2048]{1,0:T(8,128)(2,1)} %copy-done.4), custom_call_target="tpu_custom_call" | custom-call | tf_op jit(solution)/shard_map/pack_rest/pallas_call | solution.py:159
  14.7 5.0 %all-to-all-done.qkv_ref = bf16[8,128,384]{2,1,0:T(8,128)(2,1)S(1)} async-done(((bf16[8,128,384]{2,1,0:T(8,128)(2,1)}), bf16[8,128,384]{2,1,0:T(8,128)(2,1)S(1)}, u32[]{:S(2)}, u32[]{:S(2)}) %all-to-all-start) | async-done | bytes 786464 | tf_op jit(solution)/shard_map/all_to_all | solution.py:215
  19.7 3.6 %all-to-all-start.1 = ((bf16[8,256,256]{2,1,0:T(8,128)(2,1)}), bf16[8,256,256]{2,1,0:T(8,128)(2,1)S(1)}, u32[]{:S(2)}, u32[]{:S(2)}) async-start(bf16[8,256,256]{2,1,0:T(8,128)(2,1)} %pack_rest.1), calls=%async_computation.1 | async-start | bytes 2097152 | tf_op jit(solution)/shard_map/all_to_all | solution.py:215
  23.3 0.6 pad_add_fusion.idx_ref
  23.9 0.0 copy-done
  23.9 10.1 %self_fwd.1 = (bf16[2,1024,1024]{2,1,0:T(8,128)(2,1)}, f32[128,1024]{1,0:T(8,128)}) custom-call(bf16[8,128,384]{2,1,0:T(8,128)(2,1)} %copy-done), custom_call_target="tpu_custom_call" | custom-call | tf_op jit(solution)/shard_map/self_fwd/pallas_call | solution.py:40
  34.0 3.8 %all-to-all-done.1.cg_ref = bf16[8,256,256]{2,1,0:T(8,128)(2,1)S(1)} async-done(((bf16[8,256,256]{2,1,0:T(8,128)(2,1)}), bf16[8,256,256]{2,1,0:T(8,128)(2,1)S(1)}, u32[]{:S(2)}, u32[]{:S(2)}) %all-to-all-start.1) | async-done | bytes 1048608 | tf_op jit(solution)/shard_map/all_to_all | solution.py:215
  37.7 1.0 %copy-done.1 = bf16[8,256,256]{2,1,0:T(8,128)(2,1)} copy-done((bf16[8,256,256]{2,1,0:T(8,128)(2,1)}, bf16[8,256,256]{2,1,0:T(8,128)(2,1)S(1)}, u32[]{:S(2)}) %copy-start.1) | copy-done | bytes 1048600
  38.7 7.3 %cross.1 = (bf16[8,160,256]{2,1,0:T(8,128)(2,1)}, bf16[8,128,128]{2,1,0:T(8,128)(2,1)}) custom-call(s32[2]{0:T(128)} %pad_add_fusion.idx_ref, f32[128,1024]{1,0:T(8,128)} %get-tuple-element.11.oT_ref, bf16[8,256,256]{2,1,0:T(8,128)(2,1)} %copy-done.1), custom_call_target="tpu_custom_call" | custom-call | tf_op jit(solution)/shard_map/cross/pallas_call | solution.py:113
  46.1 3.7 %all-to-all-start.2 = ((bf16[8,160,256]{2,1,0:T(8,128)(2,1)}), bf16[8,160,256]{2,1,0:T(8,128)(2,1)S(1)}, u32[]{:S(2)}, u32[]{:S(2)}) async-start(bf16[8,160,256]{2,1,0:T(8,128)(2,1)} %get-tuple-element.12), calls=%async_computation.2 | async-start | bytes 1310720 | tf_op jit(solution)/shard_map/all_to_all | solution.py:215
  49.8 8.4 %self_bwd.1 = bf16[8,128,384]{2,1,0:T(8,128)(2,1)} custom-call(bf16[8,128,384]{2,1,0:T(8,128)(2,1)} %copy-done, bf16[2,1024,1024]{2,1,0:T(8,128)(2,1)} %get-tuple-element.14.pT_ref, f32[128,1024]{1,0:T(8,128)} %get-tuple-element.11.oT_ref, bf16[8,128,128]{2,1,0:T(8,128)(2,1)} %get-tuple-element.15.ag_ref), custom_call_target="tpu_custom_call" | custom-call | tf_op jit(solution)/shard_map/self_bwd/pallas_call | solution.py:73
  58.2 1.6 %all-to-all-done.2.x_ref = bf16[8,160,256]{2,1,0:T(8,128)(2,1)S(1)} async-done(((bf16[8,160,256]{2,1,0:T(8,128)(2,1)}), bf16[8,160,256]{2,1,0:T(8,128)(2,1)S(1)}, u32[]{:S(2)}, u32[]{:S(2)}) %all-to-all-start.2) | async-done | bytes 655392 | tf_op jit(solution)/shard_map/all_to_all | solution.py:215
  59.8 3.5 %all-to-all-start.3 = ((bf16[8,128,384]{2,1,0:T(8,128)(2,1)}), bf16[8,128,384]{2,1,0:T(8,128)(2,1)S(1)}, u32[]{:S(2)}, u32[]{:S(2)}) async-start(bf16[8,128,384]{2,1,0:T(8,128)(2,1)} %self_bwd.1), calls=%async_computation.3 | async-start | bytes 1572864 | tf_op jit(solution)/shard_map/all_to_all | solution.py:215
  63.4 2.1 %unpack_cross.1 = (bf16[128,1024]{1,0:T(8,128)(2,1)}, bf16[128,1024]{1,0:T(8,128)(2,1)}, bf16[32,2048]{1,0:T(8,128)(2,1)}) custom-call(bf16[8,160,256]{2,1,0:T(8,128)(2,1)} %copy-done.3), custom_call_target="tpu_custom_call" | custom-call | tf_op jit(solution)/shard_map/unpack_cross/pallas_call | solution.py:182
  65.5 9.6 %all-to-all-done.3.x_ref = bf16[8,128,384]{2,1,0:T(8,128)(2,1)S(1)} async-done(((bf16[8,128,384]{2,1,0:T(8,128)(2,1)}), bf16[8,128,384]{2,1,0:T(8,128)(2,1)S(1)}, u32[]{:S(2)}, u32[]{:S(2)}) %all-to-all-start.3) | async-done | bytes 786464 | tf_op jit(solution)/shard_map/all_to_all | solution.py:215
  75.0 0.9 %copy-done.2 = bf16[8,128,384]{2,1,0:T(8,128)(2,1)} copy-done((bf16[8,128,384]{2,1,0:T(8,128)(2,1)}, bf16[8,128,384]{2,1,0:T(8,128)(2,1)S(1)}, u32[]{:S(2)}) %copy-start.2) | copy-done | bytes 786456
  75.9 2.2 %unpack_qkv.1 = bf16[128,3072]{1,0:T(8,128)(2,1)} custom-call(bf16[8,128,384]{2,1,0:T(8,128)(2,1)} %copy-done.2), custom_call_target="tpu_custom_call" | custom-call | tf_op jit(solution)/shard_map/unpack_qkv/pallas_call | solution.py:205
  (6 shorter events, 0.0 us)
Async XLA Ops:
  2.8 16.9 %all-to-all-start = ((bf16[8,128,384]{2,1,0:T(8,128)(2,1)}), bf16[8,128,384]{2,1,0:T(8,128)(2,1)S(1)}, u32[]{:S(2)}, u32[]{:S(2)}) async-start(bf16[8,128,384]{2,1,0:T(8,128)(2,1)} %pack_qkv.1), calls=%async_computation | async-start | bytes 1572864 | tf_op jit(solution)/shard_map/all_to_all | solution.py:215
  9.0 2.1 %collective-permute-start = (bf16[128,2048]{1,0:T(8,128)(2,1)S(1)}, bf16[128,2048]{1,0:T(8,128)(2,1)S(1)}, u32[]{:S(2)}, u32[]{:S(2)}) collective-permute-start(bf16[128,2048]{1,0:T(8,128)(2,1)S(1)} %dynamic-slice_bitcast_fusion), channel_id=1, source_target_pairs={{0,2},{2,0},{4,6},{6,4},{1,3},{3,1},{5,7},{7,5},{8,10},{10,8},{12,... | collective-permute-start | bytes 1572872 | tf_op jit(solution)/shard_map/ppermute | solution.py:228
  11.1 0.8 %copy-start.4 = (bf16[128,2048]{1,0:T(8,128)(2,1)}, bf16[128,2048]{1,0:T(8,128)(2,1)S(1)}, u32[]{:S(2)}) copy-start(bf16[128,2048]{1,0:T(8,128)(2,1)S(1)} %collective-permute-done.got_ref) | copy-start | bytes 1572868
  19.7 4.2 %copy-start = (bf16[8,128,384]{2,1,0:T(8,128)(2,1)}, bf16[8,128,384]{2,1,0:T(8,128)(2,1)S(1)}, u32[]{:S(2)}) copy-start(bf16[8,128,384]{2,1,0:T(8,128)(2,1)S(1)} %all-to-all-done.qkv_ref) | copy-start | bytes 2359300
  19.7 18.0 %all-to-all-start.1 = ((bf16[8,256,256]{2,1,0:T(8,128)(2,1)}), bf16[8,256,256]{2,1,0:T(8,128)(2,1)S(1)}, u32[]{:S(2)}, u32[]{:S(2)}) async-start(bf16[8,256,256]{2,1,0:T(8,128)(2,1)} %pack_rest.1), calls=%async_computation.1 | async-start | bytes 2097152 | tf_op jit(solution)/shard_map/all_to_all | solution.py:215
  37.7 1.0 %copy-start.1 = (bf16[8,256,256]{2,1,0:T(8,128)(2,1)}, bf16[8,256,256]{2,1,0:T(8,128)(2,1)S(1)}, u32[]{:S(2)}) copy-start(bf16[8,256,256]{2,1,0:T(8,128)(2,1)S(1)} %all-to-all-done.1.cg_ref) | copy-start | bytes 3145732
  46.1 13.8 %all-to-all-start.2 = ((bf16[8,160,256]{2,1,0:T(8,128)(2,1)}), bf16[8,160,256]{2,1,0:T(8,128)(2,1)S(1)}, u32[]{:S(2)}, u32[]{:S(2)}) async-start(bf16[8,160,256]{2,1,0:T(8,128)(2,1)} %get-tuple-element.12), calls=%async_computation.2 | async-start | bytes 1310720 | tf_op jit(solution)/shard_map/all_to_all | solution.py:215
  59.8 3.6 %copy-start.3 = (bf16[8,160,256]{2,1,0:T(8,128)(2,1)}, bf16[8,160,256]{2,1,0:T(8,128)(2,1)S(1)}, u32[]{:S(2)}) copy-start(bf16[8,160,256]{2,1,0:T(8,128)(2,1)S(1)} %all-to-all-done.2.x_ref) | copy-start | bytes 1966084
  59.8 15.2 %all-to-all-start.3 = ((bf16[8,128,384]{2,1,0:T(8,128)(2,1)}), bf16[8,128,384]{2,1,0:T(8,128)(2,1)S(1)}, u32[]{:S(2)}, u32[]{:S(2)}) async-start(bf16[8,128,384]{2,1,0:T(8,128)(2,1)} %self_bwd.1), calls=%async_computation.3 | async-start | bytes 1572864 | tf_op jit(solution)/shard_map/all_to_all | solution.py:215
  75.0 0.9 %copy-start.2 = (bf16[8,128,384]{2,1,0:T(8,128)(2,1)}, bf16[8,128,384]{2,1,0:T(8,128)(2,1)S(1)}, u32[]{:S(2)}) copy-start(bf16[8,128,384]{2,1,0:T(8,128)(2,1)S(1)} %all-to-all-done.3.x_ref) | copy-start | bytes 2359300

commit v2 on v0

v2 whole, which is shorter than its diff:
```python
import functools
import math

import jax
import jax.numpy as jnp
from jax import lax
from jax.experimental import pallas as pl
from jax.experimental.pallas import tpu as pltpu
from jax.sharding import PartitionSpec as P

BF = jnp.bfloat16
F32 = jnp.float32
HD = 64
GROUP = ("seq", "head")
VM = pl.BlockSpec(memory_space=pltpu.VMEM)
SM = pl.BlockSpec(memory_space=pltpu.SMEM)
SCALE = 1.0 / math.sqrt(HD)
MIB = 1 << 20


def sds(shape, dtype=BF):
    return jax.ShapeDtypeStruct(shape, dtype)


def call(kernel, name, ins, outs, mib, scratch=(), cost=None):
    smem = [a.dtype == jnp.int32 for a in ins]
    return pl.pallas_call(
        kernel,
        out_shape=outs,
        in_specs=[SM if s else VM for s in smem],
        out_specs=jax.tree.map(lambda _: VM, outs),
        scratch_shapes=scratch,
        name=name,
        cost_estimate=cost,
        compiler_params=pltpu.CompilerParams(vmem_limit_bytes=mib * MIB),
    )(*ins)


def dot(a, b):
    return jnp.dot(a, b, preferred_element_type=F32)


def dot_nt(a, b):
    return lax.dot_general(a, b, (((1,), (1,)), ((), ())), preferred_element_type=F32)


def head_only(x, h):
    if x.shape[-1] == HD:
        return x
    lane = lax.broadcasted_iota(jnp.int32, x.shape, 1)
    return jnp.where((lane >= h * HD) & (lane < (h + 1) * HD), x, jnp.zeros_like(x))


def softmax_t(scores):
    top = jnp.max(scores, axis=0, keepdims=True)
    e = jnp.exp((scores - top) * SCALE)
    return (e * (1.0 / jnp.sum(e, axis=0, keepdims=True))).astype(BF)


def split_sides(side, pair, W):
    low, high = pair[:, :W], pair[:, W:]
    return jnp.where(side == 0, low, high), jnp.where(side == 0, high, low)


def pack_qkv_kernel(meta_ref, x_ref, *msgs):
    R, W = msgs[0].shape[0], msgs[0].shape[1] // 3
    D = x_ref.shape[1] // 3
    side = meta_ref[0]
    for d in range(len(msgs) - 1):
        for t in range(3):
            start = pl.multiple_of(t * D + meta_ref[1 + d] * 2 * W, 2 * W)
            mine, other = split_sides(side, x_ref[:, pl.ds(start, 2 * W)], W)
            lanes = slice(t * W, (t + 1) * W)
            if d == 0:
                msgs[0][:, lanes] = mine
                msgs[1][:, lanes] = other
            else:
                msgs[d + 1][0, :, lanes] = mine
                msgs[d + 1][1, :, lanes] = other


def pack_rest_kernel(meta_ref, cq_ref, go_ref, t_ref, got_ref, *msgs):
    R, D = cq_ref.shape
    half = got_ref.shape[0]
    W = msgs[0].shape[1] // 2
    C = len(msgs) - 1
    side = meta_ref[0]
    own_rows = pl.ds(pl.multiple_of(side * half, half), half)
    keep = meta_ref[2 + C] == 1
    for d in range(C):
        for t in range(4):
            at = meta_ref[1 + d] * 2 * W
            if t == 0:
                pair = cq_ref[:, pl.ds(pl.multiple_of(at, 2 * W), 2 * W)]
            elif t == 1:
                pair = go_ref[:, pl.ds(pl.multiple_of(at, 2 * W), 2 * W)]
            else:
                cols = pl.ds(pl.multiple_of((t - 2) * D + at, 2 * W), 2 * W)
                pair = jnp.where(keep, t_ref[own_rows, cols], got_ref[:, cols])
            mine, other = split_sides(side, pair, W)
            rows = slice(0, R) if t < 2 else slice(R, R + half)
            lanes = slice((t % 2) * W, (t % 2 + 1) * W)
            if d == 0:
                msgs[0][rows, lanes] = mine
                msgs[1][rows, lanes] = other
            else:
                msgs[d + 1][0, rows, lanes] = mine
                msgs[d + 1][1, rows, lanes] = other


def message_shapes(C, rows, width, dtype=BF):
    return (sds((rows, width), dtype),) * 2 + (sds((2, rows, width), dtype),) * (C - 1)


def pieces(refs):
    C = len(refs) // 2
    out = []
    for d in range(C):
        if d == 0:
            out.append(lambda *ix, ref=refs[0]: ref[ix])
        else:
            out.append(lambda *ix, ref=refs[d]: ref[(0,) + ix])
        out.append(lambda *ix, ref=refs[C + d]: ref[ix])
    return out


def put(msgs, block, rows, lanes, value):
    d, e = block // 2, block % 2
    if d == 0:
        msgs[e][rows, lanes] = value
    else:
        msgs[d + 1][e, rows, lanes] = value


def self_fwd_kernel(*refs, C):
    blocks = pieces(refs[: 2 * C])
    pT_ref, oT_ref, k_ref, vT_ref = refs[2 * C :]
    L, W = k_ref.shape
    R = L // len(blocks)
    QB = 2 * R
    every = slice(None)
    for i, block in enumerate(blocks):
        k_ref[i * R : (i + 1) * R] = block(every, slice(W, 2 * W))
        vT_ref[:, i * R : (i + 1) * R] = block(every, slice(2 * W, 3 * W)).T
    k = k_ref[...]
    for b in range(C):
        q = jnp.concatenate([block(every, slice(0, W)) for block in blocks[2 * b : 2 * b + 2]])
        cols = slice(b * QB, (b + 1) * QB)
        for h in range(W // HD):
            rows = slice(h * HD, (h + 1) * HD)
            p = softmax_t(dot_nt(k, head_only(q, h)))
            pT_ref[h, :, cols] = p
            oT_ref[rows, cols] = dot(vT_ref[rows, :], p)


def cross_kernel(meta_ref, oT_ref, *refs, C):
    blocks = pieces(refs[: 2 * C])
    msgs = refs[2 * C : 3 * C + 1]
    ag_ref, t_ref, dt_ref = refs[3 * C + 1 :]
    W, L = oT_ref.shape
    M = t_ref.shape[0]
    half = M // 2
    R = L // len(blocks)
    QB = 2 * R
    every = slice(None)
    side = meta_ref[0]
    here = meta_ref[1 + C]
    for d in range(C):

        @pl.when(here == d)
        def _():
            t_ref[pl.ds(pl.multiple_of(side * half, half), half), :] = blocks[2 * d](slice(R, None), every)
            t_ref[pl.ds(pl.multiple_of((1 - side) * half, half), half), :] = blocks[2 * d + 1](
                slice(R, None), every
            )

    tk, tv = t_ref[:, :W], t_ref[:, W:]
    tkT, tvT = tk.T, tv.T
    dtk = dtv = None
    for b in range(C):
        pair = blocks[2 * b : 2 * b + 2]
        cq = jnp.concatenate([block(slice(0, R), slice(0, W)) for block in pair])
        go = jnp.concatenate([block(slice(0, R), slice(W, 2 * W)) for block in pair])
        att = oT_ref[:, b * QB : (b + 1) * QB].T.astype(BF).astype(F32)
        goT = go.T.astype(F32)
        x = (att + cq.astype(F32)).astype(BF)
        mixed, dqs = [], []
        for h in range(W // HD):
            rows = slice(h * HD, (h + 1) * HD)
            xh, gh = head_only(x, h), head_only(go, h)
            p = softmax_t(dot_nt(tk, xh))
            mix = dot(tvT[rows], p)
            delta = jnp.sum(goT[rows] * mix, axis=0, keepdims=True)
            ds = (p.astype(F32) * (dot_nt(tv, gh) - delta)).astype(BF)
            mixed.append(mix)
            dqs.append(dot(tkT[rows], ds))
            a, v = dot(ds, xh), dot(p, gh)
            dtk = a if dtk is None else dtk + a
            dtv = v if dtv is None else dtv + v
        dq = jnp.concatenate(dqs, axis=0).T * SCALE
        combined = (att + jnp.concatenate(mixed, axis=0).T).astype(BF)
        grad_cross = dq.astype(BF)
        ag_ref[b * QB : (b + 1) * QB] = (go.astype(F32) + dq).astype(BF)
        for e in range(2):
            part = slice(e * R, (e + 1) * R)
            put(msgs, 2 * b + e, slice(0, R), slice(0, W), combined[part])
            put(msgs, 2 * b + e, slice(0, R), slice(W, 2 * W), grad_cross[part])
    dt_ref[:, :W] = (dtk * SCALE).astype(BF)
    dt_ref[:, W:] = dtv.astype(BF)
    MR = M // (2 * C)
    for i in range(2 * C):
        start = pl.multiple_of(meta_ref[3 + C + i] * MR, MR)
        put(msgs, i, slice(R, R + MR), every, dt_ref[pl.ds(start, MR), :])


def self_bwd_kernel(*refs, C):
    blocks = pieces(refs[: 2 * C])
    pT_ref, oT_ref, ag_ref = refs[2 * C : 2 * C + 3]
    msgs = refs[2 * C + 3 : 3 * C + 4]
    v_ref, kT_ref, dk_ref, dv_ref = refs[3 * C + 4 :]
    L, W = v_ref.shape
    R = L // len(blocks)
    QB = 2 * R
    every = slice(None)
    for i, block in enumerate(blocks):
        v_ref[i * R : (i + 1) * R] = block(every, slice(2 * W, 3 * W))
        kT_ref[:, i * R : (i + 1) * R] = block(every, slice(W, 2 * W)).T
    v = v_ref[...]
    for b in range(C):
        cols = slice(b * QB, (b + 1) * QB)
        ag = ag_ref[cols]
        q = jnp.concatenate([block(every, slice(0, W)) for block in blocks[2 * b : 2 * b + 2]])
        product = ag.T.astype(F32) * oT_ref[:, cols]
        dqs = []
        for h in range(W // HD):
            rows = slice(h * HD, (h + 1) * HD)
            delta = jnp.sum(product[rows], axis=0, keepdims=True)
            agh = head_only(ag, h)
            p = pT_ref[h, :, cols]
            dv = dot(p, agh)
            ds = (p.astype(F32) * (dot_nt(v, agh) - delta)).astype(BF)
            dk = dot(ds, head_only(q, h))
            dqs.append(dot(kT_ref[rows, :], ds))
            if b == 0 and h == 0:
                dk_ref[...] = dk
                dv_ref[...] = dv
            else:
                dk_ref[...] += dk
                dv_ref[...] += dv
        dq = (jnp.concatenate(dqs, axis=0).T * SCALE).astype(BF)
        for e in range(2):
            put(msgs, 2 * b + e, every, slice(0, W), dq[e * R : (e + 1) * R])
    for i in range(len(blocks)):
        part = slice(i * R, (i + 1) * R)
        put(msgs, i, every, slice(W, 2 * W), (dk_ref[part] * SCALE).astype(BF))
        put(msgs, i, every, slice(2 * W, 3 * W), dv_ref[part].astype(BF))


def unpack_qkv_kernel(meta_ref, *refs, C):
    blocks = pieces(refs[: 2 * C])
    out_ref = refs[2 * C]
    D = out_ref.shape[1] // 3
    W = D // (2 * C)
    side = meta_ref[0]
    for d in range(C):
        for t in range(3):
            lanes = slice(t * W, (t + 1) * W)
            a, b = blocks[2 * d](slice(None), lanes), blocks[2 * d + 1](slice(None), lanes)
            start = pl.multiple_of(t * D + meta_ref[1 + d] * 2 * W, 2 * W)
            pair = jnp.concatenate([jnp.where(side == 0, a, b), jnp.where(side == 0, b, a)], axis=1)
            out_ref[:, pl.ds(start, 2 * W)] = pair


def unpack_cross_kernel(meta_ref, *refs, C):
    blocks = pieces(refs[: 2 * C])
    comb_ref, dcq_ref, dt_ref = refs[2 * C :]
    R, D = comb_ref.shape
    W = D // (2 * C)
    side = meta_ref[0]
    for d in range(C):
        for t in range(4):
            lanes = slice((t % 2) * W, (t % 2 + 1) * W)
            rows = slice(0, R) if t < 2 else slice(R, None)
            a, b = blocks[2 * d](rows, lanes), blocks[2 * d + 1](rows, lanes)
            pair = jnp.concatenate([jnp.where(side == 0, a, b), jnp.where(side == 0, b, a)], axis=1)
            at = meta_ref[1 + d] * 2 * W + (D if t == 3 else 0)
            cols = pl.ds(pl.multiple_of(at, 2 * W), 2 * W)
            (comb_ref, dcq_ref, dt_ref, dt_ref)[t][:, cols] = pair


def body(self_qkv, cross_query, thermal_kv, owners, grad_out):
    S, Hd = lax.axis_size("seq"), lax.axis_size("head")
    X = S // 2
    C = X * Hd
    R, D = cross_query.shape[1:]
    W = D // (2 * C)
    L = 2 * C * R
    M = thermal_kv.shape[2]
    half = M // 2
    MR = M // (2 * C)
    offsets = [(i, j) for j in range(Hd) for i in range(X)]
    s, h = lax.axis_index("seq"), lax.axis_index("head")
    side, x = s % 2, s // 2
    owner_s, owner_h = owners[0] // Hd, owners[0] % Hd
    away = (x - owner_s // 2 + X) % X + X * ((h - owner_h + Hd) % Hd)
    keep = (owner_s % 2 == side).astype(jnp.int32)
    chips = [((x + i) % X) * Hd + (h + j) % Hd for i, j in offsets]
    ids = []
    for i, j in offsets:
        for e in (0, 1):
            ids.append((((x - i + X) % X) * 2 + (side if e == 0 else 1 - side)) * Hd + (h - j + Hd) % Hd)
    meta = jnp.stack([side, *chips, away, keep, *ids]).astype(jnp.int32)

    def to_sibling(a):
        return lax.ppermute(a, "seq", [(i, i ^ 1) for i in range(S)])

    def to_chip(a, d, sign):
        i, j = offsets[d]
        pairs = []
        for p in range(S):
            for q in range(Hd):
                there = ((p // 2 + sign * i) % X) * 2 + p % 2
                pairs.append((p * Hd + q, there * Hd + (q + sign * j) % Hd))
        return lax.ppermute(a, GROUP, pairs)

    def exchange(msgs, sign):
        got = [to_chip(msgs[d + 1], d, sign) for d in range(1, C)]
        relayed = [to_sibling(msgs[1])] + [to_sibling(g[1]) for g in got]
        return [msgs[0], *got, *relayed]

    bind = functools.partial
    qkv = exchange(
        call(pack_qkv_kernel, "pack_qkv", [meta, self_qkv[0]], message_shapes(C, R, 3 * W), 8), 1
    )
    thermal = thermal_kv[0, 0]
    got = to_sibling(lax.dynamic_slice_in_dim(thermal, (1 - side) * half, half, axis=0))
    rest = exchange(
        call(
            pack_rest_kernel,
            "pack_rest",
            [meta, cross_query[0], grad_out[0], thermal, got],
            message_shapes(C, R + half, 2 * W),
            8,
        ),
        1,
    )
    pT, oT = call(
        bind(self_fwd_kernel, C=C),
        "self_fwd",
        qkv,
        (sds((W // HD, L, L)), sds((W, L), F32)),
        24,
        [pltpu.VMEM((L, W), BF), pltpu.VMEM((W, L), BF)],
    )
    *out, ag = call(
        bind(cross_kernel, C=C),
        "cross",
        [meta, oT, *rest],
        (*message_shapes(C, R + MR, 2 * W), sds((L, W))),
        12,
        [pltpu.VMEM((M, 2 * W), BF), pltpu.VMEM((M, 2 * W), BF)],
    )
    out = exchange(out, -1)
    dqkv = call(
        bind(self_bwd_kernel, C=C),
        "self_bwd",
        [*qkv, pT, oT, ag],
        message_shapes(C, R, 3 * W),
        24,
        [
            pltpu.VMEM((L, W), BF),
            pltpu.VMEM((W, L), BF),
            pltpu.VMEM((L, W), F32),
            pltpu.VMEM((L, W), F32),
        ],
    )
    dqkv = exchange(dqkv, -1)
    combined, grad_cross, grad_thermal = call(
        bind(unpack_cross_kernel, C=C),
        "unpack_cross",
        [meta, *out],
        (sds((R, D)), sds((R, D)), sds((MR, 2 * D))),
        8,
    )
    grad_qkv = call(
        bind(unpack_qkv_kernel, C=C), "unpack_qkv", [meta, *dqkv], sds((R, 3 * D)), 8
    )
    return (combined[None], grad_qkv[None], grad_cross[None], grad_thermal[None])


def solution(mesh):
    rows = P("img", GROUP, None)
    return jax.shard_map(
        body,
        mesh=mesh,
        in_specs=(rows, rows, P("img", GROUP, None, None), P("img"), rows),
        out_specs=(rows, rows, rows, rows),
        check_vma=False,
    )
```

time: 237 us -> 80.2 us (0.34)
  waiting for transfers between devices: 110 us -> 27.2 us
  local copies, waits for them, and re-layouts: 33.4 us -> 5.54 us
  matrix products: 25.9 us -> 0 us
  blocking collectives: 22.5 us -> 0 us
  Pallas kernels: 0 us -> 22.1 us
  other arithmetic: 20 us -> 0 us
  starting transfers between devices: 7.23 us -> 23.4 us
  between operations: 16.3 us -> 1.6 us
    reduce_scatter x2 -> x0, waiting for transfers between devices: 65.7 us -> none  [the longest x1 38.1 us: body(): lax.psum_scatter(thermal_sums(cross_probs, cross_dscores, cross_heads, up...]
    ppermute x0 -> x29, waiting for transfers between devices: none -> 27.2 us  [the longest x12 25.2 us: to_chip(): return lax.ppermute(a, GROUP, pairs)]
    dot_general x12 -> x0, matrix products: 25.9 us -> none  [the longest x1 4.76 us: body(): jnp.einsum('hqk,khd->qhd', self_probs, values_heads, preferred_element_ty...]
    all_gather x2 -> x0, waiting for transfers between devices: 25.2 us -> none  [the longest x1 13.5 us: body(): lax.all_gather(by_heads[:, 1, 0], 'seq', axis=0, tiled=True)]
    ppermute x0 -> x29, starting transfers between devices: none -> 23.4 us  [the longest x12 18.7 us: to_chip(): return lax.ppermute(a, GROUP, pairs)]
    all_to_all x2 -> x0, blocking collectives: 22.5 us -> none  [the longest x1 14.9 us: body(): lax.all_to_all(packed, 'head', split_axis=2, concat_axis=0, tiled=True)]
    pallas_call x0 -> x7, Pallas kernels: none -> 22.1 us  [call(): pl.pallas_call(kernel, out_shape=outs, in_specs=[SM if s else VM for s in...]
    psum x1 -> x0, waiting for transfers between devices: 18.7 us -> none  [spread(): return lax.psum(block, axis)]
  transfers between devices with their start and end apart: 7 -> 29, of which waited for: 5 -> 10; matrix products, arithmetic and copies ran while one was open for 18% -> 0% of each run, Pallas kernels for 0% -> 19%
where the time goes in v2:
time: 80.2 us; the launch traced here: 79.9 us
  waiting for transfers between devices  27.2 us (34%)
  starting transfers between devices  23.4 us (29%)
  Pallas kernels  22.1 us (28%)
  local copies, waits for them, and re-layouts  5.54 us (7%)
  between operations  1.6 us (2%)
    ppermute x12, waiting for transfers between devices, to_chip(): return lax.ppermute(a, GROUP, pairs)  25.2 us
    pallas_call x7, Pallas kernels, call(): pl.pallas_call(kernel, out_shape=outs, in_specs=[SM if s else VM for s in...  22.1 us
    ppermute x12, starting transfers between devices, to_chip(): return lax.ppermute(a, GROUP, pairs)  18.7 us
    ppermute x17, starting transfers between devices, to_sibling(): return lax.ppermute(a, 'seq', [(i, i ^ 1) for i in range(S)])  4.7 us
    unnamed x8, local copies, waits for them, and re-layouts  4.25 us
    ppermute x17, waiting for transfers between devices, to_sibling(): return lax.ppermute(a, 'seq', [(i, i ^ 1) for i in range(S)])  2.06 us
  transfers between devices with their start and end apart: 29, of which 10 were waited for; matrix products, arithmetic and copies ran while one was open for 0% of the time, Pallas kernels for 19%

profile of v2, /device:TPU:0, one launch (start us, length us, event | category | flops | bytes accessed | tf_op | source)
XLA Modules:
  0.0 79.9 jit_solution(8616555474395894645)
XLA Ops:
  0.7 1.1 %dynamic-slice_bitcast_fusion = bf16[128,2048]{1,0:T(8,128)(2,1)S(1)} fusion(bf16[1,1,256,2048]{3,2,1,0:T(8,128)(2,1)} %param.7, s32[]{:T(128)S(6)} %select_n.110), kind=kLoop, calls=%fused_computation | loop fusion | bytes 1048580 | tf_op jit(solution)/shard_map/dynamic_slice | solution.py:336
  3.1 1.1 %copy-done.1 = bf16[1,128,3072]{2,1,0:T(8,128)(2,1)S(1)} copy-done((bf16[1,128,3072]{2,1,0:T(8,128)(2,1)S(1)}, bf16[1,128,3072]{2,1,0:T(8,128)(2,1)}, u32[]{:S(2)}) %copy-start.1) | copy-done | bytes 786456
  4.9 2.7 %collective-permute-start = (bf16[2,128,384]{2,1,0:T(8,128)(2,1)S(1)}, bf16[2,128,384]{2,1,0:T(8,128)(2,1)S(1)}, u32[]{:S(2)}, u32[]{:S(2)}) collective-permute-start(bf16[2,128,384]{2,1,0:T(8,128)(2,1)S(1)} %get-tuple-element.31), channel_id=1, source_target_pairs={{0,4},{1,5},{2,6},{3,7},{4,0},{5,1},{6,2},{7,3},{8,12},{9,13},{10,... | collective-permute-start | bytes 589832 | tf_op jit(solution)/shard_map/ppermute | solution.py:324
  7.7 1.5 %collective-permute-start.1 = (bf16[2,128,384]{2,1,0:T(8,128)(2,1)S(1)}, bf16[2,128,384]{2,1,0:T(8,128)(2,1)S(1)}, u32[]{:S(2)}, u32[]{:S(2)}) collective-permute-start(bf16[2,128,384]{2,1,0:T(8,128)(2,1)S(1)} %get-tuple-element.32), channel_id=1, source_target_pairs={{0,1},{1,0},{2,3},{3,2},{4,5},{5,4},{6,7},{7,6},{8,9},{9,8},{10,11... | collective-permute-start | bytes 589832 | tf_op jit(solution)/shard_map/ppermute | solution.py:324
  9.5 1.2 %copy-done = bf16[1,1,256,2048]{3,2,1,0:T(8,128)(2,1)S(1)} copy-done((bf16[1,1,256,2048]{3,2,1,0:T(8,128)(2,1)S(1)}, bf16[1,1,256,2048]{3,2,1,0:T(8,128)(2,1)}, u32[]{:S(2)}) %copy-start) | copy-done | bytes 1048600
  10.7 0.9 %copy-done.2 = bf16[1,128,1024]{2,1,0:T(8,128)(2,1)S(1)} copy-done((bf16[1,128,1024]{2,1,0:T(8,128)(2,1)S(1)}, bf16[1,128,1024]{2,1,0:T(8,128)(2,1)}, u32[]{:S(2)}) %copy-start.2) | copy-done | bytes 262168
  13.4 1.8 %collective-permute-start.8 = (bf16[2,256,256]{2,1,0:T(8,128)(2,1)S(1)}, bf16[2,256,256]{2,1,0:T(8,128)(2,1)S(1)}, u32[]{:S(2)}, u32[]{:S(2)}) collective-permute-start(bf16[2,256,256]{2,1,0:T(8,128)(2,1)S(1)} %get-tuple-element.37), channel_id=1, source_target_pairs={{0,4},{1,5},{2,6},{3,7},{4,0},{5,1},{6,2},{7,3},{8,12},{9,13},{10,... | collective-permute-start | bytes 786440 | tf_op jit(solution)/shard_map/ppermute | solution.py:324
  15.3 3.8 %collective-permute-done.1.refs_2_ = bf16[2,128,384]{2,1,0:T(8,128)(2,1)S(1)} collective-permute-done((bf16[2,128,384]{2,1,0:T(8,128)(2,1)S(1)}, bf16[2,128,384]{2,1,0:T(8,128)(2,1)S(1)}, u32[]{:S(2)}, u32[]{:S(2)}) %collective-permute-start.1) | collective-permute-done | bytes 196640 | tf_op jit(solution)/shard_map/ppermute | solution.py:324
  19.1 1.5 %collective-permute-start.9 = (bf16[2,256,256]{2,1,0:T(8,128)(2,1)S(1)}, bf16[2,256,256]{2,1,0:T(8,128)(2,1)S(1)}, u32[]{:S(2)}, u32[]{:S(2)}) collective-permute-start(bf16[2,256,256]{2,1,0:T(8,128)(2,1)S(1)} %get-tuple-element.38), channel_id=1, source_target_pairs={{0,1},{1,0},{2,3},{3,2},{4,5},{5,4},{6,7},{7,6},{8,9},{9,8},{10,11... | collective-permute-start | bytes 786440 | tf_op jit(solution)/shard_map/ppermute | solution.py:324
  20.6 2.3 %collective-permute-done.8.refs_1_ = bf16[2,256,256]{2,1,0:T(8,128)(2,1)S(1)} collective-permute-done((bf16[2,256,256]{2,1,0:T(8,128)(2,1)S(1)}, bf16[2,256,256]{2,1,0:T(8,128)(2,1)S(1)}, u32[]{:S(2)}, u32[]{:S(2)}) %collective-permute-start.8) | collective-permute-done | bytes 262176 | tf_op jit(solution)/shard_map/ppermute | solution.py:324
  22.9 2.7 %collective-permute-start.10 = (bf16[2,256,256]{2,1,0:T(8,128)(2,1)S(1)}, bf16[2,256,256]{2,1,0:T(8,128)(2,1)S(1)}, u32[]{:S(2)}, u32[]{:S(2)}) collective-permute-start(bf16[2,256,256]{2,1,0:T(8,128)(2,1)S(1)} %get-tuple-element.39), channel_id=1, source_target_pairs={{0,5},{1,4},{2,7},{3,6},{4,1},{5,0},{6,3},{7,2},{8,13},{9,12},{10,... | collective-permute-start | bytes 786440 | tf_op jit(solution)/shard_map/ppermute | solution.py:324
  25.6 6.6 %collective-permute-done.9.refs_2_ = bf16[2,256,256]{2,1,0:T(8,128)(2,1)S(1)} collective-permute-done((bf16[2,256,256]{2,1,0:T(8,128)(2,1)S(1)}, bf16[2,256,256]{2,1,0:T(8,128)(2,1)S(1)}, u32[]{:S(2)}, u32[]{:S(2)}) %collective-permute-start.9) | collective-permute-done | bytes 262176 | tf_op jit(solution)/shard_map/ppermute | solution.py:324
  35.0 7.0 %self_fwd.1 = (bf16[2,1024,1024]{2,1,0:T(8,128)(2,1)S(1)}, f32[128,1024]{1,0:T(8,128)S(1)}) custom-call(bf16[128,384]{1,0:T(8,128)(2,1)S(1)} %get-tuple-element.30.refs_0_, bf16[2,128,384]{2,1,0:T(8,128)(2,1)S(1)} %collective-permute-done.refs_1_, bf16[2,128,384]{2,1,0:T(8,128)(2,1)S(1)} %collective-permute-done.1.refs_2_, ...), custom_call_target="tpu_custom_call" | custom-call | tf_op jit(solution)/shard_map/self_fwd/pallas_call | solution.py:27
  42.1 5.8 %cross.1 = (bf16[160,256]{1,0:T(8,128)(2,1)S(1)}, bf16[160,256]{1,0:T(8,128)(2,1)S(1)}, bf16[2,160,256]{2,1,0:T(8,128)(2,1)S(1)}, bf16[2,160,256]{2,1,0:T(8,128)...) custom-call(s32[15]{0:T(128)S(1)} %stack.67.meta_ref, ...), custom_call_target="tpu_custom_call" | custom-call | tf_op jit(solution)/shard_map/cross/pallas_call | solution.py:27
  47.8 1.0 %collective-permute-start.15 = (bf16[2,160,256]{2,1,0:T(8,128)(2,1)S(1)}, bf16[2,160,256]{2,1,0:T(8,128)(2,1)S(1)}, u32[]{:S(2)}, u32[]{:S(2)}) collective-permute-start(bf16[2,160,256]{2,1,0:T(8,128)(2,1)S(1)} %get-tuple-element.42), channel_id=1, source_target_pairs={{0,4},{1,5},{2,6},{3,7},{4,0},{5,1},{6,2},{7,3},{8,12},{9,13},{10,... | collective-permute-start | bytes 491528 | tf_op jit(solution)/shard_map/ppermute | solution.py:324
  48.9 4.9 %self_bwd.1 = (bf16[128,384]{1,0:T(8,128)(2,1)S(1)}, bf16[128,384]{1,0:T(8,128)(2,1)S(1)}, bf16[2,128,384]{2,1,0:T(8,128)(2,1)S(1)}, bf16[2,128,384]{2,1,0:T(8,128)(2,1)S(1)}, bf16[2,128,384]{2,1,0:T(8,128)(2,1)S(1)}) custom-call(bf16[128,384]{1,0:T(8,128)(2,1)S(1)} %get-tuple-element.30.refs_0_, bf16[2,128,384]{2,1,0:T(8,128)(2,1)S(1)} %collective-permute-done.refs_1_, ...), custom_call_target="tpu_custom_call" | custom-call | tf_op jit(solution)/shard_map/self_bwd/pallas_call | solution.py:27
  54.4 1.5 %collective-permute-start.16 = (bf16[2,160,256]{2,1,0:T(8,128)(2,1)S(1)}, bf16[2,160,256]{2,1,0:T(8,128)(2,1)S(1)}, u32[]{:S(2)}, u32[]{:S(2)}) collective-permute-start(bf16[2,160,256]{2,1,0:T(8,128)(2,1)S(1)} %get-tuple-element.43), channel_id=1, source_target_pairs={{0,1},{1,0},{2,3},{3,2},{4,5},{5,4},{6,7},{7,6},{8,9},{9,8},{10,11... | collective-permute-start | bytes 491528 | tf_op jit(solution)/shard_map/ppermute | solution.py:324
  55.8 1.1 %collective-permute-start.17 = (bf16[2,160,256]{2,1,0:T(8,128)(2,1)S(1)}, bf16[2,160,256]{2,1,0:T(8,128)(2,1)S(1)}, u32[]{:S(2)}, u32[]{:S(2)}) collective-permute-start(bf16[2,160,256]{2,1,0:T(8,128)(2,1)S(1)} %get-tuple-element.44), channel_id=1, source_target_pairs={{0,5},{1,4},{2,7},{3,6},{4,1},{5,0},{6,3},{7,2},{8,13},{9,12},{10,... | collective-permute-start | bytes 491528 | tf_op jit(solution)/shard_map/ppermute | solution.py:324
  57.9 6.2 %collective-permute-done.16.refs_2_ = bf16[2,160,256]{2,1,0:T(8,128)(2,1)S(1)} collective-permute-done((bf16[2,160,256]{2,1,0:T(8,128)(2,1)S(1)}, bf16[2,160,256]{2,1,0:T(8,128)(2,1)S(1)}, u32[]{:S(2)}, u32[]{:S(2)}) %collective-permute-start.16) | collective-permute-done | bytes 163872 | tf_op jit(solution)/shard_map/ppermute | solution.py:324
  64.1 1.5 %collective-permute-start.23 = (bf16[2,128,384]{2,1,0:T(8,128)(2,1)S(1)}, bf16[2,128,384]{2,1,0:T(8,128)(2,1)S(1)}, u32[]{:S(2)}, u32[]{:S(2)}) collective-permute-start(bf16[2,128,384]{2,1,0:T(8,128)(2,1)S(1)} %get-tuple-element.51), channel_id=1, source_target_pairs={{0,1},{1,0},{2,3},{3,2},{4,5},{5,4},{6,7},{7,6},{8,9},{9,8},{10,11... | collective-permute-start | bytes 589832 | tf_op jit(solution)/shard_map/ppermute | solution.py:324
  66.0 2.3 %collective-permute-start.24 = (bf16[2,128,384]{2,1,0:T(8,128)(2,1)S(1)}, bf16[2,128,384]{2,1,0:T(8,128)(2,1)S(1)}, u32[]{:S(2)}, u32[]{:S(2)}) collective-permute-start(bf16[2,128,384]{2,1,0:T(8,128)(2,1)S(1)} %get-tuple-element.52), channel_id=1, source_target_pairs={{0,5},{1,4},{2,7},{3,6},{4,1},{5,0},{6,3},{7,2},{8,13},{9,12},{10,... | collective-permute-start | bytes 589832 | tf_op jit(solution)/shard_map/ppermute | solution.py:324
  68.3 5.8 %collective-permute-done.23.refs_2_ = bf16[2,128,384]{2,1,0:T(8,128)(2,1)S(1)} collective-permute-done((bf16[2,128,384]{2,1,0:T(8,128)(2,1)S(1)}, bf16[2,128,384]{2,1,0:T(8,128)(2,1)S(1)}, u32[]{:S(2)}, u32[]{:S(2)}) %collective-permute-start.23) | collective-permute-done | bytes 196640 | tf_op jit(solution)/shard_map/ppermute | solution.py:324
  76.8 1.5 %unpack_cross.1 = (bf16[128,1024]{1,0:T(8,128)(2,1)}, bf16[128,1024]{1,0:T(8,128)(2,1)}, bf16[32,2048]{1,0:T(8,128)(2,1)}) custom-call(s32[15]{0:T(128)S(1)} %stack.67.meta_ref, bf16[160,256]{1,0:T(8,128)(2,1)S(1)} %get-tuple-element.41.refs_0_, bf16[2,160,256]{2,1,0:T(8,128)(2,1)S(1)} %collective-permute-done.15.refs_1_, ...), custom_call_target="tpu_custom_call" | custom-call | tf_op jit(solution)/shard_map/unpack_cross/pallas_call | solution.py:27
  78.3 1.6 %unpack_qkv.1 = bf16[128,3072]{1,0:T(8,128)(2,1)} custom-call(s32[15]{0:T(128)S(1)} %stack.67.meta_ref, bf16[128,384]{1,0:T(8,128)(2,1)S(1)} %get-tuple-element.49.refs_0_, bf16[2,128,384]{2,1,0:T(8,128)(2,1)S(1)} %collective-permute-done.22.refs_1_, bf16[2,128,384]{2,1,0:T(8,128)(2,1)S(1)} %collective-permute-done.23.refs_2_, ...), custom_call_target="tpu_custom_call" | custom-call | tf_op jit(solution)/shard_map/unpack_qkv/pallas_call | solution.py:27
  (63 shorter events, 11.0 us)
Async XLA Ops:
  1.7 7.8 %collective-permute-start.7 = (bf16[128,2048]{1,0:T(8,128)(2,1)S(1)}, bf16[128,2048]{1,0:T(8,128)(2,1)S(1)}, u32[]{:S(2)}, u32[]{:S(2)}) collective-permute-start(bf16[128,2048]{1,0:T(8,128)(2,1)S(1)} %dynamic-slice_bitcast_fusion), channel_id=1, source_target_pairs={{0,2},{2,0},{4,6},{6,4},{1,3},{3,1},{5,7},{7,5},{8,10},{10,8},{12,... | collective-permute-start | bytes 1572872 | tf_op jit(solution)/shard_map/ppermute | solution.py:315
  4.9 10.3 %collective-permute-start = (bf16[2,128,384]{2,1,0:T(8,128)(2,1)S(1)}, bf16[2,128,384]{2,1,0:T(8,128)(2,1)S(1)}, u32[]{:S(2)}, u32[]{:S(2)}) collective-permute-start(bf16[2,128,384]{2,1,0:T(8,128)(2,1)S(1)} %get-tuple-element.31), channel_id=1, source_target_pairs={{0,4},{1,5},{2,6},{3,7},{4,0},{5,1},{6,2},{7,3},{8,12},{9,13},{10,... | collective-permute-start | bytes 589832 | tf_op jit(solution)/shard_map/ppermute | solution.py:324
  7.5 25.3 %collective-permute-start.3 = (bf16[128,384]{1,0:T(8,128)(2,1)S(1)}, bf16[128,384]{1,0:T(8,128)(2,1)S(1)}, u32[]{:S(2)}, u32[]{:S(2)}) collective-permute-start(bf16[128,384]{1,0:T(8,128)(2,1)S(1)} %get-tuple-element.34), channel_id=1, source_target_pairs={{0,2},{2,0},{4,6},{6,4},{1,3},{3,1},{5,7},{7,5},{8,10},{10,8},{12,... | collective-permute-start | bytes 294920 | tf_op jit(solution)/shard_map/ppermute | solution.py:315
  7.7 11.4 %collective-permute-start.1 = (bf16[2,128,384]{2,1,0:T(8,128)(2,1)S(1)}, bf16[2,128,384]{2,1,0:T(8,128)(2,1)S(1)}, u32[]{:S(2)}, u32[]{:S(2)}) collective-permute-start(bf16[2,128,384]{2,1,0:T(8,128)(2,1)S(1)} %get-tuple-element.32), channel_id=1, source_target_pairs={{0,1},{1,0},{2,3},{3,2},{4,5},{5,4},{6,7},{7,6},{8,9},{9,8},{10,11... | collective-permute-start | bytes 589832 | tf_op jit(solution)/shard_map/ppermute | solution.py:324
  9.2 23.7 %collective-permute-start.2 = (bf16[2,128,384]{2,1,0:T(8,128)(2,1)S(1)}, bf16[2,128,384]{2,1,0:T(8,128)(2,1)S(1)}, u32[]{:S(2)}, u32[]{:S(2)}) collective-permute-start(bf16[2,128,384]{2,1,0:T(8,128)(2,1)S(1)} %get-tuple-element.33), channel_id=1, source_target_pairs={{0,5},{1,4},{2,7},{3,6},{4,1},{5,0},{6,3},{7,2},{8,13},{9,12},{10,... | collective-permute-start | bytes 589832 | tf_op jit(solution)/shard_map/ppermute | solution.py:324
  13.4 9.5 %collective-permute-start.8 = (bf16[2,256,256]{2,1,0:T(8,128)(2,1)S(1)}, bf16[2,256,256]{2,1,0:T(8,128)(2,1)S(1)}, u32[]{:S(2)}, u32[]{:S(2)}) collective-permute-start(bf16[2,256,256]{2,1,0:T(8,128)(2,1)S(1)} %get-tuple-element.37), channel_id=1, source_target_pairs={{0,4},{1,5},{2,6},{3,7},{4,0},{5,1},{6,2},{7,3},{8,12},{9,13},{10,... | collective-permute-start | bytes 786440 | tf_op jit(solution)/shard_map/ppermute | solution.py:324
  15.2 18.3 %collective-permute-start.4 = (bf16[128,384]{1,0:T(8,128)(2,1)S(1)}, bf16[128,384]{1,0:T(8,128)(2,1)S(1)}, u32[]{:S(2)}, u32[]{:S(2)}) collective-permute-start(bf16[128,384]{1,0:T(8,128)(2,1)S(1)} %slice_bitcast_fusion.8), channel_id=1, source_target_pairs={{0,2},{2,0},{4,6},{6,4},{1,3},{3,1},{5,7},{7,5},{8,10},{10,8},{12,... | collective-permute-start | bytes 294920 | tf_op jit(solution)/shard_map/ppermute | solution.py:315
  19.1 13.2 %collective-permute-start.9 = (bf16[2,256,256]{2,1,0:T(8,128)(2,1)S(1)}, bf16[2,256,256]{2,1,0:T(8,128)(2,1)S(1)}, u32[]{:S(2)}, u32[]{:S(2)}) collective-permute-start(bf16[2,256,256]{2,1,0:T(8,128)(2,1)S(1)} %get-tuple-element.38), channel_id=1, source_target_pairs={{0,1},{1,0},{2,3},{3,2},{4,5},{5,4},{6,7},{7,6},{8,9},{9,8},{10,11... | collective-permute-start | bytes 786440 | tf_op jit(solution)/shard_map/ppermute | solution.py:324
  22.9 9.4 %collective-permute-start.10 = (bf16[2,256,256]{2,1,0:T(8,128)(2,1)S(1)}, bf16[2,256,256]{2,1,0:T(8,128)(2,1)S(1)}, u32[]{:S(2)}, u32[]{:S(2)}) collective-permute-start(bf16[2,256,256]{2,1,0:T(8,128)(2,1)S(1)} %get-tuple-element.39), channel_id=1, source_target_pairs={{0,5},{1,4},{2,7},{3,6},{4,1},{5,0},{6,3},{7,2},{8,13},{9,12},{10,... | collective-permute-start | bytes 786440 | tf_op jit(solution)/shard_map/ppermute | solution.py:324
  32.3 9.8 %collective-permute-start.11 = (bf16[256,256]{1,0:T(8,128)(2,1)S(1)}, bf16[256,256]{1,0:T(8,128)(2,1)S(1)}, u32[]{:S(2)}, u32[]{:S(2)}) collective-permute-start(bf16[256,256]{1,0:T(8,128)(2,1)S(1)} %get-tuple-element.40), channel_id=1, source_target_pairs={{0,2},{2,0},{4,6},{6,4},{1,3},{3,1},{5,7},{7,5},{8,10},{10,8},{12,... | collective-permute-start | bytes 393224 | tf_op jit(solution)/shard_map/ppermute | solution.py:315
  32.9 9.2 %collective-permute-start.12 = (bf16[256,256]{1,0:T(8,128)(2,1)S(1)}, bf16[256,256]{1,0:T(8,128)(2,1)S(1)}, u32[]{:S(2)}, u32[]{:S(2)}) collective-permute-start(bf16[256,256]{1,0:T(8,128)(2,1)S(1)} %slice_bitcast_fusion.2), channel_id=1, source_target_pairs={{0,2},{2,0},{4,6},{6,4},{1,3},{3,1},{5,7},{7,5},{8,10},{10,8},{12,... | collective-permute-start | bytes 393224 | tf_op jit(solution)/shard_map/ppermute | solution.py:315
  32.9 9.1 %collective-permute-start.13 = (bf16[256,256]{1,0:T(8,128)(2,1)S(1)}, bf16[256,256]{1,0:T(8,128)(2,1)S(1)}, u32[]{:S(2)}, u32[]{:S(2)}) collective-permute-start(bf16[256,256]{1,0:T(8,128)(2,1)S(1)} %slice_bitcast_fusion.1), channel_id=1, source_target_pairs={{0,2},{2,0},{4,6},{6,4},{1,3},{3,1},{5,7},{7,5},{8,10},{10,8},{12,... | collective-permute-start | bytes 393224 | tf_op jit(solution)/shard_map/ppermute | solution.py:315
  33.4 8.6 %collective-permute-start.14 = (bf16[256,256]{1,0:T(8,128)(2,1)S(1)}, bf16[256,256]{1,0:T(8,128)(2,1)S(1)}, u32[]{:S(2)}, u32[]{:S(2)}) collective-permute-start(bf16[256,256]{1,0:T(8,128)(2,1)S(1)} %slice_bitcast_fusion), channel_id=1, source_target_pairs={{0,2},{2,0},{4,6},{6,4},{1,3},{3,1},{5,7},{7,5},{8,10},{10,8},{12,... | collective-permute-start | bytes 393224 | tf_op jit(solution)/shard_map/ppermute | solution.py:315
  47.8 9.1 %collective-permute-start.15 = (bf16[2,160,256]{2,1,0:T(8,128)(2,1)S(1)}, bf16[2,160,256]{2,1,0:T(8,128)(2,1)S(1)}, u32[]{:S(2)}, u32[]{:S(2)}) collective-permute-start(bf16[2,160,256]{2,1,0:T(8,128)(2,1)S(1)} %get-tuple-element.42), channel_id=1, source_target_pairs={{0,4},{1,5},{2,6},{3,7},{4,0},{5,1},{6,2},{7,3},{8,12},{9,13},{10,... | collective-permute-start | bytes 491528 | tf_op jit(solution)/shard_map/ppermute | solution.py:324
  48.9 25.8 %collective-permute-start.18 = (bf16[160,256]{1,0:T(8,128)(2,1)S(1)}, bf16[160,256]{1,0:T(8,128)(2,1)S(1)}, u32[]{:S(2)}, u32[]{:S(2)}) collective-permute-start(bf16[160,256]{1,0:T(8,128)(2,1)S(1)} %get-tuple-element.45), channel_id=1, source_target_pairs={{0,2},{2,0},{4,6},{6,4},{1,3},{3,1},{5,7},{7,5},{8,10},{10,8},{12,... | collective-permute-start | bytes 245768 | tf_op jit(solution)/shard_map/ppermute | solution.py:315
  53.8 24.5 %collective-permute-start.25 = (bf16[128,384]{1,0:T(8,128)(2,1)S(1)}, bf16[128,384]{1,0:T(8,128)(2,1)S(1)}, u32[]{:S(2)}, u32[]{:S(2)}) collective-permute-start(bf16[128,384]{1,0:T(8,128)(2,1)S(1)} %get-tuple-element.53), channel_id=1, source_target_pairs={{0,2},{2,0},{4,6},{6,4},{1,3},{3,1},{5,7},{7,5},{8,10},{10,8},{12,... | collective-permute-start | bytes 294920 | tf_op jit(solution)/shard_map/ppermute | solution.py:315
  54.4 9.7 %collective-permute-start.16 = (bf16[2,160,256]{2,1,0:T(8,128)(2,1)S(1)}, bf16[2,160,256]{2,1,0:T(8,128)(2,1)S(1)}, u32[]{:S(2)}, u32[]{:S(2)}) collective-permute-start(bf16[2,160,256]{2,1,0:T(8,128)(2,1)S(1)} %get-tuple-element.43), channel_id=1, source_target_pairs={{0,1},{1,0},{2,3},{3,2},{4,5},{5,4},{6,7},{7,6},{8,9},{9,8},{10,11... | collective-permute-start | bytes 491528 | tf_op jit(solution)/shard_map/ppermute | solution.py:324
  55.8 18.9 %collective-permute-start.17 = (bf16[2,160,256]{2,1,0:T(8,128)(2,1)S(1)}, bf16[2,160,256]{2,1,0:T(8,128)(2,1)S(1)}, u32[]{:S(2)}, u32[]{:S(2)}) collective-permute-start(bf16[2,160,256]{2,1,0:T(8,128)(2,1)S(1)} %get-tuple-element.44), channel_id=1, source_target_pairs={{0,5},{1,4},{2,7},{3,6},{4,1},{5,0},{6,3},{7,2},{8,13},{9,12},{10,... | collective-permute-start | bytes 491528 | tf_op jit(solution)/shard_map/ppermute | solution.py:324
  56.9 9.1 %collective-permute-start.22 = (bf16[2,128,384]{2,1,0:T(8,128)(2,1)S(1)}, bf16[2,128,384]{2,1,0:T(8,128)(2,1)S(1)}, u32[]{:S(2)}, u32[]{:S(2)}) collective-permute-start(bf16[2,128,384]{2,1,0:T(8,128)(2,1)S(1)} %get-tuple-element.50), channel_id=1, source_target_pairs={{0,4},{1,5},{2,6},{3,7},{4,0},{5,1},{6,2},{7,3},{8,12},{9,13},{10,... | collective-permute-start | bytes 589832 | tf_op jit(solution)/shard_map/ppermute | solution.py:324
  64.1 10.0 %collective-permute-start.23 = (bf16[2,128,384]{2,1,0:T(8,128)(2,1)S(1)}, bf16[2,128,384]{2,1,0:T(8,128)(2,1)S(1)}, u32[]{:S(2)}, u32[]{:S(2)}) collective-permute-start(bf16[2,128,384]{2,1,0:T(8,128)(2,1)S(1)} %get-tuple-element.51), channel_id=1, source_target_pairs={{0,1},{1,0},{2,3},{3,2},{4,5},{5,4},{6,7},{7,6},{8,9},{9,8},{10,11... | collective-permute-start | bytes 589832 | tf_op jit(solution)/shard_map/ppermute | solution.py:324
  66.0 8.1 %collective-permute-start.24 = (bf16[2,128,384]{2,1,0:T(8,128)(2,1)S(1)}, bf16[2,128,384]{2,1,0:T(8,128)(2,1)S(1)}, u32[]{:S(2)}, u32[]{:S(2)}) collective-permute-start(bf16[2,128,384]{2,1,0:T(8,128)(2,1)S(1)} %get-tuple-element.52), channel_id=1, source_target_pairs={{0,5},{1,4},{2,7},{3,6},{4,1},{5,0},{6,3},{7,2},{8,13},{9,12},{10,... | collective-permute-start | bytes 589832 | tf_op jit(solution)/shard_map/ppermute | solution.py:324
  74.7 3.6 %collective-permute-start.26 = (bf16[128,384]{1,0:T(8,128)(2,1)S(1)}, bf16[128,384]{1,0:T(8,128)(2,1)S(1)}, u32[]{:S(2)}, u32[]{:S(2)}) collective-permute-start(bf16[128,384]{1,0:T(8,128)(2,1)S(1)} %slice_bitcast_fusion.5), channel_id=1, source_target_pairs={{0,2},{2,0},{4,6},{6,4},{1,3},{3,1},{5,7},{7,5},{8,10},{10,8},{12,... | collective-permute-start | bytes 294920 | tf_op jit(solution)/shard_map/ppermute | solution.py:315
  74.8 3.5 %collective-permute-start.27 = (bf16[128,384]{1,0:T(8,128)(2,1)S(1)}, bf16[128,384]{1,0:T(8,128)(2,1)S(1)}, u32[]{:S(2)}, u32[]{:S(2)}) collective-permute-start(bf16[128,384]{1,0:T(8,128)(2,1)S(1)} %slice_bitcast_fusion.4), channel_id=1, source_target_pairs={{0,2},{2,0},{4,6},{6,4},{1,3},{3,1},{5,7},{7,5},{8,10},{10,8},{12,... | collective-permute-start | bytes 294920 | tf_op jit(solution)/shard_map/ppermute | solution.py:315
  75.3 3.0 %collective-permute-start.28 = (bf16[128,384]{1,0:T(8,128)(2,1)S(1)}, bf16[128,384]{1,0:T(8,128)(2,1)S(1)}, u32[]{:S(2)}, u32[]{:S(2)}) collective-permute-start(bf16[128,384]{1,0:T(8,128)(2,1)S(1)} %slice_bitcast_fusion.3), channel_id=1, source_target_pairs={{0,2},{2,0},{4,6},{6,4},{1,3},{3,1},{5,7},{7,5},{8,10},{10,8},{12,... | collective-permute-start | bytes 294920 | tf_op jit(solution)/shard_map/ppermute | solution.py:315
  (9 other events, 11.1 us)

commit v3 on v2

v3 whole, which is shorter than its diff:
```python
import functools
import math

import jax
import jax.numpy as jnp
from jax import lax
from jax.experimental import pallas as pl
from jax.experimental.pallas import tpu as pltpu
from jax.sharding import PartitionSpec as P

BF = jnp.bfloat16
F32 = jnp.float32
HD = 64
GROUP = ("seq", "head")
VM = pl.BlockSpec(memory_space=pltpu.VMEM)
SM = pl.BlockSpec(memory_space=pltpu.SMEM)
SCALE = 1.0 / math.sqrt(HD)
MIB = 1 << 20


def sds(shape, dtype=BF):
    return jax.ShapeDtypeStruct(shape, dtype)


def call(kernel, name, ins, outs, mib, scratch=(), cost=None):
    smem = [a.dtype == jnp.int32 for a in ins]
    return pl.pallas_call(
        kernel,
        out_shape=outs,
        in_specs=[SM if s else VM for s in smem],
        out_specs=jax.tree.map(lambda _: VM, outs),
        scratch_shapes=scratch,
        name=name,
        cost_estimate=cost,
        compiler_params=pltpu.CompilerParams(vmem_limit_bytes=mib * MIB),
    )(*ins)


def cost(scores, products):
    return pl.CostEstimate(
        flops=2 * 256 * scores * products, bytes_accessed=4 * scores, transcendentals=scores
    )


def dot(a, b):
    return jnp.dot(a, b, preferred_element_type=F32)


def dot_nt(a, b):
    return lax.dot_general(a, b, (((1,), (1,)), ((), ())), preferred_element_type=F32)


def head_only(x, h):
    if x.shape[-1] == HD:
        return x
    lane = lax.broadcasted_iota(jnp.int32, x.shape, 1)
    return jnp.where((lane >= h * HD) & (lane < (h + 1) * HD), x, jnp.zeros_like(x))


def softmax_t(scores):
    top = jnp.max(scores, axis=0, keepdims=True)
    e = jnp.exp((scores - top) * SCALE)
    return (e * (1.0 / jnp.sum(e, axis=0, keepdims=True))).astype(BF)


def columns(meta_ref, d, side, base, W):
    return pl.ds(pl.multiple_of(base + meta_ref[1 + d] * 2 * W + side * W, W), W)


def pack_kernel(meta_ref, *refs, tensors, blocks, C):
    ins, msgs = refs[: 2 * blocks], refs[2 * blocks : 2 * blocks + C]
    sems = refs[-1] if len(refs) > 2 * blocks + C else None
    W = msgs[0].shape[1] // (3 if blocks == 1 else 2)
    side, keep = meta_ref[0], meta_ref[2 + C] == 1
    n = 0
    waits = []
    for d in range(C):
        for a, base, row, lane, both in tensors:
            own, sib = ins[2 * a], ins[2 * a + 1]
            rows = own.shape[0]
            lanes = slice(lane * W, (lane + 1) * W)
            if sems is None:
                at = pl.ds(pl.multiple_of(base + meta_ref[1 + d] * 2 * W, 2 * W), 2 * W)
                x, y = own[:, at], sib[:, at]
                x = jnp.where(side == 0, x[:, :W], x[:, W:])
                y = jnp.where(side == 0, y[:, :W], y[:, W:])
                if both:
                    msgs[d][row : row + rows, lanes] = x
                    msgs[d][row + rows : row + 2 * rows, lanes] = y
                else:
                    msgs[d][row : row + rows, lanes] = jnp.where(keep, x, y)
                continue
            at = columns(meta_ref, d, side, base, W)
            first = pltpu.make_async_copy(
                own.at[:, at], msgs[d].at[pl.ds(row, rows), lanes], sems.at[n]
            )
            second = pltpu.make_async_copy(
                sib.at[:, at],
                msgs[d].at[pl.ds(row + rows if both else row, rows), lanes],
                sems.at[n + 1 if both else n],
            )
            if both:
                first.start()
                second.start()
                waits += [first, second]
                n += 2
            else:
                pl.when(keep)(first.start)
                pl.when(jnp.logical_not(keep))(second.start)
                waits.append(first)
                n += 1
    for copy in waits:
        copy.wait()


def pack(name, meta, pairs, tensors, C, rows, width):
    W = width // (3 if len(pairs) == 1 else 2)
    direct = W % 128 == 0
    n = C * sum(2 if t[4] else 1 for t in tensors)
    space = pl.BlockSpec(memory_space=pl.ANY) if direct else VM
    return pl.pallas_call(
        functools.partial(pack_kernel, tensors=tensors, blocks=len(pairs), C=C),
        out_shape=(sds((rows, width)),) * C,
        in_specs=[SM] + [space] * (2 * len(pairs)),
        out_specs=(VM,) * C,
        scratch_shapes=[pltpu.SemaphoreType.DMA((n,))] if direct else [],
        name=name,
        compiler_params=pltpu.CompilerParams(vmem_limit_bytes=8 * MIB),
    )(meta, *[a for pair in pairs for a in pair])


def message_shapes(C, rows, width, dtype=BF):
    return (sds((rows, width), dtype),) * 2 + (sds((2, rows, width), dtype),) * (C - 1)


def pieces(refs):
    C = len(refs) // 2
    out = []
    for d in range(C):
        if d == 0:
            out.append(lambda *ix, ref=refs[0]: ref[ix])
        else:
            out.append(lambda *ix, ref=refs[d]: ref[(0,) + ix])
        out.append(lambda *ix, ref=refs[C + d]: ref[ix])
    return out


def put(msgs, block, rows, lanes, value):
    d, e = block // 2, block % 2
    if d == 0:
        msgs[e][rows, lanes] = value
    else:
        msgs[d + 1][e, rows, lanes] = value


def self_fwd_kernel(*refs, C):
    qkv = refs[:C]
    pT_ref, oT_ref, k_ref, vT_ref = refs[C:]
    L, W = k_ref.shape
    QB = L // C
    for b in range(C):
        k_ref[b * QB : (b + 1) * QB] = qkv[b][:, W : 2 * W]
        vT_ref[:, b * QB : (b + 1) * QB] = qkv[b][:, 2 * W :].T
    k = k_ref[...]
    for b in range(C):
        q = qkv[b][:, :W]
        cols = slice(b * QB, (b + 1) * QB)
        for h in range(W // HD):
            rows = slice(h * HD, (h + 1) * HD)
            p = softmax_t(dot_nt(k, head_only(q, h)))
            pT_ref[h, :, cols] = p
            oT_ref[rows, cols] = dot(vT_ref[rows, :], p)


def cross_kernel(meta_ref, oT_ref, *refs, C):
    rest = refs[:C]
    msgs = refs[C : 2 * C + 1]
    ag_ref, t_ref, dt_ref = refs[2 * C + 1 :]
    W, L = oT_ref.shape
    M = t_ref.shape[0]
    QB = L // C
    R = QB // 2
    every = slice(None)
    here = meta_ref[1 + C]
    for d in range(C):

        @pl.when(here == d)
        def _():
            t_ref[...] = rest[d][QB:, :]

    tk, tv = t_ref[:, :W], t_ref[:, W:]
    tkT, tvT = tk.T, tv.T
    dtk = dtv = None
    for b in range(C):
        cq, go = rest[b][:QB, :W], rest[b][:QB, W:]
        att = oT_ref[:, b * QB : (b + 1) * QB].T.astype(BF).astype(F32)
        goT = go.T.astype(F32)
        x = (att + cq.astype(F32)).astype(BF)
        mixed, dqs = [], []
        for h in range(W // HD):
            rows = slice(h * HD, (h + 1) * HD)
            xh, gh = head_only(x, h), head_only(go, h)
            p = softmax_t(dot_nt(tk, xh))
            mix = dot(tvT[rows], p)
            delta = jnp.sum(goT[rows] * mix, axis=0, keepdims=True)
            ds = (p.astype(F32) * (dot_nt(tv, gh) - delta)).astype(BF)
            mixed.append(mix)
            dqs.append(dot(tkT[rows], ds))
            a, v = dot(ds, xh), dot(p, gh)
            dtk = a if dtk is None else dtk + a
            dtv = v if dtv is None else dtv + v
        dq = jnp.concatenate(dqs, axis=0).T * SCALE
        combined = (att + jnp.concatenate(mixed, axis=0).T).astype(BF)
        grad_cross = dq.astype(BF)
        ag_ref[b * QB : (b + 1) * QB] = (go.astype(F32) + dq).astype(BF)
        for e in range(2):
            part = slice(e * R, (e + 1) * R)
            put(msgs, 2 * b + e, slice(0, R), slice(0, W), combined[part])
            put(msgs, 2 * b + e, slice(0, R), slice(W, 2 * W), grad_cross[part])
    dt_ref[:, :W] = (dtk * SCALE).astype(BF)
    dt_ref[:, W:] = dtv.astype(BF)
    MR = M // (2 * C)
    for i in range(2 * C):
        start = pl.multiple_of(meta_ref[3 + C + i] * MR, MR)
        put(msgs, i, slice(R, R + MR), every, dt_ref[pl.ds(start, MR), :])


def self_bwd_kernel(*refs, C):
    qkv = refs[:C]
    pT_ref, oT_ref, ag_ref = refs[C : C + 3]
    msgs = refs[C + 3 : 2 * C + 4]
    v_ref, kT_ref, dk_ref, dv_ref = refs[2 * C + 4 :]
    L, W = v_ref.shape
    QB = L // C
    R = QB // 2
    every = slice(None)
    for b in range(C):
        v_ref[b * QB : (b + 1) * QB] = qkv[b][:, 2 * W :]
        kT_ref[:, b * QB : (b + 1) * QB] = qkv[b][:, W : 2 * W].T
    v = v_ref[...]
    for b in range(C):
        cols = slice(b * QB, (b + 1) * QB)
        ag = ag_ref[cols]
        q = qkv[b][:, :W]
        product = ag.T.astype(F32) * oT_ref[:, cols]
        dqs = []
        for h in range(W // HD):
            rows = slice(h * HD, (h + 1) * HD)
            delta = jnp.sum(product[rows], axis=0, keepdims=True)
            agh = head_only(ag, h)
            p = pT_ref[h, :, cols]
            dv = dot(p, agh)
            ds = (p.astype(F32) * (dot_nt(v, agh) - delta)).astype(BF)
            dk = dot(ds, head_only(q, h))
            dqs.append(dot(kT_ref[rows, :], ds))
            if b == 0 and h == 0:
                dk_ref[...] = dk
                dv_ref[...] = dv
            else:
                dk_ref[...] += dk
                dv_ref[...] += dv
        dq = (jnp.concatenate(dqs, axis=0).T * SCALE).astype(BF)
        for e in range(2):
            put(msgs, 2 * b + e, every, slice(0, W), dq[e * R : (e + 1) * R])
    for i in range(2 * C):
        part = slice(i * R, (i + 1) * R)
        put(msgs, i, every, slice(W, 2 * W), (dk_ref[part] * SCALE).astype(BF))
        put(msgs, i, every, slice(2 * W, 3 * W), dv_ref[part].astype(BF))


def unpack_kernel(meta_ref, *refs, tensors, outs, C):
    blocks = pieces(refs[: 2 * C])
    targets = refs[2 * C : 2 * C + outs]
    sems = refs[-1] if len(refs) > 2 * C + outs else None
    W = refs[0].shape[1] // (3 if outs == 1 else 2)
    side = meta_ref[0]
    copies = []
    for d in range(C):
        for o, base, rows, lane in tensors:
            lanes = slice(lane * W, (lane + 1) * W)
            if sems is None:
                a, b = blocks[2 * d](rows, lanes), blocks[2 * d + 1](rows, lanes)
                start = pl.multiple_of(base + meta_ref[1 + d] * 2 * W, 2 * W)
                pair = [jnp.where(side == 0, a, b), jnp.where(side == 0, b, a)]
                targets[o][:, pl.ds(start, 2 * W)] = jnp.concatenate(pair, axis=1)
                continue
            direct = refs[0] if d == 0 else refs[d].at[0]
            for source, at in ((direct, side), (refs[C + d], 1 - side)):
                copies.append(
                    pltpu.make_async_copy(
                        source.at[rows, lanes],
                        targets[o].at[:, columns(meta_ref, d, at, base, W)],
                        sems.at[len(copies)],
                    )
                )
                copies[-1].start()
    for copy in copies:
        copy.wait()


def unpack(name, meta, arrays, tensors, outs, C):
    W = arrays[0].shape[1] // (3 if len(outs) == 1 else 2)
    direct = W % 128 == 0
    space = pl.BlockSpec(memory_space=pl.ANY) if direct else VM
    sems = [pltpu.SemaphoreType.DMA((2 * C * len(tensors),))] if direct else []
    return pl.pallas_call(
        functools.partial(unpack_kernel, tensors=tensors, outs=len(outs), C=C),
        out_shape=outs,
        in_specs=[SM] + [VM] * (2 * C),
        out_specs=(space,) * len(outs),
        scratch_shapes=sems,
        name=name,
        compiler_params=pltpu.CompilerParams(vmem_limit_bytes=8 * MIB),
    )(meta, *arrays)


def body(self_qkv, cross_query, thermal_kv, owners, grad_out):
    S, Hd = lax.axis_size("seq"), lax.axis_size("head")
    X = S // 2
    C = X * Hd
    R, D = cross_query.shape[1:]
    W = D // (2 * C)
    L = 2 * C * R
    M = thermal_kv.shape[2]
    MR = M // (2 * C)
    offsets = [(i, j) for j in range(Hd) for i in range(X)]
    s, h = lax.axis_index("seq"), lax.axis_index("head")
    side, x = s % 2, s // 2
    owner_s, owner_h = owners[0] // Hd, owners[0] % Hd
    away = (x - owner_s // 2 + X) % X + X * ((h - owner_h + Hd) % Hd)
    keep = (owner_s % 2 == side).astype(jnp.int32)
    chips = [((x + i) % X) * Hd + (h + j) % Hd for i, j in offsets]
    ids = []
    for i, j in offsets:
        for e in (0, 1):
            ids.append((((x - i + X) % X) * 2 + (side if e == 0 else 1 - side)) * Hd + (h - j + Hd) % Hd)
    meta = jnp.stack([side, *chips, away, keep, *ids]).astype(jnp.int32)

    def to_sibling(a):
        return lax.ppermute(a, "seq", [(i, i ^ 1) for i in range(S)])

    def to_chip(a, d, sign):
        i, j = offsets[d]
        pairs = []
        for p in range(S):
            for q in range(Hd):
                there = ((p // 2 + sign * i) % X) * 2 + p % 2
                pairs.append((p * Hd + q, there * Hd + (q + sign * j) % Hd))
        return lax.ppermute(a, GROUP, pairs)

    def send(msgs, sign):
        return [to_chip(msgs[d + 1], d, sign) for d in range(1, C)], to_sibling(msgs[1])

    def relay(msgs, got, sibling):
        return [msgs[0], *got, sibling, *[to_sibling(g[1]) for g in got]]

    def after(arrays, *gates):
        return lax.optimization_barrier((list(arrays), gates))[0]

    bind = functools.partial
    heads = W // HD
    x_pair = (self_qkv[0], to_sibling(self_qkv[0]))
    cq_pair = (cross_query[0], to_sibling(cross_query[0]))
    go_pair = (grad_out[0], to_sibling(grad_out[0]))
    t_pair = (thermal_kv[0, 0], to_sibling(thermal_kv[0, 0]))
    msgs = pack(
        "pack_qkv", meta, [x_pair], [(0, t * D, 0, t, True) for t in range(3)], C, 2 * R, 3 * W
    )
    got = [to_chip(msgs[d], d, 1) for d in range(1, C)]
    rest = pack(
        "pack_rest",
        meta,
        [cq_pair, go_pair, t_pair],
        [
            (0, 0, 0, 0, True),
            (1, 0, 0, 1, True),
            (2, 0, 2 * R, 0, False),
            (2, D, 2 * R, 1, False),
        ],
        C,
        2 * R + M,
        2 * W,
    )
    got = after(got, *rest)
    rest = after(rest, got[0])
    rest_got = [to_chip(rest[d], d, 1) for d in range(1, C)]
    qkv = [msgs[0], *got]
    pT, oT = call(
        bind(self_fwd_kernel, C=C),
        "self_fwd",
        qkv,
        (sds((heads, L, L)), sds((W, L), F32)),
        24,
        [pltpu.VMEM((L, W), BF), pltpu.VMEM((W, L), BF)],
        cost(heads * L * L, 2),
    )
    rest = [rest[0], *after(rest_got, oT)]
    *out, ag = call(
        bind(cross_kernel, C=C),
        "cross",
        [meta, oT, *rest],
        (*message_shapes(C, R + MR, 2 * W), sds((L, W))),
        12,
        [pltpu.VMEM((M, 2 * W), BF), pltpu.VMEM((M, 2 * W), BF)],
        cost(heads * L * M, 6),
    )
    out_got, out_sibling = send(out, -1)
    dqkv = call(
        bind(self_bwd_kernel, C=C),
        "self_bwd",
        [*qkv, pT, oT, ag],
        message_shapes(C, R, 3 * W),
        24,
        [
            pltpu.VMEM((L, W), BF),
            pltpu.VMEM((W, L), BF),
            pltpu.VMEM((L, W), F32),
            pltpu.VMEM((L, W), F32),
        ],
        cost(heads * L * L, 4),
    )
    dqkv_got, dqkv_sibling = send(dqkv, -1)
    out = relay(out, after(out_got, dqkv[0]), out_sibling)
    combined, grad_cross, grad_thermal = unpack(
        "unpack_cross",
        meta,
        out,
        [
            (0, 0, slice(0, R), 0),
            (1, 0, slice(0, R), 1),
            (2, 0, slice(R, R + MR), 0),
            (2, D, slice(R, R + MR), 1),
        ],
        (sds((R, D)), sds((R, D)), sds((MR, 2 * D))),
        C,
    )
    (first_relay,) = [to_sibling(g[1]) for g in dqkv_got[:1]]
    later = after(dqkv_got[1:], combined, first_relay)
    dqkv = [dqkv[0], dqkv_got[0], *later, dqkv_sibling, first_relay, *[to_sibling(g[1]) for g in later]]
    (grad_qkv,) = unpack(
        "unpack_qkv",
        meta,
        dqkv,
        [(0, t * D, slice(None), t) for t in range(3)],
        (sds((R, 3 * D)),),
        C,
    )
    return (combined[None], grad_qkv[None], grad_cross[None], grad_thermal[None])


def solution(mesh):
    rows = P("img", GROUP, None)
    return jax.shard_map(
        body,
        mesh=mesh,
        in_specs=(rows, rows, P("img", GROUP, None, None), P("img"), rows),
        out_specs=(rows, rows, rows, rows),
        check_vma=False,
    )
```

time: 80.2 us -> 64.4 us (0.80)
  waiting for transfers between devices: 27.2 us -> 17 us
  starting transfers between devices: 23.4 us -> 17.7 us
  Pallas kernels: 22.1 us -> 23.3 us
  local copies, waits for them, and re-layouts: 5.54 us -> 4.4 us
    ppermute x12, waiting for transfers between devices: 25.2 us -> 12.8 us  [to_chip(): return lax.ppermute(a, GROUP, pairs)]
    pallas_call x0 -> x4, Pallas kernels: none -> 5.53 us  [the longest x2 3.27 us: unpack(): pl.pallas_call(functools.partial(unpack_kernel, tensors=tensors, outs=len...]
    pallas_call x7 -> x3, Pallas kernels: 22.1 us -> 17.7 us  [call(): pl.pallas_call(kernel, out_shape=outs, in_specs=[SM if s else VM for s in...]
    ppermute x12, starting transfers between devices: 18.7 us -> 15.1 us  [to_chip(): return lax.ppermute(a, GROUP, pairs)]
    ppermute x17 -> x12, waiting for transfers between devices: 2.06 us -> 4.25 us  [to_sibling(): return lax.ppermute(a, 'seq', [(i, i ^ 1) for i in range(S)])]
    ppermute x17 -> x12, starting transfers between devices: 4.7 us -> 2.65 us  [to_sibling(): return lax.ppermute(a, 'seq', [(i, i ^ 1) for i in range(S)])]
    dynamic_slice x1 -> x0, local copies, waits for them, and re-layouts: 1.08 us -> none  [body(): lax.dynamic_slice_in_dim(thermal, (1 - side) * half, half, axis=0)]
  transfers between devices with their start and end apart: 29 -> 24, of which waited for: 10 -> 8; matrix products, arithmetic and copies ran while one was open for 0% -> 0% of each run, Pallas kernels for 19% -> 25%
where the time goes in v3:
time: 64.4 us; the launch traced here: 64.1 us
  Pallas kernels  23.3 us (36%)
  starting transfers between devices  17.7 us (27%)
  waiting for transfers between devices  17 us (26%)
  local copies, waits for them, and re-layouts  4.4 us (7%)
  between operations  1.7 us (3%)
    pallas_call x3, Pallas kernels, call(): pl.pallas_call(kernel, out_shape=outs, in_specs=[SM if s else VM for s in...  17.7 us
    ppermute x12, starting transfers between devices, to_chip(): return lax.ppermute(a, GROUP, pairs)  15.1 us
    ppermute x12, waiting for transfers between devices, to_chip(): return lax.ppermute(a, GROUP, pairs)  12.8 us
    unnamed x8, local copies, waits for them, and re-layouts  4.26 us
    ppermute x12, waiting for transfers between devices, to_sibling(): return lax.ppermute(a, 'seq', [(i, i ^ 1) for i in range(S)])  4.25 us
    pallas_call x2, Pallas kernels, unpack(): pl.pallas_call(functools.partial(unpack_kernel, tensors=tensors, outs=len...  3.27 us
    ppermute x12, starting transfers between devices, to_sibling(): return lax.ppermute(a, 'seq', [(i, i ^ 1) for i in range(S)])  2.65 us
    pallas_call x2, Pallas kernels, pack(): pl.pallas_call(functools.partial(pack_kernel, tensors=tensors, blocks=len...  2.27 us
  transfers between devices with their start and end apart: 24, of which 8 were waited for; matrix products, arithmetic and copies ran while one was open for 0% of the time, Pallas kernels for 25%

profile of v3, /device:TPU:0, one launch (start us, length us, event | category | flops | bytes accessed | tf_op | source)
XLA Modules:
  0.0 64.1 jit_solution(10027917271732389276)
XLA Ops:
  2.6 2.2 %collective-permute-done.refs_1_ = bf16[128,3072]{1,0:T(8,128)(2,1)S(1)} collective-permute-done((bf16[128,3072]{1,0:T(8,128)(2,1)}, bf16[128,3072]{1,0:T(8,128)(2,1)S(1)}, u32[]{:S(2)}, u32[]{:S(2)}) %collective-permute-start) | collective-permute-done | bytes 786464 | tf_op jit(solution)/shard_map/ppermute | solution.py:340
  4.8 1.1 %copy-done.1 = bf16[1,128,3072]{2,1,0:T(8,128)(2,1)S(1)} copy-done((bf16[1,128,3072]{2,1,0:T(8,128)(2,1)S(1)}, bf16[1,128,3072]{2,1,0:T(8,128)(2,1)}, u32[]{:S(2)}) %copy-start.1) | copy-done | bytes 786456
  5.9 1.1 %pack_qkv.1 = (bf16[256,384]{1,0:T(8,128)(2,1)S(1)}, bf16[256,384]{1,0:T(8,128)(2,1)S(1)}, bf16[256,384]{1,0:T(8,128)(2,1)S(1)}, bf16[256,384]{1,0:T(8,128)(2,1)S(1)}) custom-call(s32[15]{0:T(128)S(1)} %stack.67.meta_ref, bf16[128,3072]{1,0:T(8,128)(2,1)S(1)} %bitcast.43, bf16[128,3072]{1,0:T(8,128)(2,1)S(1)} %collective-permute-done.refs_1_), custom_call_target="tpu_custom_call" | custom-call | tf_op jit(solution)/shard_map/pack_qkv/pallas_call | solution.py:121
  7.0 2.9 %collective-permute-start.1 = (bf16[256,384]{1,0:T(8,128)(2,1)S(1)}, bf16[256,384]{1,0:T(8,128)(2,1)S(1)}, u32[]{:S(2)}, u32[]{:S(2)}) collective-permute-start(bf16[256,384]{1,0:T(8,128)(2,1)S(1)} %get-tuple-element.44), channel_id=1, source_target_pairs={{0,4},{1,5},{2,6},{3,7},{4,0},{5,1},{6,2},{7,3},{8,12},{9,13},{10,... | collective-permute-start | bytes 589832 | tf_op jit(solution)/shard_map/ppermute | solution.py:349
  9.9 1.5 %collective-permute-start.2 = (bf16[256,384]{1,0:T(8,128)(2,1)S(1)}, bf16[256,384]{1,0:T(8,128)(2,1)S(1)}, u32[]{:S(2)}, u32[]{:S(2)}) collective-permute-start(bf16[256,384]{1,0:T(8,128)(2,1)S(1)} %get-tuple-element.45), channel_id=1, source_target_pairs={{0,1},{1,0},{2,3},{3,2},{4,5},{5,4},{6,7},{7,6},{8,9},{9,8},{10,11... | collective-permute-start | bytes 589832 | tf_op jit(solution)/shard_map/ppermute | solution.py:349
  11.5 1.2 %copy-done = bf16[1,1,256,2048]{3,2,1,0:T(8,128)(2,1)S(1)} copy-done((bf16[1,1,256,2048]{3,2,1,0:T(8,128)(2,1)S(1)}, bf16[1,1,256,2048]{3,2,1,0:T(8,128)(2,1)}, u32[]{:S(2)}) %copy-start) | copy-done | bytes 1048600
  12.7 0.9 %copy-done.2 = bf16[1,128,1024]{2,1,0:T(8,128)(2,1)S(1)} copy-done((bf16[1,128,1024]{2,1,0:T(8,128)(2,1)S(1)}, bf16[1,128,1024]{2,1,0:T(8,128)(2,1)}, u32[]{:S(2)}) %copy-start.2) | copy-done | bytes 262168
  13.7 0.9 %copy-done.3 = bf16[1,128,1024]{2,1,0:T(8,128)(2,1)S(1)} copy-done((bf16[1,128,1024]{2,1,0:T(8,128)(2,1)S(1)}, bf16[1,128,1024]{2,1,0:T(8,128)(2,1)}, u32[]{:S(2)}) %copy-start.3) | copy-done | bytes 262168
  14.6 1.2 %pack_rest.1 = (bf16[512,256]{1,0:T(8,128)(2,1)S(1)}, bf16[512,256]{1,0:T(8,128)(2,1)S(1)}, bf16[512,256]{1,0:T(8,128)(2,1)S(1)}, bf16[512,256]{1,0:T(8,128)(2,1)S(1)}) custom-call(s32[15]{0:T(128)S(1)} %stack.67.meta_ref, bf16[128,1024]{1,0:T(8,128)(2,1)S(1)} %bitcast.45, bf16[128,1024]{1,0:T(8,128)(2,1)S(1)} %collective-permute-done.4.refs_1_, ...), custom_call_target="tpu_custom_call" | custom-call | tf_op jit(solution)/shard_map/pack_rest/pallas_call | solution.py:121
  15.8 5.0 %collective-permute-done.2.refs_2_ = bf16[256,384]{1,0:T(8,128)(2,1)S(1)} collective-permute-done((bf16[256,384]{1,0:T(8,128)(2,1)S(1)}, bf16[256,384]{1,0:T(8,128)(2,1)S(1)}, u32[]{:S(2)}, u32[]{:S(2)}) %collective-permute-start.2) | collective-permute-done | bytes 196640 | tf_op jit(solution)/shard_map/ppermute | solution.py:349
  20.8 1.2 %collective-permute-start.7 = (bf16[512,256]{1,0:T(8,128)(2,1)S(1)}, bf16[512,256]{1,0:T(8,128)(2,1)S(1)}, u32[]{:S(2)}, u32[]{:S(2)}) collective-permute-start(bf16[512,256]{1,0:T(8,128)(2,1)S(1)} %get-tuple-element.56), channel_id=1, source_target_pairs={{0,4},{1,5},{2,6},{3,7},{4,0},{5,1},{6,2},{7,3},{8,12},{9,13},{10,... | collective-permute-start | bytes 786440 | tf_op jit(solution)/shard_map/ppermute | solution.py:349
  22.0 0.8 %collective-permute-start.8 = (bf16[512,256]{1,0:T(8,128)(2,1)S(1)}, bf16[512,256]{1,0:T(8,128)(2,1)S(1)}, u32[]{:S(2)}, u32[]{:S(2)}) collective-permute-start(bf16[512,256]{1,0:T(8,128)(2,1)S(1)} %get-tuple-element.57), channel_id=1, source_target_pairs={{0,1},{1,0},{2,3},{3,2},{4,5},{5,4},{6,7},{7,6},{8,9},{9,8},{10,11... | collective-permute-start | bytes 786440 | tf_op jit(solution)/shard_map/ppermute | solution.py:349
  22.9 1.4 %collective-permute-start.9 = (bf16[512,256]{1,0:T(8,128)(2,1)S(1)}, bf16[512,256]{1,0:T(8,128)(2,1)S(1)}, u32[]{:S(2)}, u32[]{:S(2)}) collective-permute-start(bf16[512,256]{1,0:T(8,128)(2,1)S(1)} %get-tuple-element.58), channel_id=1, source_target_pairs={{0,5},{1,4},{2,7},{3,6},{4,1},{5,0},{6,3},{7,2},{8,13},{9,12},{10,... | collective-permute-start | bytes 786440 | tf_op jit(solution)/shard_map/ppermute | solution.py:349
  24.3 7.0 %self_fwd.1 = (bf16[2,1024,1024]{2,1,0:T(8,128)(2,1)S(1)}, f32[128,1024]{1,0:T(8,128)S(1)}) custom-call(bf16[256,384]{1,0:T(8,128)(2,1)S(1)} %get-tuple-element.43.refs_0_, bf16[256,384]{1,0:T(8,128)(2,1)S(1)} %collective-permute-done.1.refs_1_, bf16[256,384]{1,0:T(8,128)(2,1)S(1)} %collective-permute-done.2.refs_2_, ...), custom_call_target="tpu_custom_call" | custom-call | flops 2147483648 | bytes 8388608 | tf_op jit(solution)/shard_map/self_fwd/pallas_call | solution.py:27
  31.4 3.5 %collective-permute-done.8.refs_2_ = bf16[512,256]{1,0:T(8,128)(2,1)S(1)} collective-permute-done((bf16[512,256]{1,0:T(8,128)(2,1)S(1)}, bf16[512,256]{1,0:T(8,128)(2,1)S(1)}, u32[]{:S(2)}, u32[]{:S(2)}) %collective-permute-start.8) | collective-permute-done | bytes 262176 | tf_op jit(solution)/shard_map/ppermute | solution.py:349
  34.9 5.8 %cross.1 = (bf16[160,256]{1,0:T(8,128)(2,1)S(1)}, bf16[160,256]{1,0:T(8,128)(2,1)S(1)}, bf16[2,160,256]{2,1,0:T(8,128)(2,1)S(1)}, bf16[2,160,256]{2,1,0:T(8,128)...) custom-call(s32[15]{0:T(128)S(1)} %stack.67.meta_ref, ...), custom_call_target="tpu_custom_call" | custom-call | flops 1610612736 | bytes 2097152 | tf_op jit(solution)/shard_map/cross/pallas_call | solution.py:27
  41.4 1.4 %collective-permute-start.11 = (bf16[2,160,256]{2,1,0:T(8,128)(2,1)S(1)}, bf16[2,160,256]{2,1,0:T(8,128)(2,1)S(1)}, u32[]{:S(2)}, u32[]{:S(2)}) collective-permute-start(bf16[2,160,256]{2,1,0:T(8,128)(2,1)S(1)} %get-tuple-element.64), channel_id=1, source_target_pairs={{0,1},{1,0},{2,3},{3,2},{4,5},{5,4},{6,7},{7,6},{8,9},{9,8},{10,11... | collective-permute-start | bytes 491528 | tf_op jit(solution)/shard_map/ppermute | solution.py:349
  42.8 1.5 %collective-permute-start.12 = (bf16[2,160,256]{2,1,0:T(8,128)(2,1)S(1)}, bf16[2,160,256]{2,1,0:T(8,128)(2,1)S(1)}, u32[]{:S(2)}, u32[]{:S(2)}) collective-permute-start(bf16[2,160,256]{2,1,0:T(8,128)(2,1)S(1)} %get-tuple-element.65), channel_id=1, source_target_pairs={{0,5},{1,4},{2,7},{3,6},{4,1},{5,0},{6,3},{7,2},{8,13},{9,12},{10,... | collective-permute-start | bytes 491528 | tf_op jit(solution)/shard_map/ppermute | solution.py:349
  44.3 4.9 %self_bwd.1 = (bf16[128,384]{1,0:T(8,128)(2,1)S(1)}, bf16[128,384]{1,0:T(8,128)(2,1)S(1)}, bf16[2,128,384]{2,1,0:T(8,128)(2,1)S(1)}, bf16[2,128,384]{2,1,0:T(8,128)(2,1)S(1)}, bf16[2,128,384]{2,1,0:T(8,128)(2,1)S(1)}) custom-call(bf16[256,384]{1,0:T(8,128)(2,1)S(1)} %get-tuple-element.43.refs_0_, bf16[256,384]{1,0:T(8,128)(2,1)S(1)} %collective-permute-done.1.refs_1_, ...), custom_call_target="tpu_custom_call" | custom-call | flops 4294967296 | bytes 8388608 | tf_op jit(solution)/shard_map/self_bwd/pallas_call | solution.py:27
  49.9 1.4 %collective-permute-start.18 = (bf16[2,128,384]{2,1,0:T(8,128)(2,1)S(1)}, bf16[2,128,384]{2,1,0:T(8,128)(2,1)S(1)}, u32[]{:S(2)}, u32[]{:S(2)}) collective-permute-start(bf16[2,128,384]{2,1,0:T(8,128)(2,1)S(1)} %get-tuple-element.75), channel_id=1, source_target_pairs={{0,1},{1,0},{2,3},{3,2},{4,5},{5,4},{6,7},{7,6},{8,9},{9,8},{10,11... | collective-permute-start | bytes 589832 | tf_op jit(solution)/shard_map/ppermute | solution.py:349
  51.3 1.5 %collective-permute-start.19 = (bf16[2,128,384]{2,1,0:T(8,128)(2,1)S(1)}, bf16[2,128,384]{2,1,0:T(8,128)(2,1)S(1)}, u32[]{:S(2)}, u32[]{:S(2)}) collective-permute-start(bf16[2,128,384]{2,1,0:T(8,128)(2,1)S(1)} %get-tuple-element.76), channel_id=1, source_target_pairs={{0,5},{1,4},{2,7},{3,6},{4,1},{5,0},{6,3},{7,2},{8,13},{9,12},{10,... | collective-permute-start | bytes 589832 | tf_op jit(solution)/shard_map/ppermute | solution.py:349
  52.9 4.2 %collective-permute-done.17.refs_1_ = bf16[2,128,384]{2,1,0:T(8,128)(2,1)S(1)} collective-permute-done((bf16[2,128,384]{2,1,0:T(8,128)(2,1)S(1)}, bf16[2,128,384]{2,1,0:T(8,128)(2,1)S(1)}, u32[]{:S(2)}, u32[]{:S(2)}) %collective-permute-start.17) | collective-permute-done | bytes 196640 | tf_op jit(solution)/shard_map/ppermute | solution.py:349
  59.1 1.7 %unpack_cross.1 = (bf16[128,1024]{1,0:T(8,128)(2,1)}, bf16[128,1024]{1,0:T(8,128)(2,1)}, bf16[32,2048]{1,0:T(8,128)(2,1)}) custom-call(s32[15]{0:T(128)S(1)} %stack.67.meta_ref, bf16[160,256]{1,0:T(8,128)(2,1)S(1)} %get-tuple-element.62.refs_0_, bf16[2,160,256]{2,1,0:T(8,128)(2,1)S(1)} %collective-permute-done.10.refs_1_, ...), custom_call_target="tpu_custom_call" | custom-call | tf_op jit(solution)/shard_map/unpack_cross/pallas_call | solution.py:306
  62.4 1.6 %unpack_qkv.1 = bf16[128,3072]{1,0:T(8,128)(2,1)} custom-call(s32[15]{0:T(128)S(1)} %stack.67.meta_ref, bf16[128,384]{1,0:T(8,128)(2,1)S(1)} %get-tuple-element.68.refs_0_, bf16[2,128,384]{2,1,0:T(8,128)(2,1)S(1)} %collective-permute-done.17.refs_1_, bf16[2,128,384]{2,1,0:T(8,128)(2,1)S(1)} %collective-permute-done.18.refs_2_, ...), custom_call_target="tpu_custom_call" | custom-call | tf_op jit(solution)/shard_map/unpack_qkv/pallas_call | solution.py:306
  (46 shorter events, 6.2 us)
Async XLA Ops:
  0.6 10.8 %collective-permute-start.6 = (bf16[256,2048]{1,0:T(8,128)(2,1)}, bf16[256,2048]{1,0:T(8,128)(2,1)S(1)}, u32[]{:S(2)}, u32[]{:S(2)}) collective-permute-start(bf16[256,2048]{1,0:T(8,128)(2,1)} %bitcast.40), channel_id=1, source_target_pairs={{0,2},{2,0},{4,6},{6,4},{1,3},{3,1},{5,7},{7,5},{8,10},{10,8},{12,... | collective-permute-start | bytes 3145736 | tf_op jit(solution)/shard_map/ppermute | solution.py:340
  1.1 3.6 %collective-permute-start = (bf16[128,3072]{1,0:T(8,128)(2,1)}, bf16[128,3072]{1,0:T(8,128)(2,1)S(1)}, u32[]{:S(2)}, u32[]{:S(2)}) collective-permute-start(bf16[128,3072]{1,0:T(8,128)(2,1)} %bitcast.42), channel_id=1, source_target_pairs={{0,2},{2,0},{4,6},{6,4},{1,3},{3,1},{5,7},{7,5},{8,10},{10,8},{12,... | collective-permute-start | bytes 2359304 | tf_op jit(solution)/shard_map/ppermute | solution.py:340
  1.2 10.2 %collective-permute-start.4 = (bf16[128,1024]{1,0:T(8,128)(2,1)}, bf16[128,1024]{1,0:T(8,128)(2,1)S(1)}, u32[]{:S(2)}, u32[]{:S(2)}) collective-permute-start(bf16[128,1024]{1,0:T(8,128)(2,1)} %bitcast.44), channel_id=1, source_target_pairs={{0,2},{2,0},{4,6},{6,4},{1,3},{3,1},{5,7},{7,5},{8,10},{10,8},{12,... | collective-permute-start | bytes 786440 | tf_op jit(solution)/shard_map/ppermute | solution.py:340
  1.7 9.8 %collective-permute-start.5 = (bf16[128,1024]{1,0:T(8,128)(2,1)}, bf16[128,1024]{1,0:T(8,128)(2,1)S(1)}, u32[]{:S(2)}, u32[]{:S(2)}) collective-permute-start(bf16[128,1024]{1,0:T(8,128)(2,1)} %bitcast.46), channel_id=1, source_target_pairs={{0,2},{2,0},{4,6},{6,4},{1,3},{3,1},{5,7},{7,5},{8,10},{10,8},{12,... | collective-permute-start | bytes 786440 | tf_op jit(solution)/shard_map/ppermute | solution.py:340
  7.0 8.8 %collective-permute-start.1 = (bf16[256,384]{1,0:T(8,128)(2,1)S(1)}, bf16[256,384]{1,0:T(8,128)(2,1)S(1)}, u32[]{:S(2)}, u32[]{:S(2)}) collective-permute-start(bf16[256,384]{1,0:T(8,128)(2,1)S(1)} %get-tuple-element.44), channel_id=1, source_target_pairs={{0,4},{1,5},{2,6},{3,7},{4,0},{5,1},{6,2},{7,3},{8,12},{9,13},{10,... | collective-permute-start | bytes 589832 | tf_op jit(solution)/shard_map/ppermute | solution.py:349
  9.9 10.9 %collective-permute-start.2 = (bf16[256,384]{1,0:T(8,128)(2,1)S(1)}, bf16[256,384]{1,0:T(8,128)(2,1)S(1)}, u32[]{:S(2)}, u32[]{:S(2)}) collective-permute-start(bf16[256,384]{1,0:T(8,128)(2,1)S(1)} %get-tuple-element.45), channel_id=1, source_target_pairs={{0,1},{1,0},{2,3},{3,2},{4,5},{5,4},{6,7},{7,6},{8,9},{9,8},{10,11... | collective-permute-start | bytes 589832 | tf_op jit(solution)/shard_map/ppermute | solution.py:349
  11.4 9.4 %collective-permute-start.3 = (bf16[256,384]{1,0:T(8,128)(2,1)S(1)}, bf16[256,384]{1,0:T(8,128)(2,1)S(1)}, u32[]{:S(2)}, u32[]{:S(2)}) collective-permute-start(bf16[256,384]{1,0:T(8,128)(2,1)S(1)} %get-tuple-element.46), channel_id=1, source_target_pairs={{0,5},{1,4},{2,7},{3,6},{4,1},{5,0},{6,3},{7,2},{8,13},{9,12},{10,... | collective-permute-start | bytes 589832 | tf_op jit(solution)/shard_map/ppermute | solution.py:349
  20.8 10.5 %collective-permute-start.7 = (bf16[512,256]{1,0:T(8,128)(2,1)S(1)}, bf16[512,256]{1,0:T(8,128)(2,1)S(1)}, u32[]{:S(2)}, u32[]{:S(2)}) collective-permute-start(bf16[512,256]{1,0:T(8,128)(2,1)S(1)} %get-tuple-element.56), channel_id=1, source_target_pairs={{0,4},{1,5},{2,6},{3,7},{4,0},{5,1},{6,2},{7,3},{8,12},{9,13},{10,... | collective-permute-start | bytes 786440 | tf_op jit(solution)/shard_map/ppermute | solution.py:349
  22.0 12.9 %collective-permute-start.8 = (bf16[512,256]{1,0:T(8,128)(2,1)S(1)}, bf16[512,256]{1,0:T(8,128)(2,1)S(1)}, u32[]{:S(2)}, u32[]{:S(2)}) collective-permute-start(bf16[512,256]{1,0:T(8,128)(2,1)S(1)} %get-tuple-element.57), channel_id=1, source_target_pairs={{0,1},{1,0},{2,3},{3,2},{4,5},{5,4},{6,7},{7,6},{8,9},{9,8},{10,11... | collective-permute-start | bytes 786440 | tf_op jit(solution)/shard_map/ppermute | solution.py:349
  22.9 12.0 %collective-permute-start.9 = (bf16[512,256]{1,0:T(8,128)(2,1)S(1)}, bf16[512,256]{1,0:T(8,128)(2,1)S(1)}, u32[]{:S(2)}, u32[]{:S(2)}) collective-permute-start(bf16[512,256]{1,0:T(8,128)(2,1)S(1)} %get-tuple-element.58), channel_id=1, source_target_pairs={{0,5},{1,4},{2,7},{3,6},{4,1},{5,0},{6,3},{7,2},{8,13},{9,12},{10,... | collective-permute-start | bytes 786440 | tf_op jit(solution)/shard_map/ppermute | solution.py:349
  40.7 16.5 %collective-permute-start.13 = (bf16[160,256]{1,0:T(8,128)(2,1)S(1)}, bf16[160,256]{1,0:T(8,128)(2,1)S(1)}, u32[]{:S(2)}, u32[]{:S(2)}) collective-permute-start(bf16[160,256]{1,0:T(8,128)(2,1)S(1)} %get-tuple-element.72), channel_id=1, source_target_pairs={{0,2},{2,0},{4,6},{6,4},{1,3},{3,1},{5,7},{7,5},{8,10},{10,8},{12,... | collective-permute-start | bytes 245768 | tf_op jit(solution)/shard_map/ppermute | solution.py:340
  40.8 9.1 %collective-permute-start.10 = (bf16[2,160,256]{2,1,0:T(8,128)(2,1)S(1)}, bf16[2,160,256]{2,1,0:T(8,128)(2,1)S(1)}, u32[]{:S(2)}, u32[]{:S(2)}) collective-permute-start(bf16[2,160,256]{2,1,0:T(8,128)(2,1)S(1)} %get-tuple-element.63), channel_id=1, source_target_pairs={{0,4},{1,5},{2,6},{3,7},{4,0},{5,1},{6,2},{7,3},{8,12},{9,13},{10,... | collective-permute-start | bytes 491528 | tf_op jit(solution)/shard_map/ppermute | solution.py:349
  41.4 9.9 %collective-permute-start.11 = (bf16[2,160,256]{2,1,0:T(8,128)(2,1)S(1)}, bf16[2,160,256]{2,1,0:T(8,128)(2,1)S(1)}, u32[]{:S(2)}, u32[]{:S(2)}) collective-permute-start(bf16[2,160,256]{2,1,0:T(8,128)(2,1)S(1)} %get-tuple-element.64), channel_id=1, source_target_pairs={{0,1},{1,0},{2,3},{3,2},{4,5},{5,4},{6,7},{7,6},{8,9},{9,8},{10,11... | collective-permute-start | bytes 491528 | tf_op jit(solution)/shard_map/ppermute | solution.py:349
  42.8 10.0 %collective-permute-start.12 = (bf16[2,160,256]{2,1,0:T(8,128)(2,1)S(1)}, bf16[2,160,256]{2,1,0:T(8,128)(2,1)S(1)}, u32[]{:S(2)}, u32[]{:S(2)}) collective-permute-start(bf16[2,160,256]{2,1,0:T(8,128)(2,1)S(1)} %get-tuple-element.65), channel_id=1, source_target_pairs={{0,5},{1,4},{2,7},{3,6},{4,1},{5,0},{6,3},{7,2},{8,13},{9,12},{10,... | collective-permute-start | bytes 491528 | tf_op jit(solution)/shard_map/ppermute | solution.py:349
  49.2 7.9 %collective-permute-start.17 = (bf16[2,128,384]{2,1,0:T(8,128)(2,1)S(1)}, bf16[2,128,384]{2,1,0:T(8,128)(2,1)S(1)}, u32[]{:S(2)}, u32[]{:S(2)}) collective-permute-start(bf16[2,128,384]{2,1,0:T(8,128)(2,1)S(1)} %get-tuple-element.74), channel_id=1, source_target_pairs={{0,4},{1,5},{2,6},{3,7},{4,0},{5,1},{6,2},{7,3},{8,12},{9,13},{10,... | collective-permute-start | bytes 589832 | tf_op jit(solution)/shard_map/ppermute | solution.py:349
  49.9 10.9 %collective-permute-start.18 = (bf16[2,128,384]{2,1,0:T(8,128)(2,1)S(1)}, bf16[2,128,384]{2,1,0:T(8,128)(2,1)S(1)}, u32[]{:S(2)}, u32[]{:S(2)}) collective-permute-start(bf16[2,128,384]{2,1,0:T(8,128)(2,1)S(1)} %get-tuple-element.75), channel_id=1, source_target_pairs={{0,1},{1,0},{2,3},{3,2},{4,5},{5,4},{6,7},{7,6},{8,9},{9,8},{10,11... | collective-permute-start | bytes 589832 | tf_op jit(solution)/shard_map/ppermute | solution.py:349
  51.3 9.5 %collective-permute-start.19 = (bf16[2,128,384]{2,1,0:T(8,128)(2,1)S(1)}, bf16[2,128,384]{2,1,0:T(8,128)(2,1)S(1)}, u32[]{:S(2)}, u32[]{:S(2)}) collective-permute-start(bf16[2,128,384]{2,1,0:T(8,128)(2,1)S(1)} %get-tuple-element.76), channel_id=1, source_target_pairs={{0,5},{1,4},{2,7},{3,6},{4,1},{5,0},{6,3},{7,2},{8,13},{9,12},{10,... | collective-permute-start | bytes 589832 | tf_op jit(solution)/shard_map/ppermute | solution.py:349
  52.8 4.9 %collective-permute-start.16 = (bf16[160,256]{1,0:T(8,128)(2,1)S(1)}, bf16[160,256]{1,0:T(8,128)(2,1)S(1)}, u32[]{:S(2)}, u32[]{:S(2)}) collective-permute-start(bf16[160,256]{1,0:T(8,128)(2,1)S(1)} %slice_bitcast_fusion.3), channel_id=1, source_target_pairs={{0,2},{2,0},{4,6},{6,4},{1,3},{3,1},{5,7},{7,5},{8,10},{10,8},{12,... | collective-permute-start | bytes 245768 | tf_op jit(solution)/shard_map/ppermute | solution.py:340
  57.1 1.3 %collective-permute-start.15 = (bf16[160,256]{1,0:T(8,128)(2,1)S(1)}, bf16[160,256]{1,0:T(8,128)(2,1)S(1)}, u32[]{:S(2)}, u32[]{:S(2)}) collective-permute-start(bf16[160,256]{1,0:T(8,128)(2,1)S(1)} %slice_bitcast_fusion.4), channel_id=1, source_target_pairs={{0,2},{2,0},{4,6},{6,4},{1,3},{3,1},{5,7},{7,5},{8,10},{10,8},{12,... | collective-permute-start | bytes 245768 | tf_op jit(solution)/shard_map/ppermute | solution.py:340
  57.2 3.6 %collective-permute-start.20 = (bf16[128,384]{1,0:T(8,128)(2,1)S(1)}, bf16[128,384]{1,0:T(8,128)(2,1)S(1)}, u32[]{:S(2)}, u32[]{:S(2)}) collective-permute-start(bf16[128,384]{1,0:T(8,128)(2,1)S(1)} %slice_bitcast_fusion), channel_id=1, source_target_pairs={{0,2},{2,0},{4,6},{6,4},{1,3},{3,1},{5,7},{7,5},{8,10},{10,8},{12,... | collective-permute-start | bytes 294920 | tf_op jit(solution)/shard_map/ppermute | solution.py:340
  57.8 1.3 %collective-permute-start.14 = (bf16[160,256]{1,0:T(8,128)(2,1)S(1)}, bf16[160,256]{1,0:T(8,128)(2,1)S(1)}, u32[]{:S(2)}, u32[]{:S(2)}) collective-permute-start(bf16[160,256]{1,0:T(8,128)(2,1)S(1)} %slice_bitcast_fusion.5), channel_id=1, source_target_pairs={{0,2},{2,0},{4,6},{6,4},{1,3},{3,1},{5,7},{7,5},{8,10},{10,8},{12,... | collective-permute-start | bytes 245768 | tf_op jit(solution)/shard_map/ppermute | solution.py:340
  58.4 3.0 %collective-permute-start.21 = (bf16[128,384]{1,0:T(8,128)(2,1)S(1)}, bf16[128,384]{1,0:T(8,128)(2,1)S(1)}, u32[]{:S(2)}, u32[]{:S(2)}) collective-permute-start(bf16[128,384]{1,0:T(8,128)(2,1)S(1)} %get-tuple-element.79), channel_id=1, source_target_pairs={{0,2},{2,0},{4,6},{6,4},{1,3},{3,1},{5,7},{7,5},{8,10},{10,8},{12,... | collective-permute-start | bytes 294920 | tf_op jit(solution)/shard_map/ppermute | solution.py:340
  60.8 1.4 %collective-permute-start.23 = (bf16[128,384]{1,0:T(8,128)(2,1)S(1)}, bf16[128,384]{1,0:T(8,128)(2,1)S(1)}, u32[]{:S(2)}, u32[]{:S(2)}) collective-permute-start(bf16[128,384]{1,0:T(8,128)(2,1)S(1)} %slice_bitcast_fusion.1), channel_id=1, source_target_pairs={{0,2},{2,0},{4,6},{6,4},{1,3},{3,1},{5,7},{7,5},{8,10},{10,8},{12,... | collective-permute-start | bytes 294920 | tf_op jit(solution)/shard_map/ppermute | solution.py:340
  61.0 1.3 %collective-permute-start.22 = (bf16[128,384]{1,0:T(8,128)(2,1)S(1)}, bf16[128,384]{1,0:T(8,128)(2,1)S(1)}, u32[]{:S(2)}, u32[]{:S(2)}) collective-permute-start(bf16[128,384]{1,0:T(8,128)(2,1)S(1)} %slice_bitcast_fusion.2), channel_id=1, source_target_pairs={{0,2},{2,0},{4,6},{6,4},{1,3},{3,1},{5,7},{7,5},{8,10},{10,8},{12,... | collective-permute-start | bytes 294920 | tf_op jit(solution)/shard_map/ppermute | solution.py:340
  (4 other events, 4.3 us)

commit v4 on v2

v4 whole, which is shorter than its diff:
```python
import functools
import math

import jax
import jax.numpy as jnp
from jax import lax
from jax.experimental import pallas as pl
from jax.experimental.pallas import tpu as pltpu
from jax.sharding import PartitionSpec as P

BF = jnp.bfloat16
F32 = jnp.float32
HD = 64
GROUP = ("seq", "head")
VM = pl.BlockSpec(memory_space=pltpu.VMEM)
SM = pl.BlockSpec(memory_space=pltpu.SMEM)
SCALE = 1.0 / math.sqrt(HD)
MIB = 1 << 20


def sds(shape, dtype=BF):
    return jax.ShapeDtypeStruct(shape, dtype)


def call(kernel, name, ins, outs, mib, scratch=(), cost=None):
    smem = [a.dtype == jnp.int32 for a in ins]
    return pl.pallas_call(
        kernel,
        out_shape=outs,
        in_specs=[SM if s else VM for s in smem],
        out_specs=jax.tree.map(lambda _: VM, outs),
        scratch_shapes=scratch,
        name=name,
        cost_estimate=cost,
        compiler_params=pltpu.CompilerParams(vmem_limit_bytes=mib * MIB),
    )(*ins)


def cost(scores, products):
    return pl.CostEstimate(
        flops=2 * 256 * scores * products, bytes_accessed=4 * scores, transcendentals=scores
    )


def dot(a, b):
    return jnp.dot(a, b, preferred_element_type=F32)


def dot_nt(a, b):
    return lax.dot_general(a, b, (((1,), (1,)), ((), ())), preferred_element_type=F32)


def softmax_t(scores):
    top = jnp.max(scores, axis=0, keepdims=True)
    e = jnp.exp((scores - top) * SCALE)
    return (e * (1.0 / jnp.sum(e, axis=0, keepdims=True))).astype(BF)


def head_columns(meta_ref, d, ref, base, p, W):
    at = base + meta_ref[1 + d] * 2 * W
    if W == HD:
        block = ref[:, pl.ds(pl.multiple_of(at, 128), 128)]
        return jnp.where(meta_ref[0] == 0, block[:, :HD], block[:, HD:])
    at = at + meta_ref[0] * W + (p // 2) * 128
    half = slice((p % 2) * HD, (p % 2 + 1) * HD)
    return ref[:, pl.ds(pl.multiple_of(at, 128), 128)][:, half]


def beside(a, b):
    return jnp.concatenate([a, b], axis=1)


def pack_own_kernel(meta_ref, x_ref, cq_ref, out_ref, *, p):
    C, R2, _ = out_ref.shape
    R, D = cq_ref.shape
    W = D // (2 * C)
    for d in range(C):
        cols = functools.partial(head_columns, meta_ref, d, p=p, W=W)
        out_ref[d, :R] = beside(cols(x_ref, 0), cols(x_ref, D))
        out_ref[d, R:] = beside(cols(x_ref, 2 * D), cols(cq_ref, 0))


def pack_sib_kernel(meta_ref, own_ref, go_ref, t_ref, xs_ref, cqs_ref, gos_ref, ts_ref, *msgs, p):
    C = len(msgs)
    R, D = go_ref.shape
    W = D // (2 * C)
    keep = meta_ref[2 + C] == 1
    for d in range(C):
        cols = functools.partial(head_columns, meta_ref, d, p=p, W=W)
        msg = msgs[d]
        msg[:R] = own_ref[d, :R]
        msg[R : 2 * R] = beside(cols(xs_ref, 0), cols(xs_ref, D))
        msg[2 * R : 3 * R] = own_ref[d, R:]
        msg[3 * R : 4 * R] = beside(cols(xs_ref, 2 * D), cols(cqs_ref, 0))
        msg[4 * R : 5 * R] = beside(cols(go_ref, 0), cols(gos_ref, 0))
        own = beside(cols(t_ref, 0), cols(t_ref, D))
        sib = beside(cols(ts_ref, 0), cols(ts_ref, D))
        msg[5 * R :] = jnp.where(keep, own, sib)


def pieces(refs):
    C = len(refs) // 2
    out = []
    for d in range(C):
        if d == 0:
            out.append(lambda rows, lanes, ref=refs[0]: ref[rows, lanes])
        else:
            out.append(lambda rows, lanes, ref=refs[d]: ref[0, rows, lanes])
        out.append(lambda rows, lanes, ref=refs[C + d]: ref[rows, lanes])
    return out


def put(msgs, block, rows, lanes, value):
    d, e = block // 2, block % 2
    if d == 0:
        msgs[e][rows, lanes] = value
    else:
        msgs[d + 1][e, rows, lanes] = value


def message_shapes(C, rows):
    return (sds((rows, 128)),) * 2 + (sds((2, rows, 128)),) * (C - 1)


def layer_kernel(meta_ref, *refs, C, R, M):
    ins, outs = refs[:C], refs[C : 2 * C + 1]
    k_ref, v_ref, kT_ref, vT_ref, t_ref, dt_ref, dk_ref, dv_ref = refs[2 * C + 1 :]
    QB = 2 * R
    MR = M // (2 * C)
    left, right = slice(0, HD), slice(HD, 2 * HD)
    for b in range(C):
        rows = slice(b * QB, (b + 1) * QB)
        k, v = ins[b][:QB, right], ins[b][QB : 2 * QB, left]
        k_ref[rows], v_ref[rows] = k, v
        kT_ref[:, rows], vT_ref[:, rows] = k.T, v.T
    for d in range(C):

        @pl.when(meta_ref[1 + C] == d)
        def _():
            t_ref[...] = ins[d][5 * R :, :]

    tk, tv = t_ref[:, left], t_ref[:, right]
    tkT, tvT = tk.T, tv.T
    k, v, kT, vT = k_ref[...], v_ref[...], kT_ref[...], vT_ref[...]
    dtk = dtv = None
    for b in range(C):
        q, cq = ins[b][:QB, left], ins[b][QB : 2 * QB, right]
        go = ins[b][4 * R : 5 * R, :]
        go = jnp.concatenate([go[:, left], go[:, right]], axis=0)
        p = softmax_t(dot_nt(k, q))
        oT = dot(vT, p)
        att = oT.T.astype(BF).astype(F32)
        x = (att + cq.astype(F32)).astype(BF)
        cp = softmax_t(dot_nt(tk, x))
        mix = dot(tvT, cp)
        delta = jnp.sum(go.T.astype(F32) * mix, axis=0, keepdims=True)
        ds = (cp.astype(F32) * (dot_nt(tv, go) - delta)).astype(BF)
        dq = dot(tkT, ds).T * SCALE
        a, c = dot(ds, x), dot(cp, go)
        dtk = a if dtk is None else dtk + a
        dtv = c if dtv is None else dtv + c
        combined, dcq = (att + mix.T).astype(BF), dq.astype(BF)
        ag = (go.astype(F32) + dq).astype(BF)
        delta = jnp.sum(ag.T.astype(F32) * oT, axis=0, keepdims=True)
        ds = (p.astype(F32) * (dot_nt(v, ag) - delta)).astype(BF)
        dk, dv = dot(ds, q), dot(p, ag)
        if b == 0:
            dk_ref[...] = dk
            dv_ref[...] = dv
        else:
            dk_ref[...] += dk
            dv_ref[...] += dv
        dq = (dot(kT, ds).T * SCALE).astype(BF)
        for e in range(2):
            part = slice(e * R, (e + 1) * R)
            put(outs, 2 * b + e, slice(0, R), left, dq[part])
            put(outs, 2 * b + e, slice(R, 2 * R), right, combined[part])
            h = R // 2
            put(
                outs,
                2 * b + e,
                slice(2 * R, 2 * R + h),
                slice(None),
                beside(dcq[e * R : e * R + h], dcq[e * R + h : (e + 1) * R]),
            )
    dt_ref[...] = beside(dtk * SCALE, dtv).astype(BF)
    for i in range(2 * C):
        part = slice(i * R, (i + 1) * R)
        put(outs, i, slice(0, R), right, (dk_ref[part] * SCALE).astype(BF))
        put(outs, i, slice(R, 2 * R), left, dv_ref[part].astype(BF))
        start = pl.multiple_of(meta_ref[3 + C + i] * MR, MR)
        put(outs, i, slice(2 * R + R // 2, None), slice(None), dt_ref[pl.ds(start, MR), :])


def unpack_kernel(meta_ref, *refs, C, H):
    passes = [pieces(refs[2 * C * p : 2 * C * (p + 1)]) for p in range(H)]
    qkv_ref, comb_ref, dcq_ref, dt_ref = refs[2 * C * H :]
    R, D = comb_ref.shape
    W = D // (2 * C)
    side = meta_ref[0]
    left, right = slice(0, HD), slice(HD, 2 * HD)
    first, second = slice(0, R), slice(R, 2 * R)
    low, high, end = (
        slice(2 * R, 2 * R + R // 2),
        slice(2 * R, 2 * R + R // 2),
        slice(2 * R + R // 2, None),
    )

    def dcq(piece):
        return jnp.concatenate([piece(low, left), piece(high, right)], axis=0)

    parts = [
        (qkv_ref, 0, lambda piece: piece(first, left)),
        (qkv_ref, D, lambda piece: piece(first, right)),
        (qkv_ref, 2 * D, lambda piece: piece(second, left)),
        (comb_ref, 0, lambda piece: piece(second, right)),
        (dcq_ref, 0, dcq),
        (dt_ref, 0, lambda piece: piece(end, left)),
        (dt_ref, D, lambda piece: piece(end, right)),
    ]
    for d in range(C):
        for ref, base, read in parts:
            at = base + meta_ref[1 + d] * 2 * W
            if H == 1:
                a, b = read(passes[0][2 * d]), read(passes[0][2 * d + 1])
                pair = beside(jnp.where(side == 0, a, b), jnp.where(side == 0, b, a))
                ref[:, pl.ds(pl.multiple_of(at, 128), 128)] = pair
                continue
            for e in range(2):
                core = side if e == 0 else 1 - side
                for p in range(0, H, 2):
                    pair = beside(read(passes[p][2 * d + e]), read(passes[p + 1][2 * d + e]))
                    start = pl.multiple_of(at + core * W + p * HD, 128)
                    ref[:, pl.ds(start, 128)] = pair


def body(self_qkv, cross_query, thermal_kv, owners, grad_out):
    S, Hd = lax.axis_size("seq"), lax.axis_size("head")
    X = S // 2
    C = X * Hd
    R, D = cross_query.shape[1:]
    W = D // (2 * C)
    L = 2 * C * R
    M = thermal_kv.shape[2]
    MR = M // (2 * C)
    offsets = [(i, j) for j in range(Hd) for i in range(X)]
    s, h = lax.axis_index("seq"), lax.axis_index("head")
    side, x = s % 2, s // 2
    owner_s, owner_h = owners[0] // Hd, owners[0] % Hd
    away = (x - owner_s // 2 + X) % X + X * ((h - owner_h + Hd) % Hd)
    keep = (owner_s % 2 == side).astype(jnp.int32)
    chips = [((x + i) % X) * Hd + (h + j) % Hd for i, j in offsets]
    ids = []
    for i, j in offsets:
        for e in (0, 1):
            ids.append((((x - i + X) % X) * 2 + (side if e == 0 else 1 - side)) * Hd + (h - j + Hd) % Hd)
    meta = jnp.stack([side, *chips, away, keep, *ids]).astype(jnp.int32)

    def to_sibling(a):
        return lax.ppermute(a, "seq", [(i, i ^ 1) for i in range(S)])

    def to_chip(a, d, sign):
        i, j = offsets[d]
        pairs = []
        for p in range(S):
            for q in range(Hd):
                there = ((p // 2 + sign * i) % X) * 2 + p % 2
                pairs.append((p * Hd + q, there * Hd + (q + sign * j) % Hd))
        return lax.ppermute(a, GROUP, pairs)

    def after(arrays, *gates):
        return lax.optimization_barrier((list(arrays), gates))[0]

    bind = functools.partial
    H = W // HD
    RO = 2 * R + R // 2 + MR
    own = (self_qkv[0], cross_query[0], grad_out[0], thermal_kv[0, 0])
    xs, cqs, gos, ts = [to_sibling(a) for a in own]
    x, cq, go, t = own
    msgs, got = [], []
    for p in range(H):
        if p:
            x, cq = after([x, cq], *msgs[p - 1])
        half = call(
            bind(pack_own_kernel, p=p), f"pack_own_{p}", [meta, x, cq], sds((C, 2 * R, 128)), 8
        )
        msgs.append(
            call(
                bind(pack_sib_kernel, p=p),
                f"pack_sib_{p}",
                [meta, half, go, t, xs, cqs, gos, ts],
                (sds((5 * R + M, 128)),) * C,
                12,
            )
        )
        got.append([to_chip(msgs[p][d], d, 1) for d in range(1, C)])
        if p:
            got[p - 1] = after(got[p - 1], *msgs[p])
    backs, outs = [], []
    for p in range(H):
        out = call(
            bind(layer_kernel, C=C, R=R, M=M),
            f"layer_{p}",
            [meta, msgs[p][0], *got[p]],
            message_shapes(C, RO),
            32,
            [pltpu.VMEM((L, HD), BF)] * 2
            + [pltpu.VMEM((HD, L), BF)] * 2
            + [pltpu.VMEM((M, 128), BF)] * 2
            + [pltpu.VMEM((L, HD), F32)] * 2,
            cost(L * L + L * M, 6),
        )
        outs.append(out)
        if p + 1 < H:
            got[p + 1] = after(got[p + 1], *out)
        backs.append([to_chip(out[d + 1], d, -1) for d in range(1, C)])
    pieces_in = []
    for p in range(H):
        back = after(backs[p], outs[p + 1][0]) if p + 1 < H else backs[p]
        relayed = [to_sibling(outs[p][1])] + [to_sibling(g[1]) for g in back]
        if p + 1 < H:
            backs[p + 1] = after(backs[p + 1], *relayed)
        pieces_in += [outs[p][0], *back, *relayed]
    grad_qkv, combined, grad_cross, grad_thermal = call(
        bind(unpack_kernel, C=C, H=H),
        "unpack",
        [meta, *pieces_in],
        (sds((R, 3 * D)), sds((R, D)), sds((R, D)), sds((MR, 2 * D))),
        12,
    )
    return (combined[None], grad_qkv[None], grad_cross[None], grad_thermal[None])


def solution(mesh):
    rows = P("img", GROUP, None)
    return jax.shard_map(
        body,
        mesh=mesh,
        in_specs=(rows, rows, P("img", GROUP, None, None), P("img"), rows),
        out_specs=(rows, rows, rows, rows),
        check_vma=False,
    )
```

time: 80.2 us -> 63.9 us (0.80)
  waiting for transfers between devices: 27.2 us -> 12.1 us
  Pallas kernels: 22.1 us -> 27.5 us
  starting transfers between devices: 23.4 us -> 20.1 us
  local copies, waits for them, and re-layouts: 5.54 us -> 2.32 us
    ppermute x12, waiting for transfers between devices: 25.2 us -> 10.7 us  [to_chip(): return lax.ppermute(a, GROUP, pairs)]
    pallas_call x7, Pallas kernels: 22.1 us -> 27.5 us  [call(): pl.pallas_call(kernel, out_shape=outs, in_specs=[SM if s else VM for s in...]
    ppermute x17 -> x12, starting transfers between devices: 4.7 us -> 2.37 us  [to_sibling(): return lax.ppermute(a, 'seq', [(i, i ^ 1) for i in range(S)])]
    unnamed x8 -> x12, local copies, waits for them, and re-layouts: 4.25 us -> 2.18 us
    dynamic_slice x1 -> x0, local copies, waits for them, and re-layouts: 1.08 us -> none  [body(): lax.dynamic_slice_in_dim(thermal, (1 - side) * half, half, axis=0)]
    ppermute x12, starting transfers between devices: 18.7 us -> 17.8 us  [to_chip(): return lax.ppermute(a, GROUP, pairs)]
    ppermute x17 -> x12, waiting for transfers between devices: 2.06 us -> 1.36 us  [to_sibling(): return lax.ppermute(a, 'seq', [(i, i ^ 1) for i in range(S)])]
  transfers between devices with their start and end apart: 29 -> 24, of which waited for: 10 -> 8; matrix products, arithmetic and copies ran while one was open for 0% -> 0% of each run, Pallas kernels for 19% -> 38%
where the time goes in v4:
time: 63.9 us; the launch traced here: 63.6 us
  Pallas kernels  27.5 us (43%)
  starting transfers between devices  20.1 us (31%)
  waiting for transfers between devices  12.1 us (19%)
  local copies, waits for them, and re-layouts  2.32 us (4%)
  between operations  1.55 us (2%)
    pallas_call x7, Pallas kernels, call(): pl.pallas_call(kernel, out_shape=outs, in_specs=[SM if s else VM for s in...  27.5 us
    ppermute x12, starting transfers between devices, to_chip(): return lax.ppermute(a, GROUP, pairs)  17.8 us
    ppermute x12, waiting for transfers between devices, to_chip(): return lax.ppermute(a, GROUP, pairs)  10.7 us
    ppermute x12, starting transfers between devices, to_sibling(): return lax.ppermute(a, 'seq', [(i, i ^ 1) for i in range(S)])  2.37 us
    unnamed x12, local copies, waits for them, and re-layouts  2.18 us
    ppermute x12, waiting for transfers between devices, to_sibling(): return lax.ppermute(a, 'seq', [(i, i ^ 1) for i in range(S)])  1.36 us
  transfers between devices with their start and end apart: 24, of which 8 were waited for; matrix products, arithmetic and copies ran while one was open for 0% of the time, Pallas kernels for 38%

profile of v4, /device:TPU:0, one launch (start us, length us, event | category | flops | bytes accessed | tf_op | source)
XLA Modules:
  0.0 63.6 jit_solution(16137543864694088801)
XLA Ops:
  2.6 1.1 %copy-done.1 = bf16[1,128,3072]{2,1,0:T(8,128)(2,1)S(1)} copy-done((bf16[1,128,3072]{2,1,0:T(8,128)(2,1)S(1)}, bf16[1,128,3072]{2,1,0:T(8,128)(2,1)}, u32[]{:S(2)}) %copy-start.1) | copy-done | bytes 786456
  3.7 0.9 %copy-done.3 = bf16[1,128,1024]{2,1,0:T(8,128)(2,1)S(1)} copy-done((bf16[1,128,1024]{2,1,0:T(8,128)(2,1)S(1)}, bf16[1,128,1024]{2,1,0:T(8,128)(2,1)}, u32[]{:S(2)}) %copy-start.3) | copy-done | bytes 262168
  4.7 0.7 %pack_own_0.1.own_ref = bf16[4,256,128]{2,1,0:T(8,128)(2,1)S(1)} custom-call(s32[15]{0:T(128)S(1)} %stack.67.meta_ref, bf16[128,3072]{1,0:T(8,128)(2,1)S(1)} %bitcast.44, bf16[128,1024]{1,0:T(8,128)(2,1)S(1)} %bitcast.47), custom_call_target="tpu_custom_call" | custom-call | tf_op jit(solution)/shard_map/pack_own_0/pallas_call | solution.py:27
  5.6 1.0 %pack_sib_0.1 = (bf16[896,128]{1,0:T(8,128)(2,1)S(1)}, bf16[896,128]{1,0:T(8,128)(2,1)S(1)}, bf16[896,128]{1,0:T(8,128)(2,1)S(1)}, bf16[896,128]{1,0:T(8,128)(2,1)S(1)}) custom-call(s32[15]{0:T(128)S(1)} %stack.67.meta_ref, bf16[4,256,128]{2,1,0:T(8,128)(2,1)S(1)} %pack_own_0.1.own_ref, bf16[128,1024]{1,0:T(8,128)(2,1)S(1)} %bitcast.50, ...), custom_call_target="tpu_custom_call" | custom-call | tf_op jit(solution)/shard_map/pack_sib_0/pallas_call | solution.py:27
  6.7 3.0 %collective-permute-start.4 = (bf16[896,128]{1,0:T(8,128)(2,1)S(1)}, bf16[896,128]{1,0:T(8,128)(2,1)S(1)}, u32[]{:S(2)}, u32[]{:S(2)}) collective-permute-start(bf16[896,128]{1,0:T(8,128)(2,1)S(1)} %get-tuple-element.41), channel_id=1, source_target_pairs={{0,4},{1,5},{2,6},{3,7},{4,0},{5,1},{6,2},{7,3},{8,12},{9,13},{10,... | collective-permute-start | bytes 688136 | tf_op jit(solution)/shard_map/ppermute | solution.py:269
  9.6 1.5 %collective-permute-start.5 = (bf16[896,128]{1,0:T(8,128)(2,1)S(1)}, bf16[896,128]{1,0:T(8,128)(2,1)S(1)}, u32[]{:S(2)}, u32[]{:S(2)}) collective-permute-start(bf16[896,128]{1,0:T(8,128)(2,1)S(1)} %get-tuple-element.42), channel_id=1, source_target_pairs={{0,1},{1,0},{2,3},{3,2},{4,5},{5,4},{6,7},{7,6},{8,9},{9,8},{10,11... | collective-permute-start | bytes 688136 | tf_op jit(solution)/shard_map/ppermute | solution.py:269
  11.2 0.7 %pack_own_1.1.own_ref = bf16[4,256,128]{2,1,0:T(8,128)(2,1)S(1)} custom-call(s32[15]{0:T(128)S(1)} %stack.67.meta_ref, bf16[128,3072]{1,0:T(8,128)(2,1)S(1)} %bitcast.45, bf16[128,1024]{1,0:T(8,128)(2,1)S(1)} %bitcast.48), custom_call_target="tpu_custom_call" | custom-call | tf_op jit(solution)/shard_map/pack_own_1/pallas_call | solution.py:27
  11.9 1.0 %pack_sib_1.1 = (bf16[896,128]{1,0:T(8,128)(2,1)S(1)}, bf16[896,128]{1,0:T(8,128)(2,1)S(1)}, bf16[896,128]{1,0:T(8,128)(2,1)S(1)}, bf16[896,128]{1,0:T(8,128)(2,1)S(1)}) custom-call(s32[15]{0:T(128)S(1)} %stack.67.meta_ref, bf16[4,256,128]{2,1,0:T(8,128)(2,1)S(1)} %pack_own_1.1.own_ref, bf16[128,1024]{1,0:T(8,128)(2,1)S(1)} %bitcast.51, ...), custom_call_target="tpu_custom_call" | custom-call | tf_op jit(solution)/shard_map/pack_sib_1/pallas_call | solution.py:27
  12.9 2.0 %collective-permute-start.10 = (bf16[896,128]{1,0:T(8,128)(2,1)S(1)}, bf16[896,128]{1,0:T(8,128)(2,1)S(1)}, u32[]{:S(2)}, u32[]{:S(2)}) collective-permute-start(bf16[896,128]{1,0:T(8,128)(2,1)S(1)} %get-tuple-element.47), channel_id=1, source_target_pairs={{0,4},{1,5},{2,6},{3,7},{4,0},{5,1},{6,2},{7,3},{8,12},{9,13},{10,... | collective-permute-start | bytes 688136 | tf_op jit(solution)/shard_map/ppermute | solution.py:269
  14.9 1.5 %collective-permute-start.11 = (bf16[896,128]{1,0:T(8,128)(2,1)S(1)}, bf16[896,128]{1,0:T(8,128)(2,1)S(1)}, u32[]{:S(2)}, u32[]{:S(2)}) collective-permute-start(bf16[896,128]{1,0:T(8,128)(2,1)S(1)} %get-tuple-element.48), channel_id=1, source_target_pairs={{0,1},{1,0},{2,3},{3,2},{4,5},{5,4},{6,7},{7,6},{8,9},{9,8},{10,11... | collective-permute-start | bytes 688136 | tf_op jit(solution)/shard_map/ppermute | solution.py:269
  16.5 2.6 %collective-permute-start.12 = (bf16[896,128]{1,0:T(8,128)(2,1)S(1)}, bf16[896,128]{1,0:T(8,128)(2,1)S(1)}, u32[]{:S(2)}, u32[]{:S(2)}) collective-permute-start(bf16[896,128]{1,0:T(8,128)(2,1)S(1)} %get-tuple-element.49), channel_id=1, source_target_pairs={{0,5},{1,4},{2,7},{3,6},{4,1},{5,0},{6,3},{7,2},{8,13},{9,12},{10,... | collective-permute-start | bytes 688136 | tf_op jit(solution)/shard_map/ppermute | solution.py:269
  19.1 3.5 %collective-permute-done.5.refs_2_ = bf16[896,128]{1,0:T(8,128)(2,1)S(1)} collective-permute-done((bf16[896,128]{1,0:T(8,128)(2,1)S(1)}, bf16[896,128]{1,0:T(8,128)(2,1)S(1)}, u32[]{:S(2)}, u32[]{:S(2)}) %collective-permute-start.5) | collective-permute-done | bytes 229408 | tf_op jit(solution)/shard_map/ppermute | solution.py:269
  22.6 10.7 %layer_0.1 = (bf16[352,128]{1,0:T(8,128)(2,1)S(1)}, bf16[352,128]{1,0:T(8,128)(2,1)S(1)}, bf16[2,352,128]{2,1,0:T(8,128)(2,1)S(1)}, bf16[2,352,128]{2,1,0:T(8,128)(2,1)S(1)}, bf16[2,352,128]{2,1,0:T(8,128)(2,1)S(1)}) custom-call(s32[15]{0:T(128)S(1)} %stack.67.meta_ref, bf16[896,128]{1,0:T(8,128)(2,1)S(1)} %get-tuple-element.40.refs_0_, ...), custom_call_target="tpu_custom_call" | custom-call | flops 4026531840 | bytes 5242880 | tf_op jit(solution)/shard_map/layer_0/pallas_call | solution.py:27
  33.4 1.5 %collective-permute-start.7 = (bf16[2,352,128]{2,1,0:T(8,128)(2,1)S(1)}, bf16[2,352,128]{2,1,0:T(8,128)(2,1)S(1)}, u32[]{:S(2)}, u32[]{:S(2)}) collective-permute-start(bf16[2,352,128]{2,1,0:T(8,128)(2,1)S(1)} %get-tuple-element.54), channel_id=1, source_target_pairs={{0,4},{1,5},{2,6},{3,7},{4,0},{5,1},{6,2},{7,3},{8,12},{9,13},{10,... | collective-permute-start | bytes 540680 | tf_op jit(solution)/shard_map/ppermute | solution.py:269
  34.9 0.7 %collective-permute-start.8 = (bf16[2,352,128]{2,1,0:T(8,128)(2,1)S(1)}, bf16[2,352,128]{2,1,0:T(8,128)(2,1)S(1)}, u32[]{:S(2)}, u32[]{:S(2)}) collective-permute-start(bf16[2,352,128]{2,1,0:T(8,128)(2,1)S(1)} %get-tuple-element.55), channel_id=1, source_target_pairs={{0,1},{1,0},{2,3},{3,2},{4,5},{5,4},{6,7},{7,6},{8,9},{9,8},{10,11... | collective-permute-start | bytes 540680 | tf_op jit(solution)/shard_map/ppermute | solution.py:269
  35.5 1.4 %collective-permute-start.9 = (bf16[2,352,128]{2,1,0:T(8,128)(2,1)S(1)}, bf16[2,352,128]{2,1,0:T(8,128)(2,1)S(1)}, u32[]{:S(2)}, u32[]{:S(2)}) collective-permute-start(bf16[2,352,128]{2,1,0:T(8,128)(2,1)S(1)} %get-tuple-element.56), channel_id=1, source_target_pairs={{0,5},{1,4},{2,7},{3,6},{4,1},{5,0},{6,3},{7,2},{8,13},{9,12},{10,... | collective-permute-start | bytes 540680 | tf_op jit(solution)/shard_map/ppermute | solution.py:269
  37.0 10.9 %layer_1.1 = (bf16[352,128]{1,0:T(8,128)(2,1)S(1)}, bf16[352,128]{1,0:T(8,128)(2,1)S(1)}, bf16[2,352,128]{2,1,0:T(8,128)(2,1)S(1)}, bf16[2,352,128]{2,1,0:T(8,128)(2,1)S(1)}, bf16[2,352,128]{2,1,0:T(8,128)(2,1)S(1)}) custom-call(s32[15]{0:T(128)S(1)} %stack.67.meta_ref, bf16[896,128]{1,0:T(8,128)(2,1)S(1)} %get-tuple-element.46.refs_0_, ...), custom_call_target="tpu_custom_call" | custom-call | flops 4026531840 | bytes 5242880 | tf_op jit(solution)/shard_map/layer_1/pallas_call | solution.py:27
  47.9 1.4 %collective-permute-start.17 = (bf16[2,352,128]{2,1,0:T(8,128)(2,1)S(1)}, bf16[2,352,128]{2,1,0:T(8,128)(2,1)S(1)}, u32[]{:S(2)}, u32[]{:S(2)}) collective-permute-start(bf16[2,352,128]{2,1,0:T(8,128)(2,1)S(1)} %get-tuple-element.65), channel_id=1, source_target_pairs={{0,4},{1,5},{2,6},{3,7},{4,0},{5,1},{6,2},{7,3},{8,12},{9,13},{10,... | collective-permute-start | bytes 540680 | tf_op jit(solution)/shard_map/ppermute | solution.py:269
  50.0 1.4 %collective-permute-start.19 = (bf16[2,352,128]{2,1,0:T(8,128)(2,1)S(1)}, bf16[2,352,128]{2,1,0:T(8,128)(2,1)S(1)}, u32[]{:S(2)}, u32[]{:S(2)}) collective-permute-start(bf16[2,352,128]{2,1,0:T(8,128)(2,1)S(1)} %get-tuple-element.67), channel_id=1, source_target_pairs={{0,5},{1,4},{2,7},{3,6},{4,1},{5,0},{6,3},{7,2},{8,13},{9,12},{10,... | collective-permute-start | bytes 540680 | tf_op jit(solution)/shard_map/ppermute | solution.py:269
  52.1 3.3 %collective-permute-done.17.refs_9_ = bf16[2,352,128]{2,1,0:T(8,128)(2,1)S(1)} collective-permute-done((bf16[2,352,128]{2,1,0:T(8,128)(2,1)S(1)}, bf16[2,352,128]{2,1,0:T(8,128)(2,1)S(1)}, u32[]{:S(2)}, u32[]{:S(2)}) %collective-permute-start.17) | collective-permute-done | bytes 180256 | tf_op jit(solution)/shard_map/ppermute | solution.py:269
  55.4 2.1 %collective-permute-done.18.refs_10_ = bf16[2,352,128]{2,1,0:T(8,128)(2,1)S(1)} collective-permute-done((bf16[2,352,128]{2,1,0:T(8,128)(2,1)S(1)}, bf16[2,352,128]{2,1,0:T(8,128)(2,1)S(1)}, u32[]{:S(2)}, u32[]{:S(2)}) %collective-permute-start.18) | collective-permute-done | bytes 180256 | tf_op jit(solution)/shard_map/ppermute | solution.py:269
  57.5 1.8 %collective-permute-done.19.refs_11_ = bf16[2,352,128]{2,1,0:T(8,128)(2,1)S(1)} collective-permute-done((bf16[2,352,128]{2,1,0:T(8,128)(2,1)S(1)}, bf16[2,352,128]{2,1,0:T(8,128)(2,1)S(1)}, u32[]{:S(2)}, u32[]{:S(2)}) %collective-permute-start.19) | collective-permute-done | bytes 180256 | tf_op jit(solution)/shard_map/ppermute | solution.py:269
  60.0 0.7 %collective-permute-done.23.refs_15_ = bf16[352,128]{1,0:T(8,128)(2,1)S(1)} collective-permute-done((bf16[352,128]{1,0:T(8,128)(2,1)S(1)}, bf16[352,128]{1,0:T(8,128)(2,1)S(1)}, u32[]{:S(2)}, u32[]{:S(2)}) %collective-permute-start.23) | collective-permute-done | bytes 90144 | tf_op jit(solution)/shard_map/ppermute | solution.py:260
  61.2 2.5 %unpack.1 = (bf16[128,3072]{1,0:T(8,128)(2,1)}, bf16[128,1024]{1,0:T(8,128)(2,1)}, bf16[128,1024]{1,0:T(8,128)(2,1)}, bf16[32,2048]{1,0:T(8,128)(2,1)}) custom-call(s32[15]{0:T(128)S(1)} %stack.67.meta_ref, bf16[352,128]{1,0:T(8,128)(2,1)S(1)} %get-tuple-element.53.refs_0_, bf16[2,352,128]{2,1,0:T(8,128)(2,1)S(1)} %collective-permute-done.7.refs_1_, ...), custom_call_target="tpu_custom_call" | custom-call | tf_op jit(solution)/shard_map/unpack/pallas_call | solution.py:27
  (50 shorter events, 4.0 us)
Async XLA Ops:
  0.6 4.9 %collective-permute-start.3 = (bf16[256,2048]{1,0:T(8,128)(2,1)}, bf16[256,2048]{1,0:T(8,128)(2,1)S(1)}, u32[]{:S(2)}, u32[]{:S(2)}) collective-permute-start(bf16[256,2048]{1,0:T(8,128)(2,1)} %bitcast.40), channel_id=1, source_target_pairs={{0,2},{2,0},{4,6},{6,4},{1,3},{3,1},{5,7},{7,5},{8,10},{10,8},{12,... | collective-permute-start | bytes 3145736 | tf_op jit(solution)/shard_map/ppermute | solution.py:260
  1.2 4.4 %collective-permute-start = (bf16[128,3072]{1,0:T(8,128)(2,1)}, bf16[128,3072]{1,0:T(8,128)(2,1)S(1)}, u32[]{:S(2)}, u32[]{:S(2)}) collective-permute-start(bf16[128,3072]{1,0:T(8,128)(2,1)} %bitcast.43), channel_id=1, source_target_pairs={{0,2},{2,0},{4,6},{6,4},{1,3},{3,1},{5,7},{7,5},{8,10},{10,8},{12,... | collective-permute-start | bytes 2359304 | tf_op jit(solution)/shard_map/ppermute | solution.py:260
  1.2 4.2 %collective-permute-start.1 = (bf16[128,1024]{1,0:T(8,128)(2,1)}, bf16[128,1024]{1,0:T(8,128)(2,1)S(1)}, u32[]{:S(2)}, u32[]{:S(2)}) collective-permute-start(bf16[128,1024]{1,0:T(8,128)(2,1)} %bitcast.46), channel_id=1, source_target_pairs={{0,2},{2,0},{4,6},{6,4},{1,3},{3,1},{5,7},{7,5},{8,10},{10,8},{12,... | collective-permute-start | bytes 786440 | tf_op jit(solution)/shard_map/ppermute | solution.py:260
  1.7 3.9 %collective-permute-start.2 = (bf16[128,1024]{1,0:T(8,128)(2,1)}, bf16[128,1024]{1,0:T(8,128)(2,1)S(1)}, u32[]{:S(2)}, u32[]{:S(2)}) collective-permute-start(bf16[128,1024]{1,0:T(8,128)(2,1)} %bitcast.49), channel_id=1, source_target_pairs={{0,2},{2,0},{4,6},{6,4},{1,3},{3,1},{5,7},{7,5},{8,10},{10,8},{12,... | collective-permute-start | bytes 786440 | tf_op jit(solution)/shard_map/ppermute | solution.py:260
  6.7 9.8 %collective-permute-start.4 = (bf16[896,128]{1,0:T(8,128)(2,1)S(1)}, bf16[896,128]{1,0:T(8,128)(2,1)S(1)}, u32[]{:S(2)}, u32[]{:S(2)}) collective-permute-start(bf16[896,128]{1,0:T(8,128)(2,1)S(1)} %get-tuple-element.41), channel_id=1, source_target_pairs={{0,4},{1,5},{2,6},{3,7},{4,0},{5,1},{6,2},{7,3},{8,12},{9,13},{10,... | collective-permute-start | bytes 688136 | tf_op jit(solution)/shard_map/ppermute | solution.py:269
  9.6 12.9 %collective-permute-start.5 = (bf16[896,128]{1,0:T(8,128)(2,1)S(1)}, bf16[896,128]{1,0:T(8,128)(2,1)S(1)}, u32[]{:S(2)}, u32[]{:S(2)}) collective-permute-start(bf16[896,128]{1,0:T(8,128)(2,1)S(1)} %get-tuple-element.42), channel_id=1, source_target_pairs={{0,1},{1,0},{2,3},{3,2},{4,5},{5,4},{6,7},{7,6},{8,9},{9,8},{10,11... | collective-permute-start | bytes 688136 | tf_op jit(solution)/shard_map/ppermute | solution.py:269
  11.2 11.4 %collective-permute-start.6 = (bf16[896,128]{1,0:T(8,128)(2,1)S(1)}, bf16[896,128]{1,0:T(8,128)(2,1)S(1)}, u32[]{:S(2)}, u32[]{:S(2)}) collective-permute-start(bf16[896,128]{1,0:T(8,128)(2,1)S(1)} %get-tuple-element.43), channel_id=1, source_target_pairs={{0,5},{1,4},{2,7},{3,6},{4,1},{5,0},{6,3},{7,2},{8,13},{9,12},{10,... | collective-permute-start | bytes 688136 | tf_op jit(solution)/shard_map/ppermute | solution.py:269
  12.9 21.9 %collective-permute-start.10 = (bf16[896,128]{1,0:T(8,128)(2,1)S(1)}, bf16[896,128]{1,0:T(8,128)(2,1)S(1)}, u32[]{:S(2)}, u32[]{:S(2)}) collective-permute-start(bf16[896,128]{1,0:T(8,128)(2,1)S(1)} %get-tuple-element.47), channel_id=1, source_target_pairs={{0,4},{1,5},{2,6},{3,7},{4,0},{5,1},{6,2},{7,3},{8,12},{9,13},{10,... | collective-permute-start | bytes 688136 | tf_op jit(solution)/shard_map/ppermute | solution.py:269
  14.9 20.6 %collective-permute-start.11 = (bf16[896,128]{1,0:T(8,128)(2,1)S(1)}, bf16[896,128]{1,0:T(8,128)(2,1)S(1)}, u32[]{:S(2)}, u32[]{:S(2)}) collective-permute-start(bf16[896,128]{1,0:T(8,128)(2,1)S(1)} %get-tuple-element.48), channel_id=1, source_target_pairs={{0,1},{1,0},{2,3},{3,2},{4,5},{5,4},{6,7},{7,6},{8,9},{9,8},{10,11... | collective-permute-start | bytes 688136 | tf_op jit(solution)/shard_map/ppermute | solution.py:269
  16.5 20.5 %collective-permute-start.12 = (bf16[896,128]{1,0:T(8,128)(2,1)S(1)}, bf16[896,128]{1,0:T(8,128)(2,1)S(1)}, u32[]{:S(2)}, u32[]{:S(2)}) collective-permute-start(bf16[896,128]{1,0:T(8,128)(2,1)S(1)} %get-tuple-element.49), channel_id=1, source_target_pairs={{0,5},{1,4},{2,7},{3,6},{4,1},{5,0},{6,3},{7,2},{8,13},{9,12},{10,... | collective-permute-start | bytes 688136 | tf_op jit(solution)/shard_map/ppermute | solution.py:269
  33.3 18.2 %collective-permute-start.13 = (bf16[352,128]{1,0:T(8,128)(2,1)S(1)}, bf16[352,128]{1,0:T(8,128)(2,1)S(1)}, u32[]{:S(2)}, u32[]{:S(2)}) collective-permute-start(bf16[352,128]{1,0:T(8,128)(2,1)S(1)} %get-tuple-element.57), channel_id=1, source_target_pairs={{0,2},{2,0},{4,6},{6,4},{1,3},{3,1},{5,7},{7,5},{8,10},{10,8},{12,... | collective-permute-start | bytes 270344 | tf_op jit(solution)/shard_map/ppermute | solution.py:260
  33.4 16.0 %collective-permute-start.7 = (bf16[2,352,128]{2,1,0:T(8,128)(2,1)S(1)}, bf16[2,352,128]{2,1,0:T(8,128)(2,1)S(1)}, u32[]{:S(2)}, u32[]{:S(2)}) collective-permute-start(bf16[2,352,128]{2,1,0:T(8,128)(2,1)S(1)} %get-tuple-element.54), channel_id=1, source_target_pairs={{0,4},{1,5},{2,6},{3,7},{4,0},{5,1},{6,2},{7,3},{8,12},{9,13},{10,... | collective-permute-start | bytes 540680 | tf_op jit(solution)/shard_map/ppermute | solution.py:269
  34.9 15.1 %collective-permute-start.8 = (bf16[2,352,128]{2,1,0:T(8,128)(2,1)S(1)}, bf16[2,352,128]{2,1,0:T(8,128)(2,1)S(1)}, u32[]{:S(2)}, u32[]{:S(2)}) collective-permute-start(bf16[2,352,128]{2,1,0:T(8,128)(2,1)S(1)} %get-tuple-element.55), channel_id=1, source_target_pairs={{0,1},{1,0},{2,3},{3,2},{4,5},{5,4},{6,7},{7,6},{8,9},{9,8},{10,11... | collective-permute-start | bytes 540680 | tf_op jit(solution)/shard_map/ppermute | solution.py:269
  35.5 15.9 %collective-permute-start.9 = (bf16[2,352,128]{2,1,0:T(8,128)(2,1)S(1)}, bf16[2,352,128]{2,1,0:T(8,128)(2,1)S(1)}, u32[]{:S(2)}, u32[]{:S(2)}) collective-permute-start(bf16[2,352,128]{2,1,0:T(8,128)(2,1)S(1)} %get-tuple-element.56), channel_id=1, source_target_pairs={{0,5},{1,4},{2,7},{3,6},{4,1},{5,0},{6,3},{7,2},{8,13},{9,12},{10,... | collective-permute-start | bytes 540680 | tf_op jit(solution)/shard_map/ppermute | solution.py:269
  47.9 7.5 %collective-permute-start.17 = (bf16[2,352,128]{2,1,0:T(8,128)(2,1)S(1)}, bf16[2,352,128]{2,1,0:T(8,128)(2,1)S(1)}, u32[]{:S(2)}, u32[]{:S(2)}) collective-permute-start(bf16[2,352,128]{2,1,0:T(8,128)(2,1)S(1)} %get-tuple-element.65), channel_id=1, source_target_pairs={{0,4},{1,5},{2,6},{3,7},{4,0},{5,1},{6,2},{7,3},{8,12},{9,13},{10,... | collective-permute-start | bytes 540680 | tf_op jit(solution)/shard_map/ppermute | solution.py:269
  49.3 8.1 %collective-permute-start.18 = (bf16[2,352,128]{2,1,0:T(8,128)(2,1)S(1)}, bf16[2,352,128]{2,1,0:T(8,128)(2,1)S(1)}, u32[]{:S(2)}, u32[]{:S(2)}) collective-permute-start(bf16[2,352,128]{2,1,0:T(8,128)(2,1)S(1)} %get-tuple-element.66), channel_id=1, source_target_pairs={{0,1},{1,0},{2,3},{3,2},{4,5},{5,4},{6,7},{7,6},{8,9},{9,8},{10,11... | collective-permute-start | bytes 540680 | tf_op jit(solution)/shard_map/ppermute | solution.py:269
  50.0 9.2 %collective-permute-start.19 = (bf16[2,352,128]{2,1,0:T(8,128)(2,1)S(1)}, bf16[2,352,128]{2,1,0:T(8,128)(2,1)S(1)}, u32[]{:S(2)}, u32[]{:S(2)}) collective-permute-start(bf16[2,352,128]{2,1,0:T(8,128)(2,1)S(1)} %get-tuple-element.67), channel_id=1, source_target_pairs={{0,5},{1,4},{2,7},{3,6},{4,1},{5,0},{6,3},{7,2},{8,13},{9,12},{10,... | collective-permute-start | bytes 540680 | tf_op jit(solution)/shard_map/ppermute | solution.py:269
  51.5 7.8 %collective-permute-start.16 = (bf16[352,128]{1,0:T(8,128)(2,1)S(1)}, bf16[352,128]{1,0:T(8,128)(2,1)S(1)}, u32[]{:S(2)}, u32[]{:S(2)}) collective-permute-start(bf16[352,128]{1,0:T(8,128)(2,1)S(1)} %slice_bitcast_fusion.3), channel_id=1, source_target_pairs={{0,2},{2,0},{4,6},{6,4},{1,3},{3,1},{5,7},{7,5},{8,10},{10,8},{12,... | collective-permute-start | bytes 270344 | tf_op jit(solution)/shard_map/ppermute | solution.py:260
  51.6 7.7 %collective-permute-start.15 = (bf16[352,128]{1,0:T(8,128)(2,1)S(1)}, bf16[352,128]{1,0:T(8,128)(2,1)S(1)}, u32[]{:S(2)}, u32[]{:S(2)}) collective-permute-start(bf16[352,128]{1,0:T(8,128)(2,1)S(1)} %slice_bitcast_fusion.4), channel_id=1, source_target_pairs={{0,2},{2,0},{4,6},{6,4},{1,3},{3,1},{5,7},{7,5},{8,10},{10,8},{12,... | collective-permute-start | bytes 270344 | tf_op jit(solution)/shard_map/ppermute | solution.py:260
  55.4 3.9 %collective-permute-start.14 = (bf16[352,128]{1,0:T(8,128)(2,1)S(1)}, bf16[352,128]{1,0:T(8,128)(2,1)S(1)}, u32[]{:S(2)}, u32[]{:S(2)}) collective-permute-start(bf16[352,128]{1,0:T(8,128)(2,1)S(1)} %slice_bitcast_fusion.5), channel_id=1, source_target_pairs={{0,2},{2,0},{4,6},{6,4},{1,3},{3,1},{5,7},{7,5},{8,10},{10,8},{12,... | collective-permute-start | bytes 270344 | tf_op jit(solution)/shard_map/ppermute | solution.py:260
  57.5 2.5 %collective-permute-start.20 = (bf16[352,128]{1,0:T(8,128)(2,1)S(1)}, bf16[352,128]{1,0:T(8,128)(2,1)S(1)}, u32[]{:S(2)}, u32[]{:S(2)}) collective-permute-start(bf16[352,128]{1,0:T(8,128)(2,1)S(1)} %get-tuple-element.71), channel_id=1, source_target_pairs={{0,2},{2,0},{4,6},{6,4},{1,3},{3,1},{5,7},{7,5},{8,10},{10,8},{12,... | collective-permute-start | bytes 270344 | tf_op jit(solution)/shard_map/ppermute | solution.py:260
  59.3 1.4 %collective-permute-start.23 = (bf16[352,128]{1,0:T(8,128)(2,1)S(1)}, bf16[352,128]{1,0:T(8,128)(2,1)S(1)}, u32[]{:S(2)}, u32[]{:S(2)}) collective-permute-start(bf16[352,128]{1,0:T(8,128)(2,1)S(1)} %slice_bitcast_fusion), channel_id=1, source_target_pairs={{0,2},{2,0},{4,6},{6,4},{1,3},{3,1},{5,7},{7,5},{8,10},{10,8},{12,... | collective-permute-start | bytes 270344 | tf_op jit(solution)/shard_map/ppermute | solution.py:260
  59.4 1.4 %collective-permute-start.22 = (bf16[352,128]{1,0:T(8,128)(2,1)S(1)}, bf16[352,128]{1,0:T(8,128)(2,1)S(1)}, u32[]{:S(2)}, u32[]{:S(2)}) collective-permute-start(bf16[352,128]{1,0:T(8,128)(2,1)S(1)} %slice_bitcast_fusion.1), channel_id=1, source_target_pairs={{0,2},{2,0},{4,6},{6,4},{1,3},{3,1},{5,7},{7,5},{8,10},{10,8},{12,... | collective-permute-start | bytes 270344 | tf_op jit(solution)/shard_map/ppermute | solution.py:260
  59.9 1.3 %collective-permute-start.21 = (bf16[352,128]{1,0:T(8,128)(2,1)S(1)}, bf16[352,128]{1,0:T(8,128)(2,1)S(1)}, u32[]{:S(2)}, u32[]{:S(2)}) collective-permute-start(bf16[352,128]{1,0:T(8,128)(2,1)S(1)} %slice_bitcast_fusion.2), channel_id=1, source_target_pairs={{0,2},{2,0},{4,6},{6,4},{1,3},{3,1},{5,7},{7,5},{8,10},{10,8},{12,... | collective-permute-start | bytes 270344 | tf_op jit(solution)/shard_map/ppermute | solution.py:260
  (6 other events, 19.6 us)

commit v5 on v4

--- a/solution.py
+++ b/solution.py
@@ -16,6 +16,7 @@
 SM = pl.BlockSpec(memory_space=pltpu.SMEM)
 SCALE = 1.0 / math.sqrt(HD)
 MIB = 1 << 20
+LIMIT = 36
 
 
 def sds(shape, dtype=BF):
@@ -52,7 +53,7 @@
 
 def softmax_t(scores):
     top = jnp.max(scores, axis=0, keepdims=True)
-    e = jnp.exp((scores - top) * SCALE)
+    e = jnp.exp2((scores - top) * (SCALE * math.log2(math.e)))
     return (e * (1.0 / jnp.sum(e, axis=0, keepdims=True))).astype(BF)
 
 
@@ -122,17 +123,29 @@
     return (sds((rows, 128)),) * 2 + (sds((2, rows, 128)),) * (C - 1)
 
 
+def ahead(count, first, rest):
+    value = first(0)
+    for i in range(count):
+        following = first(i + 1) if i + 1 < count else None
+        rest(i, value)
+        value = following
+
+
 def layer_kernel(meta_ref, *refs, C, R, M):
     ins, outs = refs[:C], refs[C : 2 * C + 1]
-    k_ref, v_ref, kT_ref, vT_ref, t_ref, dt_ref, dk_ref, dv_ref = refs[2 * C + 1 :]
+    q_ref, k_ref, v_ref, cq_ref, go_ref, vT_ref, kT_ref, t_ref, dt_ref = refs[2 * C + 1 : 2 * C + 10]
+    oT_ref, ag_ref, pT_ref, ds_ref = refs[2 * C + 10 :]
+    L = 2 * C * R
     QB = 2 * R
     MR = M // (2 * C)
     left, right = slice(0, HD), slice(HD, 2 * HD)
     for b in range(C):
         rows = slice(b * QB, (b + 1) * QB)
-        k, v = ins[b][:QB, right], ins[b][QB : 2 * QB, left]
-        k_ref[rows], v_ref[rows] = k, v
-        kT_ref[:, rows], vT_ref[:, rows] = k.T, v.T
+        q_ref[rows], k_ref[rows] = ins[b][:QB, left], ins[b][:QB, right]
+        v_ref[rows], cq_ref[rows] = ins[b][QB : 2 * QB, left], ins[b][QB : 2 * QB, right]
+        go_ref[b * QB : b * QB + R] = ins[b][4 * R : 5 * R, left]
+        go_ref[b * QB + R : (b + 1) * QB] = ins[b][4 * R : 5 * R, right]
+        kT_ref[:, rows], vT_ref[:, rows] = k_ref[rows].T, v_ref[rows].T
     for d in range(C):
 
         @pl.when(meta_ref[1 + C] == d)
@@ -142,54 +155,73 @@
     tk, tv = t_ref[:, left], t_ref[:, right]
     tkT, tvT = tk.T, tv.T
     k, v, kT, vT = k_ref[...], v_ref[...], kT_ref[...], vT_ref[...]
-    dtk = dtv = None
-    for b in range(C):
-        q, cq = ins[b][:QB, left], ins[b][QB : 2 * QB, right]
-        go = ins[b][4 * R : 5 * R, :]
-        go = jnp.concatenate([go[:, left], go[:, right]], axis=0)
-        p = softmax_t(dot_nt(k, q))
-        oT = dot(vT, p)
-        att = oT.T.astype(BF).astype(F32)
-        x = (att + cq.astype(F32)).astype(BF)
-        cp = softmax_t(dot_nt(tk, x))
-        mix = dot(tvT, cp)
-        delta = jnp.sum(go.T.astype(F32) * mix, axis=0, keepdims=True)
-        ds = (cp.astype(F32) * (dot_nt(tv, go) - delta)).astype(BF)
-        dq = dot(tkT, ds).T * SCALE
-        a, c = dot(ds, x), dot(cp, go)
-        dtk = a if dtk is None else dtk + a
-        dtv = c if dtv is None else dtv + c
-        combined, dcq = (att + mix.T).astype(BF), dq.astype(BF)
-        ag = (go.astype(F32) + dq).astype(BF)
-        delta = jnp.sum(ag.T.astype(F32) * oT, axis=0, keepdims=True)
-        ds = (p.astype(F32) * (dot_nt(v, ag) - delta)).astype(BF)
-        dk, dv = dot(ds, q), dot(p, ag)
-        if b == 0:
-            dk_ref[...] = dk
-            dv_ref[...] = dv
-        else:
-            dk_ref[...] += dk
-            dv_ref[...] += dv
+
+    WB = 512
+
+    def block(b):
+        return slice(b * WB, (b + 1) * WB)
+
+    def attend(b, scores):
+        p = softmax_t(scores)
+        pT_ref[:, block(b)] = p
+        oT_ref[:, block(b)] = dot(vT, p)
+
+    ahead(L // WB, lambda b: dot_nt(k, q_ref[block(b)]), attend)
+    go = go_ref[...]
+    att = oT_ref[...].T.astype(BF).astype(F32)
+    x = (att + cq_ref[...].astype(F32)).astype(BF)
+    cp = softmax_t(dot_nt(tk, x))
+    dp = dot_nt(tv, go)
+    mix = dot(tvT, cp)
+    delta = jnp.sum(go.T.astype(F32) * mix, axis=0, keepdims=True)
+    ds = (cp.astype(F32) * (dp - delta)).astype(BF)
+    dq = dot(tkT, ds).T * SCALE
+    ag = (go.astype(F32) + dq).astype(BF)
+    ag_ref[...] = ag
+    dt_ref[...] = beside(dot(ds, x) * SCALE, dot(cp, go)).astype(BF)
+    combined, dcq = (att + mix.T).astype(BF), dq.astype(BF)
+    h = R // 2
+    for i in range(2 * C):
+        at = i * R
+        put(outs, i, slice(R, 2 * R), right, combined[at : at + R])
+        halves = beside(dcq[at : at + h], dcq[at + h : at + R])
+        put(outs, i, slice(2 * R, 2 * R + h), slice(None), halves)
+        start = pl.multiple_of(meta_ref[3 + C + i] * MR, MR)
+        put(outs, i, slice(2 * R + h, None), slice(None), dt_ref[pl.ds(start, MR), :])
+    delta = jnp.sum(ag.T.astype(F32) * oT_ref[...], axis=0, keepdims=True)
+
+    def back(b, dp):
+        ds = (pT_ref[:, block(b)].astype(F32) * (dp - delta[:, block(b)])).astype(BF)
+        ds_ref[:, block(b)] = ds
         dq = (dot(kT, ds).T * SCALE).astype(BF)
-        for e in range(2):
-            part = slice(e * R, (e + 1) * R)
-            put(outs, 2 * b + e, slice(0, R), left, dq[part])
-            put(outs, 2 * b + e, slice(R, 2 * R), right, combined[part])
-            h = R // 2
-            put(
-                outs,
-                2 * b + e,
-                slice(2 * R, 2 * R + h),
-                slice(None),
-                beside(dcq[e * R : e * R + h], dcq[e * R + h : (e + 1) * R]),
-            )
-    dt_ref[...] = beside(dtk * SCALE, dtv).astype(BF)
+        n = WB // R
+        for e in range(n):
+            put(outs, n * b + e, slice(0, R), left, dq[e * R : (e + 1) * R])
+
+    ahead(L // WB, lambda b: dot_nt(v, ag_ref[block(b)]), back)
+    dk = (dot(ds_ref[...], q_ref[...]) * SCALE).astype(BF)
+    dv = dot(pT_ref[...], ag).astype(BF)
     for i in range(2 * C):
         part = slice(i * R, (i + 1) * R)
-        put(outs, i, slice(0, R), right, (dk_ref[part] * SCALE).astype(BF))
-        put(outs, i, slice(R, 2 * R), left, dv_ref[part].astype(BF))
-        start = pl.multiple_of(meta_ref[3 + C + i] * MR, MR)
-        put(outs, i, slice(2 * R + R // 2, None), slice(None), dt_ref[pl.ds(start, MR), :])
+        put(outs, i, slice(0, R), right, dk[part])
+        put(outs, i, slice(R, 2 * R), left, dv[part])
+
+
+def layer(meta, msgs, C, R, M):
+    L, H = 2 * C * R, HD
+    return call(
+        functools.partial(layer_kernel, C=C, R=R, M=M),
+        "layer",
+        [meta, *msgs],
+        message_shapes(C, 2 * R + R // 2 + M // (2 * C)),
+        LIMIT,
+        [pltpu.VMEM((L, H), BF)] * 5
+        + [pltpu.VMEM((H, L), BF)] * 2
+        + [pltpu.VMEM((M, 128), BF)] * 2
+        + [pltpu.VMEM((H, L), F32), pltpu.VMEM((L, H), BF)]
+        + [pltpu.VMEM((L, L), BF)] * 2,
+        cost(L * L + L * M, 6),
+    )
 
 
 def unpack_kernel(meta_ref, *refs, C, H):
@@ -240,7 +272,6 @@
     C = X * Hd
     R, D = cross_query.shape[1:]
     W = D // (2 * C)
-    L = 2 * C * R
     M = thermal_kv.shape[2]
     MR = M // (2 * C)
     offsets = [(i, j) for j in range(Hd) for i in range(X)]
@@ -273,7 +304,6 @@
 
     bind = functools.partial
     H = W // HD
-    RO = 2 * R + R // 2 + MR
     own = (self_qkv[0], cross_query[0], grad_out[0], thermal_kv[0, 0])
     xs, cqs, gos, ts = [to_sibling(a) for a in own]
     x, cq, go, t = own
@@ -298,18 +328,7 @@
             got[p - 1] = after(got[p - 1], *msgs[p])
     backs, outs = [], []
     for p in range(H):
-        out = call(
-            bind(layer_kernel, C=C, R=R, M=M),
-            f"layer_{p}",
-            [meta, msgs[p][0], *got[p]],
-            message_shapes(C, RO),
-            32,
-            [pltpu.VMEM((L, HD), BF)] * 2
-            + [pltpu.VMEM((HD, L), BF)] * 2
-            + [pltpu.VMEM((M, 128), BF)] * 2
-            + [pltpu.VMEM((L, HD), F32)] * 2,
-            cost(L * L + L * M, 6),
-        )
+        out = layer(meta, [msgs[p][0], *got[p]], C, R, M)
         outs.append(out)
         if p + 1 < H:
             got[p + 1] = after(got[p + 1], *out)

time: 63.9 us -> 55.4 us (0.87)
  Pallas kernels: 27.5 us -> 19.1 us
    pallas_call x7, Pallas kernels: 27.5 us -> 19.1 us  [call(): pl.pallas_call(kernel, out_shape=outs, in_specs=[SM if s else VM for s in...]
  transfers between devices with their start and end apart: 24 -> 24, of which waited for: 8 -> 9; matrix products, arithmetic and copies ran while one was open for 0% -> 0% of each run, Pallas kernels for 38% -> 28%
where the time goes in v5:
time: 55.4 us; the launch traced here: 55.2 us
  starting transfers between devices  20.2 us (36%)
  Pallas kernels  19.1 us (34%)
  waiting for transfers between devices  12 us (22%)
  local copies, waits for them, and re-layouts  2.32 us (4%)
  between operations  1.55 us (3%)
    pallas_call x7, Pallas kernels, call(): pl.pallas_call(kernel, out_shape=outs, in_specs=[SM if s else VM for s in...  19.1 us
    ppermute x12, starting transfers between devices, to_chip(): return lax.ppermute(a, GROUP, pairs)  17.9 us
    ppermute x12, waiting for transfers between devices, to_chip(): return lax.ppermute(a, GROUP, pairs)  10.7 us
    ppermute x12, starting transfers between devices, to_sibling(): return lax.ppermute(a, 'seq', [(i, i ^ 1) for i in range(S)])  2.39 us
    unnamed x12, local copies, waits for them, and re-layouts  2.18 us
    ppermute x12, waiting for transfers between devices, to_sibling(): return lax.ppermute(a, 'seq', [(i, i ^ 1) for i in range(S)])  1.36 us
  transfers between devices with their start and end apart: 24, of which 9 were waited for; matrix products, arithmetic and copies ran while one was open for 0% of the time, Pallas kernels for 28%

profile of v5, /device:TPU:0, one launch (start us, length us, event | category | flops | bytes accessed | tf_op | source)
XLA Modules:
  0.0 55.2 jit_solution(17451807912513066808)
XLA Ops:
  2.6 1.1 %copy-done.1 = bf16[1,128,3072]{2,1,0:T(8,128)(2,1)S(1)} copy-done((bf16[1,128,3072]{2,1,0:T(8,128)(2,1)S(1)}, bf16[1,128,3072]{2,1,0:T(8,128)(2,1)}, u32[]{:S(2)}) %copy-start.1) | copy-done | bytes 786456
  3.7 0.9 %copy-done.3 = bf16[1,128,1024]{2,1,0:T(8,128)(2,1)S(1)} copy-done((bf16[1,128,1024]{2,1,0:T(8,128)(2,1)S(1)}, bf16[1,128,1024]{2,1,0:T(8,128)(2,1)}, u32[]{:S(2)}) %copy-start.3) | copy-done | bytes 262168
  4.7 0.7 %pack_own_0.1.own_ref = bf16[4,256,128]{2,1,0:T(8,128)(2,1)S(1)} custom-call(s32[15]{0:T(128)S(1)} %stack.67.meta_ref, bf16[128,3072]{1,0:T(8,128)(2,1)S(1)} %bitcast.44, bf16[128,1024]{1,0:T(8,128)(2,1)S(1)} %bitcast.47), custom_call_target="tpu_custom_call" | custom-call | tf_op jit(solution)/shard_map/pack_own_0/pallas_call | solution.py:28
  5.6 1.0 %pack_sib_0.1 = (bf16[896,128]{1,0:T(8,128)(2,1)S(1)}, bf16[896,128]{1,0:T(8,128)(2,1)S(1)}, bf16[896,128]{1,0:T(8,128)(2,1)S(1)}, bf16[896,128]{1,0:T(8,128)(2,1)S(1)}) custom-call(s32[15]{0:T(128)S(1)} %stack.67.meta_ref, bf16[4,256,128]{2,1,0:T(8,128)(2,1)S(1)} %pack_own_0.1.own_ref, bf16[128,1024]{1,0:T(8,128)(2,1)S(1)} %bitcast.50, ...), custom_call_target="tpu_custom_call" | custom-call | tf_op jit(solution)/shard_map/pack_sib_0/pallas_call | solution.py:28
  6.7 3.0 %collective-permute-start.4 = (bf16[896,128]{1,0:T(8,128)(2,1)S(1)}, bf16[896,128]{1,0:T(8,128)(2,1)S(1)}, u32[]{:S(2)}, u32[]{:S(2)}) collective-permute-start(bf16[896,128]{1,0:T(8,128)(2,1)S(1)} %get-tuple-element.41), channel_id=1, source_target_pairs={{0,4},{1,5},{2,6},{3,7},{4,0},{5,1},{6,2},{7,3},{8,12},{9,13},{10,... | collective-permute-start | bytes 688136 | tf_op jit(solution)/shard_map/ppermute | solution.py:300
  9.6 1.5 %collective-permute-start.5 = (bf16[896,128]{1,0:T(8,128)(2,1)S(1)}, bf16[896,128]{1,0:T(8,128)(2,1)S(1)}, u32[]{:S(2)}, u32[]{:S(2)}) collective-permute-start(bf16[896,128]{1,0:T(8,128)(2,1)S(1)} %get-tuple-element.42), channel_id=1, source_target_pairs={{0,1},{1,0},{2,3},{3,2},{4,5},{5,4},{6,7},{7,6},{8,9},{9,8},{10,11... | collective-permute-start | bytes 688136 | tf_op jit(solution)/shard_map/ppermute | solution.py:300
  11.2 0.7 %pack_own_1.1.own_ref = bf16[4,256,128]{2,1,0:T(8,128)(2,1)S(1)} custom-call(s32[15]{0:T(128)S(1)} %stack.67.meta_ref, bf16[128,3072]{1,0:T(8,128)(2,1)S(1)} %bitcast.45, bf16[128,1024]{1,0:T(8,128)(2,1)S(1)} %bitcast.48), custom_call_target="tpu_custom_call" | custom-call | tf_op jit(solution)/shard_map/pack_own_1/pallas_call | solution.py:28
  11.9 1.0 %pack_sib_1.1 = (bf16[896,128]{1,0:T(8,128)(2,1)S(1)}, bf16[896,128]{1,0:T(8,128)(2,1)S(1)}, bf16[896,128]{1,0:T(8,128)(2,1)S(1)}, bf16[896,128]{1,0:T(8,128)(2,1)S(1)}) custom-call(s32[15]{0:T(128)S(1)} %stack.67.meta_ref, bf16[4,256,128]{2,1,0:T(8,128)(2,1)S(1)} %pack_own_1.1.own_ref, bf16[128,1024]{1,0:T(8,128)(2,1)S(1)} %bitcast.51, ...), custom_call_target="tpu_custom_call" | custom-call | tf_op jit(solution)/shard_map/pack_sib_1/pallas_call | solution.py:28
  12.9 2.0 %collective-permute-start.10 = (bf16[896,128]{1,0:T(8,128)(2,1)S(1)}, bf16[896,128]{1,0:T(8,128)(2,1)S(1)}, u32[]{:S(2)}, u32[]{:S(2)}) collective-permute-start(bf16[896,128]{1,0:T(8,128)(2,1)S(1)} %get-tuple-element.47), channel_id=1, source_target_pairs={{0,4},{1,5},{2,6},{3,7},{4,0},{5,1},{6,2},{7,3},{8,12},{9,13},{10,... | collective-permute-start | bytes 688136 | tf_op jit(solution)/shard_map/ppermute | solution.py:300
  14.9 1.5 %collective-permute-start.11 = (bf16[896,128]{1,0:T(8,128)(2,1)S(1)}, bf16[896,128]{1,0:T(8,128)(2,1)S(1)}, u32[]{:S(2)}, u32[]{:S(2)}) collective-permute-start(bf16[896,128]{1,0:T(8,128)(2,1)S(1)} %get-tuple-element.48), channel_id=1, source_target_pairs={{0,1},{1,0},{2,3},{3,2},{4,5},{5,4},{6,7},{7,6},{8,9},{9,8},{10,11... | collective-permute-start | bytes 688136 | tf_op jit(solution)/shard_map/ppermute | solution.py:300
  16.5 2.6 %collective-permute-start.12 = (bf16[896,128]{1,0:T(8,128)(2,1)S(1)}, bf16[896,128]{1,0:T(8,128)(2,1)S(1)}, u32[]{:S(2)}, u32[]{:S(2)}) collective-permute-start(bf16[896,128]{1,0:T(8,128)(2,1)S(1)} %get-tuple-element.49), channel_id=1, source_target_pairs={{0,5},{1,4},{2,7},{3,6},{4,1},{5,0},{6,3},{7,2},{8,13},{9,12},{10,... | collective-permute-start | bytes 688136 | tf_op jit(solution)/shard_map/ppermute | solution.py:300
  19.1 3.5 %collective-permute-done.5.refs_2_ = bf16[896,128]{1,0:T(8,128)(2,1)S(1)} collective-permute-done((bf16[896,128]{1,0:T(8,128)(2,1)S(1)}, bf16[896,128]{1,0:T(8,128)(2,1)S(1)}, u32[]{:S(2)}, u32[]{:S(2)}) %collective-permute-start.5) | collective-permute-done | bytes 229408 | tf_op jit(solution)/shard_map/ppermute | solution.py:300
  22.6 6.5 %layer.2 = (bf16[352,128]{1,0:T(8,128)(2,1)S(1)}, bf16[352,128]{1,0:T(8,128)(2,1)S(1)}, bf16[2,352,128]{2,1,0:T(8,128)(2,1)S(1)}, bf16[2,352,128]{2,1,0:T(8,128)(2,1)S(1)}, bf16[2,352,128]{2,1,0:T(8,128)(2,1)S(1)}) custom-call(s32[15]{0:T(128)S(1)} %stack.67.meta_ref, bf16[896,128]{1,0:T(8,128)(2,1)S(1)} %get-tuple-element.40.refs_0_, ...), custom_call_target="tpu_custom_call" | custom-call | flops 4026531840 | bytes 5242880 | tf_op jit(solution)/shard_map/layer/pallas_call | solution.py:28
  29.2 1.5 %collective-permute-start.7 = (bf16[2,352,128]{2,1,0:T(8,128)(2,1)S(1)}, bf16[2,352,128]{2,1,0:T(8,128)(2,1)S(1)}, u32[]{:S(2)}, u32[]{:S(2)}) collective-permute-start(bf16[2,352,128]{2,1,0:T(8,128)(2,1)S(1)} %get-tuple-element.54), channel_id=1, source_target_pairs={{0,4},{1,5},{2,6},{3,7},{4,0},{5,1},{6,2},{7,3},{8,12},{9,13},{10,... | collective-permute-start | bytes 540680 | tf_op jit(solution)/shard_map/ppermute | solution.py:300
  30.7 0.7 %collective-permute-start.8 = (bf16[2,352,128]{2,1,0:T(8,128)(2,1)S(1)}, bf16[2,352,128]{2,1,0:T(8,128)(2,1)S(1)}, u32[]{:S(2)}, u32[]{:S(2)}) collective-permute-start(bf16[2,352,128]{2,1,0:T(8,128)(2,1)S(1)} %get-tuple-element.55), channel_id=1, source_target_pairs={{0,1},{1,0},{2,3},{3,2},{4,5},{5,4},{6,7},{7,6},{8,9},{9,8},{10,11... | collective-permute-start | bytes 540680 | tf_op jit(solution)/shard_map/ppermute | solution.py:300
  31.7 1.5 %collective-permute-start.9 = (bf16[2,352,128]{2,1,0:T(8,128)(2,1)S(1)}, bf16[2,352,128]{2,1,0:T(8,128)(2,1)S(1)}, u32[]{:S(2)}, u32[]{:S(2)}) collective-permute-start(bf16[2,352,128]{2,1,0:T(8,128)(2,1)S(1)} %get-tuple-element.56), channel_id=1, source_target_pairs={{0,5},{1,4},{2,7},{3,6},{4,1},{5,0},{6,3},{7,2},{8,13},{9,12},{10,... | collective-permute-start | bytes 540680 | tf_op jit(solution)/shard_map/ppermute | solution.py:300
  33.2 6.7 %layer.3 = (bf16[352,128]{1,0:T(8,128)(2,1)S(1)}, bf16[352,128]{1,0:T(8,128)(2,1)S(1)}, bf16[2,352,128]{2,1,0:T(8,128)(2,1)S(1)}, bf16[2,352,128]{2,1,0:T(8,128)(2,1)S(1)}, bf16[2,352,128]{2,1,0:T(8,128)(2,1)S(1)}) custom-call(s32[15]{0:T(128)S(1)} %stack.67.meta_ref, bf16[896,128]{1,0:T(8,128)(2,1)S(1)} %get-tuple-element.46.refs_0_, ...), custom_call_target="tpu_custom_call" | custom-call | flops 4026531840 | bytes 5242880 | tf_op jit(solution)/shard_map/layer/pallas_call | solution.py:28
  39.9 1.6 %collective-permute-start.17 = (bf16[2,352,128]{2,1,0:T(8,128)(2,1)S(1)}, bf16[2,352,128]{2,1,0:T(8,128)(2,1)S(1)}, u32[]{:S(2)}, u32[]{:S(2)}) collective-permute-start(bf16[2,352,128]{2,1,0:T(8,128)(2,1)S(1)} %get-tuple-element.65), channel_id=1, source_target_pairs={{0,4},{1,5},{2,6},{3,7},{4,0},{5,1},{6,2},{7,3},{8,12},{9,13},{10,... | collective-permute-start | bytes 540680 | tf_op jit(solution)/shard_map/ppermute | solution.py:300
  41.9 1.5 %collective-permute-start.19 = (bf16[2,352,128]{2,1,0:T(8,128)(2,1)S(1)}, bf16[2,352,128]{2,1,0:T(8,128)(2,1)S(1)}, u32[]{:S(2)}, u32[]{:S(2)}) collective-permute-start(bf16[2,352,128]{2,1,0:T(8,128)(2,1)S(1)} %get-tuple-element.67), channel_id=1, source_target_pairs={{0,5},{1,4},{2,7},{3,6},{4,1},{5,0},{6,3},{7,2},{8,13},{9,12},{10,... | collective-permute-start | bytes 540680 | tf_op jit(solution)/shard_map/ppermute | solution.py:300
  44.1 3.4 %collective-permute-done.17.refs_9_ = bf16[2,352,128]{2,1,0:T(8,128)(2,1)S(1)} collective-permute-done((bf16[2,352,128]{2,1,0:T(8,128)(2,1)S(1)}, bf16[2,352,128]{2,1,0:T(8,128)(2,1)S(1)}, u32[]{:S(2)}, u32[]{:S(2)}) %collective-permute-start.17) | collective-permute-done | bytes 180256 | tf_op jit(solution)/shard_map/ppermute | solution.py:300
  47.4 1.6 %collective-permute-done.18.refs_10_ = bf16[2,352,128]{2,1,0:T(8,128)(2,1)S(1)} collective-permute-done((bf16[2,352,128]{2,1,0:T(8,128)(2,1)S(1)}, bf16[2,352,128]{2,1,0:T(8,128)(2,1)S(1)}, u32[]{:S(2)}, u32[]{:S(2)}) %collective-permute-start.18) | collective-permute-done | bytes 180256 | tf_op jit(solution)/shard_map/ppermute | solution.py:300
  49.0 1.8 %collective-permute-done.19.refs_11_ = bf16[2,352,128]{2,1,0:T(8,128)(2,1)S(1)} collective-permute-done((bf16[2,352,128]{2,1,0:T(8,128)(2,1)S(1)}, bf16[2,352,128]{2,1,0:T(8,128)(2,1)S(1)}, u32[]{:S(2)}, u32[]{:S(2)}) %collective-permute-start.19) | collective-permute-done | bytes 180256 | tf_op jit(solution)/shard_map/ppermute | solution.py:300
  51.5 0.7 %collective-permute-done.23.refs_15_ = bf16[352,128]{1,0:T(8,128)(2,1)S(1)} collective-permute-done((bf16[352,128]{1,0:T(8,128)(2,1)S(1)}, bf16[352,128]{1,0:T(8,128)(2,1)S(1)}, u32[]{:S(2)}, u32[]{:S(2)}) %collective-permute-start.23) | collective-permute-done | bytes 90144 | tf_op jit(solution)/shard_map/ppermute | solution.py:291
  52.7 2.5 %unpack.1 = (bf16[128,3072]{1,0:T(8,128)(2,1)}, bf16[128,1024]{1,0:T(8,128)(2,1)}, bf16[128,1024]{1,0:T(8,128)(2,1)}, bf16[32,2048]{1,0:T(8,128)(2,1)}) custom-call(s32[15]{0:T(128)S(1)} %stack.67.meta_ref, bf16[352,128]{1,0:T(8,128)(2,1)S(1)} %get-tuple-element.53.refs_0_, bf16[2,352,128]{2,1,0:T(8,128)(2,1)S(1)} %collective-permute-done.7.refs_1_, ...), custom_call_target="tpu_custom_call" | custom-call | tf_op jit(solution)/shard_map/unpack/pallas_call | solution.py:28
  (50 shorter events, 4.2 us)
Async XLA Ops:
  0.6 4.9 %collective-permute-start.3 = (bf16[256,2048]{1,0:T(8,128)(2,1)}, bf16[256,2048]{1,0:T(8,128)(2,1)S(1)}, u32[]{:S(2)}, u32[]{:S(2)}) collective-permute-start(bf16[256,2048]{1,0:T(8,128)(2,1)} %bitcast.40), channel_id=1, source_target_pairs={{0,2},{2,0},{4,6},{6,4},{1,3},{3,1},{5,7},{7,5},{8,10},{10,8},{12,... | collective-permute-start | bytes 3145736 | tf_op jit(solution)/shard_map/ppermute | solution.py:291
  1.2 4.4 %collective-permute-start = (bf16[128,3072]{1,0:T(8,128)(2,1)}, bf16[128,3072]{1,0:T(8,128)(2,1)S(1)}, u32[]{:S(2)}, u32[]{:S(2)}) collective-permute-start(bf16[128,3072]{1,0:T(8,128)(2,1)} %bitcast.43), channel_id=1, source_target_pairs={{0,2},{2,0},{4,6},{6,4},{1,3},{3,1},{5,7},{7,5},{8,10},{10,8},{12,... | collective-permute-start | bytes 2359304 | tf_op jit(solution)/shard_map/ppermute | solution.py:291
  1.2 4.2 %collective-permute-start.1 = (bf16[128,1024]{1,0:T(8,128)(2,1)}, bf16[128,1024]{1,0:T(8,128)(2,1)S(1)}, u32[]{:S(2)}, u32[]{:S(2)}) collective-permute-start(bf16[128,1024]{1,0:T(8,128)(2,1)} %bitcast.46), channel_id=1, source_target_pairs={{0,2},{2,0},{4,6},{6,4},{1,3},{3,1},{5,7},{7,5},{8,10},{10,8},{12,... | collective-permute-start | bytes 786440 | tf_op jit(solution)/shard_map/ppermute | solution.py:291
  1.7 3.9 %collective-permute-start.2 = (bf16[128,1024]{1,0:T(8,128)(2,1)}, bf16[128,1024]{1,0:T(8,128)(2,1)S(1)}, u32[]{:S(2)}, u32[]{:S(2)}) collective-permute-start(bf16[128,1024]{1,0:T(8,128)(2,1)} %bitcast.49), channel_id=1, source_target_pairs={{0,2},{2,0},{4,6},{6,4},{1,3},{3,1},{5,7},{7,5},{8,10},{10,8},{12,... | collective-permute-start | bytes 786440 | tf_op jit(solution)/shard_map/ppermute | solution.py:291
  6.7 9.8 %collective-permute-start.4 = (bf16[896,128]{1,0:T(8,128)(2,1)S(1)}, bf16[896,128]{1,0:T(8,128)(2,1)S(1)}, u32[]{:S(2)}, u32[]{:S(2)}) collective-permute-start(bf16[896,128]{1,0:T(8,128)(2,1)S(1)} %get-tuple-element.41), channel_id=1, source_target_pairs={{0,4},{1,5},{2,6},{3,7},{4,0},{5,1},{6,2},{7,3},{8,12},{9,13},{10,... | collective-permute-start | bytes 688136 | tf_op jit(solution)/shard_map/ppermute | solution.py:300
  9.6 12.9 %collective-permute-start.5 = (bf16[896,128]{1,0:T(8,128)(2,1)S(1)}, bf16[896,128]{1,0:T(8,128)(2,1)S(1)}, u32[]{:S(2)}, u32[]{:S(2)}) collective-permute-start(bf16[896,128]{1,0:T(8,128)(2,1)S(1)} %get-tuple-element.42), channel_id=1, source_target_pairs={{0,1},{1,0},{2,3},{3,2},{4,5},{5,4},{6,7},{7,6},{8,9},{9,8},{10,11... | collective-permute-start | bytes 688136 | tf_op jit(solution)/shard_map/ppermute | solution.py:300
  11.2 11.4 %collective-permute-start.6 = (bf16[896,128]{1,0:T(8,128)(2,1)S(1)}, bf16[896,128]{1,0:T(8,128)(2,1)S(1)}, u32[]{:S(2)}, u32[]{:S(2)}) collective-permute-start(bf16[896,128]{1,0:T(8,128)(2,1)S(1)} %get-tuple-element.43), channel_id=1, source_target_pairs={{0,5},{1,4},{2,7},{3,6},{4,1},{5,0},{6,3},{7,2},{8,13},{9,12},{10,... | collective-permute-start | bytes 688136 | tf_op jit(solution)/shard_map/ppermute | solution.py:300
  12.9 17.7 %collective-permute-start.10 = (bf16[896,128]{1,0:T(8,128)(2,1)S(1)}, bf16[896,128]{1,0:T(8,128)(2,1)S(1)}, u32[]{:S(2)}, u32[]{:S(2)}) collective-permute-start(bf16[896,128]{1,0:T(8,128)(2,1)S(1)} %get-tuple-element.47), channel_id=1, source_target_pairs={{0,4},{1,5},{2,6},{3,7},{4,0},{5,1},{6,2},{7,3},{8,12},{9,13},{10,... | collective-permute-start | bytes 688136 | tf_op jit(solution)/shard_map/ppermute | solution.py:300
  14.9 16.8 %collective-permute-start.11 = (bf16[896,128]{1,0:T(8,128)(2,1)S(1)}, bf16[896,128]{1,0:T(8,128)(2,1)S(1)}, u32[]{:S(2)}, u32[]{:S(2)}) collective-permute-start(bf16[896,128]{1,0:T(8,128)(2,1)S(1)} %get-tuple-element.48), channel_id=1, source_target_pairs={{0,1},{1,0},{2,3},{3,2},{4,5},{5,4},{6,7},{7,6},{8,9},{9,8},{10,11... | collective-permute-start | bytes 688136 | tf_op jit(solution)/shard_map/ppermute | solution.py:300
  16.5 16.7 %collective-permute-start.12 = (bf16[896,128]{1,0:T(8,128)(2,1)S(1)}, bf16[896,128]{1,0:T(8,128)(2,1)S(1)}, u32[]{:S(2)}, u32[]{:S(2)}) collective-permute-start(bf16[896,128]{1,0:T(8,128)(2,1)S(1)} %get-tuple-element.49), channel_id=1, source_target_pairs={{0,5},{1,4},{2,7},{3,6},{4,1},{5,0},{6,3},{7,2},{8,13},{9,12},{10,... | collective-permute-start | bytes 688136 | tf_op jit(solution)/shard_map/ppermute | solution.py:300
  29.1 14.5 %collective-permute-start.13 = (bf16[352,128]{1,0:T(8,128)(2,1)S(1)}, bf16[352,128]{1,0:T(8,128)(2,1)S(1)}, u32[]{:S(2)}, u32[]{:S(2)}) collective-permute-start(bf16[352,128]{1,0:T(8,128)(2,1)S(1)} %get-tuple-element.57), channel_id=1, source_target_pairs={{0,2},{2,0},{4,6},{6,4},{1,3},{3,1},{5,7},{7,5},{8,10},{10,8},{12,... | collective-permute-start | bytes 270344 | tf_op jit(solution)/shard_map/ppermute | solution.py:291
  29.2 12.3 %collective-permute-start.7 = (bf16[2,352,128]{2,1,0:T(8,128)(2,1)S(1)}, bf16[2,352,128]{2,1,0:T(8,128)(2,1)S(1)}, u32[]{:S(2)}, u32[]{:S(2)}) collective-permute-start(bf16[2,352,128]{2,1,0:T(8,128)(2,1)S(1)} %get-tuple-element.54), channel_id=1, source_target_pairs={{0,4},{1,5},{2,6},{3,7},{4,0},{5,1},{6,2},{7,3},{8,12},{9,13},{10,... | collective-permute-start | bytes 540680 | tf_op jit(solution)/shard_map/ppermute | solution.py:300
  30.7 11.3 %collective-permute-start.8 = (bf16[2,352,128]{2,1,0:T(8,128)(2,1)S(1)}, bf16[2,352,128]{2,1,0:T(8,128)(2,1)S(1)}, u32[]{:S(2)}, u32[]{:S(2)}) collective-permute-start(bf16[2,352,128]{2,1,0:T(8,128)(2,1)S(1)} %get-tuple-element.55), channel_id=1, source_target_pairs={{0,1},{1,0},{2,3},{3,2},{4,5},{5,4},{6,7},{7,6},{8,9},{9,8},{10,11... | collective-permute-start | bytes 540680 | tf_op jit(solution)/shard_map/ppermute | solution.py:300
  31.7 11.7 %collective-permute-start.9 = (bf16[2,352,128]{2,1,0:T(8,128)(2,1)S(1)}, bf16[2,352,128]{2,1,0:T(8,128)(2,1)S(1)}, u32[]{:S(2)}, u32[]{:S(2)}) collective-permute-start(bf16[2,352,128]{2,1,0:T(8,128)(2,1)S(1)} %get-tuple-element.56), channel_id=1, source_target_pairs={{0,5},{1,4},{2,7},{3,6},{4,1},{5,0},{6,3},{7,2},{8,13},{9,12},{10,... | collective-permute-start | bytes 540680 | tf_op jit(solution)/shard_map/ppermute | solution.py:300
  39.9 7.6 %collective-permute-start.17 = (bf16[2,352,128]{2,1,0:T(8,128)(2,1)S(1)}, bf16[2,352,128]{2,1,0:T(8,128)(2,1)S(1)}, u32[]{:S(2)}, u32[]{:S(2)}) collective-permute-start(bf16[2,352,128]{2,1,0:T(8,128)(2,1)S(1)} %get-tuple-element.65), channel_id=1, source_target_pairs={{0,4},{1,5},{2,6},{3,7},{4,0},{5,1},{6,2},{7,3},{8,12},{9,13},{10,... | collective-permute-start | bytes 540680 | tf_op jit(solution)/shard_map/ppermute | solution.py:300
  41.4 7.6 %collective-permute-start.18 = (bf16[2,352,128]{2,1,0:T(8,128)(2,1)S(1)}, bf16[2,352,128]{2,1,0:T(8,128)(2,1)S(1)}, u32[]{:S(2)}, u32[]{:S(2)}) collective-permute-start(bf16[2,352,128]{2,1,0:T(8,128)(2,1)S(1)} %get-tuple-element.66), channel_id=1, source_target_pairs={{0,1},{1,0},{2,3},{3,2},{4,5},{5,4},{6,7},{7,6},{8,9},{9,8},{10,11... | collective-permute-start | bytes 540680 | tf_op jit(solution)/shard_map/ppermute | solution.py:300
  41.9 8.9 %collective-permute-start.19 = (bf16[2,352,128]{2,1,0:T(8,128)(2,1)S(1)}, bf16[2,352,128]{2,1,0:T(8,128)(2,1)S(1)}, u32[]{:S(2)}, u32[]{:S(2)}) collective-permute-start(bf16[2,352,128]{2,1,0:T(8,128)(2,1)S(1)} %get-tuple-element.67), channel_id=1, source_target_pairs={{0,5},{1,4},{2,7},{3,6},{4,1},{5,0},{6,3},{7,2},{8,13},{9,12},{10,... | collective-permute-start | bytes 540680 | tf_op jit(solution)/shard_map/ppermute | solution.py:300
  43.5 7.3 %collective-permute-start.16 = (bf16[352,128]{1,0:T(8,128)(2,1)S(1)}, bf16[352,128]{1,0:T(8,128)(2,1)S(1)}, u32[]{:S(2)}, u32[]{:S(2)}) collective-permute-start(bf16[352,128]{1,0:T(8,128)(2,1)S(1)} %slice_bitcast_fusion.3), channel_id=1, source_target_pairs={{0,2},{2,0},{4,6},{6,4},{1,3},{3,1},{5,7},{7,5},{8,10},{10,8},{12,... | collective-permute-start | bytes 270344 | tf_op jit(solution)/shard_map/ppermute | solution.py:291
  43.6 7.3 %collective-permute-start.15 = (bf16[352,128]{1,0:T(8,128)(2,1)S(1)}, bf16[352,128]{1,0:T(8,128)(2,1)S(1)}, u32[]{:S(2)}, u32[]{:S(2)}) collective-permute-start(bf16[352,128]{1,0:T(8,128)(2,1)S(1)} %slice_bitcast_fusion.4), channel_id=1, source_target_pairs={{0,2},{2,0},{4,6},{6,4},{1,3},{3,1},{5,7},{7,5},{8,10},{10,8},{12,... | collective-permute-start | bytes 270344 | tf_op jit(solution)/shard_map/ppermute | solution.py:291
  47.4 3.4 %collective-permute-start.14 = (bf16[352,128]{1,0:T(8,128)(2,1)S(1)}, bf16[352,128]{1,0:T(8,128)(2,1)S(1)}, u32[]{:S(2)}, u32[]{:S(2)}) collective-permute-start(bf16[352,128]{1,0:T(8,128)(2,1)S(1)} %slice_bitcast_fusion.5), channel_id=1, source_target_pairs={{0,2},{2,0},{4,6},{6,4},{1,3},{3,1},{5,7},{7,5},{8,10},{10,8},{12,... | collective-permute-start | bytes 270344 | tf_op jit(solution)/shard_map/ppermute | solution.py:291
  49.0 2.5 %collective-permute-start.20 = (bf16[352,128]{1,0:T(8,128)(2,1)S(1)}, bf16[352,128]{1,0:T(8,128)(2,1)S(1)}, u32[]{:S(2)}, u32[]{:S(2)}) collective-permute-start(bf16[352,128]{1,0:T(8,128)(2,1)S(1)} %get-tuple-element.71), channel_id=1, source_target_pairs={{0,2},{2,0},{4,6},{6,4},{1,3},{3,1},{5,7},{7,5},{8,10},{10,8},{12,... | collective-permute-start | bytes 270344 | tf_op jit(solution)/shard_map/ppermute | solution.py:291
  50.9 1.4 %collective-permute-start.23 = (bf16[352,128]{1,0:T(8,128)(2,1)S(1)}, bf16[352,128]{1,0:T(8,128)(2,1)S(1)}, u32[]{:S(2)}, u32[]{:S(2)}) collective-permute-start(bf16[352,128]{1,0:T(8,128)(2,1)S(1)} %slice_bitcast_fusion), channel_id=1, source_target_pairs={{0,2},{2,0},{4,6},{6,4},{1,3},{3,1},{5,7},{7,5},{8,10},{10,8},{12,... | collective-permute-start | bytes 270344 | tf_op jit(solution)/shard_map/ppermute | solution.py:291
  51.0 1.4 %collective-permute-start.22 = (bf16[352,128]{1,0:T(8,128)(2,1)S(1)}, bf16[352,128]{1,0:T(8,128)(2,1)S(1)}, u32[]{:S(2)}, u32[]{:S(2)}) collective-permute-start(bf16[352,128]{1,0:T(8,128)(2,1)S(1)} %slice_bitcast_fusion.1), channel_id=1, source_target_pairs={{0,2},{2,0},{4,6},{6,4},{1,3},{3,1},{5,7},{7,5},{8,10},{10,8},{12,... | collective-permute-start | bytes 270344 | tf_op jit(solution)/shard_map/ppermute | solution.py:291
  51.5 1.3 %collective-permute-start.21 = (bf16[352,128]{1,0:T(8,128)(2,1)S(1)}, bf16[352,128]{1,0:T(8,128)(2,1)S(1)}, u32[]{:S(2)}, u32[]{:S(2)}) collective-permute-start(bf16[352,128]{1,0:T(8,128)(2,1)S(1)} %slice_bitcast_fusion.2), channel_id=1, source_target_pairs={{0,2},{2,0},{4,6},{6,4},{1,3},{3,1},{5,7},{7,5},{8,10},{10,8},{12,... | collective-permute-start | bytes 270344 | tf_op jit(solution)/shard_map/ppermute | solution.py:291
  (6 other events, 19.6 us)

commit v6 on v5

--- a/solution.py
+++ b/solution.py
@@ -77,7 +77,7 @@
     W = D // (2 * C)
     for d in range(C):
         cols = functools.partial(head_columns, meta_ref, d, p=p, W=W)
-        out_ref[d, :R] = beside(cols(x_ref, 0), cols(x_ref, D))
+        out_ref[d, :R] = beside(cols(x_ref, D), cols(x_ref, 0))
         out_ref[d, R:] = beside(cols(x_ref, 2 * D), cols(cq_ref, 0))
 
 
@@ -90,7 +90,7 @@
         cols = functools.partial(head_columns, meta_ref, d, p=p, W=W)
         msg = msgs[d]
         msg[:R] = own_ref[d, :R]
-        msg[R : 2 * R] = beside(cols(xs_ref, 0), cols(xs_ref, D))
+        msg[R : 2 * R] = beside(cols(xs_ref, D), cols(xs_ref, 0))
         msg[2 * R : 3 * R] = own_ref[d, R:]
         msg[3 * R : 4 * R] = beside(cols(xs_ref, 2 * D), cols(cqs_ref, 0))
         msg[4 * R : 5 * R] = beside(cols(go_ref, 0), cols(gos_ref, 0))
@@ -106,20 +106,23 @@
         if d == 0:
             out.append(lambda rows, lanes, ref=refs[0]: ref[rows, lanes])
         else:
-            out.append(lambda rows, lanes, ref=refs[d]: ref[0, rows, lanes])
+            lead = (0,) if len(refs[d].shape) == 3 else ()
+            out.append(lambda rows, lanes, ref=refs[d], lead=lead: ref[(*lead, rows, lanes)])
         out.append(lambda rows, lanes, ref=refs[C + d]: ref[rows, lanes])
     return out
 
 
 def put(msgs, block, rows, lanes, value):
     d, e = block // 2, block % 2
-    if d == 0:
-        msgs[e][rows, lanes] = value
+    if d == 0 or len(msgs[-1].shape) == 2:
+        msgs[block][rows, lanes] = value
     else:
         msgs[d + 1][e, rows, lanes] = value
 
 
-def message_shapes(C, rows):
+def message_shapes(C, rows, direct):
+    if direct:
+        return (sds((rows, 128)),) * (2 * C)
     return (sds((rows, 128)),) * 2 + (sds((2, rows, 128)),) * (C - 1)
 
 
@@ -132,20 +135,23 @@
 
 
 def layer_kernel(meta_ref, *refs, C, R, M):
-    ins, outs = refs[:C], refs[C : 2 * C + 1]
-    q_ref, k_ref, v_ref, cq_ref, go_ref, vT_ref, kT_ref, t_ref, dt_ref = refs[2 * C + 1 : 2 * C + 10]
-    oT_ref, ag_ref, pT_ref, ds_ref = refs[2 * C + 10 :]
+    ins, outs = refs[:C], refs[C:-14]
+    k_ref, v_ref, qT_ref, kT_ref, vT_ref, cqT_ref, goT_ref, agT_ref = refs[-14:-6]
+    t_ref, dt_ref, oT_ref, back_ref, pT_ref, ds_ref = refs[-6:]
     L = 2 * C * R
     QB = 2 * R
+    WB = min(512, L)
     MR = M // (2 * C)
     left, right = slice(0, HD), slice(HD, 2 * HD)
     for b in range(C):
         rows = slice(b * QB, (b + 1) * QB)
-        q_ref[rows], k_ref[rows] = ins[b][:QB, left], ins[b][:QB, right]
-        v_ref[rows], cq_ref[rows] = ins[b][QB : 2 * QB, left], ins[b][QB : 2 * QB, right]
-        go_ref[b * QB : b * QB + R] = ins[b][4 * R : 5 * R, left]
-        go_ref[b * QB + R : (b + 1) * QB] = ins[b][4 * R : 5 * R, right]
-        kT_ref[:, rows], vT_ref[:, rows] = k_ref[rows].T, v_ref[rows].T
+        k_ref[rows], v_ref[rows] = ins[b][:QB, left], ins[b][QB : 2 * QB, left]
+        both = ins[b][:QB].T
+        kT_ref[:, rows], qT_ref[:, rows] = both[left], both[right]
+        both = ins[b][QB : 2 * QB].T
+        vT_ref[:, rows], cqT_ref[:, rows] = both[left], both[right]
+        both = ins[b][4 * R : 5 * R].T
+        goT_ref[:, b * QB : b * QB + R], goT_ref[:, b * QB + R : (b + 1) * QB] = both[left], both[right]
     for d in range(C):
 
         @pl.when(meta_ref[1 + C] == d)
@@ -153,10 +159,9 @@
             t_ref[...] = ins[d][5 * R :, :]
 
     tk, tv = t_ref[:, left], t_ref[:, right]
-    tkT, tvT = tk.T, tv.T
+    tT = t_ref[...].T
+    tkT, tvT = tT[left], tT[right]
     k, v, kT, vT = k_ref[...], v_ref[...], kT_ref[...], vT_ref[...]
-
-    WB = 512
 
     def block(b):
         return slice(b * WB, (b + 1) * WB)
@@ -166,59 +171,59 @@
         pT_ref[:, block(b)] = p
         oT_ref[:, block(b)] = dot(vT, p)
 
-    ahead(L // WB, lambda b: dot_nt(k, q_ref[block(b)]), attend)
-    go = go_ref[...]
-    att = oT_ref[...].T.astype(BF).astype(F32)
-    x = (att + cq_ref[...].astype(F32)).astype(BF)
-    cp = softmax_t(dot_nt(tk, x))
-    dp = dot_nt(tv, go)
+    ahead(L // WB, lambda b: dot(k, qT_ref[:, block(b)]), attend)
+    goT = goT_ref[...]
+    wide = goT.astype(F32)
+    att = oT_ref[...].astype(BF).astype(F32)
+    xT = (att + cqT_ref[...].astype(F32)).astype(BF)
+    dp = dot(tv, goT)
+    cp = softmax_t(dot(tk, xT))
     mix = dot(tvT, cp)
-    delta = jnp.sum(go.T.astype(F32) * mix, axis=0, keepdims=True)
+    back_ref[right] = (att + mix).astype(BF)
+    delta = jnp.sum(wide * mix, axis=0, keepdims=True)
     ds = (cp.astype(F32) * (dp - delta)).astype(BF)
-    dq = dot(tkT, ds).T * SCALE
-    ag = (go.astype(F32) + dq).astype(BF)
-    ag_ref[...] = ag
-    dt_ref[...] = beside(dot(ds, x) * SCALE, dot(cp, go)).astype(BF)
-    combined, dcq = (att + mix.T).astype(BF), dq.astype(BF)
+    dq = dot(tkT, ds) * SCALE
+    agT = (wide + dq).astype(BF)
+    agT_ref[...] = agT
+    dcq = dq.astype(BF)
+    dt_ref[...] = beside(dot_nt(ds, xT) * SCALE, dot_nt(cp, goT)).astype(BF)
     h = R // 2
     for i in range(2 * C):
         at = i * R
-        put(outs, i, slice(R, 2 * R), right, combined[at : at + R])
-        halves = beside(dcq[at : at + h], dcq[at + h : at + R])
-        put(outs, i, slice(2 * R, 2 * R + h), slice(None), halves)
+        halves = jnp.concatenate([dcq[:, at : at + h], dcq[:, at + h : at + R]], axis=0)
+        put(outs, i, slice(2 * R, 2 * R + h), slice(None), halves.T)
         start = pl.multiple_of(meta_ref[3 + C + i] * MR, MR)
         put(outs, i, slice(2 * R + h, None), slice(None), dt_ref[pl.ds(start, MR), :])
-    delta = jnp.sum(ag.T.astype(F32) * oT_ref[...], axis=0, keepdims=True)
+    delta = jnp.sum(agT.astype(F32) * oT_ref[...], axis=0, keepdims=True)
 
     def back(b, dp):
         ds = (pT_ref[:, block(b)].astype(F32) * (dp - delta[:, block(b)])).astype(BF)
         ds_ref[:, block(b)] = ds
-        dq = (dot(kT, ds).T * SCALE).astype(BF)
+        back_ref[left, block(b)] = (dot(kT, ds) * SCALE).astype(BF)
         n = WB // R
-        for e in range(n):
-            put(outs, n * b + e, slice(0, R), left, dq[e * R : (e + 1) * R])
-
-    ahead(L // WB, lambda b: dot_nt(v, ag_ref[block(b)]), back)
-    dk = (dot(ds_ref[...], q_ref[...]) * SCALE).astype(BF)
-    dv = dot(pT_ref[...], ag).astype(BF)
+        for i in range(n * b, n * b + n):
+            put(outs, i, slice(0, R), slice(None), back_ref[:, i * R : (i + 1) * R].T)
+
+    ahead(L // WB, lambda b: dot(v, agT_ref[:, block(b)]), back)
+    dk = dot(ds_ref[...], qT_ref[...].T) * SCALE
+    dv = dot(pT_ref[...], agT.T)
+    both = beside(dk.astype(BF), dv.astype(BF))
     for i in range(2 * C):
-        part = slice(i * R, (i + 1) * R)
-        put(outs, i, slice(0, R), right, dk[part])
-        put(outs, i, slice(R, 2 * R), left, dv[part])
-
-
-def layer(meta, msgs, C, R, M):
+        put(outs, i, slice(R, 2 * R), slice(None), both[i * R : (i + 1) * R])
+
+
+def layer(meta, msgs, C, R, M, direct):
     L, H = 2 * C * R, HD
     return call(
         functools.partial(layer_kernel, C=C, R=R, M=M),
         "layer",
         [meta, *msgs],
-        message_shapes(C, 2 * R + R // 2 + M // (2 * C)),
+        message_shapes(C, 2 * R + R // 2 + M // (2 * C), direct),
         LIMIT,
-        [pltpu.VMEM((L, H), BF)] * 5
-        + [pltpu.VMEM((H, L), BF)] * 2
+        [pltpu.VMEM((L, H), BF)] * 2
+        + [pltpu.VMEM((H, L), BF)] * 6
         + [pltpu.VMEM((M, 128), BF)] * 2
-        + [pltpu.VMEM((H, L), F32), pltpu.VMEM((L, H), BF)]
+        + [pltpu.VMEM((H, L), F32), pltpu.VMEM((128, L), BF)]
         + [pltpu.VMEM((L, L), BF)] * 2,
         cost(L * L + L * M, 6),
     )
@@ -226,7 +231,8 @@
 
 def unpack_kernel(meta_ref, *refs, C, H):
     passes = [pieces(refs[2 * C * p : 2 * C * (p + 1)]) for p in range(H)]
-    qkv_ref, comb_ref, dcq_ref, dt_ref = refs[2 * C * H :]
+    outs, (qkv_ref, comb_ref, dcq_ref, dt_ref) = refs[2 * C * H :][:4], refs[2 * C * H :][4:8]
+    sems = refs[-1]
     R, D = comb_ref.shape
     W = D // (2 * C)
     side = meta_ref[0]
@@ -243,15 +249,16 @@
 
     parts = [
         (qkv_ref, 0, lambda piece: piece(first, left)),
-        (qkv_ref, D, lambda piece: piece(first, right)),
-        (qkv_ref, 2 * D, lambda piece: piece(second, left)),
-        (comb_ref, 0, lambda piece: piece(second, right)),
+        (qkv_ref, D, lambda piece: piece(second, left)),
+        (qkv_ref, 2 * D, lambda piece: piece(second, right)),
+        (comb_ref, 0, lambda piece: piece(first, right)),
         (dcq_ref, 0, dcq),
         (dt_ref, 0, lambda piece: piece(end, left)),
         (dt_ref, D, lambda piece: piece(end, right)),
     ]
-    for d in range(C):
-        for ref, base, read in parts:
+    copies = []
+    for n, (ref, base, read) in enumerate(parts):
+        for d in range(C):
             at = base + meta_ref[1 + d] * 2 * W
             if H == 1:
                 a, b = read(passes[0][2 * d]), read(passes[0][2 * d + 1])
@@ -264,6 +271,12 @@
                     pair = beside(read(passes[p][2 * d + e]), read(passes[p + 1][2 * d + e]))
                     start = pl.multiple_of(at + core * W + p * HD, 128)
                     ref[:, pl.ds(start, 128)] = pair
+        target = outs[(0, 0, 0, 1, 2, 3, 3)[n]]
+        cols = slice(base, base + D)
+        copies.append(pltpu.make_async_copy(ref.at[:, cols], target.at[:, cols], sems.at[n]))
+        copies[-1].start()
+    for copy in copies:
+        copy.wait()
 
 
 def body(self_qkv, cross_query, thermal_kv, owners, grad_out):
@@ -290,12 +303,12 @@
     def to_sibling(a):
         return lax.ppermute(a, "seq", [(i, i ^ 1) for i in range(S)])
 
-    def to_chip(a, d, sign):
+    def to_chip(a, d, sign, other=0):
         i, j = offsets[d]
         pairs = []
         for p in range(S):
             for q in range(Hd):
-                there = ((p // 2 + sign * i) % X) * 2 + p % 2
+                there = ((p // 2 + sign * i) % X) * 2 + (p % 2 ^ other)
                 pairs.append((p * Hd + q, there * Hd + (q + sign * j) % Hd))
         return lax.ppermute(a, GROUP, pairs)
 
@@ -328,25 +341,31 @@
             got[p - 1] = after(got[p - 1], *msgs[p])
     backs, outs = [], []
     for p in range(H):
-        out = layer(meta, [msgs[p][0], *got[p]], C, R, M)
+        out = layer(meta, [msgs[p][0], *got[p]], C, R, M, p == H - 1)
         outs.append(out)
         if p + 1 < H:
             got[p + 1] = after(got[p + 1], *out)
-        backs.append([to_chip(out[d + 1], d, -1) for d in range(1, C)])
+        if p + 1 < H:
+            backs.append([to_chip(out[d + 1], d, -1) for d in range(1, C)])
     pieces_in = []
-    for p in range(H):
-        back = after(backs[p], outs[p + 1][0]) if p + 1 < H else backs[p]
+    for p in range(H - 1):
+        back = after(backs[p], outs[p + 1][0])
         relayed = [to_sibling(outs[p][1])] + [to_sibling(g[1]) for g in back]
-        if p + 1 < H:
-            backs[p + 1] = after(backs[p + 1], *relayed)
         pieces_in += [outs[p][0], *back, *relayed]
-    grad_qkv, combined, grad_cross, grad_thermal = call(
+    out = outs[-1]
+    straight = [to_chip(out[2 * d], d, -1) for d in range(1, C)]
+    across = [to_chip(out[2 * d + 1], d, -1, 1) for d in range(C)]
+    pieces_in += [out[0], *straight, *across]
+    shapes = (sds((R, 3 * D)), sds((R, D)), sds((R, D)), sds((MR, 2 * D)))
+    grad_qkv, combined, grad_cross, grad_thermal = pl.pallas_call(
         bind(unpack_kernel, C=C, H=H),
-        "unpack",
-        [meta, *pieces_in],
-        (sds((R, 3 * D)), sds((R, D)), sds((R, D)), sds((MR, 2 * D))),
-        12,
-    )
+        out_shape=shapes,
+        in_specs=[SM] + [VM] * len(pieces_in),
+        out_specs=(pl.BlockSpec(memory_space=pltpu.HBM),) * 4,
+        scratch_shapes=[pltpu.VMEM(o.shape, BF) for o in shapes] + [pltpu.SemaphoreType.DMA((7,))],
+        name="unpack",
+        compiler_params=pltpu.CompilerParams(vmem_limit_bytes=8 * MIB),
+    )(meta, *pieces_in)
     return (combined[None], grad_qkv[None], grad_cross[None], grad_thermal[None])
 
 

time: 55.4 us -> 54.1 us (0.977)
  waiting for transfers between devices: 12 us -> 8.61 us
  starting transfers between devices: 20.2 us -> 23.4 us
  Pallas kernels: 19.1 us -> 17.9 us
    pallas_call x7 -> x6, Pallas kernels: 19.1 us -> 15.7 us  [call(): pl.pallas_call(kernel, out_shape=outs, in_specs=[SM if s else VM for s in...]
    ppermute x12 -> x16, starting transfers between devices: 17.9 us -> 20.7 us  [to_chip(): return lax.ppermute(a, GROUP, pairs)]
    pallas_call x0 -> x1, Pallas kernels: none -> 2.22 us  [body(): pl.pallas_call(bind(unpack_kernel, C=C, H=H), out_shape=shapes, in_specs=...]
    ppermute x12 -> x16, waiting for transfers between devices: 10.7 us -> 8.46 us  [to_chip(): return lax.ppermute(a, GROUP, pairs)]
    ppermute x12 -> x8, waiting for transfers between devices: 1.36 us -> 0.15 us  [to_sibling(): return lax.ppermute(a, 'seq', [(i, i ^ 1) for i in range(S)])]
    ppermute x12 -> x8, starting transfers between devices: 2.39 us -> 2.69 us  [to_sibling(): return lax.ppermute(a, 'seq', [(i, i ^ 1) for i in range(S)])]
  transfers between devices with their start and end apart: 24 -> 24, of which waited for: 9 -> 9; matrix products, arithmetic and copies ran while one was open for 0% -> 0% of each run, Pallas kernels for 28% -> 27%
where the time goes in v6:
time: 54.1 us; the launch traced here: 53.9 us
  starting transfers between devices  23.4 us (43%)
  Pallas kernels  17.9 us (33%)
  waiting for transfers between devices  8.61 us (16%)
  local copies, waits for them, and re-layouts  2.3 us (4%)
  between operations  1.66 us (3%)
    ppermute x16, starting transfers between devices, to_chip(): return lax.ppermute(a, GROUP, pairs)  20.7 us
    pallas_call x6, Pallas kernels, call(): pl.pallas_call(kernel, out_shape=outs, in_specs=[SM if s else VM for s in...  15.7 us
    ppermute x16, waiting for transfers between devices, to_chip(): return lax.ppermute(a, GROUP, pairs)  8.46 us
    ppermute x8, starting transfers between devices, to_sibling(): return lax.ppermute(a, 'seq', [(i, i ^ 1) for i in range(S)])  2.69 us
    pallas_call x1, Pallas kernels, body(): pl.pallas_call(bind(unpack_kernel, C=C, H=H), out_shape=shapes, in_specs=...  2.22 us
    unnamed x12, local copies, waits for them, and re-layouts  2.18 us
  transfers between devices with their start and end apart: 24, of which 9 were waited for; matrix products, arithmetic and copies ran while one was open for 0% of the time, Pallas kernels for 27%

profile of v6, /device:TPU:0, one launch (start us, length us, event | category | flops | bytes accessed | tf_op | source)
XLA Modules:
  0.0 53.9 jit_solution(17422272241261205145)
XLA Ops:
  2.6 1.1 %copy-done.1 = bf16[1,128,3072]{2,1,0:T(8,128)(2,1)S(1)} copy-done((bf16[1,128,3072]{2,1,0:T(8,128)(2,1)S(1)}, bf16[1,128,3072]{2,1,0:T(8,128)(2,1)}, u32[]{:S(2)}) %copy-start.1) | copy-done | bytes 786456
  3.7 0.9 %copy-done.3 = bf16[1,128,1024]{2,1,0:T(8,128)(2,1)S(1)} copy-done((bf16[1,128,1024]{2,1,0:T(8,128)(2,1)S(1)}, bf16[1,128,1024]{2,1,0:T(8,128)(2,1)}, u32[]{:S(2)}) %copy-start.3) | copy-done | bytes 262168
  5.6 1.0 %pack_sib_0.1 = (bf16[896,128]{1,0:T(8,128)(2,1)S(1)}, bf16[896,128]{1,0:T(8,128)(2,1)S(1)}, bf16[896,128]{1,0:T(8,128)(2,1)S(1)}, bf16[896,128]{1,0:T(8,128)(2,1)S(1)}) custom-call(s32[15]{0:T(128)S(1)} %stack.67.meta_ref, bf16[4,256,128]{2,1,0:T(8,128)(2,1)S(1)} %pack_own_0.1.own_ref, bf16[128,1024]{1,0:T(8,128)(2,1)S(1)} %bitcast.44, ...), custom_call_target="tpu_custom_call" | custom-call | tf_op jit(solution)/shard_map/pack_sib_0/pallas_call | solution.py:28
  6.7 3.0 %collective-permute-start.4 = (bf16[896,128]{1,0:T(8,128)(2,1)S(1)}, bf16[896,128]{1,0:T(8,128)(2,1)S(1)}, u32[]{:S(2)}, u32[]{:S(2)}) collective-permute-start(bf16[896,128]{1,0:T(8,128)(2,1)S(1)} %get-tuple-element.41), channel_id=1, source_target_pairs={{0,4},{1,5},{2,6},{3,7},{4,0},{5,1},{6,2},{7,3},{8,12},{9,13},{10,... | collective-permute-start | bytes 688136 | tf_op jit(solution)/shard_map/ppermute | solution.py:313
  9.6 1.5 %collective-permute-start.5 = (bf16[896,128]{1,0:T(8,128)(2,1)S(1)}, bf16[896,128]{1,0:T(8,128)(2,1)S(1)}, u32[]{:S(2)}, u32[]{:S(2)}) collective-permute-start(bf16[896,128]{1,0:T(8,128)(2,1)S(1)} %get-tuple-element.42), channel_id=1, source_target_pairs={{0,1},{1,0},{2,3},{3,2},{4,5},{5,4},{6,7},{7,6},{8,9},{9,8},{10,11... | collective-permute-start | bytes 688136 | tf_op jit(solution)/shard_map/ppermute | solution.py:313
  11.9 1.0 %pack_sib_1.1 = (bf16[896,128]{1,0:T(8,128)(2,1)S(1)}, bf16[896,128]{1,0:T(8,128)(2,1)S(1)}, bf16[896,128]{1,0:T(8,128)(2,1)S(1)}, bf16[896,128]{1,0:T(8,128)(2,1)S(1)}) custom-call(s32[15]{0:T(128)S(1)} %stack.67.meta_ref, bf16[4,256,128]{2,1,0:T(8,128)(2,1)S(1)} %pack_own_1.1.own_ref, bf16[128,1024]{1,0:T(8,128)(2,1)S(1)} %bitcast.45, ...), custom_call_target="tpu_custom_call" | custom-call | tf_op jit(solution)/shard_map/pack_sib_1/pallas_call | solution.py:28
  12.9 2.0 %collective-permute-start.10 = (bf16[896,128]{1,0:T(8,128)(2,1)S(1)}, bf16[896,128]{1,0:T(8,128)(2,1)S(1)}, u32[]{:S(2)}, u32[]{:S(2)}) collective-permute-start(bf16[896,128]{1,0:T(8,128)(2,1)S(1)} %get-tuple-element.47), channel_id=1, source_target_pairs={{0,4},{1,5},{2,6},{3,7},{4,0},{5,1},{6,2},{7,3},{8,12},{9,13},{10,... | collective-permute-start | bytes 688136 | tf_op jit(solution)/shard_map/ppermute | solution.py:313
  14.9 1.5 %collective-permute-start.11 = (bf16[896,128]{1,0:T(8,128)(2,1)S(1)}, bf16[896,128]{1,0:T(8,128)(2,1)S(1)}, u32[]{:S(2)}, u32[]{:S(2)}) collective-permute-start(bf16[896,128]{1,0:T(8,128)(2,1)S(1)} %get-tuple-element.48), channel_id=1, source_target_pairs={{0,1},{1,0},{2,3},{3,2},{4,5},{5,4},{6,7},{7,6},{8,9},{9,8},{10,11... | collective-permute-start | bytes 688136 | tf_op jit(solution)/shard_map/ppermute | solution.py:313
  16.5 2.6 %collective-permute-start.12 = (bf16[896,128]{1,0:T(8,128)(2,1)S(1)}, bf16[896,128]{1,0:T(8,128)(2,1)S(1)}, u32[]{:S(2)}, u32[]{:S(2)}) collective-permute-start(bf16[896,128]{1,0:T(8,128)(2,1)S(1)} %get-tuple-element.49), channel_id=1, source_target_pairs={{0,5},{1,4},{2,7},{3,6},{4,1},{5,0},{6,3},{7,2},{8,13},{9,12},{10,... | collective-permute-start | bytes 688136 | tf_op jit(solution)/shard_map/ppermute | solution.py:313
  19.1 3.5 %collective-permute-done.5.refs_2_ = bf16[896,128]{1,0:T(8,128)(2,1)S(1)} collective-permute-done((bf16[896,128]{1,0:T(8,128)(2,1)S(1)}, bf16[896,128]{1,0:T(8,128)(2,1)S(1)}, u32[]{:S(2)}, u32[]{:S(2)}) %collective-permute-start.5) | collective-permute-done | bytes 229408 | tf_op jit(solution)/shard_map/ppermute | solution.py:313
  22.6 6.0 %layer.2 = (bf16[352,128]{1,0:T(8,128)(2,1)S(1)}, bf16[352,128]{1,0:T(8,128)(2,1)S(1)}, bf16[2,352,128]{2,1,0:T(8,128)(2,1)S(1)}, bf16[2,352,128]{2,1,0:T(8,128)(2,1)S(1)}, bf16[2,352,128]{2,1,0:T(8,128)(2,1)S(1)}) custom-call(s32[15]{0:T(128)S(1)} %stack.67.meta_ref, bf16[896,128]{1,0:T(8,128)(2,1)S(1)} %get-tuple-element.40.refs_0_, ...), custom_call_target="tpu_custom_call" | custom-call | flops 4026531840 | bytes 5242880 | tf_op jit(solution)/shard_map/layer/pallas_call | solution.py:28
  28.7 1.5 %collective-permute-start.7 = (bf16[2,352,128]{2,1,0:T(8,128)(2,1)S(1)}, bf16[2,352,128]{2,1,0:T(8,128)(2,1)S(1)}, u32[]{:S(2)}, u32[]{:S(2)}) collective-permute-start(bf16[2,352,128]{2,1,0:T(8,128)(2,1)S(1)} %get-tuple-element.54), channel_id=1, source_target_pairs={{0,4},{1,5},{2,6},{3,7},{4,0},{5,1},{6,2},{7,3},{8,12},{9,13},{10,... | collective-permute-start | bytes 540680 | tf_op jit(solution)/shard_map/ppermute | solution.py:313
  30.9 0.8 %collective-permute-done.11.refs_2_ = bf16[896,128]{1,0:T(8,128)(2,1)S(1)} collective-permute-done((bf16[896,128]{1,0:T(8,128)(2,1)S(1)}, bf16[896,128]{1,0:T(8,128)(2,1)S(1)}, u32[]{:S(2)}, u32[]{:S(2)}) %collective-permute-start.11) | collective-permute-done | bytes 229408 | tf_op jit(solution)/shard_map/ppermute | solution.py:313
  31.7 1.5 %collective-permute-start.9 = (bf16[2,352,128]{2,1,0:T(8,128)(2,1)S(1)}, bf16[2,352,128]{2,1,0:T(8,128)(2,1)S(1)}, u32[]{:S(2)}, u32[]{:S(2)}) collective-permute-start(bf16[2,352,128]{2,1,0:T(8,128)(2,1)S(1)} %get-tuple-element.56), channel_id=1, source_target_pairs={{0,5},{1,4},{2,7},{3,6},{4,1},{5,0},{6,3},{7,2},{8,13},{9,12},{10,... | collective-permute-start | bytes 540680 | tf_op jit(solution)/shard_map/ppermute | solution.py:313
  33.2 6.2 %layer.3 = (bf16[352,128]{1,0:T(8,128)(2,1)S(1)}, bf16[352,128]{1,0:T(8,128)(2,1)S(1)}, bf16[352,128]{1,0:T(8,128)(2,1)S(1)}, bf16[352,128]{1,0:T(8,128)(2,1)S(1...) custom-call(s32[15]{0:T(128)S(1)} %stack.67.meta_ref, ...), custom_call_target="tpu_custom_call" | custom-call | flops 4026531840 | bytes 5242880 | tf_op jit(solution)/shard_map/layer/pallas_call | solution.py:28
  39.4 1.5 %collective-permute-start.17 = (bf16[352,128]{1,0:T(8,128)(2,1)S(1)}, bf16[352,128]{1,0:T(8,128)(2,1)S(1)}, u32[]{:S(2)}, u32[]{:S(2)}) collective-permute-start(bf16[352,128]{1,0:T(8,128)(2,1)S(1)} %get-tuple-element.65), channel_id=1, source_target_pairs={{0,4},{1,5},{2,6},{3,7},{4,0},{5,1},{6,2},{7,3},{8,12},{9,13},{10,... | collective-permute-start | bytes 270344 | tf_op jit(solution)/shard_map/ppermute | solution.py:313
  41.5 1.5 %collective-permute-start.19 = (bf16[352,128]{1,0:T(8,128)(2,1)S(1)}, bf16[352,128]{1,0:T(8,128)(2,1)S(1)}, u32[]{:S(2)}, u32[]{:S(2)}) collective-permute-start(bf16[352,128]{1,0:T(8,128)(2,1)S(1)} %get-tuple-element.67), channel_id=1, source_target_pairs={{0,5},{1,4},{2,7},{3,6},{4,1},{5,0},{6,3},{7,2},{8,13},{9,12},{10,... | collective-permute-start | bytes 270344 | tf_op jit(solution)/shard_map/ppermute | solution.py:313
  43.0 1.6 %collective-permute-start.21 = (bf16[352,128]{1,0:T(8,128)(2,1)S(1)}, bf16[352,128]{1,0:T(8,128)(2,1)S(1)}, u32[]{:S(2)}, u32[]{:S(2)}) collective-permute-start(bf16[352,128]{1,0:T(8,128)(2,1)S(1)} %get-tuple-element.69), channel_id=1, source_target_pairs={{0,6},{1,7},{2,4},{3,5},{4,2},{5,3},{6,0},{7,1},{8,14},{9,15},{10,... | collective-permute-start | bytes 270344 | tf_op jit(solution)/shard_map/ppermute | solution.py:313
  44.9 1.0 %collective-permute-done.18.refs_10_ = bf16[352,128]{1,0:T(8,128)(2,1)S(1)} collective-permute-done((bf16[352,128]{1,0:T(8,128)(2,1)S(1)}, bf16[352,128]{1,0:T(8,128)(2,1)S(1)}, u32[]{:S(2)}, u32[]{:S(2)}) %collective-permute-start.18) | collective-permute-done | bytes 90144 | tf_op jit(solution)/shard_map/ppermute | solution.py:313
  45.9 1.2 %collective-permute-start.23 = (bf16[352,128]{1,0:T(8,128)(2,1)S(1)}, bf16[352,128]{1,0:T(8,128)(2,1)S(1)}, u32[]{:S(2)}, u32[]{:S(2)}) collective-permute-start(bf16[352,128]{1,0:T(8,128)(2,1)S(1)} %get-tuple-element.71), channel_id=1, source_target_pairs={{0,7},{1,6},{2,5},{3,4},{4,3},{5,2},{6,1},{7,0},{8,15},{9,14},{10,... | collective-permute-start | bytes 270344 | tf_op jit(solution)/shard_map/ppermute | solution.py:313
  48.0 1.0 %collective-permute-start.14 = (bf16[352,128]{1,0:T(8,128)(2,1)S(1)}, bf16[352,128]{1,0:T(8,128)(2,1)S(1)}, u32[]{:S(2)}, u32[]{:S(2)}) collective-permute-start(bf16[352,128]{1,0:T(8,128)(2,1)S(1)} %slice_bitcast_fusion.2), channel_id=1, source_target_pairs={{0,2},{2,0},{4,6},{6,4},{1,3},{3,1},{5,7},{7,5},{8,10},{10,8},{12,... | collective-permute-start | bytes 270344 | tf_op jit(solution)/shard_map/ppermute | solution.py:304
  49.0 0.8 %collective-permute-done.22.refs_14_ = bf16[352,128]{1,0:T(8,128)(2,1)S(1)} collective-permute-done((bf16[352,128]{1,0:T(8,128)(2,1)S(1)}, bf16[352,128]{1,0:T(8,128)(2,1)S(1)}, u32[]{:S(2)}, u32[]{:S(2)}) %collective-permute-start.22) | collective-permute-done | bytes 90144 | tf_op jit(solution)/shard_map/ppermute | solution.py:313
  49.8 1.7 %collective-permute-done.23.refs_15_ = bf16[352,128]{1,0:T(8,128)(2,1)S(1)} collective-permute-done((bf16[352,128]{1,0:T(8,128)(2,1)S(1)}, bf16[352,128]{1,0:T(8,128)(2,1)S(1)}, u32[]{:S(2)}, u32[]{:S(2)}) %collective-permute-start.23) | collective-permute-done | bytes 90144 | tf_op jit(solution)/shard_map/ppermute | solution.py:313
  51.5 2.2 %unpack.1 = (bf16[128,3072]{1,0:T(8,128)(2,1)}, bf16[128,1024]{1,0:T(8,128)(2,1)}, bf16[128,1024]{1,0:T(8,128)(2,1)}, bf16[32,2048]{1,0:T(8,128)(2,1)}) custom-call(s32[15]{0:T(128)S(1)} %stack.67.meta_ref, bf16[352,128]{1,0:T(8,128)(2,1)S(1)} %get-tuple-element.53.refs_0_, bf16[2,352,128]{2,1,0:T(8,128)(2,1)S(1)} %collective-permute-done.7.refs_1_, ...), custom_call_target="tpu_custom_call" | custom-call | tf_op jit(solution)/shard_map/unpack/pallas_call | solution.py:360
  (47 shorter events, 5.3 us)
Async XLA Ops:
  0.6 4.9 %collective-permute-start.3 = (bf16[256,2048]{1,0:T(8,128)(2,1)}, bf16[256,2048]{1,0:T(8,128)(2,1)S(1)}, u32[]{:S(2)}, u32[]{:S(2)}) collective-permute-start(bf16[256,2048]{1,0:T(8,128)(2,1)} %bitcast.34), channel_id=1, source_target_pairs={{0,2},{2,0},{4,6},{6,4},{1,3},{3,1},{5,7},{7,5},{8,10},{10,8},{12,... | collective-permute-start | bytes 3145736 | tf_op jit(solution)/shard_map/ppermute | solution.py:304
  1.2 4.4 %collective-permute-start = (bf16[128,3072]{1,0:T(8,128)(2,1)}, bf16[128,3072]{1,0:T(8,128)(2,1)S(1)}, u32[]{:S(2)}, u32[]{:S(2)}) collective-permute-start(bf16[128,3072]{1,0:T(8,128)(2,1)} %bitcast.37), channel_id=1, source_target_pairs={{0,2},{2,0},{4,6},{6,4},{1,3},{3,1},{5,7},{7,5},{8,10},{10,8},{12,... | collective-permute-start | bytes 2359304 | tf_op jit(solution)/shard_map/ppermute | solution.py:304
  1.2 4.2 %collective-permute-start.1 = (bf16[128,1024]{1,0:T(8,128)(2,1)}, bf16[128,1024]{1,0:T(8,128)(2,1)S(1)}, u32[]{:S(2)}, u32[]{:S(2)}) collective-permute-start(bf16[128,1024]{1,0:T(8,128)(2,1)} %bitcast.40), channel_id=1, source_target_pairs={{0,2},{2,0},{4,6},{6,4},{1,3},{3,1},{5,7},{7,5},{8,10},{10,8},{12,... | collective-permute-start | bytes 786440 | tf_op jit(solution)/shard_map/ppermute | solution.py:304
  1.7 3.9 %collective-permute-start.2 = (bf16[128,1024]{1,0:T(8,128)(2,1)}, bf16[128,1024]{1,0:T(8,128)(2,1)S(1)}, u32[]{:S(2)}, u32[]{:S(2)}) collective-permute-start(bf16[128,1024]{1,0:T(8,128)(2,1)} %bitcast.43), channel_id=1, source_target_pairs={{0,2},{2,0},{4,6},{6,4},{1,3},{3,1},{5,7},{7,5},{8,10},{10,8},{12,... | collective-permute-start | bytes 786440 | tf_op jit(solution)/shard_map/ppermute | solution.py:304
  6.7 9.8 %collective-permute-start.4 = (bf16[896,128]{1,0:T(8,128)(2,1)S(1)}, bf16[896,128]{1,0:T(8,128)(2,1)S(1)}, u32[]{:S(2)}, u32[]{:S(2)}) collective-permute-start(bf16[896,128]{1,0:T(8,128)(2,1)S(1)} %get-tuple-element.41), channel_id=1, source_target_pairs={{0,4},{1,5},{2,6},{3,7},{4,0},{5,1},{6,2},{7,3},{8,12},{9,13},{10,... | collective-permute-start | bytes 688136 | tf_op jit(solution)/shard_map/ppermute | solution.py:313
  9.6 12.9 %collective-permute-start.5 = (bf16[896,128]{1,0:T(8,128)(2,1)S(1)}, bf16[896,128]{1,0:T(8,128)(2,1)S(1)}, u32[]{:S(2)}, u32[]{:S(2)}) collective-permute-start(bf16[896,128]{1,0:T(8,128)(2,1)S(1)} %get-tuple-element.42), channel_id=1, source_target_pairs={{0,1},{1,0},{2,3},{3,2},{4,5},{5,4},{6,7},{7,6},{8,9},{9,8},{10,11... | collective-permute-start | bytes 688136 | tf_op jit(solution)/shard_map/ppermute | solution.py:313
  11.2 11.4 %collective-permute-start.6 = (bf16[896,128]{1,0:T(8,128)(2,1)S(1)}, bf16[896,128]{1,0:T(8,128)(2,1)S(1)}, u32[]{:S(2)}, u32[]{:S(2)}) collective-permute-start(bf16[896,128]{1,0:T(8,128)(2,1)S(1)} %get-tuple-element.43), channel_id=1, source_target_pairs={{0,5},{1,4},{2,7},{3,6},{4,1},{5,0},{6,3},{7,2},{8,13},{9,12},{10,... | collective-permute-start | bytes 688136 | tf_op jit(solution)/shard_map/ppermute | solution.py:313
  12.9 17.3 %collective-permute-start.10 = (bf16[896,128]{1,0:T(8,128)(2,1)S(1)}, bf16[896,128]{1,0:T(8,128)(2,1)S(1)}, u32[]{:S(2)}, u32[]{:S(2)}) collective-permute-start(bf16[896,128]{1,0:T(8,128)(2,1)S(1)} %get-tuple-element.47), channel_id=1, source_target_pairs={{0,4},{1,5},{2,6},{3,7},{4,0},{5,1},{6,2},{7,3},{8,12},{9,13},{10,... | collective-permute-start | bytes 688136 | tf_op jit(solution)/shard_map/ppermute | solution.py:313
  14.9 16.8 %collective-permute-start.11 = (bf16[896,128]{1,0:T(8,128)(2,1)S(1)}, bf16[896,128]{1,0:T(8,128)(2,1)S(1)}, u32[]{:S(2)}, u32[]{:S(2)}) collective-permute-start(bf16[896,128]{1,0:T(8,128)(2,1)S(1)} %get-tuple-element.48), channel_id=1, source_target_pairs={{0,1},{1,0},{2,3},{3,2},{4,5},{5,4},{6,7},{7,6},{8,9},{9,8},{10,11... | collective-permute-start | bytes 688136 | tf_op jit(solution)/shard_map/ppermute | solution.py:313
  16.5 16.7 %collective-permute-start.12 = (bf16[896,128]{1,0:T(8,128)(2,1)S(1)}, bf16[896,128]{1,0:T(8,128)(2,1)S(1)}, u32[]{:S(2)}, u32[]{:S(2)}) collective-permute-start(bf16[896,128]{1,0:T(8,128)(2,1)S(1)} %get-tuple-element.49), channel_id=1, source_target_pairs={{0,5},{1,4},{2,7},{3,6},{4,1},{5,0},{6,3},{7,2},{8,13},{9,12},{10,... | collective-permute-start | bytes 688136 | tf_op jit(solution)/shard_map/ppermute | solution.py:313
  28.6 14.4 %collective-permute-start.13 = (bf16[352,128]{1,0:T(8,128)(2,1)S(1)}, bf16[352,128]{1,0:T(8,128)(2,1)S(1)}, u32[]{:S(2)}, u32[]{:S(2)}) collective-permute-start(bf16[352,128]{1,0:T(8,128)(2,1)S(1)} %get-tuple-element.57), channel_id=1, source_target_pairs={{0,2},{2,0},{4,6},{6,4},{1,3},{3,1},{5,7},{7,5},{8,10},{10,8},{12,... | collective-permute-start | bytes 270344 | tf_op jit(solution)/shard_map/ppermute | solution.py:304
  28.7 12.2 %collective-permute-start.7 = (bf16[2,352,128]{2,1,0:T(8,128)(2,1)S(1)}, bf16[2,352,128]{2,1,0:T(8,128)(2,1)S(1)}, u32[]{:S(2)}, u32[]{:S(2)}) collective-permute-start(bf16[2,352,128]{2,1,0:T(8,128)(2,1)S(1)} %get-tuple-element.54), channel_id=1, source_target_pairs={{0,4},{1,5},{2,6},{3,7},{4,0},{5,1},{6,2},{7,3},{8,12},{9,13},{10,... | collective-permute-start | bytes 540680 | tf_op jit(solution)/shard_map/ppermute | solution.py:313
  30.2 11.3 %collective-permute-start.8 = (bf16[2,352,128]{2,1,0:T(8,128)(2,1)S(1)}, bf16[2,352,128]{2,1,0:T(8,128)(2,1)S(1)}, u32[]{:S(2)}, u32[]{:S(2)}) collective-permute-start(bf16[2,352,128]{2,1,0:T(8,128)(2,1)S(1)} %get-tuple-element.55), channel_id=1, source_target_pairs={{0,1},{1,0},{2,3},{3,2},{4,5},{5,4},{6,7},{7,6},{8,9},{9,8},{10,11... | collective-permute-start | bytes 540680 | tf_op jit(solution)/shard_map/ppermute | solution.py:313
  31.7 11.3 %collective-permute-start.9 = (bf16[2,352,128]{2,1,0:T(8,128)(2,1)S(1)}, bf16[2,352,128]{2,1,0:T(8,128)(2,1)S(1)}, u32[]{:S(2)}, u32[]{:S(2)}) collective-permute-start(bf16[2,352,128]{2,1,0:T(8,128)(2,1)S(1)} %get-tuple-element.56), channel_id=1, source_target_pairs={{0,5},{1,4},{2,7},{3,6},{4,1},{5,0},{6,3},{7,2},{8,13},{9,12},{10,... | collective-permute-start | bytes 540680 | tf_op jit(solution)/shard_map/ppermute | solution.py:313
  39.4 5.5 %collective-permute-start.17 = (bf16[352,128]{1,0:T(8,128)(2,1)S(1)}, bf16[352,128]{1,0:T(8,128)(2,1)S(1)}, u32[]{:S(2)}, u32[]{:S(2)}) collective-permute-start(bf16[352,128]{1,0:T(8,128)(2,1)S(1)} %get-tuple-element.65), channel_id=1, source_target_pairs={{0,4},{1,5},{2,6},{3,7},{4,0},{5,1},{6,2},{7,3},{8,12},{9,13},{10,... | collective-permute-start | bytes 270344 | tf_op jit(solution)/shard_map/ppermute | solution.py:313
  40.9 4.9 %collective-permute-start.18 = (bf16[352,128]{1,0:T(8,128)(2,1)S(1)}, bf16[352,128]{1,0:T(8,128)(2,1)S(1)}, u32[]{:S(2)}, u32[]{:S(2)}) collective-permute-start(bf16[352,128]{1,0:T(8,128)(2,1)S(1)} %get-tuple-element.66), channel_id=1, source_target_pairs={{0,1},{1,0},{2,3},{3,2},{4,5},{5,4},{6,7},{7,6},{8,9},{9,8},{10,11... | collective-permute-start | bytes 270344 | tf_op jit(solution)/shard_map/ppermute | solution.py:313
  41.5 5.9 %collective-permute-start.19 = (bf16[352,128]{1,0:T(8,128)(2,1)S(1)}, bf16[352,128]{1,0:T(8,128)(2,1)S(1)}, u32[]{:S(2)}, u32[]{:S(2)}) collective-permute-start(bf16[352,128]{1,0:T(8,128)(2,1)S(1)} %get-tuple-element.67), channel_id=1, source_target_pairs={{0,5},{1,4},{2,7},{3,6},{4,1},{5,0},{6,3},{7,2},{8,13},{9,12},{10,... | collective-permute-start | bytes 270344 | tf_op jit(solution)/shard_map/ppermute | solution.py:313
  43.0 4.4 %collective-permute-start.20 = (bf16[352,128]{1,0:T(8,128)(2,1)S(1)}, bf16[352,128]{1,0:T(8,128)(2,1)S(1)}, u32[]{:S(2)}, u32[]{:S(2)}) collective-permute-start(bf16[352,128]{1,0:T(8,128)(2,1)S(1)} %get-tuple-element.68), channel_id=1, source_target_pairs={{0,2},{1,3},{2,0},{3,1},{4,6},{5,7},{6,4},{7,5},{8,10},{9,11},{10,... | collective-permute-start | bytes 270344 | tf_op jit(solution)/shard_map/ppermute | solution.py:313
  43.0 5.0 %collective-permute-start.21 = (bf16[352,128]{1,0:T(8,128)(2,1)S(1)}, bf16[352,128]{1,0:T(8,128)(2,1)S(1)}, u32[]{:S(2)}, u32[]{:S(2)}) collective-permute-start(bf16[352,128]{1,0:T(8,128)(2,1)S(1)} %get-tuple-element.69), channel_id=1, source_target_pairs={{0,6},{1,7},{2,4},{3,5},{4,2},{5,3},{6,0},{7,1},{8,14},{9,15},{10,... | collective-permute-start | bytes 270344 | tf_op jit(solution)/shard_map/ppermute | solution.py:313
  44.9 4.9 %collective-permute-start.22 = (bf16[352,128]{1,0:T(8,128)(2,1)S(1)}, bf16[352,128]{1,0:T(8,128)(2,1)S(1)}, u32[]{:S(2)}, u32[]{:S(2)}) collective-permute-start(bf16[352,128]{1,0:T(8,128)(2,1)S(1)} %get-tuple-element.70), channel_id=1, source_target_pairs={{0,3},{1,2},{2,1},{3,0},{4,7},{5,6},{6,5},{7,4},{8,11},{9,10},{10,... | collective-permute-start | bytes 270344 | tf_op jit(solution)/shard_map/ppermute | solution.py:313
  45.9 5.6 %collective-permute-start.23 = (bf16[352,128]{1,0:T(8,128)(2,1)S(1)}, bf16[352,128]{1,0:T(8,128)(2,1)S(1)}, u32[]{:S(2)}, u32[]{:S(2)}) collective-permute-start(bf16[352,128]{1,0:T(8,128)(2,1)S(1)} %get-tuple-element.71), channel_id=1, source_target_pairs={{0,7},{1,6},{2,5},{3,4},{4,3},{5,2},{6,1},{7,0},{8,15},{9,14},{10,... | collective-permute-start | bytes 270344 | tf_op jit(solution)/shard_map/ppermute | solution.py:313
  47.3 4.2 %collective-permute-start.16 = (bf16[352,128]{1,0:T(8,128)(2,1)S(1)}, bf16[352,128]{1,0:T(8,128)(2,1)S(1)}, u32[]{:S(2)}, u32[]{:S(2)}) collective-permute-start(bf16[352,128]{1,0:T(8,128)(2,1)S(1)} %slice_bitcast_fusion), channel_id=1, source_target_pairs={{0,2},{2,0},{4,6},{6,4},{1,3},{3,1},{5,7},{7,5},{8,10},{10,8},{12,... | collective-permute-start | bytes 270344 | tf_op jit(solution)/shard_map/ppermute | solution.py:304
  47.3 4.2 %collective-permute-start.15 = (bf16[352,128]{1,0:T(8,128)(2,1)S(1)}, bf16[352,128]{1,0:T(8,128)(2,1)S(1)}, u32[]{:S(2)}, u32[]{:S(2)}) collective-permute-start(bf16[352,128]{1,0:T(8,128)(2,1)S(1)} %slice_bitcast_fusion.1), channel_id=1, source_target_pairs={{0,2},{2,0},{4,6},{6,4},{1,3},{3,1},{5,7},{7,5},{8,10},{10,8},{12,... | collective-permute-start | bytes 270344 | tf_op jit(solution)/shard_map/ppermute | solution.py:304
  48.0 3.5 %collective-permute-start.14 = (bf16[352,128]{1,0:T(8,128)(2,1)S(1)}, bf16[352,128]{1,0:T(8,128)(2,1)S(1)}, u32[]{:S(2)}, u32[]{:S(2)}) collective-permute-start(bf16[352,128]{1,0:T(8,128)(2,1)S(1)} %slice_bitcast_fusion.2), channel_id=1, source_target_pairs={{0,2},{2,0},{4,6},{6,4},{1,3},{3,1},{5,7},{7,5},{8,10},{10,8},{12,... | collective-permute-start | bytes 270344 | tf_op jit(solution)/shard_map/ppermute | solution.py:304
  (6 other events, 19.6 us)

commit v7 on v6

--- a/solution.py
+++ b/solution.py
@@ -172,28 +172,41 @@
         oT_ref[:, block(b)] = dot(vT, p)
 
     ahead(L // WB, lambda b: dot(k, qT_ref[:, block(b)]), attend)
-    goT = goT_ref[...]
-    wide = goT.astype(F32)
-    att = oT_ref[...].astype(BF).astype(F32)
-    xT = (att + cqT_ref[...].astype(F32)).astype(BF)
-    dp = dot(tv, goT)
-    cp = softmax_t(dot(tk, xT))
-    mix = dot(tvT, cp)
-    back_ref[right] = (att + mix).astype(BF)
-    delta = jnp.sum(wide * mix, axis=0, keepdims=True)
-    ds = (cp.astype(F32) * (dp - delta)).astype(BF)
-    dq = dot(tkT, ds) * SCALE
-    agT = (wide + dq).astype(BF)
-    agT_ref[...] = agT
-    dcq = dq.astype(BF)
-    dt_ref[...] = beside(dot_nt(ds, xT) * SCALE, dot_nt(cp, goT)).astype(BF)
+    dtk = dtv = None
     h = R // 2
+
+    def mingle(b, products):
+        nonlocal dtk, dtv
+        cols = block(b)
+        scores, xT, att, dp = products
+        goT = goT_ref[:, cols]
+        wide = goT.astype(F32)
+        cp = softmax_t(scores)
+        mix = dot(tvT, cp)
+        back_ref[right, cols] = (att + mix).astype(BF)
+        delta = jnp.sum(wide * mix, axis=0, keepdims=True)
+        ds = (cp.astype(F32) * (dp - delta)).astype(BF)
+        dq = dot(tkT, ds) * SCALE
+        agT_ref[:, cols] = (wide + dq).astype(BF)
+        dcq = dq.astype(BF)
+        x, y = dot_nt(ds, xT), dot_nt(cp, goT)
+        dtk, dtv = (x, y) if dtk is None else (dtk + x, dtv + y)
+        for i in range(WB // R):
+            at = i * R
+            halves = jnp.concatenate([dcq[:, at : at + h], dcq[:, at + h : at + R]], axis=0)
+            put(outs, b * (WB // R) + i, slice(2 * R, 2 * R + h), slice(None), halves.T)
+
+    def scores_of(b):
+        att = oT_ref[:, block(b)].astype(BF).astype(F32)
+        xT = (att + cqT_ref[:, block(b)].astype(F32)).astype(BF)
+        return dot(tk, xT), xT, att, dot(tv, goT_ref[:, block(b)])
+
+    ahead(L // WB, scores_of, mingle)
+    dt_ref[...] = beside(dtk * SCALE, dtv).astype(BF)
     for i in range(2 * C):
-        at = i * R
-        halves = jnp.concatenate([dcq[:, at : at + h], dcq[:, at + h : at + R]], axis=0)
-        put(outs, i, slice(2 * R, 2 * R + h), slice(None), halves.T)
         start = pl.multiple_of(meta_ref[3 + C + i] * MR, MR)
         put(outs, i, slice(2 * R + h, None), slice(None), dt_ref[pl.ds(start, MR), :])
+    agT = agT_ref[...]
     delta = jnp.sum(agT.astype(F32) * oT_ref[...], axis=0, keepdims=True)
 
     def back(b, dp):
@@ -349,8 +362,8 @@
             backs.append([to_chip(out[d + 1], d, -1) for d in range(1, C)])
     pieces_in = []
     for p in range(H - 1):
-        back = after(backs[p], outs[p + 1][0])
-        relayed = [to_sibling(outs[p][1])] + [to_sibling(g[1]) for g in back]
+        handed, *back = after([outs[p][1], *backs[p]], outs[p + 1][0])
+        relayed = [to_sibling(handed)] + [to_sibling(g[1]) for g in back]
         pieces_in += [outs[p][0], *back, *relayed]
     out = outs[-1]
     straight = [to_chip(out[2 * d], d, -1) for d in range(1, C)]

time: 54.1 us -> 53.8 us (level)
  waiting for transfers between devices: 8.61 us -> 5.8 us
  starting transfers between devices: 23.4 us -> 25.9 us
    ppermute x16, waiting for transfers between devices: 8.46 us -> 4.93 us  [to_chip(): return lax.ppermute(a, GROUP, pairs)]
    ppermute x8, starting transfers between devices: 2.69 us -> 4.15 us  [to_sibling(): return lax.ppermute(a, 'seq', [(i, i ^ 1) for i in range(S)])]
    ppermute x16, starting transfers between devices: 20.7 us -> 21.8 us  [to_chip(): return lax.ppermute(a, GROUP, pairs)]
    ppermute x8, waiting for transfers between devices: 0.15 us -> 0.87 us  [to_sibling(): return lax.ppermute(a, 'seq', [(i, i ^ 1) for i in range(S)])]
  transfers between devices with their start and end apart: 24 -> 24, of which waited for: 9 -> 8; matrix products, arithmetic and copies ran while one was open for 0% -> 0% of each run, Pallas kernels for 27% -> 27%
where the time goes in v7:
time: 53.8 us; the launch traced here: 53.5 us
  starting transfers between devices  25.9 us (48%)
  Pallas kernels  17.8 us (33%)
  waiting for transfers between devices  5.8 us (11%)
  local copies, waits for them, and re-layouts  2.29 us (4%)
  between operations  1.64 us (3%)
    ppermute x16, starting transfers between devices, to_chip(): return lax.ppermute(a, GROUP, pairs)  21.8 us
    pallas_call x6, Pallas kernels, call(): pl.pallas_call(kernel, out_shape=outs, in_specs=[SM if s else VM for s in...  15.6 us
    ppermute x16, waiting for transfers between devices, to_chip(): return lax.ppermute(a, GROUP, pairs)  4.93 us
    ppermute x8, starting transfers between devices, to_sibling(): return lax.ppermute(a, 'seq', [(i, i ^ 1) for i in range(S)])  4.15 us
    pallas_call x1, Pallas kernels, body(): pl.pallas_call(bind(unpack_kernel, C=C, H=H), out_shape=shapes, in_specs=...  2.2 us
    unnamed x12, local copies, waits for them, and re-layouts  2.18 us
  transfers between devices with their start and end apart: 24, of which 8 were waited for; matrix products, arithmetic and copies ran while one was open for 0% of the time, Pallas kernels for 27%

profile of v7, /device:TPU:0, one launch (start us, length us, event | category | flops | bytes accessed | tf_op | source)
XLA Modules:
  0.0 53.5 jit_solution(5635865757431154117)
XLA Ops:
  2.6 1.1 %copy-done.1 = bf16[1,128,3072]{2,1,0:T(8,128)(2,1)S(1)} copy-done((bf16[1,128,3072]{2,1,0:T(8,128)(2,1)S(1)}, bf16[1,128,3072]{2,1,0:T(8,128)(2,1)}, u32[]{:S(2)}) %copy-start.1) | copy-done | bytes 786456
  3.7 0.9 %copy-done.3 = bf16[1,128,1024]{2,1,0:T(8,128)(2,1)S(1)} copy-done((bf16[1,128,1024]{2,1,0:T(8,128)(2,1)S(1)}, bf16[1,128,1024]{2,1,0:T(8,128)(2,1)}, u32[]{:S(2)}) %copy-start.3) | copy-done | bytes 262168
  5.6 1.0 %pack_sib_0.1 = (bf16[896,128]{1,0:T(8,128)(2,1)S(1)}, bf16[896,128]{1,0:T(8,128)(2,1)S(1)}, bf16[896,128]{1,0:T(8,128)(2,1)S(1)}, bf16[896,128]{1,0:T(8,128)(2,1)S(1)}) custom-call(s32[15]{0:T(128)S(1)} %stack.67.meta_ref, bf16[4,256,128]{2,1,0:T(8,128)(2,1)S(1)} %pack_own_0.1.own_ref, bf16[128,1024]{1,0:T(8,128)(2,1)S(1)} %bitcast.44, ...), custom_call_target="tpu_custom_call" | custom-call | tf_op jit(solution)/shard_map/pack_sib_0/pallas_call | solution.py:28
  6.7 3.0 %collective-permute-start.4 = (bf16[896,128]{1,0:T(8,128)(2,1)S(1)}, bf16[896,128]{1,0:T(8,128)(2,1)S(1)}, u32[]{:S(2)}, u32[]{:S(2)}) collective-permute-start(bf16[896,128]{1,0:T(8,128)(2,1)S(1)} %get-tuple-element.42), channel_id=1, source_target_pairs={{0,4},{1,5},{2,6},{3,7},{4,0},{5,1},{6,2},{7,3},{8,12},{9,13},{10,... | collective-permute-start | bytes 688136 | tf_op jit(solution)/shard_map/ppermute | solution.py:326
  9.6 1.5 %collective-permute-start.5 = (bf16[896,128]{1,0:T(8,128)(2,1)S(1)}, bf16[896,128]{1,0:T(8,128)(2,1)S(1)}, u32[]{:S(2)}, u32[]{:S(2)}) collective-permute-start(bf16[896,128]{1,0:T(8,128)(2,1)S(1)} %get-tuple-element.43), channel_id=1, source_target_pairs={{0,1},{1,0},{2,3},{3,2},{4,5},{5,4},{6,7},{7,6},{8,9},{9,8},{10,11... | collective-permute-start | bytes 688136 | tf_op jit(solution)/shard_map/ppermute | solution.py:326
  11.2 0.7 %pack_own_1.1.own_ref = bf16[4,256,128]{2,1,0:T(8,128)(2,1)S(1)} custom-call(s32[15]{0:T(128)S(1)} %stack.67.meta_ref, bf16[128,3072]{1,0:T(8,128)(2,1)S(1)} %bitcast.39, bf16[128,1024]{1,0:T(8,128)(2,1)S(1)} %bitcast.42), custom_call_target="tpu_custom_call" | custom-call | tf_op jit(solution)/shard_map/pack_own_1/pallas_call | solution.py:28
  11.9 1.0 %pack_sib_1.1 = (bf16[896,128]{1,0:T(8,128)(2,1)S(1)}, bf16[896,128]{1,0:T(8,128)(2,1)S(1)}, bf16[896,128]{1,0:T(8,128)(2,1)S(1)}, bf16[896,128]{1,0:T(8,128)(2,1)S(1)}) custom-call(s32[15]{0:T(128)S(1)} %stack.67.meta_ref, bf16[4,256,128]{2,1,0:T(8,128)(2,1)S(1)} %pack_own_1.1.own_ref, bf16[128,1024]{1,0:T(8,128)(2,1)S(1)} %bitcast.45, ...), custom_call_target="tpu_custom_call" | custom-call | tf_op jit(solution)/shard_map/pack_sib_1/pallas_call | solution.py:28
  12.9 2.0 %collective-permute-start.10 = (bf16[896,128]{1,0:T(8,128)(2,1)S(1)}, bf16[896,128]{1,0:T(8,128)(2,1)S(1)}, u32[]{:S(2)}, u32[]{:S(2)}) collective-permute-start(bf16[896,128]{1,0:T(8,128)(2,1)S(1)} %get-tuple-element.48), channel_id=1, source_target_pairs={{0,4},{1,5},{2,6},{3,7},{4,0},{5,1},{6,2},{7,3},{8,12},{9,13},{10,... | collective-permute-start | bytes 688136 | tf_op jit(solution)/shard_map/ppermute | solution.py:326
  14.9 1.5 %collective-permute-start.11 = (bf16[896,128]{1,0:T(8,128)(2,1)S(1)}, bf16[896,128]{1,0:T(8,128)(2,1)S(1)}, u32[]{:S(2)}, u32[]{:S(2)}) collective-permute-start(bf16[896,128]{1,0:T(8,128)(2,1)S(1)} %get-tuple-element.49), channel_id=1, source_target_pairs={{0,1},{1,0},{2,3},{3,2},{4,5},{5,4},{6,7},{7,6},{8,9},{9,8},{10,11... | collective-permute-start | bytes 688136 | tf_op jit(solution)/shard_map/ppermute | solution.py:326
  16.5 2.6 %collective-permute-start.12 = (bf16[896,128]{1,0:T(8,128)(2,1)S(1)}, bf16[896,128]{1,0:T(8,128)(2,1)S(1)}, u32[]{:S(2)}, u32[]{:S(2)}) collective-permute-start(bf16[896,128]{1,0:T(8,128)(2,1)S(1)} %get-tuple-element.50), channel_id=1, source_target_pairs={{0,5},{1,4},{2,7},{3,6},{4,1},{5,0},{6,3},{7,2},{8,13},{9,12},{10,... | collective-permute-start | bytes 688136 | tf_op jit(solution)/shard_map/ppermute | solution.py:326
  19.1 3.5 %collective-permute-done.5.refs_2_ = bf16[896,128]{1,0:T(8,128)(2,1)S(1)} collective-permute-done((bf16[896,128]{1,0:T(8,128)(2,1)S(1)}, bf16[896,128]{1,0:T(8,128)(2,1)S(1)}, u32[]{:S(2)}, u32[]{:S(2)}) %collective-permute-start.5) | collective-permute-done | bytes 229408 | tf_op jit(solution)/shard_map/ppermute | solution.py:326
  22.6 6.0 %layer.2 = (bf16[352,128]{1,0:T(8,128)(2,1)S(1)}, bf16[352,128]{1,0:T(8,128)(2,1)S(1)}, bf16[2,352,128]{2,1,0:T(8,128)(2,1)S(1)}, bf16[2,352,128]{2,1,0:T(8,128)(2,1)S(1)}, bf16[2,352,128]{2,1,0:T(8,128)(2,1)S(1)}) custom-call(s32[15]{0:T(128)S(1)} %stack.67.meta_ref, bf16[896,128]{1,0:T(8,128)(2,1)S(1)} %get-tuple-element.41.refs_0_, ...), custom_call_target="tpu_custom_call" | custom-call | flops 4026531840 | bytes 5242880 | tf_op jit(solution)/shard_map/layer/pallas_call | solution.py:28
  28.6 1.5 %collective-permute-start.7 = (bf16[2,352,128]{2,1,0:T(8,128)(2,1)S(1)}, bf16[2,352,128]{2,1,0:T(8,128)(2,1)S(1)}, u32[]{:S(2)}, u32[]{:S(2)}) collective-permute-start(bf16[2,352,128]{2,1,0:T(8,128)(2,1)S(1)} %get-tuple-element.56), channel_id=1, source_target_pairs={{0,4},{1,5},{2,6},{3,7},{4,0},{5,1},{6,2},{7,3},{8,12},{9,13},{10,... | collective-permute-start | bytes 540680 | tf_op jit(solution)/shard_map/ppermute | solution.py:326
  30.8 1.4 %collective-permute-start.9 = (bf16[2,352,128]{2,1,0:T(8,128)(2,1)S(1)}, bf16[2,352,128]{2,1,0:T(8,128)(2,1)S(1)}, u32[]{:S(2)}, u32[]{:S(2)}) collective-permute-start(bf16[2,352,128]{2,1,0:T(8,128)(2,1)S(1)} %get-tuple-element.58), channel_id=1, source_target_pairs={{0,5},{1,4},{2,7},{3,6},{4,1},{5,0},{6,3},{7,2},{8,13},{9,12},{10,... | collective-permute-start | bytes 540680 | tf_op jit(solution)/shard_map/ppermute | solution.py:326
  32.4 6.2 %layer.3 = (bf16[352,128]{1,0:T(8,128)(2,1)S(1)}, bf16[352,128]{1,0:T(8,128)(2,1)S(1)}, bf16[352,128]{1,0:T(8,128)(2,1)S(1)}, bf16[352,128]{1,0:T(8,128)(2,1)S(1...) custom-call(s32[15]{0:T(128)S(1)} %stack.67.meta_ref, ...), custom_call_target="tpu_custom_call" | custom-call | flops 4026531840 | bytes 5242880 | tf_op jit(solution)/shard_map/layer/pallas_call | solution.py:28
  38.6 1.5 %collective-permute-start.17 = (bf16[352,128]{1,0:T(8,128)(2,1)S(1)}, bf16[352,128]{1,0:T(8,128)(2,1)S(1)}, u32[]{:S(2)}, u32[]{:S(2)}) collective-permute-start(bf16[352,128]{1,0:T(8,128)(2,1)S(1)} %get-tuple-element.67), channel_id=1, source_target_pairs={{0,4},{1,5},{2,6},{3,7},{4,0},{5,1},{6,2},{7,3},{8,12},{9,13},{10,... | collective-permute-start | bytes 270344 | tf_op jit(solution)/shard_map/ppermute | solution.py:326
  40.1 1.4 %collective-permute-start.18 = (bf16[352,128]{1,0:T(8,128)(2,1)S(1)}, bf16[352,128]{1,0:T(8,128)(2,1)S(1)}, u32[]{:S(2)}, u32[]{:S(2)}) collective-permute-start(bf16[352,128]{1,0:T(8,128)(2,1)S(1)} %get-tuple-element.68), channel_id=1, source_target_pairs={{0,1},{1,0},{2,3},{3,2},{4,5},{5,4},{6,7},{7,6},{8,9},{9,8},{10,11... | collective-permute-start | bytes 270344 | tf_op jit(solution)/shard_map/ppermute | solution.py:326
  41.5 1.4 %collective-permute-start.19 = (bf16[352,128]{1,0:T(8,128)(2,1)S(1)}, bf16[352,128]{1,0:T(8,128)(2,1)S(1)}, u32[]{:S(2)}, u32[]{:S(2)}) collective-permute-start(bf16[352,128]{1,0:T(8,128)(2,1)S(1)} %get-tuple-element.69), channel_id=1, source_target_pairs={{0,5},{1,4},{2,7},{3,6},{4,1},{5,0},{6,3},{7,2},{8,13},{9,12},{10,... | collective-permute-start | bytes 270344 | tf_op jit(solution)/shard_map/ppermute | solution.py:326
  42.9 0.8 %collective-permute-start.21 = (bf16[352,128]{1,0:T(8,128)(2,1)S(1)}, bf16[352,128]{1,0:T(8,128)(2,1)S(1)}, u32[]{:S(2)}, u32[]{:S(2)}) collective-permute-start(bf16[352,128]{1,0:T(8,128)(2,1)S(1)} %get-tuple-element.71), channel_id=1, source_target_pairs={{0,6},{1,7},{2,4},{3,5},{4,2},{5,3},{6,0},{7,1},{8,14},{9,15},{10,... | collective-permute-start | bytes 270344 | tf_op jit(solution)/shard_map/ppermute | solution.py:326
  43.9 1.2 %collective-permute-start.22 = (bf16[352,128]{1,0:T(8,128)(2,1)S(1)}, bf16[352,128]{1,0:T(8,128)(2,1)S(1)}, u32[]{:S(2)}, u32[]{:S(2)}) collective-permute-start(bf16[352,128]{1,0:T(8,128)(2,1)S(1)} %get-tuple-element.72), channel_id=1, source_target_pairs={{0,3},{1,2},{2,1},{3,0},{4,7},{5,6},{6,5},{7,4},{8,11},{9,10},{10,... | collective-permute-start | bytes 270344 | tf_op jit(solution)/shard_map/ppermute | solution.py:326
  45.1 1.2 %collective-permute-start.23 = (bf16[352,128]{1,0:T(8,128)(2,1)S(1)}, bf16[352,128]{1,0:T(8,128)(2,1)S(1)}, u32[]{:S(2)}, u32[]{:S(2)}) collective-permute-start(bf16[352,128]{1,0:T(8,128)(2,1)S(1)} %get-tuple-element.73), channel_id=1, source_target_pairs={{0,7},{1,6},{2,5},{3,4},{4,3},{5,2},{6,1},{7,0},{8,15},{9,14},{10,... | collective-permute-start | bytes 270344 | tf_op jit(solution)/shard_map/ppermute | solution.py:326
  48.3 1.8 %collective-permute-start.13 = (bf16[352,128]{1,0:T(8,128)(2,1)S(1)}, bf16[352,128]{1,0:T(8,128)(2,1)S(1)}, u32[]{:S(2)}, u32[]{:S(2)}) collective-permute-start(bf16[352,128]{1,0:T(8,128)(2,1)S(1)} %get-tuple-element.66), channel_id=1, source_target_pairs={{0,2},{2,0},{4,6},{6,4},{1,3},{3,1},{5,7},{7,5},{8,10},{10,8},{12,... | collective-permute-start | bytes 270344 | tf_op jit(solution)/shard_map/ppermute | solution.py:317
  50.4 0.7 %collective-permute-done.13.refs_4_ = bf16[352,128]{1,0:T(8,128)(2,1)S(1)} collective-permute-done((bf16[352,128]{1,0:T(8,128)(2,1)S(1)}, bf16[352,128]{1,0:T(8,128)(2,1)S(1)}, u32[]{:S(2)}, u32[]{:S(2)}) %collective-permute-start.13) | collective-permute-done | bytes 90144 | tf_op jit(solution)/shard_map/ppermute | solution.py:317
  51.1 2.2 %unpack.1 = (bf16[128,3072]{1,0:T(8,128)(2,1)}, bf16[128,1024]{1,0:T(8,128)(2,1)}, bf16[128,1024]{1,0:T(8,128)(2,1)}, bf16[32,2048]{1,0:T(8,128)(2,1)}) custom-call(s32[15]{0:T(128)S(1)} %stack.67.meta_ref, bf16[352,128]{1,0:T(8,128)(2,1)S(1)} %get-tuple-element.54.refs_0_, bf16[2,352,128]{2,1,0:T(8,128)(2,1)S(1)} %collective-permute-done.7.refs_1_, ...), custom_call_target="tpu_custom_call" | custom-call | tf_op jit(solution)/shard_map/unpack/pallas_call | solution.py:373
  (47 shorter events, 5.4 us)
Async XLA Ops:
  0.6 4.9 %collective-permute-start.3 = (bf16[256,2048]{1,0:T(8,128)(2,1)}, bf16[256,2048]{1,0:T(8,128)(2,1)S(1)}, u32[]{:S(2)}, u32[]{:S(2)}) collective-permute-start(bf16[256,2048]{1,0:T(8,128)(2,1)} %bitcast.34), channel_id=1, source_target_pairs={{0,2},{2,0},{4,6},{6,4},{1,3},{3,1},{5,7},{7,5},{8,10},{10,8},{12,... | collective-permute-start | bytes 3145736 | tf_op jit(solution)/shard_map/ppermute | solution.py:317
  1.2 4.4 %collective-permute-start = (bf16[128,3072]{1,0:T(8,128)(2,1)}, bf16[128,3072]{1,0:T(8,128)(2,1)S(1)}, u32[]{:S(2)}, u32[]{:S(2)}) collective-permute-start(bf16[128,3072]{1,0:T(8,128)(2,1)} %bitcast.37), channel_id=1, source_target_pairs={{0,2},{2,0},{4,6},{6,4},{1,3},{3,1},{5,7},{7,5},{8,10},{10,8},{12,... | collective-permute-start | bytes 2359304 | tf_op jit(solution)/shard_map/ppermute | solution.py:317
  1.2 4.2 %collective-permute-start.1 = (bf16[128,1024]{1,0:T(8,128)(2,1)}, bf16[128,1024]{1,0:T(8,128)(2,1)S(1)}, u32[]{:S(2)}, u32[]{:S(2)}) collective-permute-start(bf16[128,1024]{1,0:T(8,128)(2,1)} %bitcast.40), channel_id=1, source_target_pairs={{0,2},{2,0},{4,6},{6,4},{1,3},{3,1},{5,7},{7,5},{8,10},{10,8},{12,... | collective-permute-start | bytes 786440 | tf_op jit(solution)/shard_map/ppermute | solution.py:317
  1.7 3.9 %collective-permute-start.2 = (bf16[128,1024]{1,0:T(8,128)(2,1)}, bf16[128,1024]{1,0:T(8,128)(2,1)S(1)}, u32[]{:S(2)}, u32[]{:S(2)}) collective-permute-start(bf16[128,1024]{1,0:T(8,128)(2,1)} %bitcast.43), channel_id=1, source_target_pairs={{0,2},{2,0},{4,6},{6,4},{1,3},{3,1},{5,7},{7,5},{8,10},{10,8},{12,... | collective-permute-start | bytes 786440 | tf_op jit(solution)/shard_map/ppermute | solution.py:317
  6.7 9.8 %collective-permute-start.4 = (bf16[896,128]{1,0:T(8,128)(2,1)S(1)}, bf16[896,128]{1,0:T(8,128)(2,1)S(1)}, u32[]{:S(2)}, u32[]{:S(2)}) collective-permute-start(bf16[896,128]{1,0:T(8,128)(2,1)S(1)} %get-tuple-element.42), channel_id=1, source_target_pairs={{0,4},{1,5},{2,6},{3,7},{4,0},{5,1},{6,2},{7,3},{8,12},{9,13},{10,... | collective-permute-start | bytes 688136 | tf_op jit(solution)/shard_map/ppermute | solution.py:326
  9.6 12.9 %collective-permute-start.5 = (bf16[896,128]{1,0:T(8,128)(2,1)S(1)}, bf16[896,128]{1,0:T(8,128)(2,1)S(1)}, u32[]{:S(2)}, u32[]{:S(2)}) collective-permute-start(bf16[896,128]{1,0:T(8,128)(2,1)S(1)} %get-tuple-element.43), channel_id=1, source_target_pairs={{0,1},{1,0},{2,3},{3,2},{4,5},{5,4},{6,7},{7,6},{8,9},{9,8},{10,11... | collective-permute-start | bytes 688136 | tf_op jit(solution)/shard_map/ppermute | solution.py:326
  11.2 11.4 %collective-permute-start.6 = (bf16[896,128]{1,0:T(8,128)(2,1)S(1)}, bf16[896,128]{1,0:T(8,128)(2,1)S(1)}, u32[]{:S(2)}, u32[]{:S(2)}) collective-permute-start(bf16[896,128]{1,0:T(8,128)(2,1)S(1)} %get-tuple-element.44), channel_id=1, source_target_pairs={{0,5},{1,4},{2,7},{3,6},{4,1},{5,0},{6,3},{7,2},{8,13},{9,12},{10,... | collective-permute-start | bytes 688136 | tf_op jit(solution)/shard_map/ppermute | solution.py:326
  12.9 17.8 %collective-permute-start.10 = (bf16[896,128]{1,0:T(8,128)(2,1)S(1)}, bf16[896,128]{1,0:T(8,128)(2,1)S(1)}, u32[]{:S(2)}, u32[]{:S(2)}) collective-permute-start(bf16[896,128]{1,0:T(8,128)(2,1)S(1)} %get-tuple-element.48), channel_id=1, source_target_pairs={{0,4},{1,5},{2,6},{3,7},{4,0},{5,1},{6,2},{7,3},{8,12},{9,13},{10,... | collective-permute-start | bytes 688136 | tf_op jit(solution)/shard_map/ppermute | solution.py:326
  14.9 17.2 %collective-permute-start.11 = (bf16[896,128]{1,0:T(8,128)(2,1)S(1)}, bf16[896,128]{1,0:T(8,128)(2,1)S(1)}, u32[]{:S(2)}, u32[]{:S(2)}) collective-permute-start(bf16[896,128]{1,0:T(8,128)(2,1)S(1)} %get-tuple-element.49), channel_id=1, source_target_pairs={{0,1},{1,0},{2,3},{3,2},{4,5},{5,4},{6,7},{7,6},{8,9},{9,8},{10,11... | collective-permute-start | bytes 688136 | tf_op jit(solution)/shard_map/ppermute | solution.py:326
  16.5 15.9 %collective-permute-start.12 = (bf16[896,128]{1,0:T(8,128)(2,1)S(1)}, bf16[896,128]{1,0:T(8,128)(2,1)S(1)}, u32[]{:S(2)}, u32[]{:S(2)}) collective-permute-start(bf16[896,128]{1,0:T(8,128)(2,1)S(1)} %get-tuple-element.50), channel_id=1, source_target_pairs={{0,5},{1,4},{2,7},{3,6},{4,1},{5,0},{6,3},{7,2},{8,13},{9,12},{10,... | collective-permute-start | bytes 688136 | tf_op jit(solution)/shard_map/ppermute | solution.py:326
  28.6 12.9 %collective-permute-start.7 = (bf16[2,352,128]{2,1,0:T(8,128)(2,1)S(1)}, bf16[2,352,128]{2,1,0:T(8,128)(2,1)S(1)}, u32[]{:S(2)}, u32[]{:S(2)}) collective-permute-start(bf16[2,352,128]{2,1,0:T(8,128)(2,1)S(1)} %get-tuple-element.56), channel_id=1, source_target_pairs={{0,4},{1,5},{2,6},{3,7},{4,0},{5,1},{6,2},{7,3},{8,12},{9,13},{10,... | collective-permute-start | bytes 540680 | tf_op jit(solution)/shard_map/ppermute | solution.py:326
  30.1 12.8 %collective-permute-start.8 = (bf16[2,352,128]{2,1,0:T(8,128)(2,1)S(1)}, bf16[2,352,128]{2,1,0:T(8,128)(2,1)S(1)}, u32[]{:S(2)}, u32[]{:S(2)}) collective-permute-start(bf16[2,352,128]{2,1,0:T(8,128)(2,1)S(1)} %get-tuple-element.57), channel_id=1, source_target_pairs={{0,1},{1,0},{2,3},{3,2},{4,5},{5,4},{6,7},{7,6},{8,9},{9,8},{10,11... | collective-permute-start | bytes 540680 | tf_op jit(solution)/shard_map/ppermute | solution.py:326
  30.8 12.1 %collective-permute-start.9 = (bf16[2,352,128]{2,1,0:T(8,128)(2,1)S(1)}, bf16[2,352,128]{2,1,0:T(8,128)(2,1)S(1)}, u32[]{:S(2)}, u32[]{:S(2)}) collective-permute-start(bf16[2,352,128]{2,1,0:T(8,128)(2,1)S(1)} %get-tuple-element.58), channel_id=1, source_target_pairs={{0,5},{1,4},{2,7},{3,6},{4,1},{5,0},{6,3},{7,2},{8,13},{9,12},{10,... | collective-permute-start | bytes 540680 | tf_op jit(solution)/shard_map/ppermute | solution.py:326
  38.6 5.3 %collective-permute-start.17 = (bf16[352,128]{1,0:T(8,128)(2,1)S(1)}, bf16[352,128]{1,0:T(8,128)(2,1)S(1)}, u32[]{:S(2)}, u32[]{:S(2)}) collective-permute-start(bf16[352,128]{1,0:T(8,128)(2,1)S(1)} %get-tuple-element.67), channel_id=1, source_target_pairs={{0,4},{1,5},{2,6},{3,7},{4,0},{5,1},{6,2},{7,3},{8,12},{9,13},{10,... | collective-permute-start | bytes 270344 | tf_op jit(solution)/shard_map/ppermute | solution.py:326
  40.1 5.0 %collective-permute-start.18 = (bf16[352,128]{1,0:T(8,128)(2,1)S(1)}, bf16[352,128]{1,0:T(8,128)(2,1)S(1)}, u32[]{:S(2)}, u32[]{:S(2)}) collective-permute-start(bf16[352,128]{1,0:T(8,128)(2,1)S(1)} %get-tuple-element.68), channel_id=1, source_target_pairs={{0,1},{1,0},{2,3},{3,2},{4,5},{5,4},{6,7},{7,6},{8,9},{9,8},{10,11... | collective-permute-start | bytes 270344 | tf_op jit(solution)/shard_map/ppermute | solution.py:326
  41.5 5.4 %collective-permute-start.19 = (bf16[352,128]{1,0:T(8,128)(2,1)S(1)}, bf16[352,128]{1,0:T(8,128)(2,1)S(1)}, u32[]{:S(2)}, u32[]{:S(2)}) collective-permute-start(bf16[352,128]{1,0:T(8,128)(2,1)S(1)} %get-tuple-element.69), channel_id=1, source_target_pairs={{0,5},{1,4},{2,7},{3,6},{4,1},{5,0},{6,3},{7,2},{8,13},{9,12},{10,... | collective-permute-start | bytes 270344 | tf_op jit(solution)/shard_map/ppermute | solution.py:326
  42.9 4.7 %collective-permute-start.20 = (bf16[352,128]{1,0:T(8,128)(2,1)S(1)}, bf16[352,128]{1,0:T(8,128)(2,1)S(1)}, u32[]{:S(2)}, u32[]{:S(2)}) collective-permute-start(bf16[352,128]{1,0:T(8,128)(2,1)S(1)} %get-tuple-element.70), channel_id=1, source_target_pairs={{0,2},{1,3},{2,0},{3,1},{4,6},{5,7},{6,4},{7,5},{8,10},{9,11},{10,... | collective-permute-start | bytes 270344 | tf_op jit(solution)/shard_map/ppermute | solution.py:326
  42.9 4.7 %collective-permute-start.21 = (bf16[352,128]{1,0:T(8,128)(2,1)S(1)}, bf16[352,128]{1,0:T(8,128)(2,1)S(1)}, u32[]{:S(2)}, u32[]{:S(2)}) collective-permute-start(bf16[352,128]{1,0:T(8,128)(2,1)S(1)} %get-tuple-element.71), channel_id=1, source_target_pairs={{0,6},{1,7},{2,4},{3,5},{4,2},{5,3},{6,0},{7,1},{8,14},{9,15},{10,... | collective-permute-start | bytes 270344 | tf_op jit(solution)/shard_map/ppermute | solution.py:326
  43.9 4.4 %collective-permute-start.22 = (bf16[352,128]{1,0:T(8,128)(2,1)S(1)}, bf16[352,128]{1,0:T(8,128)(2,1)S(1)}, u32[]{:S(2)}, u32[]{:S(2)}) collective-permute-start(bf16[352,128]{1,0:T(8,128)(2,1)S(1)} %get-tuple-element.72), channel_id=1, source_target_pairs={{0,3},{1,2},{2,1},{3,0},{4,7},{5,6},{6,5},{7,4},{8,11},{9,10},{10,... | collective-permute-start | bytes 270344 | tf_op jit(solution)/shard_map/ppermute | solution.py:326
  45.1 5.2 %collective-permute-start.23 = (bf16[352,128]{1,0:T(8,128)(2,1)S(1)}, bf16[352,128]{1,0:T(8,128)(2,1)S(1)}, u32[]{:S(2)}, u32[]{:S(2)}) collective-permute-start(bf16[352,128]{1,0:T(8,128)(2,1)S(1)} %get-tuple-element.73), channel_id=1, source_target_pairs={{0,7},{1,6},{2,5},{3,4},{4,3},{5,2},{6,1},{7,0},{8,15},{9,14},{10,... | collective-permute-start | bytes 270344 | tf_op jit(solution)/shard_map/ppermute | solution.py:326
  46.9 3.5 %collective-permute-start.16 = (bf16[352,128]{1,0:T(8,128)(2,1)S(1)}, bf16[352,128]{1,0:T(8,128)(2,1)S(1)}, u32[]{:S(2)}, u32[]{:S(2)}) collective-permute-start(bf16[352,128]{1,0:T(8,128)(2,1)S(1)} %slice_bitcast_fusion), channel_id=1, source_target_pairs={{0,2},{2,0},{4,6},{6,4},{1,3},{3,1},{5,7},{7,5},{8,10},{10,8},{12,... | collective-permute-start | bytes 270344 | tf_op jit(solution)/shard_map/ppermute | solution.py:317
  47.5 2.9 %collective-permute-start.15 = (bf16[352,128]{1,0:T(8,128)(2,1)S(1)}, bf16[352,128]{1,0:T(8,128)(2,1)S(1)}, u32[]{:S(2)}, u32[]{:S(2)}) collective-permute-start(bf16[352,128]{1,0:T(8,128)(2,1)S(1)} %slice_bitcast_fusion.1), channel_id=1, source_target_pairs={{0,2},{2,0},{4,6},{6,4},{1,3},{3,1},{5,7},{7,5},{8,10},{10,8},{12,... | collective-permute-start | bytes 270344 | tf_op jit(solution)/shard_map/ppermute | solution.py:317
  47.6 2.8 %collective-permute-start.14 = (bf16[352,128]{1,0:T(8,128)(2,1)S(1)}, bf16[352,128]{1,0:T(8,128)(2,1)S(1)}, u32[]{:S(2)}, u32[]{:S(2)}) collective-permute-start(bf16[352,128]{1,0:T(8,128)(2,1)S(1)} %slice_bitcast_fusion.2), channel_id=1, source_target_pairs={{0,2},{2,0},{4,6},{6,4},{1,3},{3,1},{5,7},{7,5},{8,10},{10,8},{12,... | collective-permute-start | bytes 270344 | tf_op jit(solution)/shard_map/ppermute | solution.py:317
  48.3 2.8 %collective-permute-start.13 = (bf16[352,128]{1,0:T(8,128)(2,1)S(1)}, bf16[352,128]{1,0:T(8,128)(2,1)S(1)}, u32[]{:S(2)}, u32[]{:S(2)}) collective-permute-start(bf16[352,128]{1,0:T(8,128)(2,1)S(1)} %get-tuple-element.66), channel_id=1, source_target_pairs={{0,2},{2,0},{4,6},{6,4},{1,3},{3,1},{5,7},{7,5},{8,10},{10,8},{12,... | collective-permute-start | bytes 270344 | tf_op jit(solution)/shard_map/ppermute | solution.py:317
  (6 other events, 19.6 us)

commit v8 on v7

--- a/solution.py
+++ b/solution.py
@@ -94,9 +94,9 @@
         msg[2 * R : 3 * R] = own_ref[d, R:]
         msg[3 * R : 4 * R] = beside(cols(xs_ref, 2 * D), cols(cqs_ref, 0))
         msg[4 * R : 5 * R] = beside(cols(go_ref, 0), cols(gos_ref, 0))
-        own = beside(cols(t_ref, 0), cols(t_ref, D))
-        sib = beside(cols(ts_ref, 0), cols(ts_ref, D))
-        msg[5 * R :] = jnp.where(keep, own, sib)
+        tk = jnp.where(keep, cols(t_ref, 0), cols(ts_ref, 0))
+        tv = jnp.where(keep, cols(t_ref, D), cols(ts_ref, D))
+        msg[5 * R :] = beside(tk, tv)
 
 
 def pieces(refs):

time: 53.8 us -> 53.7 us (level)
  transfers between devices with their start and end apart: 24 -> 24, of which waited for: 8 -> 9; matrix products, arithmetic and copies ran while one was open for 0% -> 0% of each run, Pallas kernels for 27% -> 27%
where the time goes in v8:
time: 53.7 us; the launch traced here: 53.5 us
  starting transfers between devices  25.9 us (48%)
  Pallas kernels  17.8 us (33%)
  waiting for transfers between devices  5.81 us (11%)
  local copies, waits for them, and re-layouts  2.29 us (4%)
  between operations  1.64 us (3%)
    ppermute x16, starting transfers between devices, to_chip(): return lax.ppermute(a, GROUP, pairs)  21.8 us
    pallas_call x6, Pallas kernels, call(): pl.pallas_call(kernel, out_shape=outs, in_specs=[SM if s else VM for s in...  15.6 us
    ppermute x16, waiting for transfers between devices, to_chip(): return lax.ppermute(a, GROUP, pairs)  4.94 us
    ppermute x8, starting transfers between devices, to_sibling(): return lax.ppermute(a, 'seq', [(i, i ^ 1) for i in range(S)])  4.11 us
    pallas_call x1, Pallas kernels, body(): pl.pallas_call(bind(unpack_kernel, C=C, H=H), out_shape=shapes, in_specs=...  2.2 us
    unnamed x12, local copies, waits for them, and re-layouts  2.18 us
  transfers between devices with their start and end apart: 24, of which 9 were waited for; matrix products, arithmetic and copies ran while one was open for 0% of the time, Pallas kernels for 27%

profile of v8, /device:TPU:0, one launch (start us, length us, event | category | flops | bytes accessed | tf_op | source)
XLA Modules:
  0.0 53.5 jit_solution(2011650016410216338)
XLA Ops:
  2.6 1.1 %copy-done.1 = bf16[1,128,3072]{2,1,0:T(8,128)(2,1)S(1)} copy-done((bf16[1,128,3072]{2,1,0:T(8,128)(2,1)S(1)}, bf16[1,128,3072]{2,1,0:T(8,128)(2,1)}, u32[]{:S(2)}) %copy-start.1) | copy-done | bytes 786456
  3.7 0.9 %copy-done.3 = bf16[1,128,1024]{2,1,0:T(8,128)(2,1)S(1)} copy-done((bf16[1,128,1024]{2,1,0:T(8,128)(2,1)S(1)}, bf16[1,128,1024]{2,1,0:T(8,128)(2,1)}, u32[]{:S(2)}) %copy-start.3) | copy-done | bytes 262168
  5.6 1.0 %pack_sib_0.1 = (bf16[896,128]{1,0:T(8,128)(2,1)S(1)}, bf16[896,128]{1,0:T(8,128)(2,1)S(1)}, bf16[896,128]{1,0:T(8,128)(2,1)S(1)}, bf16[896,128]{1,0:T(8,128)(2,1)S(1)}) custom-call(s32[15]{0:T(128)S(1)} %stack.67.meta_ref, bf16[4,256,128]{2,1,0:T(8,128)(2,1)S(1)} %pack_own_0.1.own_ref, bf16[128,1024]{1,0:T(8,128)(2,1)S(1)} %bitcast.44, ...), custom_call_target="tpu_custom_call" | custom-call | tf_op jit(solution)/shard_map/pack_sib_0/pallas_call | solution.py:28
  6.7 3.0 %collective-permute-start.4 = (bf16[896,128]{1,0:T(8,128)(2,1)S(1)}, bf16[896,128]{1,0:T(8,128)(2,1)S(1)}, u32[]{:S(2)}, u32[]{:S(2)}) collective-permute-start(bf16[896,128]{1,0:T(8,128)(2,1)S(1)} %get-tuple-element.42), channel_id=1, source_target_pairs={{0,4},{1,5},{2,6},{3,7},{4,0},{5,1},{6,2},{7,3},{8,12},{9,13},{10,... | collective-permute-start | bytes 688136 | tf_op jit(solution)/shard_map/ppermute | solution.py:326
  9.6 1.5 %collective-permute-start.5 = (bf16[896,128]{1,0:T(8,128)(2,1)S(1)}, bf16[896,128]{1,0:T(8,128)(2,1)S(1)}, u32[]{:S(2)}, u32[]{:S(2)}) collective-permute-start(bf16[896,128]{1,0:T(8,128)(2,1)S(1)} %get-tuple-element.43), channel_id=1, source_target_pairs={{0,1},{1,0},{2,3},{3,2},{4,5},{5,4},{6,7},{7,6},{8,9},{9,8},{10,11... | collective-permute-start | bytes 688136 | tf_op jit(solution)/shard_map/ppermute | solution.py:326
  11.2 0.7 %pack_own_1.1.own_ref = bf16[4,256,128]{2,1,0:T(8,128)(2,1)S(1)} custom-call(s32[15]{0:T(128)S(1)} %stack.67.meta_ref, bf16[128,3072]{1,0:T(8,128)(2,1)S(1)} %bitcast.39, bf16[128,1024]{1,0:T(8,128)(2,1)S(1)} %bitcast.42), custom_call_target="tpu_custom_call" | custom-call | tf_op jit(solution)/shard_map/pack_own_1/pallas_call | solution.py:28
  11.9 1.0 %pack_sib_1.1 = (bf16[896,128]{1,0:T(8,128)(2,1)S(1)}, bf16[896,128]{1,0:T(8,128)(2,1)S(1)}, bf16[896,128]{1,0:T(8,128)(2,1)S(1)}, bf16[896,128]{1,0:T(8,128)(2,1)S(1)}) custom-call(s32[15]{0:T(128)S(1)} %stack.67.meta_ref, bf16[4,256,128]{2,1,0:T(8,128)(2,1)S(1)} %pack_own_1.1.own_ref, bf16[128,1024]{1,0:T(8,128)(2,1)S(1)} %bitcast.45, ...), custom_call_target="tpu_custom_call" | custom-call | tf_op jit(solution)/shard_map/pack_sib_1/pallas_call | solution.py:28
  12.9 2.0 %collective-permute-start.10 = (bf16[896,128]{1,0:T(8,128)(2,1)S(1)}, bf16[896,128]{1,0:T(8,128)(2,1)S(1)}, u32[]{:S(2)}, u32[]{:S(2)}) collective-permute-start(bf16[896,128]{1,0:T(8,128)(2,1)S(1)} %get-tuple-element.48), channel_id=1, source_target_pairs={{0,4},{1,5},{2,6},{3,7},{4,0},{5,1},{6,2},{7,3},{8,12},{9,13},{10,... | collective-permute-start | bytes 688136 | tf_op jit(solution)/shard_map/ppermute | solution.py:326
  14.9 1.5 %collective-permute-start.11 = (bf16[896,128]{1,0:T(8,128)(2,1)S(1)}, bf16[896,128]{1,0:T(8,128)(2,1)S(1)}, u32[]{:S(2)}, u32[]{:S(2)}) collective-permute-start(bf16[896,128]{1,0:T(8,128)(2,1)S(1)} %get-tuple-element.49), channel_id=1, source_target_pairs={{0,1},{1,0},{2,3},{3,2},{4,5},{5,4},{6,7},{7,6},{8,9},{9,8},{10,11... | collective-permute-start | bytes 688136 | tf_op jit(solution)/shard_map/ppermute | solution.py:326
  16.5 2.6 %collective-permute-start.12 = (bf16[896,128]{1,0:T(8,128)(2,1)S(1)}, bf16[896,128]{1,0:T(8,128)(2,1)S(1)}, u32[]{:S(2)}, u32[]{:S(2)}) collective-permute-start(bf16[896,128]{1,0:T(8,128)(2,1)S(1)} %get-tuple-element.50), channel_id=1, source_target_pairs={{0,5},{1,4},{2,7},{3,6},{4,1},{5,0},{6,3},{7,2},{8,13},{9,12},{10,... | collective-permute-start | bytes 688136 | tf_op jit(solution)/shard_map/ppermute | solution.py:326
  19.1 3.5 %collective-permute-done.5.refs_2_ = bf16[896,128]{1,0:T(8,128)(2,1)S(1)} collective-permute-done((bf16[896,128]{1,0:T(8,128)(2,1)S(1)}, bf16[896,128]{1,0:T(8,128)(2,1)S(1)}, u32[]{:S(2)}, u32[]{:S(2)}) %collective-permute-start.5) | collective-permute-done | bytes 229408 | tf_op jit(solution)/shard_map/ppermute | solution.py:326
  22.6 6.0 %layer.2 = (bf16[352,128]{1,0:T(8,128)(2,1)S(1)}, bf16[352,128]{1,0:T(8,128)(2,1)S(1)}, bf16[2,352,128]{2,1,0:T(8,128)(2,1)S(1)}, bf16[2,352,128]{2,1,0:T(8,128)(2,1)S(1)}, bf16[2,352,128]{2,1,0:T(8,128)(2,1)S(1)}) custom-call(s32[15]{0:T(128)S(1)} %stack.67.meta_ref, bf16[896,128]{1,0:T(8,128)(2,1)S(1)} %get-tuple-element.41.refs_0_, ...), custom_call_target="tpu_custom_call" | custom-call | flops 4026531840 | bytes 5242880 | tf_op jit(solution)/shard_map/layer/pallas_call | solution.py:28
  28.6 1.5 %collective-permute-start.7 = (bf16[2,352,128]{2,1,0:T(8,128)(2,1)S(1)}, bf16[2,352,128]{2,1,0:T(8,128)(2,1)S(1)}, u32[]{:S(2)}, u32[]{:S(2)}) collective-permute-start(bf16[2,352,128]{2,1,0:T(8,128)(2,1)S(1)} %get-tuple-element.56), channel_id=1, source_target_pairs={{0,4},{1,5},{2,6},{3,7},{4,0},{5,1},{6,2},{7,3},{8,12},{9,13},{10,... | collective-permute-start | bytes 540680 | tf_op jit(solution)/shard_map/ppermute | solution.py:326
  30.7 1.4 %collective-permute-start.9 = (bf16[2,352,128]{2,1,0:T(8,128)(2,1)S(1)}, bf16[2,352,128]{2,1,0:T(8,128)(2,1)S(1)}, u32[]{:S(2)}, u32[]{:S(2)}) collective-permute-start(bf16[2,352,128]{2,1,0:T(8,128)(2,1)S(1)} %get-tuple-element.58), channel_id=1, source_target_pairs={{0,5},{1,4},{2,7},{3,6},{4,1},{5,0},{6,3},{7,2},{8,13},{9,12},{10,... | collective-permute-start | bytes 540680 | tf_op jit(solution)/shard_map/ppermute | solution.py:326
  32.4 6.2 %layer.3 = (bf16[352,128]{1,0:T(8,128)(2,1)S(1)}, bf16[352,128]{1,0:T(8,128)(2,1)S(1)}, bf16[352,128]{1,0:T(8,128)(2,1)S(1)}, bf16[352,128]{1,0:T(8,128)(2,1)S(1...) custom-call(s32[15]{0:T(128)S(1)} %stack.67.meta_ref, ...), custom_call_target="tpu_custom_call" | custom-call | flops 4026531840 | bytes 5242880 | tf_op jit(solution)/shard_map/layer/pallas_call | solution.py:28
  38.6 1.5 %collective-permute-start.17 = (bf16[352,128]{1,0:T(8,128)(2,1)S(1)}, bf16[352,128]{1,0:T(8,128)(2,1)S(1)}, u32[]{:S(2)}, u32[]{:S(2)}) collective-permute-start(bf16[352,128]{1,0:T(8,128)(2,1)S(1)} %get-tuple-element.67), channel_id=1, source_target_pairs={{0,4},{1,5},{2,6},{3,7},{4,0},{5,1},{6,2},{7,3},{8,12},{9,13},{10,... | collective-permute-start | bytes 270344 | tf_op jit(solution)/shard_map/ppermute | solution.py:326
  40.1 1.3 %collective-permute-start.18 = (bf16[352,128]{1,0:T(8,128)(2,1)S(1)}, bf16[352,128]{1,0:T(8,128)(2,1)S(1)}, u32[]{:S(2)}, u32[]{:S(2)}) collective-permute-start(bf16[352,128]{1,0:T(8,128)(2,1)S(1)} %get-tuple-element.68), channel_id=1, source_target_pairs={{0,1},{1,0},{2,3},{3,2},{4,5},{5,4},{6,7},{7,6},{8,9},{9,8},{10,11... | collective-permute-start | bytes 270344 | tf_op jit(solution)/shard_map/ppermute | solution.py:326
  41.5 1.4 %collective-permute-start.19 = (bf16[352,128]{1,0:T(8,128)(2,1)S(1)}, bf16[352,128]{1,0:T(8,128)(2,1)S(1)}, u32[]{:S(2)}, u32[]{:S(2)}) collective-permute-start(bf16[352,128]{1,0:T(8,128)(2,1)S(1)} %get-tuple-element.69), channel_id=1, source_target_pairs={{0,5},{1,4},{2,7},{3,6},{4,1},{5,0},{6,3},{7,2},{8,13},{9,12},{10,... | collective-permute-start | bytes 270344 | tf_op jit(solution)/shard_map/ppermute | solution.py:326
  42.9 0.9 %collective-permute-start.21 = (bf16[352,128]{1,0:T(8,128)(2,1)S(1)}, bf16[352,128]{1,0:T(8,128)(2,1)S(1)}, u32[]{:S(2)}, u32[]{:S(2)}) collective-permute-start(bf16[352,128]{1,0:T(8,128)(2,1)S(1)} %get-tuple-element.71), channel_id=1, source_target_pairs={{0,6},{1,7},{2,4},{3,5},{4,2},{5,3},{6,0},{7,1},{8,14},{9,15},{10,... | collective-permute-start | bytes 270344 | tf_op jit(solution)/shard_map/ppermute | solution.py:326
  43.9 1.2 %collective-permute-start.22 = (bf16[352,128]{1,0:T(8,128)(2,1)S(1)}, bf16[352,128]{1,0:T(8,128)(2,1)S(1)}, u32[]{:S(2)}, u32[]{:S(2)}) collective-permute-start(bf16[352,128]{1,0:T(8,128)(2,1)S(1)} %get-tuple-element.72), channel_id=1, source_target_pairs={{0,3},{1,2},{2,1},{3,0},{4,7},{5,6},{6,5},{7,4},{8,11},{9,10},{10,... | collective-permute-start | bytes 270344 | tf_op jit(solution)/shard_map/ppermute | solution.py:326
  45.1 1.2 %collective-permute-start.23 = (bf16[352,128]{1,0:T(8,128)(2,1)S(1)}, bf16[352,128]{1,0:T(8,128)(2,1)S(1)}, u32[]{:S(2)}, u32[]{:S(2)}) collective-permute-start(bf16[352,128]{1,0:T(8,128)(2,1)S(1)} %get-tuple-element.73), channel_id=1, source_target_pairs={{0,7},{1,6},{2,5},{3,4},{4,3},{5,2},{6,1},{7,0},{8,15},{9,14},{10,... | collective-permute-start | bytes 270344 | tf_op jit(solution)/shard_map/ppermute | solution.py:326
  48.3 1.8 %collective-permute-start.13 = (bf16[352,128]{1,0:T(8,128)(2,1)S(1)}, bf16[352,128]{1,0:T(8,128)(2,1)S(1)}, u32[]{:S(2)}, u32[]{:S(2)}) collective-permute-start(bf16[352,128]{1,0:T(8,128)(2,1)S(1)} %get-tuple-element.66), channel_id=1, source_target_pairs={{0,2},{2,0},{4,6},{6,4},{1,3},{3,1},{5,7},{7,5},{8,10},{10,8},{12,... | collective-permute-start | bytes 270344 | tf_op jit(solution)/shard_map/ppermute | solution.py:317
  50.4 0.7 %collective-permute-done.13.refs_4_ = bf16[352,128]{1,0:T(8,128)(2,1)S(1)} collective-permute-done((bf16[352,128]{1,0:T(8,128)(2,1)S(1)}, bf16[352,128]{1,0:T(8,128)(2,1)S(1)}, u32[]{:S(2)}, u32[]{:S(2)}) %collective-permute-start.13) | collective-permute-done | bytes 90144 | tf_op jit(solution)/shard_map/ppermute | solution.py:317
  51.1 2.2 %unpack.1 = (bf16[128,3072]{1,0:T(8,128)(2,1)}, bf16[128,1024]{1,0:T(8,128)(2,1)}, bf16[128,1024]{1,0:T(8,128)(2,1)}, bf16[32,2048]{1,0:T(8,128)(2,1)}) custom-call(s32[15]{0:T(128)S(1)} %stack.67.meta_ref, bf16[352,128]{1,0:T(8,128)(2,1)S(1)} %get-tuple-element.54.refs_0_, bf16[2,352,128]{2,1,0:T(8,128)(2,1)S(1)} %collective-permute-done.7.refs_1_, ...), custom_call_target="tpu_custom_call" | custom-call | tf_op jit(solution)/shard_map/unpack/pallas_call | solution.py:373
  (47 shorter events, 5.4 us)
Async XLA Ops:
  0.6 4.9 %collective-permute-start.3 = (bf16[256,2048]{1,0:T(8,128)(2,1)}, bf16[256,2048]{1,0:T(8,128)(2,1)S(1)}, u32[]{:S(2)}, u32[]{:S(2)}) collective-permute-start(bf16[256,2048]{1,0:T(8,128)(2,1)} %bitcast.34), channel_id=1, source_target_pairs={{0,2},{2,0},{4,6},{6,4},{1,3},{3,1},{5,7},{7,5},{8,10},{10,8},{12,... | collective-permute-start | bytes 3145736 | tf_op jit(solution)/shard_map/ppermute | solution.py:317
  1.2 4.4 %collective-permute-start = (bf16[128,3072]{1,0:T(8,128)(2,1)}, bf16[128,3072]{1,0:T(8,128)(2,1)S(1)}, u32[]{:S(2)}, u32[]{:S(2)}) collective-permute-start(bf16[128,3072]{1,0:T(8,128)(2,1)} %bitcast.37), channel_id=1, source_target_pairs={{0,2},{2,0},{4,6},{6,4},{1,3},{3,1},{5,7},{7,5},{8,10},{10,8},{12,... | collective-permute-start | bytes 2359304 | tf_op jit(solution)/shard_map/ppermute | solution.py:317
  1.2 4.2 %collective-permute-start.1 = (bf16[128,1024]{1,0:T(8,128)(2,1)}, bf16[128,1024]{1,0:T(8,128)(2,1)S(1)}, u32[]{:S(2)}, u32[]{:S(2)}) collective-permute-start(bf16[128,1024]{1,0:T(8,128)(2,1)} %bitcast.40), channel_id=1, source_target_pairs={{0,2},{2,0},{4,6},{6,4},{1,3},{3,1},{5,7},{7,5},{8,10},{10,8},{12,... | collective-permute-start | bytes 786440 | tf_op jit(solution)/shard_map/ppermute | solution.py:317
  1.7 3.9 %collective-permute-start.2 = (bf16[128,1024]{1,0:T(8,128)(2,1)}, bf16[128,1024]{1,0:T(8,128)(2,1)S(1)}, u32[]{:S(2)}, u32[]{:S(2)}) collective-permute-start(bf16[128,1024]{1,0:T(8,128)(2,1)} %bitcast.43), channel_id=1, source_target_pairs={{0,2},{2,0},{4,6},{6,4},{1,3},{3,1},{5,7},{7,5},{8,10},{10,8},{12,... | collective-permute-start | bytes 786440 | tf_op jit(solution)/shard_map/ppermute | solution.py:317
  6.7 9.8 %collective-permute-start.4 = (bf16[896,128]{1,0:T(8,128)(2,1)S(1)}, bf16[896,128]{1,0:T(8,128)(2,1)S(1)}, u32[]{:S(2)}, u32[]{:S(2)}) collective-permute-start(bf16[896,128]{1,0:T(8,128)(2,1)S(1)} %get-tuple-element.42), channel_id=1, source_target_pairs={{0,4},{1,5},{2,6},{3,7},{4,0},{5,1},{6,2},{7,3},{8,12},{9,13},{10,... | collective-permute-start | bytes 688136 | tf_op jit(solution)/shard_map/ppermute | solution.py:326
  9.6 12.9 %collective-permute-start.5 = (bf16[896,128]{1,0:T(8,128)(2,1)S(1)}, bf16[896,128]{1,0:T(8,128)(2,1)S(1)}, u32[]{:S(2)}, u32[]{:S(2)}) collective-permute-start(bf16[896,128]{1,0:T(8,128)(2,1)S(1)} %get-tuple-element.43), channel_id=1, source_target_pairs={{0,1},{1,0},{2,3},{3,2},{4,5},{5,4},{6,7},{7,6},{8,9},{9,8},{10,11... | collective-permute-start | bytes 688136 | tf_op jit(solution)/shard_map/ppermute | solution.py:326
  11.2 11.4 %collective-permute-start.6 = (bf16[896,128]{1,0:T(8,128)(2,1)S(1)}, bf16[896,128]{1,0:T(8,128)(2,1)S(1)}, u32[]{:S(2)}, u32[]{:S(2)}) collective-permute-start(bf16[896,128]{1,0:T(8,128)(2,1)S(1)} %get-tuple-element.44), channel_id=1, source_target_pairs={{0,5},{1,4},{2,7},{3,6},{4,1},{5,0},{6,3},{7,2},{8,13},{9,12},{10,... | collective-permute-start | bytes 688136 | tf_op jit(solution)/shard_map/ppermute | solution.py:326
  12.9 17.8 %collective-permute-start.10 = (bf16[896,128]{1,0:T(8,128)(2,1)S(1)}, bf16[896,128]{1,0:T(8,128)(2,1)S(1)}, u32[]{:S(2)}, u32[]{:S(2)}) collective-permute-start(bf16[896,128]{1,0:T(8,128)(2,1)S(1)} %get-tuple-element.48), channel_id=1, source_target_pairs={{0,4},{1,5},{2,6},{3,7},{4,0},{5,1},{6,2},{7,3},{8,12},{9,13},{10,... | collective-permute-start | bytes 688136 | tf_op jit(solution)/shard_map/ppermute | solution.py:326
  14.9 17.2 %collective-permute-start.11 = (bf16[896,128]{1,0:T(8,128)(2,1)S(1)}, bf16[896,128]{1,0:T(8,128)(2,1)S(1)}, u32[]{:S(2)}, u32[]{:S(2)}) collective-permute-start(bf16[896,128]{1,0:T(8,128)(2,1)S(1)} %get-tuple-element.49), channel_id=1, source_target_pairs={{0,1},{1,0},{2,3},{3,2},{4,5},{5,4},{6,7},{7,6},{8,9},{9,8},{10,11... | collective-permute-start | bytes 688136 | tf_op jit(solution)/shard_map/ppermute | solution.py:326
  16.5 15.9 %collective-permute-start.12 = (bf16[896,128]{1,0:T(8,128)(2,1)S(1)}, bf16[896,128]{1,0:T(8,128)(2,1)S(1)}, u32[]{:S(2)}, u32[]{:S(2)}) collective-permute-start(bf16[896,128]{1,0:T(8,128)(2,1)S(1)} %get-tuple-element.50), channel_id=1, source_target_pairs={{0,5},{1,4},{2,7},{3,6},{4,1},{5,0},{6,3},{7,2},{8,13},{9,12},{10,... | collective-permute-start | bytes 688136 | tf_op jit(solution)/shard_map/ppermute | solution.py:326
  28.6 12.9 %collective-permute-start.7 = (bf16[2,352,128]{2,1,0:T(8,128)(2,1)S(1)}, bf16[2,352,128]{2,1,0:T(8,128)(2,1)S(1)}, u32[]{:S(2)}, u32[]{:S(2)}) collective-permute-start(bf16[2,352,128]{2,1,0:T(8,128)(2,1)S(1)} %get-tuple-element.56), channel_id=1, source_target_pairs={{0,4},{1,5},{2,6},{3,7},{4,0},{5,1},{6,2},{7,3},{8,12},{9,13},{10,... | collective-permute-start | bytes 540680 | tf_op jit(solution)/shard_map/ppermute | solution.py:326
  30.1 12.8 %collective-permute-start.8 = (bf16[2,352,128]{2,1,0:T(8,128)(2,1)S(1)}, bf16[2,352,128]{2,1,0:T(8,128)(2,1)S(1)}, u32[]{:S(2)}, u32[]{:S(2)}) collective-permute-start(bf16[2,352,128]{2,1,0:T(8,128)(2,1)S(1)} %get-tuple-element.57), channel_id=1, source_target_pairs={{0,1},{1,0},{2,3},{3,2},{4,5},{5,4},{6,7},{7,6},{8,9},{9,8},{10,11... | collective-permute-start | bytes 540680 | tf_op jit(solution)/shard_map/ppermute | solution.py:326
  30.7 12.1 %collective-permute-start.9 = (bf16[2,352,128]{2,1,0:T(8,128)(2,1)S(1)}, bf16[2,352,128]{2,1,0:T(8,128)(2,1)S(1)}, u32[]{:S(2)}, u32[]{:S(2)}) collective-permute-start(bf16[2,352,128]{2,1,0:T(8,128)(2,1)S(1)} %get-tuple-element.58), channel_id=1, source_target_pairs={{0,5},{1,4},{2,7},{3,6},{4,1},{5,0},{6,3},{7,2},{8,13},{9,12},{10,... | collective-permute-start | bytes 540680 | tf_op jit(solution)/shard_map/ppermute | solution.py:326
  38.6 5.3 %collective-permute-start.17 = (bf16[352,128]{1,0:T(8,128)(2,1)S(1)}, bf16[352,128]{1,0:T(8,128)(2,1)S(1)}, u32[]{:S(2)}, u32[]{:S(2)}) collective-permute-start(bf16[352,128]{1,0:T(8,128)(2,1)S(1)} %get-tuple-element.67), channel_id=1, source_target_pairs={{0,4},{1,5},{2,6},{3,7},{4,0},{5,1},{6,2},{7,3},{8,12},{9,13},{10,... | collective-permute-start | bytes 270344 | tf_op jit(solution)/shard_map/ppermute | solution.py:326
  40.1 5.0 %collective-permute-start.18 = (bf16[352,128]{1,0:T(8,128)(2,1)S(1)}, bf16[352,128]{1,0:T(8,128)(2,1)S(1)}, u32[]{:S(2)}, u32[]{:S(2)}) collective-permute-start(bf16[352,128]{1,0:T(8,128)(2,1)S(1)} %get-tuple-element.68), channel_id=1, source_target_pairs={{0,1},{1,0},{2,3},{3,2},{4,5},{5,4},{6,7},{7,6},{8,9},{9,8},{10,11... | collective-permute-start | bytes 270344 | tf_op jit(solution)/shard_map/ppermute | solution.py:326
  41.5 5.4 %collective-permute-start.19 = (bf16[352,128]{1,0:T(8,128)(2,1)S(1)}, bf16[352,128]{1,0:T(8,128)(2,1)S(1)}, u32[]{:S(2)}, u32[]{:S(2)}) collective-permute-start(bf16[352,128]{1,0:T(8,128)(2,1)S(1)} %get-tuple-element.69), channel_id=1, source_target_pairs={{0,5},{1,4},{2,7},{3,6},{4,1},{5,0},{6,3},{7,2},{8,13},{9,12},{10,... | collective-permute-start | bytes 270344 | tf_op jit(solution)/shard_map/ppermute | solution.py:326
  42.9 4.7 %collective-permute-start.20 = (bf16[352,128]{1,0:T(8,128)(2,1)S(1)}, bf16[352,128]{1,0:T(8,128)(2,1)S(1)}, u32[]{:S(2)}, u32[]{:S(2)}) collective-permute-start(bf16[352,128]{1,0:T(8,128)(2,1)S(1)} %get-tuple-element.70), channel_id=1, source_target_pairs={{0,2},{1,3},{2,0},{3,1},{4,6},{5,7},{6,4},{7,5},{8,10},{9,11},{10,... | collective-permute-start | bytes 270344 | tf_op jit(solution)/shard_map/ppermute | solution.py:326
  42.9 4.8 %collective-permute-start.21 = (bf16[352,128]{1,0:T(8,128)(2,1)S(1)}, bf16[352,128]{1,0:T(8,128)(2,1)S(1)}, u32[]{:S(2)}, u32[]{:S(2)}) collective-permute-start(bf16[352,128]{1,0:T(8,128)(2,1)S(1)} %get-tuple-element.71), channel_id=1, source_target_pairs={{0,6},{1,7},{2,4},{3,5},{4,2},{5,3},{6,0},{7,1},{8,14},{9,15},{10,... | collective-permute-start | bytes 270344 | tf_op jit(solution)/shard_map/ppermute | solution.py:326
  43.9 4.4 %collective-permute-start.22 = (bf16[352,128]{1,0:T(8,128)(2,1)S(1)}, bf16[352,128]{1,0:T(8,128)(2,1)S(1)}, u32[]{:S(2)}, u32[]{:S(2)}) collective-permute-start(bf16[352,128]{1,0:T(8,128)(2,1)S(1)} %get-tuple-element.72), channel_id=1, source_target_pairs={{0,3},{1,2},{2,1},{3,0},{4,7},{5,6},{6,5},{7,4},{8,11},{9,10},{10,... | collective-permute-start | bytes 270344 | tf_op jit(solution)/shard_map/ppermute | solution.py:326
  45.1 5.2 %collective-permute-start.23 = (bf16[352,128]{1,0:T(8,128)(2,1)S(1)}, bf16[352,128]{1,0:T(8,128)(2,1)S(1)}, u32[]{:S(2)}, u32[]{:S(2)}) collective-permute-start(bf16[352,128]{1,0:T(8,128)(2,1)S(1)} %get-tuple-element.73), channel_id=1, source_target_pairs={{0,7},{1,6},{2,5},{3,4},{4,3},{5,2},{6,1},{7,0},{8,15},{9,14},{10,... | collective-permute-start | bytes 270344 | tf_op jit(solution)/shard_map/ppermute | solution.py:326
  46.9 3.5 %collective-permute-start.16 = (bf16[352,128]{1,0:T(8,128)(2,1)S(1)}, bf16[352,128]{1,0:T(8,128)(2,1)S(1)}, u32[]{:S(2)}, u32[]{:S(2)}) collective-permute-start(bf16[352,128]{1,0:T(8,128)(2,1)S(1)} %slice_bitcast_fusion), channel_id=1, source_target_pairs={{0,2},{2,0},{4,6},{6,4},{1,3},{3,1},{5,7},{7,5},{8,10},{10,8},{12,... | collective-permute-start | bytes 270344 | tf_op jit(solution)/shard_map/ppermute | solution.py:317
  47.5 2.9 %collective-permute-start.15 = (bf16[352,128]{1,0:T(8,128)(2,1)S(1)}, bf16[352,128]{1,0:T(8,128)(2,1)S(1)}, u32[]{:S(2)}, u32[]{:S(2)}) collective-permute-start(bf16[352,128]{1,0:T(8,128)(2,1)S(1)} %slice_bitcast_fusion.1), channel_id=1, source_target_pairs={{0,2},{2,0},{4,6},{6,4},{1,3},{3,1},{5,7},{7,5},{8,10},{10,8},{12,... | collective-permute-start | bytes 270344 | tf_op jit(solution)/shard_map/ppermute | solution.py:317
  47.7 2.7 %collective-permute-start.14 = (bf16[352,128]{1,0:T(8,128)(2,1)S(1)}, bf16[352,128]{1,0:T(8,128)(2,1)S(1)}, u32[]{:S(2)}, u32[]{:S(2)}) collective-permute-start(bf16[352,128]{1,0:T(8,128)(2,1)S(1)} %slice_bitcast_fusion.2), channel_id=1, source_target_pairs={{0,2},{2,0},{4,6},{6,4},{1,3},{3,1},{5,7},{7,5},{8,10},{10,8},{12,... | collective-permute-start | bytes 270344 | tf_op jit(solution)/shard_map/ppermute | solution.py:317
  48.3 2.8 %collective-permute-start.13 = (bf16[352,128]{1,0:T(8,128)(2,1)S(1)}, bf16[352,128]{1,0:T(8,128)(2,1)S(1)}, u32[]{:S(2)}, u32[]{:S(2)}) collective-permute-start(bf16[352,128]{1,0:T(8,128)(2,1)S(1)} %get-tuple-element.66), channel_id=1, source_target_pairs={{0,2},{2,0},{4,6},{6,4},{1,3},{3,1},{5,7},{7,5},{8,10},{10,8},{12,... | collective-permute-start | bytes 270344 | tf_op jit(solution)/shard_map/ppermute | solution.py:317
  (6 other events, 19.6 us)

commit v9 on v7

--- a/solution.py
+++ b/solution.py
@@ -171,7 +171,6 @@
         pT_ref[:, block(b)] = p
         oT_ref[:, block(b)] = dot(vT, p)
 
-    ahead(L // WB, lambda b: dot(k, qT_ref[:, block(b)]), attend)
     dtk = dtv = None
     h = R // 2
 
@@ -201,23 +200,33 @@
         xT = (att + cqT_ref[:, block(b)].astype(F32)).astype(BF)
         return dot(tk, xT), xT, att, dot(tv, goT_ref[:, block(b)])
 
-    ahead(L // WB, scores_of, mingle)
+    def back(b, dp):
+        delta = jnp.sum(agT_ref[:, block(b)].astype(F32) * oT_ref[:, block(b)], axis=0, keepdims=True)
+        ds = (pT_ref[:, block(b)].astype(F32) * (dp - delta)).astype(BF)
+        ds_ref[:, block(b)] = ds
+        back_ref[left, block(b)] = (dot(kT, ds) * SCALE).astype(BF)
+        n = WB // R
+        for i in range(n * b, n * b + n):
+            put(outs, i, slice(0, R), slice(None), back_ref[:, i * R : (i + 1) * R].T)
+
+    stages = [
+        lambda b, _: dot(k, qT_ref[:, block(b)]),
+        attend,
+        lambda b, _: scores_of(b),
+        mingle,
+        lambda b, _: dot(v, agT_ref[:, block(b)]),
+        back,
+    ]
+    n = L // WB
+    values = [None] * n
+    for stage in range(len(stages)):
+        for b in range(n):
+            values[b] = stages[stage](b, values[b])
     dt_ref[...] = beside(dtk * SCALE, dtv).astype(BF)
     for i in range(2 * C):
         start = pl.multiple_of(meta_ref[3 + C + i] * MR, MR)
         put(outs, i, slice(2 * R + h, None), slice(None), dt_ref[pl.ds(start, MR), :])
     agT = agT_ref[...]
-    delta = jnp.sum(agT.astype(F32) * oT_ref[...], axis=0, keepdims=True)
-
-    def back(b, dp):
-        ds = (pT_ref[:, block(b)].astype(F32) * (dp - delta[:, block(b)])).astype(BF)
-        ds_ref[:, block(b)] = ds
-        back_ref[left, block(b)] = (dot(kT, ds) * SCALE).astype(BF)
-        n = WB // R
-        for i in range(n * b, n * b + n):
-            put(outs, i, slice(0, R), slice(None), back_ref[:, i * R : (i + 1) * R].T)
-
-    ahead(L // WB, lambda b: dot(v, agT_ref[:, block(b)]), back)
     dk = dot(ds_ref[...], qT_ref[...].T) * SCALE
     dv = dot(pT_ref[...], agT.T)
     both = beside(dk.astype(BF), dv.astype(BF))
@@ -270,7 +279,8 @@
         (dt_ref, D, lambda piece: piece(end, right)),
     ]
     copies = []
-    for n, (ref, base, read) in enumerate(parts):
+    for n in (5, 6, 4, 3, 2, 1, 0):
+        ref, base, read = parts[n]
         for d in range(C):
             at = base + meta_ref[1 + d] * 2 * W
             if H == 1:

time: 53.8 us -> 53.9 us (level)
  no operation moved by 1% of the time
where the time goes in v9:
time: 53.9 us; the launch traced here: 53.6 us
  starting transfers between devices  25.9 us (48%)
  Pallas kernels  17.9 us (33%)
  waiting for transfers between devices  5.8 us (11%)
  local copies, waits for them, and re-layouts  2.29 us (4%)
  between operations  1.64 us (3%)
    ppermute x16, starting transfers between devices, to_chip(): return lax.ppermute(a, GROUP, pairs)  21.8 us
    pallas_call x6, Pallas kernels, call(): pl.pallas_call(kernel, out_shape=outs, in_specs=[SM if s else VM for s in...  15.6 us
    ppermute x16, waiting for transfers between devices, to_chip(): return lax.ppermute(a, GROUP, pairs)  4.93 us
    ppermute x8, starting transfers between devices, to_sibling(): return lax.ppermute(a, 'seq', [(i, i ^ 1) for i in range(S)])  4.15 us
    pallas_call x1, Pallas kernels, body(): pl.pallas_call(bind(unpack_kernel, C=C, H=H), out_shape=shapes, in_specs=...  2.31 us
    unnamed x12, local copies, waits for them, and re-layouts  2.18 us
  transfers between devices with their start and end apart: 24, of which 8 were waited for; matrix products, arithmetic and copies ran while one was open for 0% of the time, Pallas kernels for 27%

profile of v9, /device:TPU:0, one launch (start us, length us, event | category | flops | bytes accessed | tf_op | source)
XLA Modules:
  0.0 53.6 jit_solution(7629533980653024192)
XLA Ops:
  2.6 1.1 %copy-done.1 = bf16[1,128,3072]{2,1,0:T(8,128)(2,1)S(1)} copy-done((bf16[1,128,3072]{2,1,0:T(8,128)(2,1)S(1)}, bf16[1,128,3072]{2,1,0:T(8,128)(2,1)}, u32[]{:S(2)}) %copy-start.1) | copy-done | bytes 786456
  3.7 0.9 %copy-done.3 = bf16[1,128,1024]{2,1,0:T(8,128)(2,1)S(1)} copy-done((bf16[1,128,1024]{2,1,0:T(8,128)(2,1)S(1)}, bf16[1,128,1024]{2,1,0:T(8,128)(2,1)}, u32[]{:S(2)}) %copy-start.3) | copy-done | bytes 262168
  5.6 1.0 %pack_sib_0.1 = (bf16[896,128]{1,0:T(8,128)(2,1)S(1)}, bf16[896,128]{1,0:T(8,128)(2,1)S(1)}, bf16[896,128]{1,0:T(8,128)(2,1)S(1)}, bf16[896,128]{1,0:T(8,128)(2,1)S(1)}) custom-call(s32[15]{0:T(128)S(1)} %stack.67.meta_ref, bf16[4,256,128]{2,1,0:T(8,128)(2,1)S(1)} %pack_own_0.1.own_ref, bf16[128,1024]{1,0:T(8,128)(2,1)S(1)} %bitcast.44, ...), custom_call_target="tpu_custom_call" | custom-call | tf_op jit(solution)/shard_map/pack_sib_0/pallas_call | solution.py:28
  6.7 3.0 %collective-permute-start.4 = (bf16[896,128]{1,0:T(8,128)(2,1)S(1)}, bf16[896,128]{1,0:T(8,128)(2,1)S(1)}, u32[]{:S(2)}, u32[]{:S(2)}) collective-permute-start(bf16[896,128]{1,0:T(8,128)(2,1)S(1)} %get-tuple-element.42), channel_id=1, source_target_pairs={{0,4},{1,5},{2,6},{3,7},{4,0},{5,1},{6,2},{7,3},{8,12},{9,13},{10,... | collective-permute-start | bytes 688136 | tf_op jit(solution)/shard_map/ppermute | solution.py:336
  9.6 1.5 %collective-permute-start.5 = (bf16[896,128]{1,0:T(8,128)(2,1)S(1)}, bf16[896,128]{1,0:T(8,128)(2,1)S(1)}, u32[]{:S(2)}, u32[]{:S(2)}) collective-permute-start(bf16[896,128]{1,0:T(8,128)(2,1)S(1)} %get-tuple-element.43), channel_id=1, source_target_pairs={{0,1},{1,0},{2,3},{3,2},{4,5},{5,4},{6,7},{7,6},{8,9},{9,8},{10,11... | collective-permute-start | bytes 688136 | tf_op jit(solution)/shard_map/ppermute | solution.py:336
  11.2 0.7 %pack_own_1.1.own_ref = bf16[4,256,128]{2,1,0:T(8,128)(2,1)S(1)} custom-call(s32[15]{0:T(128)S(1)} %stack.67.meta_ref, bf16[128,3072]{1,0:T(8,128)(2,1)S(1)} %bitcast.39, bf16[128,1024]{1,0:T(8,128)(2,1)S(1)} %bitcast.42), custom_call_target="tpu_custom_call" | custom-call | tf_op jit(solution)/shard_map/pack_own_1/pallas_call | solution.py:28
  11.9 1.0 %pack_sib_1.1 = (bf16[896,128]{1,0:T(8,128)(2,1)S(1)}, bf16[896,128]{1,0:T(8,128)(2,1)S(1)}, bf16[896,128]{1,0:T(8,128)(2,1)S(1)}, bf16[896,128]{1,0:T(8,128)(2,1)S(1)}) custom-call(s32[15]{0:T(128)S(1)} %stack.67.meta_ref, bf16[4,256,128]{2,1,0:T(8,128)(2,1)S(1)} %pack_own_1.1.own_ref, bf16[128,1024]{1,0:T(8,128)(2,1)S(1)} %bitcast.45, ...), custom_call_target="tpu_custom_call" | custom-call | tf_op jit(solution)/shard_map/pack_sib_1/pallas_call | solution.py:28
  12.9 2.0 %collective-permute-start.10 = (bf16[896,128]{1,0:T(8,128)(2,1)S(1)}, bf16[896,128]{1,0:T(8,128)(2,1)S(1)}, u32[]{:S(2)}, u32[]{:S(2)}) collective-permute-start(bf16[896,128]{1,0:T(8,128)(2,1)S(1)} %get-tuple-element.48), channel_id=1, source_target_pairs={{0,4},{1,5},{2,6},{3,7},{4,0},{5,1},{6,2},{7,3},{8,12},{9,13},{10,... | collective-permute-start | bytes 688136 | tf_op jit(solution)/shard_map/ppermute | solution.py:336
  14.9 1.5 %collective-permute-start.11 = (bf16[896,128]{1,0:T(8,128)(2,1)S(1)}, bf16[896,128]{1,0:T(8,128)(2,1)S(1)}, u32[]{:S(2)}, u32[]{:S(2)}) collective-permute-start(bf16[896,128]{1,0:T(8,128)(2,1)S(1)} %get-tuple-element.49), channel_id=1, source_target_pairs={{0,1},{1,0},{2,3},{3,2},{4,5},{5,4},{6,7},{7,6},{8,9},{9,8},{10,11... | collective-permute-start | bytes 688136 | tf_op jit(solution)/shard_map/ppermute | solution.py:336
  16.5 2.6 %collective-permute-start.12 = (bf16[896,128]{1,0:T(8,128)(2,1)S(1)}, bf16[896,128]{1,0:T(8,128)(2,1)S(1)}, u32[]{:S(2)}, u32[]{:S(2)}) collective-permute-start(bf16[896,128]{1,0:T(8,128)(2,1)S(1)} %get-tuple-element.50), channel_id=1, source_target_pairs={{0,5},{1,4},{2,7},{3,6},{4,1},{5,0},{6,3},{7,2},{8,13},{9,12},{10,... | collective-permute-start | bytes 688136 | tf_op jit(solution)/shard_map/ppermute | solution.py:336
  19.1 3.5 %collective-permute-done.5.refs_2_ = bf16[896,128]{1,0:T(8,128)(2,1)S(1)} collective-permute-done((bf16[896,128]{1,0:T(8,128)(2,1)S(1)}, bf16[896,128]{1,0:T(8,128)(2,1)S(1)}, u32[]{:S(2)}, u32[]{:S(2)}) %collective-permute-start.5) | collective-permute-done | bytes 229408 | tf_op jit(solution)/shard_map/ppermute | solution.py:336
  22.6 6.0 %layer.2 = (bf16[352,128]{1,0:T(8,128)(2,1)S(1)}, bf16[352,128]{1,0:T(8,128)(2,1)S(1)}, bf16[2,352,128]{2,1,0:T(8,128)(2,1)S(1)}, bf16[2,352,128]{2,1,0:T(8,128)(2,1)S(1)}, bf16[2,352,128]{2,1,0:T(8,128)(2,1)S(1)}) custom-call(s32[15]{0:T(128)S(1)} %stack.67.meta_ref, bf16[896,128]{1,0:T(8,128)(2,1)S(1)} %get-tuple-element.41.refs_0_, ...), custom_call_target="tpu_custom_call" | custom-call | flops 4026531840 | bytes 5242880 | tf_op jit(solution)/shard_map/layer/pallas_call | solution.py:28
  28.6 1.5 %collective-permute-start.7 = (bf16[2,352,128]{2,1,0:T(8,128)(2,1)S(1)}, bf16[2,352,128]{2,1,0:T(8,128)(2,1)S(1)}, u32[]{:S(2)}, u32[]{:S(2)}) collective-permute-start(bf16[2,352,128]{2,1,0:T(8,128)(2,1)S(1)} %get-tuple-element.56), channel_id=1, source_target_pairs={{0,4},{1,5},{2,6},{3,7},{4,0},{5,1},{6,2},{7,3},{8,12},{9,13},{10,... | collective-permute-start | bytes 540680 | tf_op jit(solution)/shard_map/ppermute | solution.py:336
  30.8 1.4 %collective-permute-start.9 = (bf16[2,352,128]{2,1,0:T(8,128)(2,1)S(1)}, bf16[2,352,128]{2,1,0:T(8,128)(2,1)S(1)}, u32[]{:S(2)}, u32[]{:S(2)}) collective-permute-start(bf16[2,352,128]{2,1,0:T(8,128)(2,1)S(1)} %get-tuple-element.58), channel_id=1, source_target_pairs={{0,5},{1,4},{2,7},{3,6},{4,1},{5,0},{6,3},{7,2},{8,13},{9,12},{10,... | collective-permute-start | bytes 540680 | tf_op jit(solution)/shard_map/ppermute | solution.py:336
  32.4 6.2 %layer.3 = (bf16[352,128]{1,0:T(8,128)(2,1)S(1)}, bf16[352,128]{1,0:T(8,128)(2,1)S(1)}, bf16[352,128]{1,0:T(8,128)(2,1)S(1)}, bf16[352,128]{1,0:T(8,128)(2,1)S(1...) custom-call(s32[15]{0:T(128)S(1)} %stack.67.meta_ref, ...), custom_call_target="tpu_custom_call" | custom-call | flops 4026531840 | bytes 5242880 | tf_op jit(solution)/shard_map/layer/pallas_call | solution.py:28
  38.6 1.5 %collective-permute-start.17 = (bf16[352,128]{1,0:T(8,128)(2,1)S(1)}, bf16[352,128]{1,0:T(8,128)(2,1)S(1)}, u32[]{:S(2)}, u32[]{:S(2)}) collective-permute-start(bf16[352,128]{1,0:T(8,128)(2,1)S(1)} %get-tuple-element.67), channel_id=1, source_target_pairs={{0,4},{1,5},{2,6},{3,7},{4,0},{5,1},{6,2},{7,3},{8,12},{9,13},{10,... | collective-permute-start | bytes 270344 | tf_op jit(solution)/shard_map/ppermute | solution.py:336
  40.1 1.4 %collective-permute-start.18 = (bf16[352,128]{1,0:T(8,128)(2,1)S(1)}, bf16[352,128]{1,0:T(8,128)(2,1)S(1)}, u32[]{:S(2)}, u32[]{:S(2)}) collective-permute-start(bf16[352,128]{1,0:T(8,128)(2,1)S(1)} %get-tuple-element.68), channel_id=1, source_target_pairs={{0,1},{1,0},{2,3},{3,2},{4,5},{5,4},{6,7},{7,6},{8,9},{9,8},{10,11... | collective-permute-start | bytes 270344 | tf_op jit(solution)/shard_map/ppermute | solution.py:336
  41.5 1.4 %collective-permute-start.19 = (bf16[352,128]{1,0:T(8,128)(2,1)S(1)}, bf16[352,128]{1,0:T(8,128)(2,1)S(1)}, u32[]{:S(2)}, u32[]{:S(2)}) collective-permute-start(bf16[352,128]{1,0:T(8,128)(2,1)S(1)} %get-tuple-element.69), channel_id=1, source_target_pairs={{0,5},{1,4},{2,7},{3,6},{4,1},{5,0},{6,3},{7,2},{8,13},{9,12},{10,... | collective-permute-start | bytes 270344 | tf_op jit(solution)/shard_map/ppermute | solution.py:336
  42.9 0.8 %collective-permute-start.21 = (bf16[352,128]{1,0:T(8,128)(2,1)S(1)}, bf16[352,128]{1,0:T(8,128)(2,1)S(1)}, u32[]{:S(2)}, u32[]{:S(2)}) collective-permute-start(bf16[352,128]{1,0:T(8,128)(2,1)S(1)} %get-tuple-element.71), channel_id=1, source_target_pairs={{0,6},{1,7},{2,4},{3,5},{4,2},{5,3},{6,0},{7,1},{8,14},{9,15},{10,... | collective-permute-start | bytes 270344 | tf_op jit(solution)/shard_map/ppermute | solution.py:336
  43.9 1.2 %collective-permute-start.22 = (bf16[352,128]{1,0:T(8,128)(2,1)S(1)}, bf16[352,128]{1,0:T(8,128)(2,1)S(1)}, u32[]{:S(2)}, u32[]{:S(2)}) collective-permute-start(bf16[352,128]{1,0:T(8,128)(2,1)S(1)} %get-tuple-element.72), channel_id=1, source_target_pairs={{0,3},{1,2},{2,1},{3,0},{4,7},{5,6},{6,5},{7,4},{8,11},{9,10},{10,... | collective-permute-start | bytes 270344 | tf_op jit(solution)/shard_map/ppermute | solution.py:336
  45.1 1.2 %collective-permute-start.23 = (bf16[352,128]{1,0:T(8,128)(2,1)S(1)}, bf16[352,128]{1,0:T(8,128)(2,1)S(1)}, u32[]{:S(2)}, u32[]{:S(2)}) collective-permute-start(bf16[352,128]{1,0:T(8,128)(2,1)S(1)} %get-tuple-element.73), channel_id=1, source_target_pairs={{0,7},{1,6},{2,5},{3,4},{4,3},{5,2},{6,1},{7,0},{8,15},{9,14},{10,... | collective-permute-start | bytes 270344 | tf_op jit(solution)/shard_map/ppermute | solution.py:336
  48.3 1.8 %collective-permute-start.13 = (bf16[352,128]{1,0:T(8,128)(2,1)S(1)}, bf16[352,128]{1,0:T(8,128)(2,1)S(1)}, u32[]{:S(2)}, u32[]{:S(2)}) collective-permute-start(bf16[352,128]{1,0:T(8,128)(2,1)S(1)} %get-tuple-element.66), channel_id=1, source_target_pairs={{0,2},{2,0},{4,6},{6,4},{1,3},{3,1},{5,7},{7,5},{8,10},{10,8},{12,... | collective-permute-start | bytes 270344 | tf_op jit(solution)/shard_map/ppermute | solution.py:327
  50.4 0.7 %collective-permute-done.13.refs_4_ = bf16[352,128]{1,0:T(8,128)(2,1)S(1)} collective-permute-done((bf16[352,128]{1,0:T(8,128)(2,1)S(1)}, bf16[352,128]{1,0:T(8,128)(2,1)S(1)}, u32[]{:S(2)}, u32[]{:S(2)}) %collective-permute-start.13) | collective-permute-done | bytes 90144 | tf_op jit(solution)/shard_map/ppermute | solution.py:327
  51.1 2.3 %unpack.1 = (bf16[128,3072]{1,0:T(8,128)(2,1)}, bf16[128,1024]{1,0:T(8,128)(2,1)}, bf16[128,1024]{1,0:T(8,128)(2,1)}, bf16[32,2048]{1,0:T(8,128)(2,1)}) custom-call(s32[15]{0:T(128)S(1)} %stack.67.meta_ref, bf16[352,128]{1,0:T(8,128)(2,1)S(1)} %get-tuple-element.54.refs_0_, bf16[2,352,128]{2,1,0:T(8,128)(2,1)S(1)} %collective-permute-done.7.refs_1_, ...), custom_call_target="tpu_custom_call" | custom-call | tf_op jit(solution)/shard_map/unpack/pallas_call | solution.py:383
  (47 shorter events, 5.4 us)
Async XLA Ops:
  0.6 4.9 %collective-permute-start.3 = (bf16[256,2048]{1,0:T(8,128)(2,1)}, bf16[256,2048]{1,0:T(8,128)(2,1)S(1)}, u32[]{:S(2)}, u32[]{:S(2)}) collective-permute-start(bf16[256,2048]{1,0:T(8,128)(2,1)} %bitcast.34), channel_id=1, source_target_pairs={{0,2},{2,0},{4,6},{6,4},{1,3},{3,1},{5,7},{7,5},{8,10},{10,8},{12,... | collective-permute-start | bytes 3145736 | tf_op jit(solution)/shard_map/ppermute | solution.py:327
  1.2 4.4 %collective-permute-start = (bf16[128,3072]{1,0:T(8,128)(2,1)}, bf16[128,3072]{1,0:T(8,128)(2,1)S(1)}, u32[]{:S(2)}, u32[]{:S(2)}) collective-permute-start(bf16[128,3072]{1,0:T(8,128)(2,1)} %bitcast.37), channel_id=1, source_target_pairs={{0,2},{2,0},{4,6},{6,4},{1,3},{3,1},{5,7},{7,5},{8,10},{10,8},{12,... | collective-permute-start | bytes 2359304 | tf_op jit(solution)/shard_map/ppermute | solution.py:327
  1.2 4.2 %collective-permute-start.1 = (bf16[128,1024]{1,0:T(8,128)(2,1)}, bf16[128,1024]{1,0:T(8,128)(2,1)S(1)}, u32[]{:S(2)}, u32[]{:S(2)}) collective-permute-start(bf16[128,1024]{1,0:T(8,128)(2,1)} %bitcast.40), channel_id=1, source_target_pairs={{0,2},{2,0},{4,6},{6,4},{1,3},{3,1},{5,7},{7,5},{8,10},{10,8},{12,... | collective-permute-start | bytes 786440 | tf_op jit(solution)/shard_map/ppermute | solution.py:327
  1.7 3.9 %collective-permute-start.2 = (bf16[128,1024]{1,0:T(8,128)(2,1)}, bf16[128,1024]{1,0:T(8,128)(2,1)S(1)}, u32[]{:S(2)}, u32[]{:S(2)}) collective-permute-start(bf16[128,1024]{1,0:T(8,128)(2,1)} %bitcast.43), channel_id=1, source_target_pairs={{0,2},{2,0},{4,6},{6,4},{1,3},{3,1},{5,7},{7,5},{8,10},{10,8},{12,... | collective-permute-start | bytes 786440 | tf_op jit(solution)/shard_map/ppermute | solution.py:327
  6.7 9.8 %collective-permute-start.4 = (bf16[896,128]{1,0:T(8,128)(2,1)S(1)}, bf16[896,128]{1,0:T(8,128)(2,1)S(1)}, u32[]{:S(2)}, u32[]{:S(2)}) collective-permute-start(bf16[896,128]{1,0:T(8,128)(2,1)S(1)} %get-tuple-element.42), channel_id=1, source_target_pairs={{0,4},{1,5},{2,6},{3,7},{4,0},{5,1},{6,2},{7,3},{8,12},{9,13},{10,... | collective-permute-start | bytes 688136 | tf_op jit(solution)/shard_map/ppermute | solution.py:336
  9.6 12.9 %collective-permute-start.5 = (bf16[896,128]{1,0:T(8,128)(2,1)S(1)}, bf16[896,128]{1,0:T(8,128)(2,1)S(1)}, u32[]{:S(2)}, u32[]{:S(2)}) collective-permute-start(bf16[896,128]{1,0:T(8,128)(2,1)S(1)} %get-tuple-element.43), channel_id=1, source_target_pairs={{0,1},{1,0},{2,3},{3,2},{4,5},{5,4},{6,7},{7,6},{8,9},{9,8},{10,11... | collective-permute-start | bytes 688136 | tf_op jit(solution)/shard_map/ppermute | solution.py:336
  11.2 11.4 %collective-permute-start.6 = (bf16[896,128]{1,0:T(8,128)(2,1)S(1)}, bf16[896,128]{1,0:T(8,128)(2,1)S(1)}, u32[]{:S(2)}, u32[]{:S(2)}) collective-permute-start(bf16[896,128]{1,0:T(8,128)(2,1)S(1)} %get-tuple-element.44), channel_id=1, source_target_pairs={{0,5},{1,4},{2,7},{3,6},{4,1},{5,0},{6,3},{7,2},{8,13},{9,12},{10,... | collective-permute-start | bytes 688136 | tf_op jit(solution)/shard_map/ppermute | solution.py:336
  12.9 17.8 %collective-permute-start.10 = (bf16[896,128]{1,0:T(8,128)(2,1)S(1)}, bf16[896,128]{1,0:T(8,128)(2,1)S(1)}, u32[]{:S(2)}, u32[]{:S(2)}) collective-permute-start(bf16[896,128]{1,0:T(8,128)(2,1)S(1)} %get-tuple-element.48), channel_id=1, source_target_pairs={{0,4},{1,5},{2,6},{3,7},{4,0},{5,1},{6,2},{7,3},{8,12},{9,13},{10,... | collective-permute-start | bytes 688136 | tf_op jit(solution)/shard_map/ppermute | solution.py:336
  14.9 17.2 %collective-permute-start.11 = (bf16[896,128]{1,0:T(8,128)(2,1)S(1)}, bf16[896,128]{1,0:T(8,128)(2,1)S(1)}, u32[]{:S(2)}, u32[]{:S(2)}) collective-permute-start(bf16[896,128]{1,0:T(8,128)(2,1)S(1)} %get-tuple-element.49), channel_id=1, source_target_pairs={{0,1},{1,0},{2,3},{3,2},{4,5},{5,4},{6,7},{7,6},{8,9},{9,8},{10,11... | collective-permute-start | bytes 688136 | tf_op jit(solution)/shard_map/ppermute | solution.py:336
  16.5 15.9 %collective-permute-start.12 = (bf16[896,128]{1,0:T(8,128)(2,1)S(1)}, bf16[896,128]{1,0:T(8,128)(2,1)S(1)}, u32[]{:S(2)}, u32[]{:S(2)}) collective-permute-start(bf16[896,128]{1,0:T(8,128)(2,1)S(1)} %get-tuple-element.50), channel_id=1, source_target_pairs={{0,5},{1,4},{2,7},{3,6},{4,1},{5,0},{6,3},{7,2},{8,13},{9,12},{10,... | collective-permute-start | bytes 688136 | tf_op jit(solution)/shard_map/ppermute | solution.py:336
  28.6 12.9 %collective-permute-start.7 = (bf16[2,352,128]{2,1,0:T(8,128)(2,1)S(1)}, bf16[2,352,128]{2,1,0:T(8,128)(2,1)S(1)}, u32[]{:S(2)}, u32[]{:S(2)}) collective-permute-start(bf16[2,352,128]{2,1,0:T(8,128)(2,1)S(1)} %get-tuple-element.56), channel_id=1, source_target_pairs={{0,4},{1,5},{2,6},{3,7},{4,0},{5,1},{6,2},{7,3},{8,12},{9,13},{10,... | collective-permute-start | bytes 540680 | tf_op jit(solution)/shard_map/ppermute | solution.py:336
  30.1 12.8 %collective-permute-start.8 = (bf16[2,352,128]{2,1,0:T(8,128)(2,1)S(1)}, bf16[2,352,128]{2,1,0:T(8,128)(2,1)S(1)}, u32[]{:S(2)}, u32[]{:S(2)}) collective-permute-start(bf16[2,352,128]{2,1,0:T(8,128)(2,1)S(1)} %get-tuple-element.57), channel_id=1, source_target_pairs={{0,1},{1,0},{2,3},{3,2},{4,5},{5,4},{6,7},{7,6},{8,9},{9,8},{10,11... | collective-permute-start | bytes 540680 | tf_op jit(solution)/shard_map/ppermute | solution.py:336
  30.8 12.1 %collective-permute-start.9 = (bf16[2,352,128]{2,1,0:T(8,128)(2,1)S(1)}, bf16[2,352,128]{2,1,0:T(8,128)(2,1)S(1)}, u32[]{:S(2)}, u32[]{:S(2)}) collective-permute-start(bf16[2,352,128]{2,1,0:T(8,128)(2,1)S(1)} %get-tuple-element.58), channel_id=1, source_target_pairs={{0,5},{1,4},{2,7},{3,6},{4,1},{5,0},{6,3},{7,2},{8,13},{9,12},{10,... | collective-permute-start | bytes 540680 | tf_op jit(solution)/shard_map/ppermute | solution.py:336
  38.6 5.3 %collective-permute-start.17 = (bf16[352,128]{1,0:T(8,128)(2,1)S(1)}, bf16[352,128]{1,0:T(8,128)(2,1)S(1)}, u32[]{:S(2)}, u32[]{:S(2)}) collective-permute-start(bf16[352,128]{1,0:T(8,128)(2,1)S(1)} %get-tuple-element.67), channel_id=1, source_target_pairs={{0,4},{1,5},{2,6},{3,7},{4,0},{5,1},{6,2},{7,3},{8,12},{9,13},{10,... | collective-permute-start | bytes 270344 | tf_op jit(solution)/shard_map/ppermute | solution.py:336
  40.1 5.0 %collective-permute-start.18 = (bf16[352,128]{1,0:T(8,128)(2,1)S(1)}, bf16[352,128]{1,0:T(8,128)(2,1)S(1)}, u32[]{:S(2)}, u32[]{:S(2)}) collective-permute-start(bf16[352,128]{1,0:T(8,128)(2,1)S(1)} %get-tuple-element.68), channel_id=1, source_target_pairs={{0,1},{1,0},{2,3},{3,2},{4,5},{5,4},{6,7},{7,6},{8,9},{9,8},{10,11... | collective-permute-start | bytes 270344 | tf_op jit(solution)/shard_map/ppermute | solution.py:336
  41.5 5.4 %collective-permute-start.19 = (bf16[352,128]{1,0:T(8,128)(2,1)S(1)}, bf16[352,128]{1,0:T(8,128)(2,1)S(1)}, u32[]{:S(2)}, u32[]{:S(2)}) collective-permute-start(bf16[352,128]{1,0:T(8,128)(2,1)S(1)} %get-tuple-element.69), channel_id=1, source_target_pairs={{0,5},{1,4},{2,7},{3,6},{4,1},{5,0},{6,3},{7,2},{8,13},{9,12},{10,... | collective-permute-start | bytes 270344 | tf_op jit(solution)/shard_map/ppermute | solution.py:336
  42.9 4.7 %collective-permute-start.20 = (bf16[352,128]{1,0:T(8,128)(2,1)S(1)}, bf16[352,128]{1,0:T(8,128)(2,1)S(1)}, u32[]{:S(2)}, u32[]{:S(2)}) collective-permute-start(bf16[352,128]{1,0:T(8,128)(2,1)S(1)} %get-tuple-element.70), channel_id=1, source_target_pairs={{0,2},{1,3},{2,0},{3,1},{4,6},{5,7},{6,4},{7,5},{8,10},{9,11},{10,... | collective-permute-start | bytes 270344 | tf_op jit(solution)/shard_map/ppermute | solution.py:336
  42.9 4.7 %collective-permute-start.21 = (bf16[352,128]{1,0:T(8,128)(2,1)S(1)}, bf16[352,128]{1,0:T(8,128)(2,1)S(1)}, u32[]{:S(2)}, u32[]{:S(2)}) collective-permute-start(bf16[352,128]{1,0:T(8,128)(2,1)S(1)} %get-tuple-element.71), channel_id=1, source_target_pairs={{0,6},{1,7},{2,4},{3,5},{4,2},{5,3},{6,0},{7,1},{8,14},{9,15},{10,... | collective-permute-start | bytes 270344 | tf_op jit(solution)/shard_map/ppermute | solution.py:336
  43.9 4.4 %collective-permute-start.22 = (bf16[352,128]{1,0:T(8,128)(2,1)S(1)}, bf16[352,128]{1,0:T(8,128)(2,1)S(1)}, u32[]{:S(2)}, u32[]{:S(2)}) collective-permute-start(bf16[352,128]{1,0:T(8,128)(2,1)S(1)} %get-tuple-element.72), channel_id=1, source_target_pairs={{0,3},{1,2},{2,1},{3,0},{4,7},{5,6},{6,5},{7,4},{8,11},{9,10},{10,... | collective-permute-start | bytes 270344 | tf_op jit(solution)/shard_map/ppermute | solution.py:336
  45.1 5.2 %collective-permute-start.23 = (bf16[352,128]{1,0:T(8,128)(2,1)S(1)}, bf16[352,128]{1,0:T(8,128)(2,1)S(1)}, u32[]{:S(2)}, u32[]{:S(2)}) collective-permute-start(bf16[352,128]{1,0:T(8,128)(2,1)S(1)} %get-tuple-element.73), channel_id=1, source_target_pairs={{0,7},{1,6},{2,5},{3,4},{4,3},{5,2},{6,1},{7,0},{8,15},{9,14},{10,... | collective-permute-start | bytes 270344 | tf_op jit(solution)/shard_map/ppermute | solution.py:336
  46.9 3.5 %collective-permute-start.16 = (bf16[352,128]{1,0:T(8,128)(2,1)S(1)}, bf16[352,128]{1,0:T(8,128)(2,1)S(1)}, u32[]{:S(2)}, u32[]{:S(2)}) collective-permute-start(bf16[352,128]{1,0:T(8,128)(2,1)S(1)} %slice_bitcast_fusion), channel_id=1, source_target_pairs={{0,2},{2,0},{4,6},{6,4},{1,3},{3,1},{5,7},{7,5},{8,10},{10,8},{12,... | collective-permute-start | bytes 270344 | tf_op jit(solution)/shard_map/ppermute | solution.py:327
  47.5 2.9 %collective-permute-start.15 = (bf16[352,128]{1,0:T(8,128)(2,1)S(1)}, bf16[352,128]{1,0:T(8,128)(2,1)S(1)}, u32[]{:S(2)}, u32[]{:S(2)}) collective-permute-start(bf16[352,128]{1,0:T(8,128)(2,1)S(1)} %slice_bitcast_fusion.1), channel_id=1, source_target_pairs={{0,2},{2,0},{4,6},{6,4},{1,3},{3,1},{5,7},{7,5},{8,10},{10,8},{12,... | collective-permute-start | bytes 270344 | tf_op jit(solution)/shard_map/ppermute | solution.py:327
  47.6 2.8 %collective-permute-start.14 = (bf16[352,128]{1,0:T(8,128)(2,1)S(1)}, bf16[352,128]{1,0:T(8,128)(2,1)S(1)}, u32[]{:S(2)}, u32[]{:S(2)}) collective-permute-start(bf16[352,128]{1,0:T(8,128)(2,1)S(1)} %slice_bitcast_fusion.2), channel_id=1, source_target_pairs={{0,2},{2,0},{4,6},{6,4},{1,3},{3,1},{5,7},{7,5},{8,10},{10,8},{12,... | collective-permute-start | bytes 270344 | tf_op jit(solution)/shard_map/ppermute | solution.py:327
  48.3 2.8 %collective-permute-start.13 = (bf16[352,128]{1,0:T(8,128)(2,1)S(1)}, bf16[352,128]{1,0:T(8,128)(2,1)S(1)}, u32[]{:S(2)}, u32[]{:S(2)}) collective-permute-start(bf16[352,128]{1,0:T(8,128)(2,1)S(1)} %get-tuple-element.66), channel_id=1, source_target_pairs={{0,2},{2,0},{4,6},{6,4},{1,3},{3,1},{5,7},{7,5},{8,10},{10,8},{12,... | collective-permute-start | bytes 270344 | tf_op jit(solution)/shard_map/ppermute | solution.py:327
  (6 other events, 19.6 us)
